TPU v7x, 512 devices: a whole 4x4x16 slice. The times are simulated.
512 devices in a mesh: ed: 64 (over y, z), tp: 8 (over x, core).
Axes of the slice: x: 4, y: 4, z: 16, core: 2. Of those that a mesh axis runs over, the one named last changes fastest.
Arguments:
- tokens: bfloat16 [8192, 2048], P('ed'), may hold values from -6 to 6
- cotangent: bfloat16 [8192, 2048], P('ed'), may hold values from -4 to 4
- expert_ids: int32 [8192, 2], P('ed'), may hold values from 0 to 3, all different within a row; in each aligned block of 128 rows (0 to 127, 128 to 255, ...) at most 80 rows name the same one
- route_weights: float32 [8192, 2], P('ed'), may hold values from 0.1 to 0.9
- w_gate: bfloat16 [8192, 7168], P('ed', 'tp'), may hold values from -0.125 to 0.125
- w_up: bfloat16 [8192, 7168], P('ed', 'tp'), may hold values from -0.125 to 0.125
- w_down: bfloat16 [7168, 8192], P('tp', 'ed'), may hold values from -0.0625 to 0.0625
Outputs:
- mixed: bfloat16 [8192, 2048], P('ed', 'tp')
- grad_tokens: bfloat16 [8192, 2048], P('ed', 'tp')
Inputs may be any that keep to these rules, and one draw needn't show every extreme that they name: `expert_ids`: the two experts of a token differ. Among the 128 tokens of one index of ed (aligned blocks), each expert is named by at most 80 tokens, and in some blocks one expert by exactly 80.
All inputs are finite; a program needn't handle non-finite values.
Results may differ from a plain program's by a relative error of at most 0.015.
Values may be sent and summed in bfloat16 or wider, within the bound.
A program may use at most 128 MiB of HBM per device.

v0:
```python
import jax
import jax.numpy as jnp
from jax import lax
from jax.sharding import PartitionSpec as P

EXPERTS = 4
TOP = 2
CAP = 80


def as_sent(shard):

    def short(part):
        return part.astype(jnp.bfloat16) if part.dtype == jnp.float32 else part

    return jax.tree.map(short, shard)


def from_partner(value, axis, distance):
    mask = 2**distance
    pairs = [(source, source ^ mask) for source in range(lax.axis_size(axis))]
    return lax.ppermute(value, axis, pairs)


def activate(gate_pre, up_pre, hidden_grad):
    sig_gate = jax.nn.sigmoid(gate_pre)
    silu_gate = gate_pre * sig_gate
    hidden = (silu_gate * up_pre).astype(jnp.bfloat16)
    gate_grad = (hidden_grad * up_pre * sig_gate * (1.0 + gate_pre * (1.0 - sig_gate))).astype(
        jnp.bfloat16
    )
    up_grad = (hidden_grad * silu_gate).astype(jnp.bfloat16)
    return (hidden, gate_grad, up_grad)


def order_block(lower_set, upper_set):
    return tuple(
        (jnp.concatenate([first, second], axis=0) for first, second in zip(lower_set, upper_set))
    )


def trade(pieces, bit_place):
    partner = jax.tree.map(
        lambda part, own: part.astype(own.dtype),
        from_partner(as_sent(pieces), "ed", bit_place),
        pieces,
    )
    upper_half = lax.axis_index("ed") // (1 << bit_place) % 2 == 1
    return (partner, upper_half)


def place_pieces(joiner, own_set, other_set, upper_half):
    return lax.cond(
        upper_half, lambda: joiner(other_set, own_set), lambda: joiner(own_set, other_set)
    )


def per_device(tokens, cotangent, expert_ids, route_weights, w_gate, w_up, w_down):
    ed_size = lax.axis_size("ed")
    member_count = ed_size // EXPERTS
    levels = member_count.bit_length() - 1
    share = CAP // member_count
    slot_count = EXPERTS * CAP
    tok_count = tokens.shape[0]
    model_width = tokens.shape[1]
    block_width = w_gate.shape[0]
    row_total = ed_size * share
    routes = expert_ids.reshape(-1)
    onehot = (routes[:, None] == jnp.arange(EXPERTS, dtype=jnp.int32)[None, :]).astype(jnp.int32)
    before = jnp.cumsum(onehot, axis=0) - onehot
    slot_place = jnp.sum(before * onehot, axis=1)
    target = routes * CAP + slot_place % member_count * share + slot_place // member_count
    matches = (jnp.arange(slot_count, dtype=jnp.int32)[:, None] == target[None, :]).reshape(
        slot_count, tok_count, TOP
    )
    picker = jnp.any(matches, axis=2)
    slot_weight = jnp.sum(
        jnp.where(matches, route_weights[None, :, :], jnp.float32(0.0)), axis=(1, 2)
    )
    picker_low = picker.astype(jnp.bfloat16)
    sent_tokens = jnp.dot(picker_low, tokens, preferred_element_type=jnp.float32)
    sent_tokens = sent_tokens.astype(jnp.bfloat16).reshape(ed_size, share, model_width)
    sent_cot = jnp.dot(picker_low, cotangent, preferred_element_type=jnp.float32)
    sent_cot = (
        (sent_cot * slot_weight[:, None]).astype(jnp.bfloat16).reshape(ed_size, share, model_width)
    )
    member_tokens, member_cot = (
        lax.all_to_all(sent_tokens, "ed", split_axis=0, concat_axis=0, tiled=True),
        lax.all_to_all(sent_cot, "ed", split_axis=0, concat_axis=0, tiled=True),
    )
    member_tokens = member_tokens.reshape(row_total, model_width)
    member_cot = member_cot.reshape(row_total, member_count, block_width)
    pieces = (w_gate[None], w_up[None], w_down[None])
    for bit_place in range(levels):
        partner, upper_half = trade(pieces, bit_place)
        pieces = place_pieces(order_block, pieces, partner, upper_half)
    gate_full = pieces[0].reshape(model_width, -1)
    up_full = pieces[1].reshape(model_width, -1)
    down_pieces = pieces[2]
    gate_pre = jnp.dot(member_tokens, gate_full, preferred_element_type=jnp.float32)
    up_pre = jnp.dot(member_tokens, up_full, preferred_element_type=jnp.float32)
    hidden_grad = lax.dot_general(
        member_cot, down_pieces, (((1, 2), (0, 2)), ((), ())), preferred_element_type=jnp.float32
    )
    hidden, gate_grad, up_grad = activate(gate_pre, up_pre, hidden_grad)
    out_part = lax.dot_general(
        hidden, down_pieces, (((1,), (1,)), ((), ())), preferred_element_type=jnp.float32
    )
    out_part = out_part.reshape(row_total, model_width)
    in_part = lax.dot_general(
        gate_grad, gate_full, (((1,), (1,)), ((), ())), preferred_element_type=jnp.float32
    )
    in_part = in_part + lax.dot_general(
        up_grad, up_full, (((1,), (1,)), ((), ())), preferred_element_type=jnp.float32
    )
    results = jnp.stack([out_part, in_part], axis=1)
    summed = lax.psum_scatter(results.astype(jnp.bfloat16), "tp", scatter_dimension=2, tiled=True)
    rounded = summed.reshape(ed_size, share, 2, -1)
    returned = lax.all_to_all(rounded, "ed", split_axis=0, concat_axis=0, tiled=True)
    returned = returned.reshape(slot_count, 2, -1).astype(jnp.float32)
    picker_full = picker.astype(jnp.float32)
    weighted = picker_full * slot_weight[:, None]
    mixed = jnp.dot(weighted.T, returned[:, 0], precision=lax.Precision.HIGHEST).astype(
        jnp.bfloat16
    )
    grad_tokens = jnp.dot(picker_full.T, returned[:, 1], precision=lax.Precision.HIGHEST).astype(
        jnp.bfloat16
    )
    return (mixed, grad_tokens)


def solution(mesh):
    return jax.shard_map(
        per_device,
        mesh=mesh,
        in_specs=(
            P("ed", None),
            P("ed", None),
            P("ed", None),
            P("ed", None),
            P("ed", "tp"),
            P("ed", "tp"),
            P("tp", "ed"),
        ),
        out_specs=(P("ed", "tp"), P("ed", "tp")),
        check_vma=False,
    )
```

profile of v0, /device:TPU:1, one launch (start us, length us, event | category | flops | bytes accessed | tf_op | source)
XLA Modules:
  0.0 1160.0 jit_solution(15797206400940934127)
XLA Ops:
  11.4 1.6 reshape.102
  13.1 19.4 %all-to-all-start = ((bf16[64,5,2048]{2,1,0:T(8,128)(2,1)}), bf16[64,5,2048]{2,1,0:T(8,128)(2,1)S(1)}, u32[]{:S(2)}, u32[]{:S(2)}) async-start(bf16[64,5,2048]{2,1,0:T(8,128)(2,1)} %reshape.102), calls=%async_computation | async-start | bytes 4194304 | tf_op jit(solution)/shard_map/all_to_all | solution.py:88
  32.6 1.6 fusion.1
  34.2 3.4 reshape.104
  37.6 89.5 %all-to-all-done = bf16[64,5,2048]{2,1,0:T(8,128)(2,1)S(1)} async-done(((bf16[64,5,2048]{2,1,0:T(8,128)(2,1)}), bf16[64,5,2048]{2,1,0:T(8,128)(2,1)S(1)}, u32[]{:S(2)}, u32[]{:S(2)}) %all-to-all-start) | async-done | bytes 1310752 | tf_op jit(solution)/shard_map/all_to_all | solution.py:88
  128.4 11.3 all-to-all-start.1
  139.8 2.8 collective-permute-start
  142.6 2.4 collective-permute-start.1
  145.1 2.8 collective-permute-start.2
  148.0 87.5 %collective-permute-done = bf16[1,128,896]{2,1,0:T(8,128)(2,1)S(1)} collective-permute-done((bf16[1,128,896]{2,1,0:T(8,128)(2,1)S(1)}, bf16[1,128,896]{2,1,0:T(8,128)(2,1)S(1)}, u32[]{:S(2)}, u32[]{:S(2)}) %collective-permute-start) | collective-permute-done | bytes 229408 | tf_op jit(solution)/shard_map/ppermute | solution.py:22
  235.5 4.8 collective-permute-done.1
  240.3 4.9 collective-permute-done.2
  245.4 3.9 collective-permute-start.3
  249.3 2.3 collective-permute-start.4
  251.6 3.9 collective-permute-start.5
  255.5 34.0 %collective-permute-done.3 = bf16[2,128,896]{2,1,0:T(8,128)(2,1)S(1)} collective-permute-done((bf16[2,128,896]{2,1,0:T(8,128)(2,1)S(1)}, bf16[2,128,896]{2,1,0:T(8,128)(2,1)S(1)}, u32[]{:S(2)}, u32[]{:S(2)}) %collective-permute-start.3) | collective-permute-done | bytes 458784 | tf_op jit(solution)/shard_map/ppermute | solution.py:22
  289.5 9.8 collective-permute-done.4
  299.3 9.8 collective-permute-done.5
  309.2 2.8 conditional.5
  312.0 7.0 collective-permute-start.6
  319.0 2.2 collective-permute-start.7
  321.2 7.0 collective-permute-start.8
  328.2 306.7 %collective-permute-done.6 = bf16[4,128,896]{2,1,0:T(8,128)(2,1)} collective-permute-done((bf16[4,128,896]{2,1,0:T(8,128)(2,1)S(1)}, bf16[4,128,896]{2,1,0:T(8,128)(2,1)}, u32[]{:S(2)}, u32[]{:S(2)}) %collective-permute-start.6) | collective-permute-done | bytes 917536 | tf_op jit(solution)/shard_map/ppermute | solution.py:22
  634.9 19.8 %collective-permute-done.7 = bf16[4,128,896]{2,1,0:T(8,128)(2,1)} collective-permute-done((bf16[4,128,896]{2,1,0:T(8,128)(2,1)S(1)}, bf16[4,128,896]{2,1,0:T(8,128)(2,1)}, u32[]{:S(2)}, u32[]{:S(2)}) %collective-permute-start.7) | collective-permute-done | bytes 917536 | tf_op jit(solution)/shard_map/ppermute | solution.py:22
  654.7 19.8 %collective-permute-done.8 = bf16[4,896,128]{2,1,0:T(8,128)(2,1)} collective-permute-done((bf16[4,896,128]{2,1,0:T(8,128)(2,1)S(1)}, bf16[4,896,128]{2,1,0:T(8,128)(2,1)}, u32[]{:S(2)}, u32[]{:S(2)}) %collective-permute-start.8) | collective-permute-done | bytes 917536 | tf_op jit(solution)/shard_map/ppermute | solution.py:22
  674.5 7.3 conditional.6
  675.8 3.5 pad_maximum_fusion.12
  679.3 2.6 pad_maximum_fusion.14
  681.9 10.9 collective-permute-start.10
  692.7 3.1 collective-permute-start.11
  695.9 10.9 collective-permute-start.9
  706.8 132.4 %collective-permute-done.10 = bf16[8,128,896]{2,1,0:T(8,128)(2,1)} collective-permute-done((bf16[8,128,896]{2,1,0:T(8,128)(2,1)S(1)}, bf16[8,128,896]{2,1,0:T(8,128)(2,1)}, u32[]{:S(2)}, u32[]{:S(2)}) %collective-permute-start.10) | collective-permute-done | bytes 1835040 | tf_op jit(solution)/shard_map/ppermute | solution.py:22
  839.2 39.5 %collective-permute-done.11 = bf16[8,128,896]{2,1,0:T(8,128)(2,1)} collective-permute-done((bf16[8,128,896]{2,1,0:T(8,128)(2,1)}, bf16[8,128,896]{2,1,0:T(8,128)(2,1)}, u32[]{:S(2)}, u32[]{:S(2)}) %collective-permute-start.11) | collective-permute-done | bytes 1835040 | tf_op jit(solution)/shard_map/ppermute | solution.py:22
  878.7 39.5 %collective-permute-done.9 = bf16[8,896,128]{2,1,0:T(8,128)(2,1)} collective-permute-done((bf16[8,896,128]{2,1,0:T(8,128)(2,1)}, bf16[8,896,128]{2,1,0:T(8,128)(2,1)}, u32[]{:S(2)}, u32[]{:S(2)}) %collective-permute-start.9) | collective-permute-done | bytes 1835040 | tf_op jit(solution)/shard_map/ppermute | solution.py:22
  918.2 9.3 conditional.7
  918.2 5.2 pad_maximum_fusion.19
  923.4 4.2 pad_maximum_fusion.18
  927.6 2.6 reshape.103
  930.1 3.5 fusion.30
  933.7 4.0 fusion.31
  937.7 4.0 convolution_convert_fusion.1
  943.2 3.3 reshape.105
  946.6 3.7 convolution_bitcast_fusion
  950.3 3.7 fusion.7
  954.0 3.8 fusion.2
  957.8 1.7 pad_maximum_fusion.24
  959.5 156.4 %reduce-scatter.2.cloned.1.call-done = bf16[320,2,256]{2,0,1:T(8,128)(2,1)} async-done(((bf16[320,2,2048]{2,0,1:T(8,128)(2,1)}), bf16[320,2,256]{2,0,1:T(8,128)(2,1)}) %reduce-scatter.2.cloned.1.call-update) | async-done | bytes 327696 | tf_op jit(solution)/shard_map/reduce_scatter | solution.py:117
  1117.3 33.5 %all_to_all.15 = bf16[64,5,2,256]{3,2,1,0:T(2,128)(2,1)S(1)} all-to-all(bf16[64,5,2,256]{3,2,1,0:T(2,128)(2,1)S(1)} %bitcast.55), channel_id=1, replica_groups=mesh['ed'=64,'tp'=8] {'ed'}, dimensions={0} | all-to-all | bytes 655360 | tf_op jit(solution)/shard_map/all_to_all | solution.py:119
  (72 shorter events, 15.3 us)
Async XLA Ops:
  7.2 3.8 copy-start
  13.1 19.4 %copy-start.24 = (f32[128,2]{0,1:T(2,128)S(1)}, f32[128,2]{0,1:T(2,128)}, u32[]{:S(2)}) copy-start(f32[128,2]{0,1:T(2,128)} %param.18) | copy-start | bytes 3076
  13.1 19.6 %copy-start.23 = (bf16[128,2048]{1,0:T(8,128)(2,1)S(1)}, bf16[128,2048]{1,0:T(8,128)(2,1)}, u32[]{:S(2)}) copy-start(bf16[128,2048]{1,0:T(8,128)(2,1)} %param.16) | copy-start | bytes 1572868
  13.1 114.1 %all-to-all-start = ((bf16[64,5,2048]{2,1,0:T(8,128)(2,1)}), bf16[64,5,2048]{2,1,0:T(8,128)(2,1)S(1)}, u32[]{:S(2)}, u32[]{:S(2)}) async-start(bf16[64,5,2048]{2,1,0:T(8,128)(2,1)} %reshape.102), calls=%async_computation | async-start | bytes 4194304 | tf_op jit(solution)/shard_map/all_to_all | solution.py:88
  37.6 102.2 %copy-start.20 = (bf16[128,896]{1,0:T(8,128)(2,1)S(1)}, bf16[128,896]{1,0:T(8,128)(2,1)}, u32[]{:S(2)}) copy-start(bf16[128,896]{1,0:T(8,128)(2,1)} %param.19) | copy-start | bytes 688132
  37.6 105.0 %copy-start.21 = (bf16[128,896]{1,0:T(8,128)(2,1)S(1)}, bf16[128,896]{1,0:T(8,128)(2,1)}, u32[]{:S(2)}) copy-start(bf16[128,896]{1,0:T(8,128)(2,1)} %param.20) | copy-start | bytes 688132
  37.6 107.5 %copy-start.22 = (bf16[896,128]{1,0:T(8,128)(2,1)S(1)}, bf16[896,128]{1,0:T(8,128)(2,1)}, u32[]{:S(2)}) copy-start(bf16[896,128]{1,0:T(8,128)(2,1)} %param.21) | copy-start | bytes 688132
  127.1 1.3 copy-start.1
  128.4 814.8 %all-to-all-start.1 = ((bf16[64,5,2048]{2,1,0:T(8,128)(2,1)}), bf16[64,5,2048]{2,1,0:T(8,128)(2,1)}, u32[]{:S(2)}, u32[]{:S(2)}) async-start(bf16[64,5,2048]{2,1,0:T(8,128)(2,1)} %reshape.104), calls=%async_computation.1 | async-start | bytes 4194304 | tf_op jit(solution)/shard_map/all_to_all | solution.py:89
  139.7 976.2 %reduce-scatter.2.cloned.1.call-start = ((), (), s32[]{:S(2)}) async-start(), calls=%async_computation.4 | async-start | bytes 2949120 | tf_op jit(solution)/shard_map/reduce_scatter | solution.py:117
  139.8 95.7 %collective-permute-start = (bf16[1,128,896]{2,1,0:T(8,128)(2,1)S(1)}, bf16[1,128,896]{2,1,0:T(8,128)(2,1)S(1)}, u32[]{:S(2)}, u32[]{:S(2)}) collective-permute-start(bf16[1,128,896]{2,1,0:T(8,128)(2,1)S(1)} %bitcast.56), channel_id=1, source_target_pairs={{0,8},{8,0},{16,24},{24,16},{32,40},{40,32},{48,56},{56,48},{64,72... | collective-permute-start | bytes 688136 | tf_op jit(solution)/shard_map/ppermute | solution.py:22
  142.6 97.7 %collective-permute-start.1 = (bf16[1,128,896]{2,1,0:T(8,128)(2,1)S(1)}, bf16[1,128,896]{2,1,0:T(8,128)(2,1)S(1)}, u32[]{:S(2)}, u32[]{:S(2)}) collective-permute-start(bf16[1,128,896]{2,1,0:T(8,128)(2,1)S(1)} %bitcast.59), channel_id=1, source_target_pairs={{0,8},{8,0},{16,24},{24,16},{32,40},{40,32},{48,56},{56,48},{64,72... | collective-permute-start | bytes 688136 | tf_op jit(solution)/shard_map/ppermute | solution.py:22
  145.1 100.1 %collective-permute-start.2 = (bf16[1,896,128]{2,1,0:T(8,128)(2,1)S(1)}, bf16[1,896,128]{2,1,0:T(8,128)(2,1)S(1)}, u32[]{:S(2)}, u32[]{:S(2)}) collective-permute-start(bf16[1,896,128]{2,1,0:T(8,128)(2,1)S(1)} %bitcast.62), channel_id=1, source_target_pairs={{0,8},{8,0},{16,24},{24,16},{32,40},{40,32},{48,56},{56,48},{64,72... | collective-permute-start | bytes 688136 | tf_op jit(solution)/shard_map/ppermute | solution.py:22
  245.4 44.1 %collective-permute-start.3 = (bf16[2,128,896]{2,1,0:T(8,128)(2,1)S(1)}, bf16[2,128,896]{2,1,0:T(8,128)(2,1)S(1)}, u32[]{:S(2)}, u32[]{:S(2)}) collective-permute-start(bf16[2,128,896]{2,1,0:T(8,128)(2,1)S(1)} %get-tuple-element.160), channel_id=1, source_target_pairs={{0,16},{8,24},{16,0},{24,8},{32,48},{40,56},{48,32},{56,40},{64,80... | collective-permute-start | bytes 1376264 | tf_op jit(solution)/shard_map/ppermute | solution.py:22
  249.3 50.0 %collective-permute-start.4 = (bf16[2,128,896]{2,1,0:T(8,128)(2,1)S(1)}, bf16[2,128,896]{2,1,0:T(8,128)(2,1)S(1)}, u32[]{:S(2)}, u32[]{:S(2)}) collective-permute-start(bf16[2,128,896]{2,1,0:T(8,128)(2,1)S(1)} %get-tuple-element.161), channel_id=1, source_target_pairs={{0,16},{8,24},{16,0},{24,8},{32,48},{40,56},{48,32},{56,40},{64,80... | collective-permute-start | bytes 1376264 | tf_op jit(solution)/shard_map/ppermute | solution.py:22
  251.6 57.6 %collective-permute-start.5 = (bf16[2,896,128]{2,1,0:T(8,128)(2,1)S(1)}, bf16[2,896,128]{2,1,0:T(8,128)(2,1)S(1)}, u32[]{:S(2)}, u32[]{:S(2)}) collective-permute-start(bf16[2,896,128]{2,1,0:T(8,128)(2,1)S(1)} %get-tuple-element.162), channel_id=1, source_target_pairs={{0,16},{8,24},{16,0},{24,8},{32,48},{40,56},{48,32},{56,40},{64,80... | collective-permute-start | bytes 1376264 | tf_op jit(solution)/shard_map/ppermute | solution.py:22
  309.2 0.8 copy-start.8
  309.2 0.9 copy-start.12
  309.2 1.1 copy-start.14
  309.2 1.3 copy-start.16
  310.4 1.4 copy-start.9
  310.4 1.4 copy-start.17
  312.0 322.9 %collective-permute-start.6 = (bf16[4,128,896]{2,1,0:T(8,128)(2,1)S(1)}, bf16[4,128,896]{2,1,0:T(8,128)(2,1)}, u32[]{:S(2)}, u32[]{:S(2)}) collective-permute-start(bf16[4,128,896]{2,1,0:T(8,128)(2,1)S(1)} %get-tuple-element.163), channel_id=1, source_target_pairs={{0,32},{8,40},{16,48},{24,56},{32,0},{40,8},{48,16},{56,24},{64,96... | collective-permute-start | bytes 2752520 | tf_op jit(solution)/shard_map/ppermute | solution.py:22
  319.0 335.7 %collective-permute-start.7 = (bf16[4,128,896]{2,1,0:T(8,128)(2,1)S(1)}, bf16[4,128,896]{2,1,0:T(8,128)(2,1)}, u32[]{:S(2)}, u32[]{:S(2)}) collective-permute-start(bf16[4,128,896]{2,1,0:T(8,128)(2,1)S(1)} %get-tuple-element.164), channel_id=1, source_target_pairs={{0,32},{8,40},{16,48},{24,56},{32,0},{40,8},{48,16},{56,24},{64,96... | collective-permute-start | bytes 2752520 | tf_op jit(solution)/shard_map/ppermute | solution.py:22
  321.2 353.4 %collective-permute-start.8 = (bf16[4,896,128]{2,1,0:T(8,128)(2,1)S(1)}, bf16[4,896,128]{2,1,0:T(8,128)(2,1)}, u32[]{:S(2)}, u32[]{:S(2)}) collective-permute-start(bf16[4,896,128]{2,1,0:T(8,128)(2,1)S(1)} %get-tuple-element.165), channel_id=1, source_target_pairs={{0,32},{8,40},{16,48},{24,56},{32,0},{40,8},{48,16},{56,24},{64,96... | collective-permute-start | bytes 2752520 | tf_op jit(solution)/shard_map/ppermute | solution.py:22
  674.5 0.9 copy-start.2
  674.5 1.2 copy-start.4
  675.8 3.5 copy-start.5
  681.9 157.4 %collective-permute-start.10 = (bf16[8,128,896]{2,1,0:T(8,128)(2,1)S(1)}, bf16[8,128,896]{2,1,0:T(8,128)(2,1)}, u32[]{:S(2)}, u32[]{:S(2)}) collective-permute-start(bf16[8,128,896]{2,1,0:T(8,128)(2,1)S(1)} %get-tuple-element.167), channel_id=1, source_target_pairs={{0,64},{8,72},{16,80},{24,88},{32,96},{40,104},{48,112},{56,120},{... | collective-permute-start | bytes 5505032 | tf_op jit(solution)/shard_map/ppermute | solution.py:22
  692.7 186.0 %collective-permute-start.11 = (bf16[8,128,896]{2,1,0:T(8,128)(2,1)}, bf16[8,128,896]{2,1,0:T(8,128)(2,1)}, u32[]{:S(2)}, u32[]{:S(2)}) collective-permute-start(bf16[8,128,896]{2,1,0:T(8,128)(2,1)} %get-tuple-element.168), channel_id=1, source_target_pairs={{0,64},{8,72},{16,80},{24,88},{32,96},{40,104},{48,112},{56,120},{... | collective-permute-start | bytes 5505032 | tf_op jit(solution)/shard_map/ppermute | solution.py:22
  695.9 222.3 %collective-permute-start.9 = (bf16[8,896,128]{2,1,0:T(8,128)(2,1)}, bf16[8,896,128]{2,1,0:T(8,128)(2,1)}, u32[]{:S(2)}, u32[]{:S(2)}) collective-permute-start(bf16[8,896,128]{2,1,0:T(8,128)(2,1)} %get-tuple-element.166), channel_id=1, source_target_pairs={{0,64},{8,72},{16,80},{24,88},{32,96},{40,104},{48,112},{56,120},{... | collective-permute-start | bytes 5505032 | tf_op jit(solution)/shard_map/ppermute | solution.py:22
  933.7 4.0 copy-start.25
  937.7 4.1 copy-start.27
  946.5 3.7 copy-start.26
  950.3 3.7 copy-start.28
Sparse Core Ops, SparseCore 0:
  959.6 156.2 reduce-scatter.1
where the time goes:
time: 1170 us; the launch traced here: 1160 us
  waiting for transfers between devices  955 us (82%)
  starting transfers between devices  90 us (8%)
  blocking collectives  33.5 us (3%)
  matrix products  26.7 us (2%)
  other arithmetic  21.1 us (2%)
  local copies, waits for them, and re-layouts  19.6 us (2%)
  between operations  14.5 us (1%)
    ppermute x12, waiting for transfers between devices, from_partner(): return lax.ppermute(value, axis, pairs)  709 us
    reduce_scatter x1, waiting for transfers between devices, per_device(): lax.psum_scatter(results.astype(jnp.bfloat16), 'tp', scatter_dimension=2,...  156 us
    all_to_all x1, waiting for transfers between devices, per_device(): lax.all_to_all(sent_tokens, 'ed', split_axis=0, concat_axis=0, tiled=True)  89.5 us
    ppermute x12, starting transfers between devices, from_partner(): return lax.ppermute(value, axis, pairs)  59.3 us
    all_to_all x1, blocking collectives, per_device(): lax.all_to_all(rounded, 'ed', split_axis=0, concat_axis=0, tiled=True)  33.5 us
  transfers between devices with their start and end apart: 15, of which 14 were waited for; matrix products, arithmetic and copies ran while one was open for 3% of the time, Pallas kernels for 0%

commit v1 on v0

v1 whole, which is shorter than its diff:
```python
import jax
import jax.numpy as jnp
import numpy as np
from jax import lax
from jax.sharding import Mesh
from jax.sharding import PartitionSpec as P

EXPERTS = 4
TOP = 2
CAP = 80


def activate(gate_pre, up_pre, hidden_grad):
    sig_gate = jax.nn.sigmoid(gate_pre)
    silu_gate = gate_pre * sig_gate
    hidden = (silu_gate * up_pre).astype(jnp.bfloat16)
    gate_grad = (hidden_grad * up_pre * sig_gate * (1.0 + gate_pre * (1.0 - sig_gate))).astype(
        jnp.bfloat16
    )
    up_grad = (hidden_grad * silu_gate).astype(jnp.bfloat16)
    return (hidden, gate_grad, up_grad)


def per_device(tokens, cotangent, expert_ids, route_weights, w_gate, w_up, w_down):
    plane_count = lax.axis_size("ey")
    slot_count = EXPERTS * CAP
    tok_count = tokens.shape[0]
    model_width = tokens.shape[1]
    routes = expert_ids.reshape(-1)
    onehot = (routes[:, None] == jnp.arange(EXPERTS, dtype=jnp.int32)[None, :]).astype(jnp.int32)
    before = jnp.cumsum(onehot, axis=0) - onehot
    slot_place = jnp.sum(before * onehot, axis=1)
    target = routes * CAP + slot_place
    matches = (jnp.arange(slot_count, dtype=jnp.int32)[:, None] == target[None, :]).reshape(
        slot_count, tok_count, TOP
    )
    picker = jnp.any(matches, axis=2)
    slot_weight = jnp.sum(
        jnp.where(matches, route_weights[None, :, :], jnp.float32(0.0)), axis=(1, 2)
    )
    picker_low = picker.astype(jnp.bfloat16)
    sent_tokens = jnp.dot(picker_low, tokens, preferred_element_type=jnp.float32)
    sent_tokens = sent_tokens.astype(jnp.bfloat16).reshape(plane_count, CAP, model_width)
    sent_cot = jnp.dot(picker_low, cotangent, preferred_element_type=jnp.float32)
    sent_cot = (
        (sent_cot * slot_weight[:, None]).astype(jnp.bfloat16).reshape(plane_count, CAP, model_width)
    )
    gate_full = lax.all_gather(w_gate, "ez", axis=0, tiled=True)
    up_full = lax.all_gather(w_up, "ez", axis=0, tiled=True)
    down_pieces = lax.all_gather(w_down, "ez", axis=0, tiled=False)
    member_tokens = lax.all_to_all(sent_tokens, "ey", split_axis=0, concat_axis=0, tiled=True)
    member_cot = lax.all_to_all(sent_cot, "ey", split_axis=0, concat_axis=0, tiled=True)
    row_total = plane_count * CAP
    member_count = down_pieces.shape[0]
    block_width = down_pieces.shape[2]
    member_tokens = member_tokens.reshape(row_total, model_width)
    member_cot = member_cot.reshape(row_total, member_count, block_width)
    gate_pre = jnp.dot(member_tokens, gate_full, preferred_element_type=jnp.float32)
    up_pre = jnp.dot(member_tokens, up_full, preferred_element_type=jnp.float32)
    hidden_grad = lax.dot_general(
        member_cot, down_pieces, (((1, 2), (0, 2)), ((), ())), preferred_element_type=jnp.float32
    )
    hidden, gate_grad, up_grad = activate(gate_pre, up_pre, hidden_grad)
    out_part = lax.dot_general(
        hidden, down_pieces, (((1,), (1,)), ((), ())), preferred_element_type=jnp.float32
    )
    out_part = out_part.reshape(row_total, model_width)
    in_part = lax.dot_general(
        gate_grad, gate_full, (((1,), (1,)), ((), ())), preferred_element_type=jnp.float32
    )
    in_part = in_part + lax.dot_general(
        up_grad, up_full, (((1,), (1,)), ((), ())), preferred_element_type=jnp.float32
    )
    results = jnp.stack([out_part, in_part], axis=1)
    summed = lax.psum_scatter(results.astype(jnp.bfloat16), "tp", scatter_dimension=2, tiled=True)
    rounded = summed.reshape(plane_count, CAP, 2, -1)
    returned = lax.all_to_all(rounded, "ey", split_axis=0, concat_axis=0, tiled=True)
    returned = returned.reshape(slot_count, 2, -1).astype(jnp.float32)
    picker_full = picker.astype(jnp.float32)
    weighted = picker_full * slot_weight[:, None]
    mixed = jnp.dot(weighted.T, returned[:, 0], precision=lax.Precision.HIGHEST).astype(
        jnp.bfloat16
    )
    grad_tokens = jnp.dot(picker_full.T, returned[:, 1], precision=lax.Precision.HIGHEST).astype(
        jnp.bfloat16
    )
    return (mixed, grad_tokens)


def solution(mesh):
    ed_size = mesh.shape["ed"]
    member_count = ed_size // EXPERTS
    devices = np.asarray(mesh.devices).reshape(EXPERTS, member_count, mesh.shape["tp"])
    split_mesh = Mesh(devices, ("ey", "ez", "tp"))
    ed = ("ey", "ez")
    return jax.shard_map(
        per_device,
        mesh=split_mesh,
        in_specs=(
            P(ed, None),
            P(ed, None),
            P(ed, None),
            P(ed, None),
            P(ed, "tp"),
            P(ed, "tp"),
            P("tp", ed),
        ),
        out_specs=(P(ed, "tp"), P(ed, "tp")),
        check_vma=False,
    )
```

time: 1170 us -> 319 us (0.27)
  waiting for transfers between devices: 955 us -> 248 us
  starting transfers between devices: 90 us -> 8.83 us
  blocking collectives: 33.5 us -> 8.68 us
  other arithmetic: 21.1 us -> 4.69 us
  local copies, waits for them, and re-layouts: 19.6 us -> 5.49 us
    ppermute x12 -> x0, waiting for transfers between devices: 709 us -> none  [from_partner(): return lax.ppermute(value, axis, pairs)]
    all_gather x0 -> x3, waiting for transfers between devices: none -> 188 us  [the longest x1 72.4 us: per_device(): up_full = lax.all_gather(w_up, 'ez', axis=0, tiled=True)]
    reduce_scatter x1, waiting for transfers between devices: 156 us -> 47.2 us  [per_device(): lax.psum_scatter(results.astype(jnp.bfloat16), 'tp', scatter_dimension=2,...]
    all_to_all x2, waiting for transfers between devices: 89.5 us -> 10.8 us  [the longest x1 10.8 us: per_device(): lax.all_to_all(sent_cot, 'ey', split_axis=0, concat_axis=0, tiled=True)]
    ppermute x12 -> x0, starting transfers between devices: 59.3 us -> none  [from_partner(): return lax.ppermute(value, axis, pairs)]
    all_to_all x1, blocking collectives: 33.5 us -> 8.68 us  [per_device(): lax.all_to_all(rounded, 'ey', split_axis=0, concat_axis=0, tiled=True)]
    all_to_all x2, starting transfers between devices: 30.7 us -> 8.67 us  [the longest x1 5.13 us: per_device(): lax.all_to_all(sent_cot, 'ey', split_axis=0, concat_axis=0, tiled=True)]
    concatenate x8 -> x0, other arithmetic: 17.1 us -> none  [order_block(): jnp.concatenate([first, second], axis=0)]
  transfers between devices with their start and end apart: 15 -> 6, of which waited for: 14 -> 5; matrix products, arithmetic and copies ran while one was open for 3% -> 6% of each run, Pallas kernels for 0% -> 0%
where the time goes in v1:
time: 319 us; the launch traced here: 316 us
  waiting for transfers between devices  248 us (78%)
  matrix products  25.5 us (8%)
  between operations  14 us (4%)
  starting transfers between devices  8.83 us (3%)
  blocking collectives  8.68 us (3%)
  local copies, waits for them, and re-layouts  5.49 us (2%)
  other arithmetic  4.69 us (1%)
    all_gather x1, waiting for transfers between devices, per_device(): up_full = lax.all_gather(w_up, 'ez', axis=0, tiled=True)  72.4 us
    all_gather x1, waiting for transfers between devices, per_device(): gate_full = lax.all_gather(w_gate, 'ez', axis=0, tiled=True)  70.7 us
    reduce_scatter x1, waiting for transfers between devices, per_device(): lax.psum_scatter(results.astype(jnp.bfloat16), 'tp', scatter_dimension=2,...  47.2 us
    all_gather x1, waiting for transfers between devices, per_device(): down_pieces = lax.all_gather(w_down, 'ez', axis=0, tiled=False)  45.2 us
    all_to_all x1, waiting for transfers between devices, per_device(): lax.all_to_all(sent_cot, 'ey', split_axis=0, concat_axis=0, tiled=True)  10.8 us
    all_to_all x1, blocking collectives, per_device(): lax.all_to_all(rounded, 'ey', split_axis=0, concat_axis=0, tiled=True)  8.68 us
  transfers between devices with their start and end apart: 6, of which 5 were waited for; matrix products, arithmetic and copies ran while one was open for 6% of the time, Pallas kernels for 0%

profile of v1, /device:TPU:1, one launch (start us, length us, event | category | flops | bytes accessed | tf_op | source)
XLA Modules:
  0.0 315.6 jit_solution(16984197880702710667)
XLA Ops:
  7.2 0.0 copy-start
  7.2 0.0 all-gather.9.cloned.1.call-start
  7.2 0.7 all-gather.9.cloned.1.call-update
  7.9 0.0 all-gather.5.cloned.1.call-start
  8.0 0.7 all-gather.5.cloned.1.call-update
  8.7 0.0 all-gather.7.cloned.1.call-start
  8.7 0.7 all-gather.7.cloned.1.call-update
  9.4 0.8 copy.54
  10.2 0.1 eq.44
  10.3 0.1 eq.40
  10.5 1.2 reduce-window.6
  11.7 0.1 slice.16
  11.8 0.1 copy.56
  11.9 0.1 copy.57
  12.0 0.1 add_bitcast_fusion
  12.1 0.1 reduce_sum.21
  12.3 0.1 copy.58
  12.3 0.7 multiply_add_fusion
  13.1 0.8 select_reduce_fusion
  13.9 1.6 fusion.1
  15.6 5.1 %all-to-all-start.1 = ((bf16[4,80,2048]{2,1,0:T(8,128)(2,1)}), bf16[4,80,2048]{2,1,0:T(8,128)(2,1)S(1)}, u32[]{:S(2)}, u32[]{:S(2)}) async-start(bf16[4,80,2048]{2,1,0:T(8,128)(2,1)} %bitcast.6), calls=%async_computation.1 | async-start | bytes 2621440 | tf_op jit(solution)/shard_map/all_to_all | solution.py:52
  20.7 1.5 convolution_convert_fusion
  22.2 10.8 %all-to-all-done.1 = bf16[4,80,2048]{2,1,0:T(8,128)(2,1)S(1)} async-done(((bf16[4,80,2048]{2,1,0:T(8,128)(2,1)}), bf16[4,80,2048]{2,1,0:T(8,128)(2,1)S(1)}, u32[]{:S(2)}, u32[]{:S(2)}) %all-to-all-start.1) | async-done | bytes 1310752 | tf_op jit(solution)/shard_map/all_to_all | solution.py:52
  33.1 3.5 %all-to-all-start = ((bf16[4,80,2048]{2,1,0:T(8,128)(2,1)}), bf16[4,80,2048]{2,1,0:T(8,128)(2,1)S(1)}, u32[]{:S(2)}, u32[]{:S(2)}) async-start(bf16[4,80,2048]{2,1,0:T(8,128)(2,1)} %bitcast.2), calls=%async_computation | async-start | bytes 2621440 | tf_op jit(solution)/shard_map/all_to_all | solution.py:51
  36.6 0.0 reduce-scatter.2.cloned.1.call-start
  36.7 1.4 copy.64
  38.1 45.2 %all-gather.9.cloned.1.call-done = bf16[14336,128]{1,0:T(8,128)(2,1)} async-done(((bf16[896,128]{1,0:T(8,128)(2,1)}), bf16[14336,128]{1,0:T(8,128)(2,1)}) %all-gather.9.cloned.1.call-update) | async-done | bytes 3670032 | tf_op jit(solution)/shard_map/all_gather | solution.py:50
  83.3 5.0 %convolution_bitcast_fusion = f32[320,896]{1,0:T(8,128)} fusion(bf16[16,896,128]{2,1,0:T(8,128)(2,1)} %bitcast.62, bf16[320,16,128]{2,1,0:T(8,128)(2,1)} %bitcast.57), kind=kOutput, calls=%fused_computation.8 | convolution fusion | flops 1174405120 | bytes 6127616 | tf_op jit(solution)/shard_map/dot_general | solution.py:60
  88.3 0.0 all-to-all-done
  88.3 70.7 %all-gather.5.cloned.1.call-done = bf16[2048,896]{1,0:T(8,128)(2,1)} async-done(((bf16[128,896]{1,0:T(8,128)(2,1)}), bf16[2048,896]{1,0:T(8,128)(2,1)}) %all-gather.5.cloned.1.call-update) | async-done | bytes 3670032 | tf_op jit(solution)/shard_map/all_gather | solution.py:48
  159.0 3.6 %fusion.22 = f32[320,896]{1,0:T(8,128)S(1)} fusion(bf16[320,2048]{1,0:T(8,128)(2,1)S(1)} %bitcast.55, bf16[2048,896]{1,0:T(8,128)(2,1)} %all-gather.5.cloned.1.call-done), kind=kOutput, calls=%fused_computation.40 | convolution fusion | flops 1174405120 | bytes 6127616 | tf_op jit(solution)/shard_map/dot_general | solution.py:58
  162.6 72.4 %all-gather.7.cloned.1.call-done = bf16[2048,896]{1,0:T(8,128)(2,1)} async-done(((bf16[128,896]{1,0:T(8,128)(2,1)}), bf16[2048,896]{1,0:T(8,128)(2,1)}) %all-gather.7.cloned.1.call-update) | async-done | bytes 3670032 | tf_op jit(solution)/shard_map/all_gather | solution.py:49
  235.0 3.7 %fusion.23 = f32[320,896]{1,0:T(8,128)S(1)} fusion(bf16[320,2048]{1,0:T(8,128)(2,1)S(1)} %bitcast.56, bf16[2048,896]{1,0:T(8,128)(2,1)} %all-gather.7.cloned.1.call-done), kind=kOutput, calls=%fused_computation.41 | convolution fusion | flops 1174405120 | bytes 6127616 | tf_op jit(solution)/shard_map/dot_general | solution.py:59
  238.7 0.0 copy-done.4
  238.7 0.0 copy-done.2
  238.7 0.0 copy-start.6
  238.8 1.6 convolution_convert_fusion.1
  240.4 0.8 copy.59
  241.2 0.6 stack_reshape.4
  241.9 4.9 %fusion.7 = f32[320,2048]{1,0:T(8,128)S(1)} fusion(bf16[2048,896]{1,0:T(8,128)(2,1)} %all-gather.5.cloned.1.call-done, f32[320,896]{1,0:T(8,128)} %copy-done.4, f32[320,896]{1,0:T(8,128)} %convolution_bitcast_fusion, f32[320,896]{1,0:T(8,128)} %copy-done.6), kind=kOutput, calls=%fused_computation.18 | convolution fusion | flops 1177272320 | bytes 9732096 | tf_op jit(solution)/shard_map/dot_general | solution.py:68
  246.8 1.6 fusion.2
  248.4 1.8 pad_maximum_fusion
  250.1 0.0 reduce-scatter.2.cloned.1.call-update
  250.2 47.2 %reduce-scatter.2.cloned.1.call-done = bf16[320,2,256]{2,0,1:T(8,128)(2,1)} async-done(((bf16[320,2,2048]{2,0,1:T(8,128)(2,1)}), bf16[320,2,256]{2,0,1:T(8,128)(2,1)}) %reduce-scatter.2.cloned.1.call-update) | async-done | bytes 327696 | tf_op jit(solution)/shard_map/reduce_scatter | solution.py:75
  297.4 1.0 copy.61
  298.4 8.7 %all_to_all.15 = bf16[4,80,2,256]{3,1,2,0:T(8,128)(2,1)S(1)} all-to-all(bf16[4,80,2,256]{3,1,2,0:T(8,128)(2,1)S(1)} %copy.61), channel_id=1, replica_groups=mesh['ey'=4,'ez'=16,'tp'=8] {'ey'}, dimensions={0} | all-to-all | bytes 655360 | tf_op jit(solution)/shard_map/all_to_all | solution.py:77
  307.1 1.1 convolution_convert_fusion.3
  308.2 0.9 convolution_convert_fusion.2
  (18 shorter events, 0.2 us)
Async XLA Ops:
  7.2 6.7 %copy-start = (bf16[128,2048]{1,0:T(8,128)(2,1)S(1)}, bf16[128,2048]{1,0:T(8,128)(2,1)}, u32[]{:S(2)}) copy-start(bf16[128,2048]{1,0:T(8,128)(2,1)} %param.8) | copy-start | bytes 1572868
  7.2 76.1 %all-gather.9.cloned.1.call-start = ((), (), s32[]{:S(2)}) async-start(), calls=%async_computation.7 | async-start | bytes 3899392 | tf_op jit(solution)/shard_map/all_gather | solution.py:50
  7.9 151.1 %all-gather.5.cloned.1.call-start = ((), (), s32[]{:S(2)}) async-start(), calls=%async_computation.4 | async-start | bytes 3899392 | tf_op jit(solution)/shard_map/all_gather | solution.py:48
  8.7 226.3 %all-gather.7.cloned.1.call-start = ((), (), s32[]{:S(2)}) async-start(), calls=%async_computation.5 | async-start | bytes 3899392 | tf_op jit(solution)/shard_map/all_gather | solution.py:49
  15.6 5.1 %copy-start.1 = (bf16[128,2048]{1,0:T(8,128)(2,1)S(1)}, bf16[128,2048]{1,0:T(8,128)(2,1)}, u32[]{:S(2)}) copy-start(bf16[128,2048]{1,0:T(8,128)(2,1)} %param.7) | copy-start | bytes 1572868
  15.6 17.5 %all-to-all-start.1 = ((bf16[4,80,2048]{2,1,0:T(8,128)(2,1)}), bf16[4,80,2048]{2,1,0:T(8,128)(2,1)S(1)}, u32[]{:S(2)}, u32[]{:S(2)}) async-start(bf16[4,80,2048]{2,1,0:T(8,128)(2,1)} %bitcast.6), calls=%async_computation.1 | async-start | bytes 2621440 | tf_op jit(solution)/shard_map/all_to_all | solution.py:52
  33.1 55.3 %all-to-all-start = ((bf16[4,80,2048]{2,1,0:T(8,128)(2,1)}), bf16[4,80,2048]{2,1,0:T(8,128)(2,1)S(1)}, u32[]{:S(2)}, u32[]{:S(2)}) async-start(bf16[4,80,2048]{2,1,0:T(8,128)(2,1)} %bitcast.2), calls=%async_computation | async-start | bytes 2621440 | tf_op jit(solution)/shard_map/all_to_all | solution.py:51
  36.6 260.8 %reduce-scatter.2.cloned.1.call-start = ((), (), s32[]{:S(2)}) async-start(), calls=%async_computation.6 | async-start | bytes 2949120 | tf_op jit(solution)/shard_map/reduce_scatter | solution.py:75
  162.6 76.1 %copy-start.4 = (f32[320,896]{1,0:T(8,128)}, f32[320,896]{1,0:T(8,128)S(1)}, u32[]{:S(2)}) copy-start(f32[320,896]{1,0:T(8,128)S(1)} %fusion.22) | copy-start | bytes 3440644
  235.0 3.7 %copy-start.2 = (bf16[14336,128]{1,0:T(8,128)(2,1)S(1)}, bf16[14336,128]{1,0:T(8,128)(2,1)}, u32[]{:S(2)}) copy-start(bf16[14336,128]{1,0:T(8,128)(2,1)} %all-gather.9.cloned.1.call-done) | copy-start | bytes 11010052
  238.7 1.6 copy-start.6
  241.8 4.9 %copy-start.3 = (bf16[2048,896]{1,0:T(8,128)(2,1)S(1)}, bf16[2048,896]{1,0:T(8,128)(2,1)}, u32[]{:S(2)}) copy-start(bf16[2048,896]{1,0:T(8,128)(2,1)} %all-gather.7.cloned.1.call-done) | copy-start | bytes 11010052
  241.9 4.9 %copy-start.5 = (f32[320,896]{1,0:T(8,128)S(1)}, f32[320,896]{1,0:T(8,128)}, u32[]{:S(2)}) copy-start(f32[320,896]{1,0:T(8,128)} %copy-done.4) | copy-start | bytes 3440644
  241.9 4.9 %copy-start.7 = (f32[320,896]{1,0:T(8,128)S(1)}, f32[320,896]{1,0:T(8,128)}, u32[]{:S(2)}) copy-start(f32[320,896]{1,0:T(8,128)} %convolution_bitcast_fusion) | copy-start | bytes 3440644
Sparse Core Ops, SparseCore 0:
  10.1 73.2 all-gather.8
  85.4 73.5 all-gather.4
  161.1 73.8 all-gather.6
  250.3 47.0 reduce-scatter.1

commit v2 on v1

--- a/solution.py
+++ b/solution.py
@@ -45,26 +45,44 @@
     sent_cot = (
         (sent_cot * slot_weight[:, None]).astype(jnp.bfloat16).reshape(plane_count, CAP, model_width)
     )
-    gate_full = lax.all_gather(w_gate, "ez", axis=0, tiled=True)
-    up_full = lax.all_gather(w_up, "ez", axis=0, tiled=True)
-    down_pieces = lax.all_gather(w_down, "ez", axis=0, tiled=False)
+    member_count = lax.axis_size("ez")
+    place = lax.axis_index("ez")
+    block_width = w_gate.shape[0]
+    stacked = jnp.stack([w_gate, w_up, w_down.T], axis=0)
+    forward = [(i, (i + 1) % member_count) for i in range(member_count)]
+    backward = [(i, (i - 1) % member_count) for i in range(member_count)]
+    half_steps = member_count // 2
+    cw = stacked
+    ccw = stacked
+    by_distance = [None] * member_count
+    by_distance[0] = stacked
+    for step in range(1, half_steps):
+        cw = lax.ppermute(cw, "ez", forward)
+        ccw = lax.ppermute(ccw, "ez", backward)
+        by_distance[step] = cw
+        by_distance[member_count - step] = ccw
+    cut = block_width // 2
+    far_low = lax.ppermute(cw[:, :cut], "ez", forward)
+    far_high = lax.ppermute(ccw[:, cut:], "ez", backward)
+    by_distance[half_steps] = jnp.concatenate([far_low, far_high], axis=1)
+    gathered = jnp.stack(by_distance, axis=0)
+    origin = (place - jnp.arange(member_count, dtype=jnp.int32)) % member_count
+    gathered = jnp.take(gathered, origin, axis=0)
+    gate_full = gathered[:, 0].reshape(member_count * block_width, -1)
+    up_full = gathered[:, 1].reshape(member_count * block_width, -1)
+    down_full = gathered[:, 2].reshape(member_count * block_width, -1)
     member_tokens = lax.all_to_all(sent_tokens, "ey", split_axis=0, concat_axis=0, tiled=True)
     member_cot = lax.all_to_all(sent_cot, "ey", split_axis=0, concat_axis=0, tiled=True)
     row_total = plane_count * CAP
-    member_count = down_pieces.shape[0]
-    block_width = down_pieces.shape[2]
     member_tokens = member_tokens.reshape(row_total, model_width)
-    member_cot = member_cot.reshape(row_total, member_count, block_width)
+    member_cot = member_cot.reshape(row_total, model_width)
     gate_pre = jnp.dot(member_tokens, gate_full, preferred_element_type=jnp.float32)
     up_pre = jnp.dot(member_tokens, up_full, preferred_element_type=jnp.float32)
-    hidden_grad = lax.dot_general(
-        member_cot, down_pieces, (((1, 2), (0, 2)), ((), ())), preferred_element_type=jnp.float32
-    )
+    hidden_grad = jnp.dot(member_cot, down_full, preferred_element_type=jnp.float32)
     hidden, gate_grad, up_grad = activate(gate_pre, up_pre, hidden_grad)
     out_part = lax.dot_general(
-        hidden, down_pieces, (((1,), (1,)), ((), ())), preferred_element_type=jnp.float32
+        hidden, down_full, (((1,), (1,)), ((), ())), preferred_element_type=jnp.float32
     )
-    out_part = out_part.reshape(row_total, model_width)
     in_part = lax.dot_general(
         gate_grad, gate_full, (((1,), (1,)), ((), ())), preferred_element_type=jnp.float32
     )

time: 319 us -> 279 us (0.87)
  waiting for transfers between devices: 248 us -> 105 us
  starting transfers between devices: 8.83 us -> 68.5 us
  local copies, waits for them, and re-layouts: 5.49 us -> 40.7 us
  other arithmetic: 4.69 us -> 16.9 us
  matrix products: 25.5 us -> 20.4 us
    all_gather x3 -> x0, waiting for transfers between devices: 188 us -> none  [the longest x1 72.4 us: per_device(): up_full = lax.all_gather(w_up, 'ez', axis=0, tiled=True)]
    ppermute x0 -> x16, starting transfers between devices: none -> 60 us  [the longest x7 36.9 us: per_device(): ccw = lax.ppermute(ccw, 'ez', backward)]
    ppermute x0 -> x16, waiting for transfers between devices: none -> 59.5 us  [the longest x7 51.2 us: per_device(): cw = lax.ppermute(cw, 'ez', forward)]
    unnamed x18 -> x47, local copies, waits for them, and re-layouts: 2.27 us -> 21.7 us
    all_to_all x1, waiting for transfers between devices: 10.8 us -> 0.01 us  [per_device(): lax.all_to_all(sent_cot, 'ey', split_axis=0, concat_axis=0, tiled=True)]
    gather x0 -> x1, local copies, waits for them, and re-layouts: none -> 10.1 us  [per_device(): gathered = jnp.take(gathered, origin, axis=0)]
    select_n x0 -> x2, other arithmetic: none -> 9.9 us  [per_device(): gathered = jnp.take(gathered, origin, axis=0)]
    slice x2 -> x5, local copies, waits for them, and re-layouts: 0.18 us -> 6.31 us  [the longest x1 6.07 us: per_device(): up_full = gathered[:, 1].reshape(member_count * block_width, -1)]
  transfers between devices with their start and end apart: 6 -> 19, of which waited for: 5 -> 10; matrix products, arithmetic and copies ran while one was open for 6% -> 22% of each run, Pallas kernels for 0% -> 0%
where the time goes in v2:
time: 279 us; the launch traced here: 275 us
  waiting for transfers between devices  105 us (38%)
  starting transfers between devices  68.5 us (25%)
  local copies, waits for them, and re-layouts  40.7 us (15%)
  matrix products  20.4 us (7%)
  other arithmetic  16.9 us (6%)
  between operations  14.4 us (5%)
  blocking collectives  8.74 us (3%)
    ppermute x7, waiting for transfers between devices, per_device(): cw = lax.ppermute(cw, 'ez', forward)  51.2 us
    reduce_scatter x1, waiting for transfers between devices, per_device(): lax.psum_scatter(results.astype(jnp.bfloat16), 'tp', scatter_dimension=2,...  45.9 us
    ppermute x7, starting transfers between devices, per_device(): ccw = lax.ppermute(ccw, 'ez', backward)  36.9 us
    unnamed x47, local copies, waits for them, and re-layouts  21.7 us
    ppermute x7, starting transfers between devices, per_device(): cw = lax.ppermute(cw, 'ez', forward)  15.8 us
    gather x1, local copies, waits for them, and re-layouts, per_device(): gathered = jnp.take(gathered, origin, axis=0)  10.1 us
    select_n x2, other arithmetic, per_device(): gathered = jnp.take(gathered, origin, axis=0)  9.9 us
    all_to_all x1, blocking collectives, per_device(): lax.all_to_all(rounded, 'ey', split_axis=0, concat_axis=0, tiled=True)  8.74 us
  transfers between devices with their start and end apart: 19, of which 10 were waited for; matrix products, arithmetic and copies ran while one was open for 22% of the time, Pallas kernels for 0%

profile of v2, /device:TPU:1, one launch (start us, length us, event | category | flops | bytes accessed | tf_op | source)
XLA Modules:
  0.0 275.1 jit_solution(12132775858612738613)
XLA Ops:
  7.2 1.1 copy.66
  9.5 4.4 %collective-permute-start = (bf16[3,128,896]{2,1,0:T(8,128)(2,1)S(1)}, bf16[3,128,896]{2,1,0:T(8,128)(2,1)S(1)}, u32[]{:S(2)}, u32[]{:S(2)}) collective-permute-start(bf16[3,128,896]{2,1,0:T(8,128)(2,1)S(1)} %pad_maximum_fusion.1), channel_id=1, source_target_pairs={{0,8},{8,16},{16,24},{24,32},{32,40},{40,48},{48,56},{56,64},{64,7... | collective-permute-start | bytes 2064392 | tf_op jit(solution)/shard_map/ppermute | solution.py:60
  13.9 9.5 %collective-permute-start.8 = (bf16[3,128,896]{2,1,0:T(8,128)(2,1)S(1)}, bf16[3,128,896]{2,1,0:T(8,128)(2,1)S(1)}, u32[]{:S(2)}, u32[]{:S(2)}) collective-permute-start(bf16[3,128,896]{2,1,0:T(8,128)(2,1)S(1)} %pad_maximum_fusion.1), channel_id=1, source_target_pairs={{0,120},{8,0},{16,8},{24,16},{32,24},{40,32},{48,40},{56,48},{64,5... | collective-permute-start | bytes 2064392 | tf_op jit(solution)/shard_map/ppermute | solution.py:61
  23.4 13.2 %collective-permute-done = bf16[3,128,896]{2,1,0:T(8,128)(2,1)S(1)} collective-permute-done((bf16[3,128,896]{2,1,0:T(8,128)(2,1)S(1)}, bf16[3,128,896]{2,1,0:T(8,128)(2,1)S(1)}, u32[]{:S(2)}, u32[]{:S(2)}) %collective-permute-start) | collective-permute-done | bytes 688160 | tf_op jit(solution)/shard_map/ppermute | solution.py:60
  36.6 1.9 collective-permute-start.1
  38.5 4.6 %collective-permute-start.9 = (bf16[3,128,896]{2,1,0:T(8,128)(2,1)S(1)}, bf16[3,128,896]{2,1,0:T(8,128)(2,1)S(1)}, u32[]{:S(2)}, u32[]{:S(2)}) collective-permute-start(bf16[3,128,896]{2,1,0:T(8,128)(2,1)S(1)} %collective-permute-done.8), channel_id=1, source_target_pairs={{0,120},{8,0},{16,8},{24,16},{32,24},{40,32},{48,40},{56,48},{64,5... | collective-permute-start | bytes 2064392 | tf_op jit(solution)/shard_map/ppermute | solution.py:61
  43.1 12.4 %collective-permute-done.1 = bf16[3,128,896]{2,1,0:T(8,128)(2,1)} collective-permute-done((bf16[3,128,896]{2,1,0:T(8,128)(2,1)S(1)}, bf16[3,128,896]{2,1,0:T(8,128)(2,1)}, u32[]{:S(2)}, u32[]{:S(2)}) %collective-permute-start.1) | collective-permute-done | bytes 688160 | tf_op jit(solution)/shard_map/ppermute | solution.py:60
  55.5 1.9 collective-permute-start.2
  57.4 4.6 %collective-permute-start.10 = (bf16[3,128,896]{2,1,0:T(8,128)(2,1)S(1)}, bf16[3,128,896]{2,1,0:T(8,128)(2,1)S(1)}, u32[]{:S(2)}, u32[]{:S(2)}) collective-permute-start(bf16[3,128,896]{2,1,0:T(8,128)(2,1)S(1)} %collective-permute-done.9), channel_id=1, source_target_pairs={{0,120},{8,0},{16,8},{24,16},{32,24},{40,32},{48,40},{56,48},{64,5... | collective-permute-start | bytes 2064392 | tf_op jit(solution)/shard_map/ppermute | solution.py:61
  63.0 10.9 %collective-permute-done.2 = bf16[3,128,896]{2,1,0:T(8,128)(2,1)} collective-permute-done((bf16[3,128,896]{2,1,0:T(8,128)(2,1)}, bf16[3,128,896]{2,1,0:T(8,128)(2,1)}, u32[]{:S(2)}, u32[]{:S(2)}) %collective-permute-start.2) | collective-permute-done | bytes 688160 | tf_op jit(solution)/shard_map/ppermute | solution.py:60
  73.8 1.9 collective-permute-start.3
  75.7 4.6 %collective-permute-start.11 = (bf16[3,128,896]{2,1,0:T(8,128)(2,1)S(1)}, bf16[3,128,896]{2,1,0:T(8,128)(2,1)}, u32[]{:S(2)}, u32[]{:S(2)}) collective-permute-start(bf16[3,128,896]{2,1,0:T(8,128)(2,1)S(1)} %collective-permute-done.10), channel_id=1, source_target_pairs={{0,120},{8,0},{16,8},{24,16},{32,24},{40,32},{48,40},{56,48},{64,5... | collective-permute-start | bytes 2064392 | tf_op jit(solution)/shard_map/ppermute | solution.py:61
  80.5 1.2 reduce-window.6
  83.1 8.2 %collective-permute-done.3 = bf16[3,128,896]{2,1,0:T(8,128)(2,1)} collective-permute-done((bf16[3,128,896]{2,1,0:T(8,128)(2,1)}, bf16[3,128,896]{2,1,0:T(8,128)(2,1)}, u32[]{:S(2)}, u32[]{:S(2)}) %collective-permute-start.3) | collective-permute-done | bytes 688160 | tf_op jit(solution)/shard_map/ppermute | solution.py:60
  91.2 1.9 collective-permute-start.4
  93.2 4.6 %collective-permute-start.12 = (bf16[3,128,896]{2,1,0:T(8,128)(2,1)}, bf16[3,128,896]{2,1,0:T(8,128)(2,1)}, u32[]{:S(2)}, u32[]{:S(2)}) collective-permute-start(bf16[3,128,896]{2,1,0:T(8,128)(2,1)} %collective-permute-done.11), channel_id=1, source_target_pairs={{0,120},{8,0},{16,8},{24,16},{32,24},{40,32},{48,40},{56,48},{64,5... | collective-permute-start | bytes 2064392 | tf_op jit(solution)/shard_map/ppermute | solution.py:61
  97.8 1.6 convolution_convert_fusion
  99.3 4.3 %all-to-all-start = ((bf16[4,80,2048]{2,1,0:T(8,128)(2,1)}), bf16[4,80,2048]{2,1,0:T(8,128)(2,1)S(1)}, u32[]{:S(2)}, u32[]{:S(2)}) async-start(bf16[4,80,2048]{2,1,0:T(8,128)(2,1)} %bitcast.2), calls=%async_computation | async-start | bytes 2621440 | tf_op jit(solution)/shard_map/all_to_all | solution.py:74
  103.8 2.7 fusion.1
  106.5 1.3 collective-permute-done.4
  107.8 1.9 collective-permute-start.5
  109.8 4.6 %collective-permute-start.13 = (bf16[3,128,896]{2,1,0:T(8,128)(2,1)}, bf16[3,128,896]{2,1,0:T(8,128)(2,1)S(1)}, u32[]{:S(2)}, u32[]{:S(2)}) collective-permute-start(bf16[3,128,896]{2,1,0:T(8,128)(2,1)} %collective-permute-done.12), channel_id=1, source_target_pairs={{0,120},{8,0},{16,8},{24,16},{32,24},{40,32},{48,40},{56,48},{64,5... | collective-permute-start | bytes 2064392 | tf_op jit(solution)/shard_map/ppermute | solution.py:61
  116.3 2.0 bitcast_dynamic-update-slice_fusion.12
  118.3 5.2 %collective-permute-done.5 = bf16[3,128,896]{2,1,0:T(8,128)(2,1)S(1)} collective-permute-done((bf16[3,128,896]{2,1,0:T(8,128)(2,1)}, bf16[3,128,896]{2,1,0:T(8,128)(2,1)S(1)}, u32[]{:S(2)}, u32[]{:S(2)}) %collective-permute-start.5) | collective-permute-done | bytes 688160 | tf_op jit(solution)/shard_map/ppermute | solution.py:60
  123.5 1.9 collective-permute-start.6
  125.4 4.6 %collective-permute-start.14 = (bf16[3,128,896]{2,1,0:T(8,128)(2,1)S(1)}, bf16[3,128,896]{2,1,0:T(8,128)(2,1)S(1)}, u32[]{:S(2)}, u32[]{:S(2)}) collective-permute-start(bf16[3,128,896]{2,1,0:T(8,128)(2,1)S(1)} %collective-permute-done.13), channel_id=1, source_target_pairs={{0,120},{8,0},{16,8},{24,16},{32,24},{40,32},{48,40},{56,48},{64,5... | collective-permute-start | bytes 2064392 | tf_op jit(solution)/shard_map/ppermute | solution.py:61
  130.0 2.0 bitcast_dynamic-update-slice_fusion.11
  132.0 2.0 bitcast_dynamic-update-slice_fusion.10
  134.0 2.0 bitcast_dynamic-update-slice_fusion.9
  136.0 2.9 %collective-permute-done.14 = bf16[3,128,896]{2,1,0:T(8,128)(2,1)S(1)} collective-permute-done((bf16[3,128,896]{2,1,0:T(8,128)(2,1)S(1)}, bf16[3,128,896]{2,1,0:T(8,128)(2,1)S(1)}, u32[]{:S(2)}, u32[]{:S(2)}) %collective-permute-start.14) | collective-permute-done | bytes 688160 | tf_op jit(solution)/shard_map/ppermute | solution.py:61
  139.0 5.3 %collective-permute-start.15 = (bf16[3,64,896]{2,1,0:T(8,128)(2,1)S(1)}, bf16[3,64,896]{2,1,0:T(8,128)(2,1)S(1)}, u32[]{:S(2)}, u32[]{:S(2)}) collective-permute-start(bf16[3,64,896]{2,1,0:T(8,128)(2,1)S(1)} %slice.40), channel_id=1, source_target_pairs={{0,120},{8,0},{16,8},{24,16},{32,24},{40,32},{48,40},{56,48},{64,5... | collective-permute-start | bytes 1032200 | tf_op jit(solution)/shard_map/ppermute | solution.py:66
  144.3 1.9 collective-permute-start.7
  148.9 4.7 %collective-permute-done.7 = bf16[3,64,896]{2,1,0:T(8,128)(2,1)S(1)} collective-permute-done((bf16[3,64,896]{2,1,0:T(8,128)(2,1)S(1)}, bf16[3,64,896]{2,1,0:T(8,128)(2,1)S(1)}, u32[]{:S(2)}, u32[]{:S(2)}) %collective-permute-start.7) | collective-permute-done | bytes 344096 | tf_op jit(solution)/shard_map/ppermute | solution.py:65
  156.3 2.0 bitcast_dynamic-update-slice_fusion.4
  158.3 2.1 bitcast_dynamic-update-slice_fusion.3
  163.1 10.1 %gather_fusion = bf16[16,3,128,896]{3,2,1,0:T(8,128)(2,1)} fusion(bf16[16,3,128,896]{3,2,1,0:T(8,128)(2,1)} %bitcast_dynamic-update-slice_fusion, s32[1024]{0:T(1024)S(1)} %pad_clamp_fusion), kind=kCustom, calls=%fused_computation | custom fusion | bytes 22020160 | tf_op jit(solution)/shard_map/jit(_take)/gather | solution.py:70
  173.3 9.9 %broadcast_select_fusion = bf16[16,3,128,896]{3,2,1,0:T(8,128)(2,1)} fusion(bf16[16,3,128,896]{3,2,1,0:T(8,128)(2,1)} %gather_fusion, pred[16]{0:T(512)(128)(4,1)S(1)} %compare_and_fusion), kind=kLoop, calls=%fused_computation.1 | loop fusion | flops 5505024 | bytes 22020112 | tf_op jit(solution)/shard_map/jit(_take)/select_n | solution.py:70
  183.2 4.2 %all-to-all-start.1 = ((bf16[4,80,2048]{2,1,0:T(8,128)(2,1)}), bf16[4,80,2048]{2,1,0:T(8,128)(2,1)S(1)}, u32[]{:S(2)}, u32[]{:S(2)}) async-start(bf16[4,80,2048]{2,1,0:T(8,128)(2,1)} %bitcast.29), calls=%async_computation.1 | async-start | bytes 2621440 | tf_op jit(solution)/shard_map/all_to_all | solution.py:75
  187.4 6.1 %fusion.24 = (bf16[16,1,128,896]{3,2,1,0:T(8,128)(2,1)S(1)}, bf16[16,1,128,896]{3,2,1,0:T(8,128)(2,1)}, bf16[16,1,128,896]{3,2,1,0:T(8,128)(2,1)S(1)}) fusion(bf16[16,3,128,896]{3,2,1,0:T(8,128)(2,1)} %broadcast_select_fusion), kind=kLoop, calls=%fused_computation.71 | loop fusion | bytes 22020096 | tf_op jit(solution)/shard_map/slice | solution.py:72
  193.4 3.0 %fusion.26 = f32[320,896]{1,0:T(8,128)} fusion(bf16[320,2048]{1,0:T(8,128)(2,1)S(1)} %bitcast.101, bf16[2048,896]{1,0:T(8,128)(2,1)S(1)} %bitcast.93), kind=kOutput, calls=%fused_computation.73 | convolution fusion | flops 1174405120 | bytes 6127616 | tf_op jit(solution)/shard_map/dot_general | solution.py:80
  196.7 2.6 fusion.25
  199.3 3.7 %fusion.27 = f32[320,896]{1,0:T(8,128)S(1)} fusion(bf16[320,2048]{1,0:T(8,128)(2,1)S(1)} %bitcast.103, bf16[2048,896]{1,0:T(8,128)(2,1)} %bitcast.97), kind=kOutput, calls=%fused_computation.74 | convolution fusion | flops 1174405120 | bytes 6127616 | tf_op jit(solution)/shard_map/dot_general | solution.py:81
  203.1 1.6 fusion.2
  205.2 1.7 fusion.6
  207.2 1.6 fusion.3
  208.8 1.7 pad_maximum_fusion
  210.6 45.9 %reduce-scatter.2.cloned.1.call-done = bf16[320,2,256]{2,0,1:T(8,128)(2,1)} async-done(((bf16[320,2,2048]{2,0,1:T(8,128)(2,1)}), bf16[320,2,256]{2,0,1:T(8,128)(2,1)}) %reduce-scatter.2.cloned.1.call-update) | async-done | bytes 327696 | tf_op jit(solution)/shard_map/reduce_scatter | solution.py:93
  257.5 8.7 %all_to_all.15 = bf16[4,80,2,256]{3,1,2,0:T(8,128)(2,1)S(1)} all-to-all(bf16[4,80,2,256]{3,1,2,0:T(8,128)(2,1)S(1)} %copy.67), channel_id=1, replica_groups=mesh['ey'=4,'ez'=16,'tp'=8] {'ey'}, dimensions={0} | all-to-all | bytes 655360 | tf_op jit(solution)/shard_map/all_to_all | solution.py:95
  (80 shorter events, 18.0 us)
Async XLA Ops:
  7.2 90.6 %copy-start = (bf16[128,2048]{1,0:T(8,128)(2,1)S(1)}, bf16[128,2048]{1,0:T(8,128)(2,1)}, u32[]{:S(2)}) copy-start(bf16[128,2048]{1,0:T(8,128)(2,1)} %param.7) | copy-start | bytes 1572868
  9.5 94.2 %copy-start.13 = (f32[128,2]{0,1:T(2,128)S(1)}, f32[128,2]{0,1:T(2,128)}, u32[]{:S(2)}) copy-start(f32[128,2]{0,1:T(2,128)} %param.10) | copy-start | bytes 3076
  9.5 27.1 %collective-permute-start = (bf16[3,128,896]{2,1,0:T(8,128)(2,1)S(1)}, bf16[3,128,896]{2,1,0:T(8,128)(2,1)S(1)}, u32[]{:S(2)}, u32[]{:S(2)}) collective-permute-start(bf16[3,128,896]{2,1,0:T(8,128)(2,1)S(1)} %pad_maximum_fusion.1), channel_id=1, source_target_pairs={{0,8},{8,16},{16,24},{24,32},{32,40},{40,48},{48,56},{56,64},{64,7... | collective-permute-start | bytes 2064392 | tf_op jit(solution)/shard_map/ppermute | solution.py:60
  13.9 24.6 %collective-permute-start.8 = (bf16[3,128,896]{2,1,0:T(8,128)(2,1)S(1)}, bf16[3,128,896]{2,1,0:T(8,128)(2,1)S(1)}, u32[]{:S(2)}, u32[]{:S(2)}) collective-permute-start(bf16[3,128,896]{2,1,0:T(8,128)(2,1)S(1)} %pad_maximum_fusion.1), channel_id=1, source_target_pairs={{0,120},{8,0},{16,8},{24,16},{32,24},{40,32},{48,40},{56,48},{64,5... | collective-permute-start | bytes 2064392 | tf_op jit(solution)/shard_map/ppermute | solution.py:61
  36.6 20.9 %copy-start.11 = (bf16[3,128,896]{2,1,0:T(8,128)(2,1)}, bf16[3,128,896]{2,1,0:T(8,128)(2,1)S(1)}, u32[]{:S(2)}) copy-start(bf16[3,128,896]{2,1,0:T(8,128)(2,1)S(1)} %collective-permute-done) | copy-start | bytes 2064388
  36.6 18.9 %collective-permute-start.1 = (bf16[3,128,896]{2,1,0:T(8,128)(2,1)S(1)}, bf16[3,128,896]{2,1,0:T(8,128)(2,1)}, u32[]{:S(2)}, u32[]{:S(2)}) collective-permute-start(bf16[3,128,896]{2,1,0:T(8,128)(2,1)S(1)} %collective-permute-done), channel_id=1, source_target_pairs={{0,8},{8,16},{16,24},{24,32},{32,40},{40,48},{48,56},{56,64},{64,7... | collective-permute-start | bytes 2064392 | tf_op jit(solution)/shard_map/ppermute | solution.py:60
  38.5 18.9 %collective-permute-start.9 = (bf16[3,128,896]{2,1,0:T(8,128)(2,1)S(1)}, bf16[3,128,896]{2,1,0:T(8,128)(2,1)S(1)}, u32[]{:S(2)}, u32[]{:S(2)}) collective-permute-start(bf16[3,128,896]{2,1,0:T(8,128)(2,1)S(1)} %collective-permute-done.8), channel_id=1, source_target_pairs={{0,120},{8,0},{16,8},{24,16},{32,24},{40,32},{48,40},{56,48},{64,5... | collective-permute-start | bytes 2064392 | tf_op jit(solution)/shard_map/ppermute | solution.py:61
  55.5 18.3 %collective-permute-start.2 = (bf16[3,128,896]{2,1,0:T(8,128)(2,1)}, bf16[3,128,896]{2,1,0:T(8,128)(2,1)}, u32[]{:S(2)}, u32[]{:S(2)}) collective-permute-start(bf16[3,128,896]{2,1,0:T(8,128)(2,1)} %collective-permute-done.1), channel_id=1, source_target_pairs={{0,8},{8,16},{16,24},{24,32},{32,40},{40,48},{48,56},{56,64},{64,7... | collective-permute-start | bytes 2064392 | tf_op jit(solution)/shard_map/ppermute | solution.py:60
  57.4 18.3 %collective-permute-start.10 = (bf16[3,128,896]{2,1,0:T(8,128)(2,1)S(1)}, bf16[3,128,896]{2,1,0:T(8,128)(2,1)S(1)}, u32[]{:S(2)}, u32[]{:S(2)}) collective-permute-start(bf16[3,128,896]{2,1,0:T(8,128)(2,1)S(1)} %collective-permute-done.9), channel_id=1, source_target_pairs={{0,120},{8,0},{16,8},{24,16},{32,24},{40,32},{48,40},{56,48},{64,5... | collective-permute-start | bytes 2064392 | tf_op jit(solution)/shard_map/ppermute | solution.py:61
  73.8 17.4 %collective-permute-start.3 = (bf16[3,128,896]{2,1,0:T(8,128)(2,1)}, bf16[3,128,896]{2,1,0:T(8,128)(2,1)}, u32[]{:S(2)}, u32[]{:S(2)}) collective-permute-start(bf16[3,128,896]{2,1,0:T(8,128)(2,1)} %collective-permute-done.2), channel_id=1, source_target_pairs={{0,8},{8,16},{16,24},{24,32},{32,40},{40,48},{48,56},{56,64},{64,7... | collective-permute-start | bytes 2064392 | tf_op jit(solution)/shard_map/ppermute | solution.py:60
  75.7 23.6 %copy-start.9 = (bf16[3,128,896]{2,1,0:T(8,128)(2,1)}, bf16[3,128,896]{2,1,0:T(8,128)(2,1)S(1)}, u32[]{:S(2)}) copy-start(bf16[3,128,896]{2,1,0:T(8,128)(2,1)S(1)} %collective-permute-done.10) | copy-start | bytes 2064388
  75.7 17.4 %collective-permute-start.11 = (bf16[3,128,896]{2,1,0:T(8,128)(2,1)S(1)}, bf16[3,128,896]{2,1,0:T(8,128)(2,1)}, u32[]{:S(2)}, u32[]{:S(2)}) collective-permute-start(bf16[3,128,896]{2,1,0:T(8,128)(2,1)S(1)} %collective-permute-done.10), channel_id=1, source_target_pairs={{0,120},{8,0},{16,8},{24,16},{32,24},{40,32},{48,40},{56,48},{64,5... | collective-permute-start | bytes 2064392 | tf_op jit(solution)/shard_map/ppermute | solution.py:61
  91.2 16.6 %collective-permute-start.4 = (bf16[3,128,896]{2,1,0:T(8,128)(2,1)}, bf16[3,128,896]{2,1,0:T(8,128)(2,1)}, u32[]{:S(2)}, u32[]{:S(2)}) collective-permute-start(bf16[3,128,896]{2,1,0:T(8,128)(2,1)} %collective-permute-done.3), channel_id=1, source_target_pairs={{0,8},{8,16},{16,24},{24,32},{32,40},{40,48},{48,56},{56,64},{64,7... | collective-permute-start | bytes 2064392 | tf_op jit(solution)/shard_map/ppermute | solution.py:60
  93.2 16.6 %collective-permute-start.12 = (bf16[3,128,896]{2,1,0:T(8,128)(2,1)}, bf16[3,128,896]{2,1,0:T(8,128)(2,1)}, u32[]{:S(2)}, u32[]{:S(2)}) collective-permute-start(bf16[3,128,896]{2,1,0:T(8,128)(2,1)} %collective-permute-done.11), channel_id=1, source_target_pairs={{0,120},{8,0},{16,8},{24,16},{32,24},{40,32},{48,40},{56,48},{64,5... | collective-permute-start | bytes 2064392 | tf_op jit(solution)/shard_map/ppermute | solution.py:61
  99.3 15.0 %copy-start.7 = (bf16[128,896]{1,0:T(8,128)(2,1)S(1)}, bf16[128,896]{1,0:T(8,128)(2,1)}, u32[]{:S(2)}) copy-start(bf16[128,896]{1,0:T(8,128)(2,1)} %param.12) | copy-start | bytes 688132
  99.3 15.0 %copy-start.8 = (bf16[128,896]{1,0:T(8,128)(2,1)S(1)}, bf16[128,896]{1,0:T(8,128)(2,1)}, u32[]{:S(2)}) copy-start(bf16[128,896]{1,0:T(8,128)(2,1)} %param.11) | copy-start | bytes 688132
  99.3 83.8 %all-to-all-start = ((bf16[4,80,2048]{2,1,0:T(8,128)(2,1)}), bf16[4,80,2048]{2,1,0:T(8,128)(2,1)S(1)}, u32[]{:S(2)}, u32[]{:S(2)}) async-start(bf16[4,80,2048]{2,1,0:T(8,128)(2,1)} %bitcast.2), calls=%async_computation | async-start | bytes 2621440 | tf_op jit(solution)/shard_map/all_to_all | solution.py:74
  103.6 11.7 %copy-start.12 = (bf16[3,128,896]{2,1,0:T(8,128)(2,1)S(1)}, bf16[3,128,896]{2,1,0:T(8,128)(2,1)}, u32[]{:S(2)}) copy-start(bf16[3,128,896]{2,1,0:T(8,128)(2,1)} %copy-done.11) | copy-start | bytes 2064388
  107.8 15.6 %collective-permute-start.5 = (bf16[3,128,896]{2,1,0:T(8,128)(2,1)}, bf16[3,128,896]{2,1,0:T(8,128)(2,1)S(1)}, u32[]{:S(2)}, u32[]{:S(2)}) collective-permute-start(bf16[3,128,896]{2,1,0:T(8,128)(2,1)} %collective-permute-done.4), channel_id=1, source_target_pairs={{0,8},{8,16},{16,24},{24,32},{32,40},{40,48},{48,56},{56,64},{64,7... | collective-permute-start | bytes 2064392 | tf_op jit(solution)/shard_map/ppermute | solution.py:60
  109.8 15.6 %collective-permute-start.13 = (bf16[3,128,896]{2,1,0:T(8,128)(2,1)}, bf16[3,128,896]{2,1,0:T(8,128)(2,1)S(1)}, u32[]{:S(2)}, u32[]{:S(2)}) collective-permute-start(bf16[3,128,896]{2,1,0:T(8,128)(2,1)} %collective-permute-done.12), channel_id=1, source_target_pairs={{0,120},{8,0},{16,8},{24,16},{32,24},{40,32},{48,40},{56,48},{64,5... | collective-permute-start | bytes 2064392 | tf_op jit(solution)/shard_map/ppermute | solution.py:61
  123.5 20.8 %collective-permute-start.6 = (bf16[3,128,896]{2,1,0:T(8,128)(2,1)S(1)}, bf16[3,128,896]{2,1,0:T(8,128)(2,1)S(1)}, u32[]{:S(2)}, u32[]{:S(2)}) collective-permute-start(bf16[3,128,896]{2,1,0:T(8,128)(2,1)S(1)} %collective-permute-done.5), channel_id=1, source_target_pairs={{0,8},{8,16},{16,24},{24,32},{32,40},{40,48},{48,56},{56,64},{64,7... | collective-permute-start | bytes 2064392 | tf_op jit(solution)/shard_map/ppermute | solution.py:60
  125.4 13.5 %collective-permute-start.14 = (bf16[3,128,896]{2,1,0:T(8,128)(2,1)S(1)}, bf16[3,128,896]{2,1,0:T(8,128)(2,1)S(1)}, u32[]{:S(2)}, u32[]{:S(2)}) collective-permute-start(bf16[3,128,896]{2,1,0:T(8,128)(2,1)S(1)} %collective-permute-done.13), channel_id=1, source_target_pairs={{0,120},{8,0},{16,8},{24,16},{32,24},{40,32},{48,40},{56,48},{64,5... | collective-permute-start | bytes 2064392 | tf_op jit(solution)/shard_map/ppermute | solution.py:61
  139.0 9.9 %collective-permute-start.15 = (bf16[3,64,896]{2,1,0:T(8,128)(2,1)S(1)}, bf16[3,64,896]{2,1,0:T(8,128)(2,1)S(1)}, u32[]{:S(2)}, u32[]{:S(2)}) collective-permute-start(bf16[3,64,896]{2,1,0:T(8,128)(2,1)S(1)} %slice.40), channel_id=1, source_target_pairs={{0,120},{8,0},{16,8},{24,16},{32,24},{40,32},{48,40},{56,48},{64,5... | collective-permute-start | bytes 1032200 | tf_op jit(solution)/shard_map/ppermute | solution.py:66
  144.3 9.2 %collective-permute-start.7 = (bf16[3,64,896]{2,1,0:T(8,128)(2,1)S(1)}, bf16[3,64,896]{2,1,0:T(8,128)(2,1)S(1)}, u32[]{:S(2)}, u32[]{:S(2)}) collective-permute-start(bf16[3,64,896]{2,1,0:T(8,128)(2,1)S(1)} %slice.39), channel_id=1, source_target_pairs={{0,8},{8,16},{16,24},{24,32},{32,40},{40,48},{48,56},{56,64},{64,7... | collective-permute-start | bytes 1032200 | tf_op jit(solution)/shard_map/ppermute | solution.py:65
  154.5 6.0 %copy-start.10 = (bf16[3,128,896]{2,1,0:T(8,128)(2,1)S(1)}, bf16[3,128,896]{2,1,0:T(8,128)(2,1)}, u32[]{:S(2)}) copy-start(bf16[3,128,896]{2,1,0:T(8,128)(2,1)} %copy-done.9) | copy-start | bytes 2064388
  183.2 16.2 %all-to-all-start.1 = ((bf16[4,80,2048]{2,1,0:T(8,128)(2,1)}), bf16[4,80,2048]{2,1,0:T(8,128)(2,1)S(1)}, u32[]{:S(2)}, u32[]{:S(2)}) async-start(bf16[4,80,2048]{2,1,0:T(8,128)(2,1)} %bitcast.29), calls=%async_computation.1 | async-start | bytes 2621440 | tf_op jit(solution)/shard_map/all_to_all | solution.py:75
  187.4 69.1 %reduce-scatter.2.cloned.1.call-start = ((), (), s32[]{:S(2)}) async-start(), calls=%async_computation.4 | async-start | bytes 2949120 | tf_op jit(solution)/shard_map/reduce_scatter | solution.py:93
  193.4 3.0 %copy-start.2 = (bf16[16,1,128,896]{3,2,1,0:T(8,128)(2,1)}, bf16[16,1,128,896]{3,2,1,0:T(8,128)(2,1)S(1)}, u32[]{:S(2)}) copy-start(bf16[16,1,128,896]{3,2,1,0:T(8,128)(2,1)S(1)} %get-tuple-element.2) | copy-start | bytes 11010052
  193.4 3.3 %copy-start.4 = (bf16[16,1,128,896]{3,2,1,0:T(8,128)(2,1)}, bf16[16,1,128,896]{3,2,1,0:T(8,128)(2,1)S(1)}, u32[]{:S(2)}) copy-start(bf16[16,1,128,896]{3,2,1,0:T(8,128)(2,1)S(1)} %get-tuple-element.4) | copy-start | bytes 11010052
  199.3 3.7 %copy-start.6 = (bf16[16,1,128,896]{3,2,1,0:T(8,128)(2,1)S(1)}, bf16[16,1,128,896]{3,2,1,0:T(8,128)(2,1)}, u32[]{:S(2)}) copy-start(bf16[16,1,128,896]{3,2,1,0:T(8,128)(2,1)} %get-tuple-element.3) | copy-start | bytes 11010052
  199.3 3.7 %copy-start.14 = (f32[320,896]{1,0:T(8,128)S(1)}, f32[320,896]{1,0:T(8,128)}, u32[]{:S(2)}) copy-start(f32[320,896]{1,0:T(8,128)} %fusion.25) | copy-start | bytes 3440644
  199.3 3.8 %copy-start.15 = (f32[320,896]{1,0:T(8,128)S(1)}, f32[320,896]{1,0:T(8,128)}, u32[]{:S(2)}) copy-start(f32[320,896]{1,0:T(8,128)} %fusion.26) | copy-start | bytes 3440644
  203.1 2.0 copy-start.5
  205.2 2.0 copy-start.3
  210.5 57.7 %copy-start.1 = (bf16[128,2048]{1,0:T(8,128)(2,1)S(1)}, bf16[128,2048]{1,0:T(8,128)(2,1)}, u32[]{:S(2)}) copy-start(bf16[128,2048]{1,0:T(8,128)(2,1)} %param.7) | copy-start | bytes 1572868
Sparse Core Ops, SparseCore 0:
  210.7 45.7 reduce-scatter.1

commit v3 on v2

--- a/solution.py
+++ b/solution.py
@@ -65,17 +65,19 @@
     far_low = lax.ppermute(cw[:, :cut], "ez", forward)
     far_high = lax.ppermute(ccw[:, cut:], "ez", backward)
     by_distance[half_steps] = jnp.concatenate([far_low, far_high], axis=1)
-    gathered = jnp.stack(by_distance, axis=0)
     origin = (place - jnp.arange(member_count, dtype=jnp.int32)) % member_count
-    gathered = jnp.take(gathered, origin, axis=0)
-    gate_full = gathered[:, 0].reshape(member_count * block_width, -1)
-    up_full = gathered[:, 1].reshape(member_count * block_width, -1)
-    down_full = gathered[:, 2].reshape(member_count * block_width, -1)
+    gate_full = jnp.concatenate([chunk[0] for chunk in by_distance], axis=0)
+    up_full = jnp.concatenate([chunk[1] for chunk in by_distance], axis=0)
+    down_full = jnp.concatenate([chunk[2] for chunk in by_distance], axis=0)
     member_tokens = lax.all_to_all(sent_tokens, "ey", split_axis=0, concat_axis=0, tiled=True)
     member_cot = lax.all_to_all(sent_cot, "ey", split_axis=0, concat_axis=0, tiled=True)
     row_total = plane_count * CAP
-    member_tokens = member_tokens.reshape(row_total, model_width)
-    member_cot = member_cot.reshape(row_total, model_width)
+    member_tokens = jnp.take(
+        member_tokens.reshape(row_total, member_count, block_width), origin, axis=1
+    ).reshape(row_total, model_width)
+    member_cot = jnp.take(
+        member_cot.reshape(row_total, member_count, block_width), origin, axis=1
+    ).reshape(row_total, model_width)
     gate_pre = jnp.dot(member_tokens, gate_full, preferred_element_type=jnp.float32)
     up_pre = jnp.dot(member_tokens, up_full, preferred_element_type=jnp.float32)
     hidden_grad = jnp.dot(member_cot, down_full, preferred_element_type=jnp.float32)
@@ -89,8 +91,11 @@
     in_part = in_part + lax.dot_general(
         up_grad, up_full, (((1,), (1,)), ((), ())), preferred_element_type=jnp.float32
     )
-    results = jnp.stack([out_part, in_part], axis=1)
-    summed = lax.psum_scatter(results.astype(jnp.bfloat16), "tp", scatter_dimension=2, tiled=True)
+    results = jnp.stack([out_part, in_part], axis=1).astype(jnp.bfloat16)
+    results = jnp.take(
+        results.reshape(row_total, 2, member_count, block_width), origin, axis=2
+    ).reshape(row_total, 2, model_width)
+    summed = lax.psum_scatter(results, "tp", scatter_dimension=2, tiled=True)
     rounded = summed.reshape(plane_count, CAP, 2, -1)
     returned = lax.all_to_all(rounded, "ey", split_axis=0, concat_axis=0, tiled=True)
     returned = returned.reshape(slot_count, 2, -1).astype(jnp.float32)

time: 279 us -> 254 us (0.910)
  waiting for transfers between devices: 105 us -> 91.1 us
  other arithmetic: 16.9 us -> 9.77 us
  local copies, waits for them, and re-layouts: 40.7 us -> 37 us
  matrix products: 20.4 us -> 17.6 us
    ppermute x7, waiting for transfers between devices: 51.2 us -> 37.1 us  [per_device(): cw = lax.ppermute(cw, 'ez', forward)]
    unnamed x47 -> x43, local copies, waits for them, and re-layouts: 21.7 us -> 27.8 us
    select_n x2 -> x3, other arithmetic: 9.9 us -> 3.82 us  [per_device(): jnp.take(results.reshape(row_total, 2, member_count, block_width), origin...]
    slice x3 -> x2, local copies, waits for them, and re-layouts: 6.25 us -> 0.18 us  [the longest x1 6.07 us: per_device(): up_full = gathered[:, 1].reshape(member_count * block_width, -1)]
    gather x1 -> x3, local copies, waits for them, and re-layouts: 10.1 us -> 5.02 us  [the longest x1 2.43 us: per_device(): jnp.take(results.reshape(row_total, 2, member_count, block_width), origin...]
    ppermute x1, waiting for transfers between devices: 4.65 us -> 0.01 us  [per_device(): far_low = lax.ppermute(cw[:, :cut], 'ez', forward)]
  transfers between devices with their start and end apart: 19 -> 19, of which waited for: 10 -> 13; matrix products, arithmetic and copies ran while one was open for 22% -> 11% of each run, Pallas kernels for 0% -> 0%
where the time goes in v3:
time: 254 us; the launch traced here: 249 us
  waiting for transfers between devices  91.1 us (36%)
  starting transfers between devices  70.6 us (28%)
  local copies, waits for them, and re-layouts  37 us (15%)
  matrix products  17.6 us (7%)
  between operations  14.5 us (6%)
  other arithmetic  9.77 us (4%)
  blocking collectives  8.69 us (3%)
    reduce_scatter x1, waiting for transfers between devices, per_device(): summed = lax.psum_scatter(results, 'tp', scatter_dimension=2, tiled=True)  45.4 us
    ppermute x7, starting transfers between devices, per_device(): ccw = lax.ppermute(ccw, 'ez', backward)  39.4 us
    ppermute x7, waiting for transfers between devices, per_device(): cw = lax.ppermute(cw, 'ez', forward)  37.1 us
    unnamed x43, local copies, waits for them, and re-layouts  27.8 us
    ppermute x7, starting transfers between devices, per_device(): cw = lax.ppermute(cw, 'ez', forward)  15.8 us
    all_to_all x1, blocking collectives, per_device(): lax.all_to_all(rounded, 'ey', split_axis=0, concat_axis=0, tiled=True)  8.69 us
    ppermute x1, starting transfers between devices, per_device(): far_high = lax.ppermute(ccw[:, cut:], 'ez', backward)  5.5 us
  transfers between devices with their start and end apart: 19, of which 13 were waited for; matrix products, arithmetic and copies ran while one was open for 11% of the time, Pallas kernels for 0%

profile of v3, /device:TPU:1, one launch (start us, length us, event | category | flops | bytes accessed | tf_op | source)
XLA Modules:
  0.0 249.2 jit_solution(12047825134626301986)
XLA Ops:
  9.5 4.4 %collective-permute-start = (bf16[3,128,896]{2,1,0:T(8,128)(2,1)S(1)}, bf16[3,128,896]{2,1,0:T(8,128)(2,1)}, u32[]{:S(2)}, u32[]{:S(2)}) collective-permute-start(bf16[3,128,896]{2,1,0:T(8,128)(2,1)S(1)} %pad_maximum_fusion.1), channel_id=1, source_target_pairs={{0,8},{8,16},{16,24},{24,32},{32,40},{40,48},{48,56},{56,64},{64,7... | collective-permute-start | bytes 2064392 | tf_op jit(solution)/shard_map/ppermute | solution.py:60
  13.8 9.5 %collective-permute-start.8 = (bf16[3,128,896]{2,1,0:T(8,128)(2,1)S(1)}, bf16[3,128,896]{2,1,0:T(8,128)(2,1)S(1)}, u32[]{:S(2)}, u32[]{:S(2)}) collective-permute-start(bf16[3,128,896]{2,1,0:T(8,128)(2,1)S(1)} %pad_maximum_fusion.1), channel_id=1, source_target_pairs={{0,120},{8,0},{16,8},{24,16},{32,24},{40,32},{48,40},{56,48},{64,5... | collective-permute-start | bytes 2064392 | tf_op jit(solution)/shard_map/ppermute | solution.py:61
  24.3 12.4 %collective-permute-done = bf16[3,128,896]{2,1,0:T(8,128)(2,1)} collective-permute-done((bf16[3,128,896]{2,1,0:T(8,128)(2,1)S(1)}, bf16[3,128,896]{2,1,0:T(8,128)(2,1)}, u32[]{:S(2)}, u32[]{:S(2)}) %collective-permute-start) | collective-permute-done | bytes 688160 | tf_op jit(solution)/shard_map/ppermute | solution.py:60
  36.7 1.9 collective-permute-start.1
  40.3 4.6 %collective-permute-start.9 = (bf16[3,128,896]{2,1,0:T(8,128)(2,1)S(1)}, bf16[3,128,896]{2,1,0:T(8,128)(2,1)S(1)}, u32[]{:S(2)}, u32[]{:S(2)}) collective-permute-start(bf16[3,128,896]{2,1,0:T(8,128)(2,1)S(1)} %collective-permute-done.8), channel_id=1, source_target_pairs={{0,120},{8,0},{16,8},{24,16},{32,24},{40,32},{48,40},{56,48},{64,5... | collective-permute-start | bytes 2064392 | tf_op jit(solution)/shard_map/ppermute | solution.py:61
  46.7 9.0 %collective-permute-done.1 = bf16[3,128,896]{2,1,0:T(8,128)(2,1)S(1)} collective-permute-done((bf16[3,128,896]{2,1,0:T(8,128)(2,1)}, bf16[3,128,896]{2,1,0:T(8,128)(2,1)S(1)}, u32[]{:S(2)}, u32[]{:S(2)}) %collective-permute-start.1) | collective-permute-done | bytes 688160 | tf_op jit(solution)/shard_map/ppermute | solution.py:60
  55.7 1.9 collective-permute-start.2
  58.1 5.3 %collective-permute-start.10 = (bf16[3,128,896]{2,1,0:T(8,128)(2,1)S(1)}, bf16[3,128,896]{2,1,0:T(8,128)(2,1)}, u32[]{:S(2)}, u32[]{:S(2)}) collective-permute-start(bf16[3,128,896]{2,1,0:T(8,128)(2,1)S(1)} %collective-permute-done.9), channel_id=1, source_target_pairs={{0,120},{8,0},{16,8},{24,16},{32,24},{40,32},{48,40},{56,48},{64,5... | collective-permute-start | bytes 2064392 | tf_op jit(solution)/shard_map/ppermute | solution.py:61
  63.4 1.6 fusion.1
  65.0 4.2 %all-to-all-start.1 = ((bf16[4,80,2048]{2,1,0:T(8,128)(2,1)}), bf16[4,80,2048]{2,1,0:T(8,128)(2,1)S(1)}, u32[]{:S(2)}, u32[]{:S(2)}) async-start(bf16[4,80,2048]{2,1,0:T(8,128)(2,1)} %bitcast.54), calls=%async_computation.1 | async-start | bytes 2621440 | tf_op jit(solution)/shard_map/all_to_all | solution.py:73
  69.2 4.6 %collective-permute-done.2 = bf16[3,128,896]{2,1,0:T(8,128)(2,1)} collective-permute-done((bf16[3,128,896]{2,1,0:T(8,128)(2,1)S(1)}, bf16[3,128,896]{2,1,0:T(8,128)(2,1)}, u32[]{:S(2)}, u32[]{:S(2)}) %collective-permute-start.2) | collective-permute-done | bytes 688160 | tf_op jit(solution)/shard_map/ppermute | solution.py:60
  73.8 1.9 collective-permute-start.3
  75.8 5.4 %collective-permute-start.11 = (bf16[3,128,896]{2,1,0:T(8,128)(2,1)}, bf16[3,128,896]{2,1,0:T(8,128)(2,1)}, u32[]{:S(2)}, u32[]{:S(2)}) collective-permute-start(bf16[3,128,896]{2,1,0:T(8,128)(2,1)} %collective-permute-done.10), channel_id=1, source_target_pairs={{0,120},{8,0},{16,8},{24,16},{32,24},{40,32},{48,40},{56,48},{64,5... | collective-permute-start | bytes 2064392 | tf_op jit(solution)/shard_map/ppermute | solution.py:61
  81.2 2.6 %convolution_convert_fusion = bf16[320,2048]{1,0:T(8,128)(2,1)} fusion(pred[320,128]{1,0:T(8,128)(4,1)S(1)} %fusion.16, bf16[128,2048]{1,0:T(8,128)(2,1)} %param.9), kind=kOutput, calls=%fused_computation.6 | convolution fusion | flops 168427520 | bytes 1875968 | tf_op jit(solution)/shard_map/dot_general | solution.py:42
  84.2 3.8 %all-to-all-start = ((bf16[4,80,2048]{2,1,0:T(8,128)(2,1)}), bf16[4,80,2048]{2,1,0:T(8,128)(2,1)S(1)}, u32[]{:S(2)}, u32[]{:S(2)}) async-start(bf16[4,80,2048]{2,1,0:T(8,128)(2,1)} %bitcast.3), calls=%async_computation | async-start | bytes 2621440 | tf_op jit(solution)/shard_map/all_to_all | solution.py:72
  88.1 3.2 %collective-permute-done.3 = bf16[3,128,896]{2,1,0:T(8,128)(2,1)} collective-permute-done((bf16[3,128,896]{2,1,0:T(8,128)(2,1)}, bf16[3,128,896]{2,1,0:T(8,128)(2,1)}, u32[]{:S(2)}, u32[]{:S(2)}) %collective-permute-start.3) | collective-permute-done | bytes 688160 | tf_op jit(solution)/shard_map/ppermute | solution.py:60
  91.2 1.9 collective-permute-start.4
  93.2 1.8 constant_dynamic-update-slice_fusion.2
  95.0 4.6 %collective-permute-start.12 = (bf16[3,128,896]{2,1,0:T(8,128)(2,1)}, bf16[3,128,896]{2,1,0:T(8,128)(2,1)}, u32[]{:S(2)}, u32[]{:S(2)}) collective-permute-start(bf16[3,128,896]{2,1,0:T(8,128)(2,1)} %collective-permute-done.11), channel_id=1, source_target_pairs={{0,120},{8,0},{16,8},{24,16},{32,24},{40,32},{48,40},{56,48},{64,5... | collective-permute-start | bytes 2064392 | tf_op jit(solution)/shard_map/ppermute | solution.py:61
  100.4 7.4 %collective-permute-done.4 = bf16[3,128,896]{2,1,0:T(8,128)(2,1)} collective-permute-done((bf16[3,128,896]{2,1,0:T(8,128)(2,1)}, bf16[3,128,896]{2,1,0:T(8,128)(2,1)}, u32[]{:S(2)}, u32[]{:S(2)}) %collective-permute-start.4) | collective-permute-done | bytes 688160 | tf_op jit(solution)/shard_map/ppermute | solution.py:60
  107.8 1.9 collective-permute-start.5
  109.7 2.0 fusion.61
  113.1 1.8 gather_fusion.2
  115.7 4.8 %collective-permute-start.13 = (bf16[3,128,896]{2,1,0:T(8,128)(2,1)}, bf16[3,128,896]{2,1,0:T(8,128)(2,1)S(1)}, u32[]{:S(2)}, u32[]{:S(2)}) collective-permute-start(bf16[3,128,896]{2,1,0:T(8,128)(2,1)} %collective-permute-done.12), channel_id=1, source_target_pairs={{0,120},{8,0},{16,8},{24,16},{32,24},{40,32},{48,40},{56,48},{64,5... | collective-permute-start | bytes 2064392 | tf_op jit(solution)/shard_map/ppermute | solution.py:61
  120.6 1.6 select_bitcast_fusion.1
  123.5 1.9 collective-permute-start.6
  125.5 2.0 fusion.59
  127.5 3.3 %collective-permute-done.13 = bf16[3,128,896]{2,1,0:T(8,128)(2,1)S(1)} collective-permute-done((bf16[3,128,896]{2,1,0:T(8,128)(2,1)}, bf16[3,128,896]{2,1,0:T(8,128)(2,1)S(1)}, u32[]{:S(2)}, u32[]{:S(2)}) %collective-permute-start.13) | collective-permute-done | bytes 688160 | tf_op jit(solution)/shard_map/ppermute | solution.py:61
  130.7 5.2 %collective-permute-start.14 = (bf16[3,128,896]{2,1,0:T(8,128)(2,1)S(1)}, bf16[3,128,896]{2,1,0:T(8,128)(2,1)S(1)}, u32[]{:S(2)}, u32[]{:S(2)}) collective-permute-start(bf16[3,128,896]{2,1,0:T(8,128)(2,1)S(1)} %collective-permute-done.13), channel_id=1, source_target_pairs={{0,120},{8,0},{16,8},{24,16},{32,24},{40,32},{48,40},{56,48},{64,5... | collective-permute-start | bytes 2064392 | tf_op jit(solution)/shard_map/ppermute | solution.py:61
  135.9 2.0 fusion.58
  137.9 2.0 fusion.57
  139.9 1.9 collective-permute-start.7
  141.9 2.0 fusion.56
  144.9 5.5 %collective-permute-start.15 = (bf16[3,64,896]{2,1,0:T(8,128)(2,1)S(1)}, bf16[3,64,896]{2,1,0:T(8,128)(2,1)S(1)}, u32[]{:S(2)}, u32[]{:S(2)}) collective-permute-start(bf16[3,64,896]{2,1,0:T(8,128)(2,1)S(1)} %slice.219), channel_id=1, source_target_pairs={{0,120},{8,0},{16,8},{24,16},{32,24},{40,32},{48,40},{56,48},{64,5... | collective-permute-start | bytes 1032200 | tf_op jit(solution)/shard_map/ppermute | solution.py:66
  151.3 3.5 %collective-permute-done.15 = bf16[3,64,896]{2,1,0:T(8,128)(2,1)S(1)} collective-permute-done((bf16[3,64,896]{2,1,0:T(8,128)(2,1)S(1)}, bf16[3,64,896]{2,1,0:T(8,128)(2,1)S(1)}, u32[]{:S(2)}, u32[]{:S(2)}) %collective-permute-start.15) | collective-permute-done | bytes 344096 | tf_op jit(solution)/shard_map/ppermute | solution.py:66
  157.4 2.0 fusion.51
  159.4 2.0 fusion.50
  161.4 2.0 fusion.49
  165.1 3.6 %fusion.7 = f32[320,896]{1,0:T(8,128)S(1)} fusion(bf16[2048,896]{1,0:T(8,128)(2,1)} %get-tuple-element.5, bf16[16,40,8,128]{3,2,1,0:T(8,128)(2,1)S(1)} %get-tuple-element.48), kind=kOutput, calls=%fused_computation.16 | convolution fusion | flops 1174405120 | bytes 6127616 | tf_op jit(solution)/shard_map/dot_general | solution.py:82
  168.6 1.5 fusion.9
  170.7 1.6 fusion.3
  172.9 1.5 fusion.4
  174.9 1.6 fusion.14
  176.5 1.7 fusion.2
  179.1 2.4 gather_fusion
  181.5 3.8 %bitcast_select_fusion = bf16[320,2,2048]{2,0,1:T(8,128)(2,1)} fusion(pred[2048]{0:T(1024)(128)(4,1)S(1)} %broadcast_bitcast_fusion, bf16[16,320,2,128]{3,1,2,0:T(8,128)(2,1)} %gather_fusion), kind=kLoop, calls=%fused_computation.9 | loop fusion | flops 1310720 | bytes 5244928 | tf_op jit(solution)/shard_map/jit(_take)/select_n | solution.py:95
  185.3 45.4 %reduce-scatter.2.cloned.1.call-done = bf16[320,2,256]{2,0,1:T(8,128)(2,1)} async-done(((bf16[320,2,2048]{2,0,1:T(8,128)(2,1)}), bf16[320,2,256]{2,0,1:T(8,128)(2,1)}) %reduce-scatter.2.cloned.1.call-update) | async-done | bytes 327696 | tf_op jit(solution)/shard_map/reduce_scatter | solution.py:98
  231.7 8.7 %all_to_all.15 = bf16[4,80,2,256]{3,1,2,0:T(8,128)(2,1)S(1)} all-to-all(bf16[4,80,2,256]{3,1,2,0:T(8,128)(2,1)S(1)} %copy.95), channel_id=1, replica_groups=mesh['ey'=4,'ez'=16,'tp'=8] {'ey'}, dimensions={0} | all-to-all | bytes 655360 | tf_op jit(solution)/shard_map/all_to_all | solution.py:100
  (83 shorter events, 23.6 us)
Async XLA Ops:
  7.2 56.2 %copy-start = (bf16[128,2048]{1,0:T(8,128)(2,1)S(1)}, bf16[128,2048]{1,0:T(8,128)(2,1)}, u32[]{:S(2)}) copy-start(bf16[128,2048]{1,0:T(8,128)(2,1)} %param.10) | copy-start | bytes 1572868
  9.5 27.2 %collective-permute-start = (bf16[3,128,896]{2,1,0:T(8,128)(2,1)S(1)}, bf16[3,128,896]{2,1,0:T(8,128)(2,1)}, u32[]{:S(2)}, u32[]{:S(2)}) collective-permute-start(bf16[3,128,896]{2,1,0:T(8,128)(2,1)S(1)} %pad_maximum_fusion.1), channel_id=1, source_target_pairs={{0,8},{8,16},{16,24},{24,32},{32,40},{40,48},{48,56},{56,64},{64,7... | collective-permute-start | bytes 2064392 | tf_op jit(solution)/shard_map/ppermute | solution.py:60
  13.8 26.4 %collective-permute-start.8 = (bf16[3,128,896]{2,1,0:T(8,128)(2,1)S(1)}, bf16[3,128,896]{2,1,0:T(8,128)(2,1)S(1)}, u32[]{:S(2)}, u32[]{:S(2)}) collective-permute-start(bf16[3,128,896]{2,1,0:T(8,128)(2,1)S(1)} %pad_maximum_fusion.1), channel_id=1, source_target_pairs={{0,120},{8,0},{16,8},{24,16},{32,24},{40,32},{48,40},{56,48},{64,5... | collective-permute-start | bytes 2064392 | tf_op jit(solution)/shard_map/ppermute | solution.py:61
  36.7 19.0 %collective-permute-start.1 = (bf16[3,128,896]{2,1,0:T(8,128)(2,1)}, bf16[3,128,896]{2,1,0:T(8,128)(2,1)S(1)}, u32[]{:S(2)}, u32[]{:S(2)}) collective-permute-start(bf16[3,128,896]{2,1,0:T(8,128)(2,1)} %collective-permute-done), channel_id=1, source_target_pairs={{0,8},{8,16},{16,24},{24,32},{32,40},{40,48},{48,56},{56,64},{64,7... | collective-permute-start | bytes 2064392 | tf_op jit(solution)/shard_map/ppermute | solution.py:60
  40.3 24.7 %copy-start.1 = (bf16[3,128,896]{2,1,0:T(8,128)(2,1)}, bf16[3,128,896]{2,1,0:T(8,128)(2,1)S(1)}, u32[]{:S(2)}) copy-start(bf16[3,128,896]{2,1,0:T(8,128)(2,1)S(1)} %collective-permute-done.8) | copy-start | bytes 2064388
  40.3 17.8 %collective-permute-start.9 = (bf16[3,128,896]{2,1,0:T(8,128)(2,1)S(1)}, bf16[3,128,896]{2,1,0:T(8,128)(2,1)S(1)}, u32[]{:S(2)}, u32[]{:S(2)}) collective-permute-start(bf16[3,128,896]{2,1,0:T(8,128)(2,1)S(1)} %collective-permute-done.8), channel_id=1, source_target_pairs={{0,120},{8,0},{16,8},{24,16},{32,24},{40,32},{48,40},{56,48},{64,5... | collective-permute-start | bytes 2064392 | tf_op jit(solution)/shard_map/ppermute | solution.py:61
  55.7 28.5 %copy-start.5 = (bf16[3,128,896]{2,1,0:T(8,128)(2,1)}, bf16[3,128,896]{2,1,0:T(8,128)(2,1)S(1)}, u32[]{:S(2)}) copy-start(bf16[3,128,896]{2,1,0:T(8,128)(2,1)S(1)} %collective-permute-done.1) | copy-start | bytes 2064388
  55.7 18.1 %collective-permute-start.2 = (bf16[3,128,896]{2,1,0:T(8,128)(2,1)S(1)}, bf16[3,128,896]{2,1,0:T(8,128)(2,1)}, u32[]{:S(2)}, u32[]{:S(2)}) collective-permute-start(bf16[3,128,896]{2,1,0:T(8,128)(2,1)S(1)} %collective-permute-done.1), channel_id=1, source_target_pairs={{0,8},{8,16},{16,24},{24,32},{32,40},{40,48},{48,56},{56,64},{64,7... | collective-permute-start | bytes 2064392 | tf_op jit(solution)/shard_map/ppermute | solution.py:60
  58.1 26.2 %copy-start.3 = (bf16[3,128,896]{2,1,0:T(8,128)(2,1)}, bf16[3,128,896]{2,1,0:T(8,128)(2,1)S(1)}, u32[]{:S(2)}) copy-start(bf16[3,128,896]{2,1,0:T(8,128)(2,1)S(1)} %collective-permute-done.9) | copy-start | bytes 2064388
  58.1 17.7 %collective-permute-start.10 = (bf16[3,128,896]{2,1,0:T(8,128)(2,1)S(1)}, bf16[3,128,896]{2,1,0:T(8,128)(2,1)}, u32[]{:S(2)}, u32[]{:S(2)}) collective-permute-start(bf16[3,128,896]{2,1,0:T(8,128)(2,1)S(1)} %collective-permute-done.9), channel_id=1, source_target_pairs={{0,120},{8,0},{16,8},{24,16},{32,24},{40,32},{48,40},{56,48},{64,5... | collective-permute-start | bytes 2064392 | tf_op jit(solution)/shard_map/ppermute | solution.py:61
  65.0 19.2 %all-to-all-start.1 = ((bf16[4,80,2048]{2,1,0:T(8,128)(2,1)}), bf16[4,80,2048]{2,1,0:T(8,128)(2,1)S(1)}, u32[]{:S(2)}, u32[]{:S(2)}) async-start(bf16[4,80,2048]{2,1,0:T(8,128)(2,1)} %bitcast.54), calls=%async_computation.1 | async-start | bytes 2621440 | tf_op jit(solution)/shard_map/all_to_all | solution.py:73
  73.8 17.4 %collective-permute-start.3 = (bf16[3,128,896]{2,1,0:T(8,128)(2,1)}, bf16[3,128,896]{2,1,0:T(8,128)(2,1)}, u32[]{:S(2)}, u32[]{:S(2)}) collective-permute-start(bf16[3,128,896]{2,1,0:T(8,128)(2,1)} %collective-permute-done.2), channel_id=1, source_target_pairs={{0,8},{8,16},{16,24},{24,32},{32,40},{40,48},{48,56},{56,64},{64,7... | collective-permute-start | bytes 2064392 | tf_op jit(solution)/shard_map/ppermute | solution.py:60
  75.8 19.2 %collective-permute-start.11 = (bf16[3,128,896]{2,1,0:T(8,128)(2,1)}, bf16[3,128,896]{2,1,0:T(8,128)(2,1)}, u32[]{:S(2)}, u32[]{:S(2)}) collective-permute-start(bf16[3,128,896]{2,1,0:T(8,128)(2,1)} %collective-permute-done.10), channel_id=1, source_target_pairs={{0,120},{8,0},{16,8},{24,16},{32,24},{40,32},{48,40},{56,48},{64,5... | collective-permute-start | bytes 2064392 | tf_op jit(solution)/shard_map/ppermute | solution.py:61
  84.2 28.2 %all-to-all-start = ((bf16[4,80,2048]{2,1,0:T(8,128)(2,1)}), bf16[4,80,2048]{2,1,0:T(8,128)(2,1)S(1)}, u32[]{:S(2)}, u32[]{:S(2)}) async-start(bf16[4,80,2048]{2,1,0:T(8,128)(2,1)} %bitcast.3), calls=%async_computation | async-start | bytes 2621440 | tf_op jit(solution)/shard_map/all_to_all | solution.py:72
  88.1 142.6 %reduce-scatter.2.cloned.1.call-start = ((), (), s32[]{:S(2)}) async-start(), calls=%async_computation.4 | async-start | bytes 2949120 | tf_op jit(solution)/shard_map/reduce_scatter | solution.py:98
  91.2 16.6 %collective-permute-start.4 = (bf16[3,128,896]{2,1,0:T(8,128)(2,1)}, bf16[3,128,896]{2,1,0:T(8,128)(2,1)}, u32[]{:S(2)}, u32[]{:S(2)}) collective-permute-start(bf16[3,128,896]{2,1,0:T(8,128)(2,1)} %collective-permute-done.3), channel_id=1, source_target_pairs={{0,8},{8,16},{16,24},{24,32},{32,40},{40,48},{48,56},{56,64},{64,7... | collective-permute-start | bytes 2064392 | tf_op jit(solution)/shard_map/ppermute | solution.py:60
  95.0 20.7 %collective-permute-start.12 = (bf16[3,128,896]{2,1,0:T(8,128)(2,1)}, bf16[3,128,896]{2,1,0:T(8,128)(2,1)}, u32[]{:S(2)}, u32[]{:S(2)}) collective-permute-start(bf16[3,128,896]{2,1,0:T(8,128)(2,1)} %collective-permute-done.11), channel_id=1, source_target_pairs={{0,120},{8,0},{16,8},{24,16},{32,24},{40,32},{48,40},{56,48},{64,5... | collective-permute-start | bytes 2064392 | tf_op jit(solution)/shard_map/ppermute | solution.py:61
  107.8 15.7 %collective-permute-start.5 = (bf16[3,128,896]{2,1,0:T(8,128)(2,1)}, bf16[3,128,896]{2,1,0:T(8,128)(2,1)}, u32[]{:S(2)}, u32[]{:S(2)}) collective-permute-start(bf16[3,128,896]{2,1,0:T(8,128)(2,1)} %collective-permute-done.4), channel_id=1, source_target_pairs={{0,8},{8,16},{16,24},{24,32},{32,40},{40,48},{48,56},{56,64},{64,7... | collective-permute-start | bytes 2064392 | tf_op jit(solution)/shard_map/ppermute | solution.py:60
  115.7 6.5 %copy-start.6 = (bf16[3,128,896]{2,1,0:T(8,128)(2,1)S(1)}, bf16[3,128,896]{2,1,0:T(8,128)(2,1)}, u32[]{:S(2)}) copy-start(bf16[3,128,896]{2,1,0:T(8,128)(2,1)} %copy-done.5) | copy-start | bytes 2064388
  115.7 6.5 %copy-start.7 = (bf16[2048,896]{1,0:T(8,128)(2,1)S(1)}, bf16[2048,896]{1,0:T(8,128)(2,1)}, u32[]{:S(2)}) copy-start(bf16[2048,896]{1,0:T(8,128)(2,1)} %get-tuple-element.45) | copy-start | bytes 11010052
  115.7 15.0 %collective-permute-start.13 = (bf16[3,128,896]{2,1,0:T(8,128)(2,1)}, bf16[3,128,896]{2,1,0:T(8,128)(2,1)S(1)}, u32[]{:S(2)}, u32[]{:S(2)}) collective-permute-start(bf16[3,128,896]{2,1,0:T(8,128)(2,1)} %collective-permute-done.12), channel_id=1, source_target_pairs={{0,120},{8,0},{16,8},{24,16},{32,24},{40,32},{48,40},{56,48},{64,5... | collective-permute-start | bytes 2064392 | tf_op jit(solution)/shard_map/ppermute | solution.py:61
  123.5 16.4 %collective-permute-start.6 = (bf16[3,128,896]{2,1,0:T(8,128)(2,1)}, bf16[3,128,896]{2,1,0:T(8,128)(2,1)S(1)}, u32[]{:S(2)}, u32[]{:S(2)}) collective-permute-start(bf16[3,128,896]{2,1,0:T(8,128)(2,1)} %collective-permute-done.5), channel_id=1, source_target_pairs={{0,8},{8,16},{16,24},{24,32},{32,40},{40,48},{48,56},{56,64},{64,7... | collective-permute-start | bytes 2064392 | tf_op jit(solution)/shard_map/ppermute | solution.py:60
  130.7 14.2 %collective-permute-start.14 = (bf16[3,128,896]{2,1,0:T(8,128)(2,1)S(1)}, bf16[3,128,896]{2,1,0:T(8,128)(2,1)S(1)}, u32[]{:S(2)}, u32[]{:S(2)}) collective-permute-start(bf16[3,128,896]{2,1,0:T(8,128)(2,1)S(1)} %collective-permute-done.13), channel_id=1, source_target_pairs={{0,120},{8,0},{16,8},{24,16},{32,24},{40,32},{48,40},{56,48},{64,5... | collective-permute-start | bytes 2064392 | tf_op jit(solution)/shard_map/ppermute | solution.py:61
  139.9 11.3 %collective-permute-start.7 = (bf16[3,64,896]{2,1,0:T(8,128)(2,1)S(1)}, bf16[3,64,896]{2,1,0:T(8,128)(2,1)S(1)}, u32[]{:S(2)}, u32[]{:S(2)}) collective-permute-start(bf16[3,64,896]{2,1,0:T(8,128)(2,1)S(1)} %slice.218), channel_id=1, source_target_pairs={{0,8},{8,16},{16,24},{24,32},{32,40},{40,48},{48,56},{56,64},{64,7... | collective-permute-start | bytes 1032200 | tf_op jit(solution)/shard_map/ppermute | solution.py:65
  144.9 9.9 %collective-permute-start.15 = (bf16[3,64,896]{2,1,0:T(8,128)(2,1)S(1)}, bf16[3,64,896]{2,1,0:T(8,128)(2,1)S(1)}, u32[]{:S(2)}, u32[]{:S(2)}) collective-permute-start(bf16[3,64,896]{2,1,0:T(8,128)(2,1)S(1)} %slice.219), channel_id=1, source_target_pairs={{0,120},{8,0},{16,8},{24,16},{32,24},{40,32},{48,40},{56,48},{64,5... | collective-permute-start | bytes 1032200 | tf_op jit(solution)/shard_map/ppermute | solution.py:66
  155.8 7.6 %copy-start.4 = (bf16[3,128,896]{2,1,0:T(8,128)(2,1)S(1)}, bf16[3,128,896]{2,1,0:T(8,128)(2,1)}, u32[]{:S(2)}) copy-start(bf16[3,128,896]{2,1,0:T(8,128)(2,1)} %copy-done.3) | copy-start | bytes 2064388
  156.6 7.7 %copy-start.2 = (bf16[3,128,896]{2,1,0:T(8,128)(2,1)S(1)}, bf16[3,128,896]{2,1,0:T(8,128)(2,1)}, u32[]{:S(2)}) copy-start(bf16[3,128,896]{2,1,0:T(8,128)(2,1)} %copy-done.1) | copy-start | bytes 2064388
  168.6 2.0 copy-start.9
  172.9 2.0 copy-start.8
Sparse Core Ops, SparseCore 0:
  185.4 45.2 reduce-scatter.1

commit v4 on v3

--- a/solution.py
+++ b/solution.py
@@ -65,10 +65,23 @@
     far_low = lax.ppermute(cw[:, :cut], "ez", forward)
     far_high = lax.ppermute(ccw[:, cut:], "ez", backward)
     by_distance[half_steps] = jnp.concatenate([far_low, far_high], axis=1)
-    origin = (place - jnp.arange(member_count, dtype=jnp.int32)) % member_count
-    gate_full = jnp.concatenate([chunk[0] for chunk in by_distance], axis=0)
-    up_full = jnp.concatenate([chunk[1] for chunk in by_distance], axis=0)
-    down_full = jnp.concatenate([chunk[2] for chunk in by_distance], axis=0)
+    order = [0]
+    for step in range(1, half_steps):
+        order += [step, member_count - step]
+    order += [half_steps]
+    early = 1 + 2 * (half_steps // 2)
+    group_a, group_b = order[:early], order[early:]
+    origin = (place - jnp.asarray(order, dtype=jnp.int32)) % member_count
+    back_index = jnp.asarray(np.argsort(order), dtype=jnp.int32)
+    back = jnp.take(back_index, (place - jnp.arange(member_count, dtype=jnp.int32)) % member_count)
+
+    def joined(group, which):
+        return jnp.concatenate([by_distance[k][which] for k in group], axis=0)
+
+    gate_a, gate_b = joined(group_a, 0), joined(group_b, 0)
+    up_a, up_b = joined(group_a, 1), joined(group_b, 1)
+    down_a, down_b = joined(group_a, 2), joined(group_b, 2)
+    cut_at = early * block_width
     member_tokens = lax.all_to_all(sent_tokens, "ey", split_axis=0, concat_axis=0, tiled=True)
     member_cot = lax.all_to_all(sent_cot, "ey", split_axis=0, concat_axis=0, tiled=True)
     row_total = plane_count * CAP
@@ -78,24 +91,42 @@
     member_cot = jnp.take(
         member_cot.reshape(row_total, member_count, block_width), origin, axis=1
     ).reshape(row_total, model_width)
-    gate_pre = jnp.dot(member_tokens, gate_full, preferred_element_type=jnp.float32)
-    up_pre = jnp.dot(member_tokens, up_full, preferred_element_type=jnp.float32)
-    hidden_grad = jnp.dot(member_cot, down_full, preferred_element_type=jnp.float32)
+    tokens_a, tokens_b = member_tokens[:, :cut_at], member_tokens[:, cut_at:]
+    cot_a, cot_b = member_cot[:, :cut_at], member_cot[:, cut_at:]
+
+    def dot(left, right):
+        return jnp.dot(left, right, preferred_element_type=jnp.float32)
+
+    def dot_t(left, right):
+        return lax.dot_general(
+            left, right, (((1,), (1,)), ((), ())), preferred_element_type=jnp.float32
+        )
+
+    gate_pre = dot(tokens_a, gate_a) + dot(tokens_b, gate_b)
+    up_pre = dot(tokens_a, up_a) + dot(tokens_b, up_b)
+    hidden_grad = dot(cot_a, down_a) + dot(cot_b, down_b)
     hidden, gate_grad, up_grad = activate(gate_pre, up_pre, hidden_grad)
-    out_part = lax.dot_general(
-        hidden, down_full, (((1,), (1,)), ((), ())), preferred_element_type=jnp.float32
-    )
-    in_part = lax.dot_general(
-        gate_grad, gate_full, (((1,), (1,)), ((), ())), preferred_element_type=jnp.float32
-    )
-    in_part = in_part + lax.dot_general(
-        up_grad, up_full, (((1,), (1,)), ((), ())), preferred_element_type=jnp.float32
+    out_part = jnp.concatenate([dot_t(hidden, down_a), dot_t(hidden, down_b)], axis=1)
+    in_part = jnp.concatenate(
+        [
+            dot_t(gate_grad, gate_a) + dot_t(up_grad, up_a),
+            dot_t(gate_grad, gate_b) + dot_t(up_grad, up_b),
+        ],
+        axis=1,
     )
     results = jnp.stack([out_part, in_part], axis=1).astype(jnp.bfloat16)
     results = jnp.take(
-        results.reshape(row_total, 2, member_count, block_width), origin, axis=2
-    ).reshape(row_total, 2, model_width)
-    summed = lax.psum_scatter(results, "tp", scatter_dimension=2, tiled=True)
+        results.reshape(row_total, 2, member_count, block_width), back, axis=2
+    )
+    pair_count = lax.axis_size("tc")
+    core = lax.axis_index("tc")
+    out_width = model_width // (lax.axis_size("tx") * pair_count)
+    results = results.reshape(row_total, 2, -1, pair_count, out_width)
+    own = jnp.where(core == 0, results[:, :, :, 0], results[:, :, :, 1])
+    other = jnp.where(core == 0, results[:, :, :, 1], results[:, :, :, 0])
+    other = lax.ppermute(other, "tc", [(0, 1), (1, 0)])
+    pair_sum = (own.astype(jnp.float32) + other.astype(jnp.float32)).astype(jnp.bfloat16)
+    summed = lax.psum_scatter(pair_sum, "tx", scatter_dimension=2, tiled=True)
     rounded = summed.reshape(plane_count, CAP, 2, -1)
     returned = lax.all_to_all(rounded, "ey", split_axis=0, concat_axis=0, tiled=True)
     returned = returned.reshape(slot_count, 2, -1).astype(jnp.float32)
@@ -113,9 +144,13 @@
 def solution(mesh):
     ed_size = mesh.shape["ed"]
     member_count = ed_size // EXPERTS
-    devices = np.asarray(mesh.devices).reshape(EXPERTS, member_count, mesh.shape["tp"])
-    split_mesh = Mesh(devices, ("ey", "ez", "tp"))
+    pair_count = 2
+    devices = np.asarray(mesh.devices).reshape(
+        EXPERTS, member_count, mesh.shape["tp"] // pair_count, pair_count
+    )
+    split_mesh = Mesh(devices, ("ey", "ez", "tx", "tc"))
     ed = ("ey", "ez")
+    tp = ("tx", "tc")
     return jax.shard_map(
         per_device,
         mesh=split_mesh,
@@ -124,10 +159,10 @@
             P(ed, None),
             P(ed, None),
             P(ed, None),
-            P(ed, "tp"),
-            P(ed, "tp"),
-            P("tp", ed),
+            P(ed, tp),
+            P(ed, tp),
+            P(tp, ed),
         ),
-        out_specs=(P(ed, "tp"), P(ed, "tp")),
+        out_specs=(P(ed, tp), P(ed, tp)),
         check_vma=False,
     )

time: 254 us -> 260 us (1.024)
  starting transfers between devices: 70.6 us -> 77.4 us
  waiting for transfers between devices: 91.1 us -> 84.6 us
  other arithmetic: 9.77 us -> 14.7 us
    reduce_scatter x1, waiting for transfers between devices: 45.4 us -> 27.3 us  [per_device(): summed = lax.psum_scatter(pair_sum, 'tx', scatter_dimension=2, tiled=True)]
    all_to_all x1, waiting for transfers between devices: 0.01 us -> 14 us  [per_device(): lax.all_to_all(sent_tokens, 'ey', split_axis=0, concat_axis=0, tiled=True)]
    unnamed x43 -> x48, local copies, waits for them, and re-layouts: 27.8 us -> 15.3 us
    ppermute x0 -> x1, starting transfers between devices: none -> 10 us  [per_device(): other = lax.ppermute(other, 'tc', [(0, 1), (1, 0)])]
    gather x1 -> x5, local copies, waits for them, and re-layouts: 2.43 us -> 12.2 us  [the longest x3 11.5 us: per_device(): jnp.take(results.reshape(row_total, 2, member_count, block_width), back,...]
    ppermute x7, waiting for transfers between devices: 4.71 us -> 0.02 us  [per_device(): ccw = lax.ppermute(ccw, 'ez', backward)]
    select_n x3 -> x4, other arithmetic: 3.82 us -> 7.78 us  [the longest x1 5.5 us: per_device(): other = jnp.where(core == 0, results[:, :, :, 1], results[:, :, :, 0])]
    ppermute x1, waiting for transfers between devices: 0.01 us -> 2.95 us  [per_device(): far_low = lax.ppermute(cw[:, :cut], 'ez', forward)]
  transfers between devices with their start and end apart: 19 -> 20, of which waited for: 13 -> 10; matrix products, arithmetic and copies ran while one was open for 11% -> 11% of each run, Pallas kernels for 0% -> 0%
where the time goes in v4:
time: 260 us; the launch traced here: 256 us
  waiting for transfers between devices  84.6 us (33%)
  starting transfers between devices  77.4 us (30%)
  local copies, waits for them, and re-layouts  38.6 us (15%)
  matrix products  16.5 us (6%)
  between operations  14.8 us (6%)
  other arithmetic  14.7 us (6%)
  blocking collectives  9.68 us (4%)
    ppermute x7, starting transfers between devices, per_device(): ccw = lax.ppermute(ccw, 'ez', backward)  36.9 us
    ppermute x7, waiting for transfers between devices, per_device(): cw = lax.ppermute(cw, 'ez', forward)  36.2 us
    reduce_scatter x1, waiting for transfers between devices, per_device(): summed = lax.psum_scatter(pair_sum, 'tx', scatter_dimension=2, tiled=True)  27.3 us
    ppermute x7, starting transfers between devices, per_device(): cw = lax.ppermute(cw, 'ez', forward)  15.8 us
    unnamed x48, local copies, waits for them, and re-layouts  15.3 us
    all_to_all x1, waiting for transfers between devices, per_device(): lax.all_to_all(sent_tokens, 'ey', split_axis=0, concat_axis=0, tiled=True)  14 us
    gather x3, local copies, waits for them, and re-layouts, per_device(): jnp.take(results.reshape(row_total, 2, member_count, block_width), back,...  11.5 us
    ppermute x1, starting transfers between devices, per_device(): other = lax.ppermute(other, 'tc', [(0, 1), (1, 0)])  10 us
  transfers between devices with their start and end apart: 20, of which 10 were waited for; matrix products, arithmetic and copies ran while one was open for 11% of the time, Pallas kernels for 0%

profile of v4, /device:TPU:1, one launch (start us, length us, event | category | flops | bytes accessed | tf_op | source)
XLA Modules:
  0.0 256.2 jit_solution(16967280391280029813)
XLA Ops:
  8.3 2.0 pad_maximum_fusion.1
  10.4 4.4 %collective-permute-start = (bf16[3,128,896]{2,1,0:T(8,128)(2,1)}, bf16[3,128,896]{2,1,0:T(8,128)(2,1)}, u32[]{:S(2)}, u32[]{:S(2)}) collective-permute-start(bf16[3,128,896]{2,1,0:T(8,128)(2,1)} %pad_maximum_fusion.1), channel_id=1, source_target_pairs={{0,8},{8,16},{16,24},{24,32},{32,40},{40,48},{48,56},{56,64},{64,7... | collective-permute-start | bytes 2064392 | tf_op jit(solution)/shard_map/ppermute | solution.py:60
  14.7 9.5 %collective-permute-start.1 = (bf16[3,128,896]{2,1,0:T(8,128)(2,1)}, bf16[3,128,896]{2,1,0:T(8,128)(2,1)}, u32[]{:S(2)}, u32[]{:S(2)}) collective-permute-start(bf16[3,128,896]{2,1,0:T(8,128)(2,1)} %pad_maximum_fusion.1), channel_id=1, source_target_pairs={{0,120},{8,0},{16,8},{24,16},{32,24},{40,32},{48,40},{56,48},{64,5... | collective-permute-start | bytes 2064392 | tf_op jit(solution)/shard_map/ppermute | solution.py:61
  26.6 1.6 convolution_convert_fusion
  28.2 4.3 %all-to-all-start = ((bf16[4,80,2048]{2,1,0:T(8,128)(2,1)}), bf16[4,80,2048]{2,1,0:T(8,128)(2,1)S(1)}, u32[]{:S(2)}, u32[]{:S(2)}) async-start(bf16[4,80,2048]{2,1,0:T(8,128)(2,1)} %bitcast.4), calls=%async_computation | async-start | bytes 2621440 | tf_op jit(solution)/shard_map/all_to_all | solution.py:85
  33.7 1.6 fusion
  35.3 14.0 %all-to-all-done = bf16[4,80,2048]{2,1,0:T(8,128)(2,1)S(1)} async-done(((bf16[4,80,2048]{2,1,0:T(8,128)(2,1)}), bf16[4,80,2048]{2,1,0:T(8,128)(2,1)S(1)}, u32[]{:S(2)}, u32[]{:S(2)}) %all-to-all-start) | async-done | bytes 1310752 | tf_op jit(solution)/shard_map/all_to_all | solution.py:85
  49.3 3.5 %all-to-all-start.1 = ((bf16[4,80,2048]{2,1,0:T(8,128)(2,1)}), bf16[4,80,2048]{2,1,0:T(8,128)(2,1)S(1)}, u32[]{:S(2)}, u32[]{:S(2)}) async-start(bf16[4,80,2048]{2,1,0:T(8,128)(2,1)} %bitcast.55), calls=%async_computation.1 | async-start | bytes 2621440 | tf_op jit(solution)/shard_map/all_to_all | solution.py:86
  52.9 1.9 collective-permute-start.2
  54.9 4.6 %collective-permute-start.3 = (bf16[3,128,896]{2,1,0:T(8,128)(2,1)}, bf16[3,128,896]{2,1,0:T(8,128)(2,1)}, u32[]{:S(2)}, u32[]{:S(2)}) collective-permute-start(bf16[3,128,896]{2,1,0:T(8,128)(2,1)} %collective-permute-done.1), channel_id=1, source_target_pairs={{0,120},{8,0},{16,8},{24,16},{32,24},{40,32},{48,40},{56,48},{64,5... | collective-permute-start | bytes 2064392 | tf_op jit(solution)/shard_map/ppermute | solution.py:61
  61.0 2.0 fusion.45
  63.0 8.2 %collective-permute-done.2 = bf16[3,128,896]{2,1,0:T(8,128)(2,1)} collective-permute-done((bf16[3,128,896]{2,1,0:T(8,128)(2,1)}, bf16[3,128,896]{2,1,0:T(8,128)(2,1)}, u32[]{:S(2)}, u32[]{:S(2)}) %collective-permute-start.2) | collective-permute-done | bytes 688160 | tf_op jit(solution)/shard_map/ppermute | solution.py:60
  71.2 1.9 collective-permute-start.4
  73.2 4.6 %collective-permute-start.5 = (bf16[3,128,896]{2,1,0:T(8,128)(2,1)}, bf16[3,128,896]{2,1,0:T(8,128)(2,1)}, u32[]{:S(2)}, u32[]{:S(2)}) collective-permute-start(bf16[3,128,896]{2,1,0:T(8,128)(2,1)} %collective-permute-done.3), channel_id=1, source_target_pairs={{0,120},{8,0},{16,8},{24,16},{32,24},{40,32},{48,40},{56,48},{64,5... | collective-permute-start | bytes 2064392 | tf_op jit(solution)/shard_map/ppermute | solution.py:61
  77.7 2.0 fusion.44
  81.1 1.8 gather_fusion.2
  82.9 1.9 gather_fusion.3
  84.7 1.8 select_bitcast_fusion.1
  88.8 1.2 fusion.43
  90.0 1.9 collective-permute-start.6
  92.0 4.6 %collective-permute-start.7 = (bf16[3,128,896]{2,1,0:T(8,128)(2,1)}, bf16[3,128,896]{2,1,0:T(8,128)(2,1)S(1)}, u32[]{:S(2)}, u32[]{:S(2)}) collective-permute-start(bf16[3,128,896]{2,1,0:T(8,128)(2,1)} %collective-permute-done.5), channel_id=1, source_target_pairs={{0,120},{8,0},{16,8},{24,16},{32,24},{40,32},{48,40},{56,48},{64,5... | collective-permute-start | bytes 2064392 | tf_op jit(solution)/shard_map/ppermute | solution.py:61
  96.6 1.3 fusion.42
  97.8 1.3 fusion.41
  99.1 1.3 fusion.40
  100.3 6.5 %collective-permute-done.6 = bf16[3,128,896]{2,1,0:T(8,128)(2,1)S(1)} collective-permute-done((bf16[3,128,896]{2,1,0:T(8,128)(2,1)}, bf16[3,128,896]{2,1,0:T(8,128)(2,1)S(1)}, u32[]{:S(2)}, u32[]{:S(2)}) %collective-permute-start.6) | collective-permute-done | bytes 688160 | tf_op jit(solution)/shard_map/ppermute | solution.py:60
  106.8 1.9 collective-permute-start.8
  108.8 4.6 %collective-permute-start.9 = (bf16[3,128,896]{2,1,0:T(8,128)(2,1)S(1)}, bf16[3,128,896]{2,1,0:T(8,128)(2,1)S(1)}, u32[]{:S(2)}, u32[]{:S(2)}) collective-permute-start(bf16[3,128,896]{2,1,0:T(8,128)(2,1)S(1)} %collective-permute-done.7), channel_id=1, source_target_pairs={{0,120},{8,0},{16,8},{24,16},{32,24},{40,32},{48,40},{56,48},{64,5... | collective-permute-start | bytes 2064392 | tf_op jit(solution)/shard_map/ppermute | solution.py:61
  114.5 8.0 %collective-permute-done.8 = bf16[3,128,896]{2,1,0:T(8,128)(2,1)S(1)} collective-permute-done((bf16[3,128,896]{2,1,0:T(8,128)(2,1)S(1)}, bf16[3,128,896]{2,1,0:T(8,128)(2,1)S(1)}, u32[]{:S(2)}, u32[]{:S(2)}) %collective-permute-start.8) | collective-permute-done | bytes 688160 | tf_op jit(solution)/shard_map/ppermute | solution.py:60
  122.6 1.9 collective-permute-start.10
  124.5 4.6 %collective-permute-start.11 = (bf16[3,128,896]{2,1,0:T(8,128)(2,1)S(1)}, bf16[3,128,896]{2,1,0:T(8,128)(2,1)S(1)}, u32[]{:S(2)}, u32[]{:S(2)}) collective-permute-start(bf16[3,128,896]{2,1,0:T(8,128)(2,1)S(1)} %collective-permute-done.9), channel_id=1, source_target_pairs={{0,120},{8,0},{16,8},{24,16},{32,24},{40,32},{48,40},{56,48},{64,5... | collective-permute-start | bytes 2064392 | tf_op jit(solution)/shard_map/ppermute | solution.py:61
  131.1 6.3 %collective-permute-done.10 = bf16[3,128,896]{2,1,0:T(8,128)(2,1)S(1)} collective-permute-done((bf16[3,128,896]{2,1,0:T(8,128)(2,1)S(1)}, bf16[3,128,896]{2,1,0:T(8,128)(2,1)S(1)}, u32[]{:S(2)}, u32[]{:S(2)}) %collective-permute-start.10) | collective-permute-done | bytes 688160 | tf_op jit(solution)/shard_map/ppermute | solution.py:60
  137.4 1.9 collective-permute-start.12
  139.4 4.6 %collective-permute-start.13 = (bf16[3,128,896]{2,1,0:T(8,128)(2,1)S(1)}, bf16[3,128,896]{2,1,0:T(8,128)(2,1)S(1)}, u32[]{:S(2)}, u32[]{:S(2)}) collective-permute-start(bf16[3,128,896]{2,1,0:T(8,128)(2,1)S(1)} %collective-permute-done.11), channel_id=1, source_target_pairs={{0,120},{8,0},{16,8},{24,16},{32,24},{40,32},{48,40},{56,48},{64,5... | collective-permute-start | bytes 2064392 | tf_op jit(solution)/shard_map/ppermute | solution.py:61
  144.2 7.2 %collective-permute-done.12 = bf16[3,128,896]{2,1,0:T(8,128)(2,1)S(1)} collective-permute-done((bf16[3,128,896]{2,1,0:T(8,128)(2,1)S(1)}, bf16[3,128,896]{2,1,0:T(8,128)(2,1)S(1)}, u32[]{:S(2)}, u32[]{:S(2)}) %collective-permute-start.12) | collective-permute-done | bytes 688160 | tf_op jit(solution)/shard_map/ppermute | solution.py:60
  151.5 1.9 collective-permute-start.14
  153.4 4.8 %collective-permute-start.15 = (bf16[3,64,896]{2,1,0:T(8,128)(2,1)S(1)}, bf16[3,64,896]{2,1,0:T(8,128)(2,1)S(1)}, u32[]{:S(2)}, u32[]{:S(2)}) collective-permute-start(bf16[3,64,896]{2,1,0:T(8,128)(2,1)S(1)} %slice.256), channel_id=1, source_target_pairs={{0,120},{8,0},{16,8},{24,16},{32,24},{40,32},{48,40},{56,48},{64,5... | collective-permute-start | bytes 1032200 | tf_op jit(solution)/shard_map/ppermute | solution.py:66
  158.4 3.0 %collective-permute-done.14 = bf16[3,64,896]{2,1,0:T(8,128)(2,1)S(1)} collective-permute-done((bf16[3,64,896]{2,1,0:T(8,128)(2,1)S(1)}, bf16[3,64,896]{2,1,0:T(8,128)(2,1)S(1)}, u32[]{:S(2)}, u32[]{:S(2)}) %collective-permute-start.14) | collective-permute-done | bytes 344096 | tf_op jit(solution)/shard_map/ppermute | solution.py:65
  161.4 1.5 collective-permute-done.15
  173.5 2.4 gather_fusion.1
  175.8 5.0 %copy.139 = bf16[320,2,16,128]{3,2,1,0:T(8,128)(2,1)} copy(bf16[320,2,16,128]{3,0,1,2:T(8,128)(2,1)} %bitcast.286) | data formatting | bytes 5242880 | tf_op jit(solution)/shard_map/jit(_take)/gather | solution.py:118
  180.8 4.2 %gather.21 = bf16[320,2,4,2,256]{4,3,2,1,0:T(2,128)(2,1)S(1)} reshape(bf16[320,2,16,128]{3,2,1,0:T(8,128)(2,1)} %copy.139) | data formatting | bytes 5242880 | tf_op jit(solution)/shard_map/jit(_take)/gather | solution.py:118
  184.9 2.3 broadcast_select_fusion
  187.2 5.5 %broadcast_select_fusion.1 = (bf16[320,2,4,1,256]{4,3,2,1,0:T(2,128)(2,1)S(1)}, f32[320,2,4,1,256]{4,3,2,1,0:T(1,128)S(1)}) fusion(pred[]{:T(512)S(6)} %eq.57, bf16[320,2,4,2,256]{4,3,2,1,0:T(2,128)(2,1)S(1)} %broadcast_select_fusion), kind=kLoop, calls=%fused_computation.5 | loop fusion | flops 1966080 | bytes 6553601 | tf_op jit(solution)/shard_map/jit(_where)/select_n | solution.py:126
  194.5 10.0 %collective-permute-start.16 = (bf16[320,2,4,256]{3,2,1,0:T(4,128)(2,1)S(1)}, bf16[320,2,4,256]{3,2,1,0:T(4,128)(2,1)S(1)}, u32[]{:S(2)}, u32[]{:S(2)}) collective-permute-start(bf16[320,2,4,256]{3,2,1,0:T(4,128)(2,1)S(1)} %copy.141), channel_id=1, source_target_pairs={{0,1},{1,0},{2,3},{3,2},{4,5},{5,4},{6,7},{7,6},{8,9},{9,8},{10,11... | collective-permute-start | bytes 3932168 | tf_op jit(solution)/shard_map/ppermute | solution.py:127
  204.5 2.6 %collective-permute-done.16 = bf16[320,2,4,256]{3,2,1,0:T(4,128)(2,1)S(1)} collective-permute-done((bf16[320,2,4,256]{3,2,1,0:T(4,128)(2,1)S(1)}, bf16[320,2,4,256]{3,2,1,0:T(4,128)(2,1)S(1)}, u32[]{:S(2)}, u32[]{:S(2)}) %collective-permute-start.16) | collective-permute-done | bytes 1310752 | tf_op jit(solution)/shard_map/ppermute | solution.py:127
  208.0 1.3 copy.142
  209.4 27.3 %reduce-scatter.2.cloned.1.call-done = bf16[320,2,1,256]{3,0,1,2:T(8,128)(2,1)} async-done(((bf16[320,2,4,256]{3,0,1,2:T(8,128)(2,1)}), bf16[320,2,1,256]{3,0,1,2:T(8,128)(2,1)}) %reduce-scatter.2.cloned.1.call-update) | async-done | bytes 327696 | tf_op jit(solution)/shard_map/reduce_scatter | solution.py:129
  237.7 9.7 %all_to_all.15 = bf16[4,80,2,256]{3,1,2,0:T(8,128)(2,1)S(1)} all-to-all(bf16[4,80,2,256]{3,1,2,0:T(8,128)(2,1)S(1)} %copy.143), channel_id=1, replica_groups=mesh['ey'=4,'ez'=16,'tx'=4,'tc'=2] {'ey'}, dimensions={0} | all-to-all | bytes 655360 | tf_op jit(solution)/shard_map/all_to_all | solution.py:131
  (114 shorter events, 29.7 us)
Async XLA Ops:
  7.2 19.4 %copy-start = (bf16[128,2048]{1,0:T(8,128)(2,1)S(1)}, bf16[128,2048]{1,0:T(8,128)(2,1)}, u32[]{:S(2)}) copy-start(bf16[128,2048]{1,0:T(8,128)(2,1)} %param.11) | copy-start | bytes 1572868
  7.2 17.1 %copy-start.10 = (s32[128,2]{0,1:T(2,128)S(1)}, s32[128,2]{0,1:T(2,128)}, u32[]{:S(2)}) copy-start(s32[128,2]{0,1:T(2,128)} %param.13) | copy-start | bytes 3076
  10.4 42.5 %collective-permute-start = (bf16[3,128,896]{2,1,0:T(8,128)(2,1)}, bf16[3,128,896]{2,1,0:T(8,128)(2,1)}, u32[]{:S(2)}, u32[]{:S(2)}) collective-permute-start(bf16[3,128,896]{2,1,0:T(8,128)(2,1)} %pad_maximum_fusion.1), channel_id=1, source_target_pairs={{0,8},{8,16},{16,24},{24,32},{32,40},{40,48},{48,56},{56,64},{64,7... | collective-permute-start | bytes 2064392 | tf_op jit(solution)/shard_map/ppermute | solution.py:60
  14.7 40.1 %collective-permute-start.1 = (bf16[3,128,896]{2,1,0:T(8,128)(2,1)}, bf16[3,128,896]{2,1,0:T(8,128)(2,1)}, u32[]{:S(2)}, u32[]{:S(2)}) collective-permute-start(bf16[3,128,896]{2,1,0:T(8,128)(2,1)} %pad_maximum_fusion.1), channel_id=1, source_target_pairs={{0,120},{8,0},{16,8},{24,16},{32,24},{40,32},{48,40},{56,48},{64,5... | collective-permute-start | bytes 2064392 | tf_op jit(solution)/shard_map/ppermute | solution.py:61
  28.2 4.4 %copy-start.2 = (s32[16]{0:T(128)S(1)}, s32[16]{0:T(128)}, u32[]{:S(2)}) copy-start(s32[16]{0:T(128)} %constant.91.clone) | copy-start | bytes 196
  28.2 5.3 %copy-start.11 = (f32[128,2]{0,1:T(2,128)S(1)}, f32[128,2]{0,1:T(2,128)}, u32[]{:S(2)}) copy-start(f32[128,2]{0,1:T(2,128)} %param.14) | copy-start | bytes 3076
  28.2 5.5 %copy-start.12 = (s32[16]{0:T(128)S(1)}, s32[16]{0:T(128)}, u32[]{:S(2)}) copy-start(s32[16]{0:T(128)} %constant.92) | copy-start | bytes 196
  28.2 5.5 %copy-start.6 = (bf16[128,2048]{1,0:T(8,128)(2,1)S(1)}, bf16[128,2048]{1,0:T(8,128)(2,1)}, u32[]{:S(2)}) copy-start(bf16[128,2048]{1,0:T(8,128)(2,1)} %param.12) | copy-start | bytes 1572868
  28.2 21.1 %all-to-all-start = ((bf16[4,80,2048]{2,1,0:T(8,128)(2,1)}), bf16[4,80,2048]{2,1,0:T(8,128)(2,1)S(1)}, u32[]{:S(2)}, u32[]{:S(2)}) async-start(bf16[4,80,2048]{2,1,0:T(8,128)(2,1)} %bitcast.4), calls=%async_computation | async-start | bytes 2621440 | tf_op jit(solution)/shard_map/all_to_all | solution.py:85
  35.3 24.2 %copy-start.4 = (bf16[128,896]{1,0:T(8,128)(2,1)S(1)}, bf16[128,896]{1,0:T(8,128)(2,1)}, u32[]{:S(2)}) copy-start(bf16[128,896]{1,0:T(8,128)(2,1)} %param.15) | copy-start | bytes 688132
  35.3 24.2 %copy-start.5 = (bf16[128,896]{1,0:T(8,128)(2,1)S(1)}, bf16[128,896]{1,0:T(8,128)(2,1)}, u32[]{:S(2)}) copy-start(bf16[128,896]{1,0:T(8,128)(2,1)} %param.16) | copy-start | bytes 688132
  49.3 31.1 %all-to-all-start.1 = ((bf16[4,80,2048]{2,1,0:T(8,128)(2,1)}), bf16[4,80,2048]{2,1,0:T(8,128)(2,1)S(1)}, u32[]{:S(2)}, u32[]{:S(2)}) async-start(bf16[4,80,2048]{2,1,0:T(8,128)(2,1)} %bitcast.55), calls=%async_computation.1 | async-start | bytes 2621440 | tf_op jit(solution)/shard_map/all_to_all | solution.py:86
  52.8 183.9 %reduce-scatter.2.cloned.1.call-start = ((), (), s32[]{:S(2)}) async-start(), calls=%async_computation.4 | async-start | bytes 1638400 | tf_op jit(solution)/shard_map/reduce_scatter | solution.py:129
  52.9 18.3 %collective-permute-start.2 = (bf16[3,128,896]{2,1,0:T(8,128)(2,1)}, bf16[3,128,896]{2,1,0:T(8,128)(2,1)}, u32[]{:S(2)}, u32[]{:S(2)}) collective-permute-start(bf16[3,128,896]{2,1,0:T(8,128)(2,1)} %collective-permute-done), channel_id=1, source_target_pairs={{0,8},{8,16},{16,24},{24,32},{32,40},{40,48},{48,56},{56,64},{64,7... | collective-permute-start | bytes 2064392 | tf_op jit(solution)/shard_map/ppermute | solution.py:60
  54.9 18.3 %collective-permute-start.3 = (bf16[3,128,896]{2,1,0:T(8,128)(2,1)}, bf16[3,128,896]{2,1,0:T(8,128)(2,1)}, u32[]{:S(2)}, u32[]{:S(2)}) collective-permute-start(bf16[3,128,896]{2,1,0:T(8,128)(2,1)} %collective-permute-done.1), channel_id=1, source_target_pairs={{0,120},{8,0},{16,8},{24,16},{32,24},{40,32},{48,40},{56,48},{64,5... | collective-permute-start | bytes 2064392 | tf_op jit(solution)/shard_map/ppermute | solution.py:61
  71.2 18.8 %collective-permute-start.4 = (bf16[3,128,896]{2,1,0:T(8,128)(2,1)}, bf16[3,128,896]{2,1,0:T(8,128)(2,1)}, u32[]{:S(2)}, u32[]{:S(2)}) collective-permute-start(bf16[3,128,896]{2,1,0:T(8,128)(2,1)} %collective-permute-done.2), channel_id=1, source_target_pairs={{0,8},{8,16},{16,24},{24,32},{32,40},{40,48},{48,56},{56,64},{64,7... | collective-permute-start | bytes 2064392 | tf_op jit(solution)/shard_map/ppermute | solution.py:60
  73.2 18.8 %collective-permute-start.5 = (bf16[3,128,896]{2,1,0:T(8,128)(2,1)}, bf16[3,128,896]{2,1,0:T(8,128)(2,1)}, u32[]{:S(2)}, u32[]{:S(2)}) collective-permute-start(bf16[3,128,896]{2,1,0:T(8,128)(2,1)} %collective-permute-done.3), channel_id=1, source_target_pairs={{0,120},{8,0},{16,8},{24,16},{32,24},{40,32},{48,40},{56,48},{64,5... | collective-permute-start | bytes 2064392 | tf_op jit(solution)/shard_map/ppermute | solution.py:61
  82.9 1.9 copy-start.3
  84.7 2.5 copy-start.9
  86.5 1.6 copy-start.8
  86.9 1.9 copy-start.7
  90.0 16.8 %collective-permute-start.6 = (bf16[3,128,896]{2,1,0:T(8,128)(2,1)}, bf16[3,128,896]{2,1,0:T(8,128)(2,1)S(1)}, u32[]{:S(2)}, u32[]{:S(2)}) collective-permute-start(bf16[3,128,896]{2,1,0:T(8,128)(2,1)} %collective-permute-done.4), channel_id=1, source_target_pairs={{0,8},{8,16},{16,24},{24,32},{32,40},{40,48},{48,56},{56,64},{64,7... | collective-permute-start | bytes 2064392 | tf_op jit(solution)/shard_map/ppermute | solution.py:60
  92.0 16.8 %collective-permute-start.7 = (bf16[3,128,896]{2,1,0:T(8,128)(2,1)}, bf16[3,128,896]{2,1,0:T(8,128)(2,1)S(1)}, u32[]{:S(2)}, u32[]{:S(2)}) collective-permute-start(bf16[3,128,896]{2,1,0:T(8,128)(2,1)} %collective-permute-done.5), channel_id=1, source_target_pairs={{0,120},{8,0},{16,8},{24,16},{32,24},{40,32},{48,40},{56,48},{64,5... | collective-permute-start | bytes 2064392 | tf_op jit(solution)/shard_map/ppermute | solution.py:61
  106.8 15.7 %collective-permute-start.8 = (bf16[3,128,896]{2,1,0:T(8,128)(2,1)S(1)}, bf16[3,128,896]{2,1,0:T(8,128)(2,1)S(1)}, u32[]{:S(2)}, u32[]{:S(2)}) collective-permute-start(bf16[3,128,896]{2,1,0:T(8,128)(2,1)S(1)} %collective-permute-done.6), channel_id=1, source_target_pairs={{0,8},{8,16},{16,24},{24,32},{32,40},{40,48},{48,56},{56,64},{64,7... | collective-permute-start | bytes 2064392 | tf_op jit(solution)/shard_map/ppermute | solution.py:60
  108.8 15.7 %collective-permute-start.9 = (bf16[3,128,896]{2,1,0:T(8,128)(2,1)S(1)}, bf16[3,128,896]{2,1,0:T(8,128)(2,1)S(1)}, u32[]{:S(2)}, u32[]{:S(2)}) collective-permute-start(bf16[3,128,896]{2,1,0:T(8,128)(2,1)S(1)} %collective-permute-done.7), channel_id=1, source_target_pairs={{0,120},{8,0},{16,8},{24,16},{32,24},{40,32},{48,40},{56,48},{64,5... | collective-permute-start | bytes 2064392 | tf_op jit(solution)/shard_map/ppermute | solution.py:61
  122.6 14.9 %collective-permute-start.10 = (bf16[3,128,896]{2,1,0:T(8,128)(2,1)S(1)}, bf16[3,128,896]{2,1,0:T(8,128)(2,1)S(1)}, u32[]{:S(2)}, u32[]{:S(2)}) collective-permute-start(bf16[3,128,896]{2,1,0:T(8,128)(2,1)S(1)} %collective-permute-done.8), channel_id=1, source_target_pairs={{0,8},{8,16},{16,24},{24,32},{32,40},{40,48},{48,56},{56,64},{64,7... | collective-permute-start | bytes 2064392 | tf_op jit(solution)/shard_map/ppermute | solution.py:60
  124.5 14.9 %collective-permute-start.11 = (bf16[3,128,896]{2,1,0:T(8,128)(2,1)S(1)}, bf16[3,128,896]{2,1,0:T(8,128)(2,1)S(1)}, u32[]{:S(2)}, u32[]{:S(2)}) collective-permute-start(bf16[3,128,896]{2,1,0:T(8,128)(2,1)S(1)} %collective-permute-done.9), channel_id=1, source_target_pairs={{0,120},{8,0},{16,8},{24,16},{32,24},{40,32},{48,40},{56,48},{64,5... | collective-permute-start | bytes 2064392 | tf_op jit(solution)/shard_map/ppermute | solution.py:61
  137.4 14.0 %collective-permute-start.12 = (bf16[3,128,896]{2,1,0:T(8,128)(2,1)S(1)}, bf16[3,128,896]{2,1,0:T(8,128)(2,1)S(1)}, u32[]{:S(2)}, u32[]{:S(2)}) collective-permute-start(bf16[3,128,896]{2,1,0:T(8,128)(2,1)S(1)} %collective-permute-done.10), channel_id=1, source_target_pairs={{0,8},{8,16},{16,24},{24,32},{32,40},{40,48},{48,56},{56,64},{64,7... | collective-permute-start | bytes 2064392 | tf_op jit(solution)/shard_map/ppermute | solution.py:60
  139.4 14.0 %collective-permute-start.13 = (bf16[3,128,896]{2,1,0:T(8,128)(2,1)S(1)}, bf16[3,128,896]{2,1,0:T(8,128)(2,1)S(1)}, u32[]{:S(2)}, u32[]{:S(2)}) collective-permute-start(bf16[3,128,896]{2,1,0:T(8,128)(2,1)S(1)} %collective-permute-done.11), channel_id=1, source_target_pairs={{0,120},{8,0},{16,8},{24,16},{32,24},{40,32},{48,40},{56,48},{64,5... | collective-permute-start | bytes 2064392 | tf_op jit(solution)/shard_map/ppermute | solution.py:61
  151.5 9.9 %collective-permute-start.14 = (bf16[3,64,896]{2,1,0:T(8,128)(2,1)S(1)}, bf16[3,64,896]{2,1,0:T(8,128)(2,1)S(1)}, u32[]{:S(2)}, u32[]{:S(2)}) collective-permute-start(bf16[3,64,896]{2,1,0:T(8,128)(2,1)S(1)} %slice.255), channel_id=1, source_target_pairs={{0,8},{8,16},{16,24},{24,32},{32,40},{40,48},{48,56},{56,64},{64,7... | collective-permute-start | bytes 1032200 | tf_op jit(solution)/shard_map/ppermute | solution.py:65
  153.4 9.4 %collective-permute-start.15 = (bf16[3,64,896]{2,1,0:T(8,128)(2,1)S(1)}, bf16[3,64,896]{2,1,0:T(8,128)(2,1)S(1)}, u32[]{:S(2)}, u32[]{:S(2)}) collective-permute-start(bf16[3,64,896]{2,1,0:T(8,128)(2,1)S(1)} %slice.256), channel_id=1, source_target_pairs={{0,120},{8,0},{16,8},{24,16},{32,24},{40,32},{48,40},{56,48},{64,5... | collective-permute-start | bytes 1032200 | tf_op jit(solution)/shard_map/ppermute | solution.py:66
  194.5 12.7 %collective-permute-start.16 = (bf16[320,2,4,256]{3,2,1,0:T(4,128)(2,1)S(1)}, bf16[320,2,4,256]{3,2,1,0:T(4,128)(2,1)S(1)}, u32[]{:S(2)}, u32[]{:S(2)}) collective-permute-start(bf16[320,2,4,256]{3,2,1,0:T(4,128)(2,1)S(1)} %copy.141), channel_id=1, source_target_pairs={{0,1},{1,0},{2,3},{3,2},{4,5},{5,4},{6,7},{7,6},{8,9},{9,8},{10,11... | collective-permute-start | bytes 3932168 | tf_op jit(solution)/shard_map/ppermute | solution.py:127
  209.4 40.0 %copy-start.1 = (bf16[128,2048]{1,0:T(8,128)(2,1)S(1)}, bf16[128,2048]{1,0:T(8,128)(2,1)}, u32[]{:S(2)}) copy-start(bf16[128,2048]{1,0:T(8,128)(2,1)} %param.11) | copy-start | bytes 1572868
Sparse Core Ops, SparseCore 0:
  209.5 27.1 reduce-scatter.1

commit v5 on v3

--- a/solution.py
+++ b/solution.py
@@ -92,12 +92,36 @@
         up_grad, up_full, (((1,), (1,)), ((), ())), preferred_element_type=jnp.float32
     )
     results = jnp.stack([out_part, in_part], axis=1).astype(jnp.bfloat16)
-    results = jnp.take(
-        results.reshape(row_total, 2, member_count, block_width), origin, axis=2
-    ).reshape(row_total, 2, model_width)
-    summed = lax.psum_scatter(results, "tp", scatter_dimension=2, tiled=True)
+    results = results.reshape(row_total, 2, member_count, block_width)
+    pair_count = lax.axis_size("tc")
+    chip_count = lax.axis_size("tx")
+    core = lax.axis_index("tc")
+    out_width = model_width // (chip_count * pair_count)
+    per_out = out_width // block_width
+    base = (
+        jnp.arange(chip_count, dtype=jnp.int32)[:, None] * (pair_count * per_out)
+        + jnp.arange(per_out, dtype=jnp.int32)[None, :]
+    ).reshape(-1)
+    own = jnp.take(results, origin[base + core * per_out], axis=2)
+    other = jnp.take(results, origin[base + (1 - core) * per_out], axis=2)
+    other = lax.ppermute(other, "tc", [(0, 1), (1, 0)])
+    pair_sum = (own.astype(jnp.float32) + other.astype(jnp.float32)).astype(jnp.bfloat16)
+    pair_sum = pair_sum.reshape(row_total, 2, chip_count, out_width)
+    summed = lax.psum_scatter(pair_sum, "tx", scatter_dimension=2, tiled=True)
     rounded = summed.reshape(plane_count, CAP, 2, -1)
-    returned = lax.all_to_all(rounded, "ey", split_axis=0, concat_axis=0, tiled=True)
+    plane = lax.axis_index("ey")
+    from_shift = [lax.dynamic_index_in_dim(rounded, plane, axis=0, keepdims=False)]
+    for shift in range(1, plane_count):
+        piece = lax.dynamic_index_in_dim(
+            rounded, (plane + shift) % plane_count, axis=0, keepdims=False
+        )
+        pairs = [(i, (i + shift) % plane_count) for i in range(plane_count)]
+        from_shift.append(lax.ppermute(piece, "ey", pairs))
+    returned = jnp.take(
+        jnp.stack(from_shift, axis=0),
+        (plane - jnp.arange(plane_count, dtype=jnp.int32)) % plane_count,
+        axis=0,
+    )
     returned = returned.reshape(slot_count, 2, -1).astype(jnp.float32)
     picker_full = picker.astype(jnp.float32)
     weighted = picker_full * slot_weight[:, None]
@@ -113,9 +137,13 @@
 def solution(mesh):
     ed_size = mesh.shape["ed"]
     member_count = ed_size // EXPERTS
-    devices = np.asarray(mesh.devices).reshape(EXPERTS, member_count, mesh.shape["tp"])
-    split_mesh = Mesh(devices, ("ey", "ez", "tp"))
+    pair_count = 2
+    devices = np.asarray(mesh.devices).reshape(
+        EXPERTS, member_count, mesh.shape["tp"] // pair_count, pair_count
+    )
+    split_mesh = Mesh(devices, ("ey", "ez", "tx", "tc"))
     ed = ("ey", "ez")
+    tp = ("tx", "tc")
     return jax.shard_map(
         per_device,
         mesh=split_mesh,
@@ -124,10 +152,10 @@
             P(ed, None),
             P(ed, None),
             P(ed, None),
-            P(ed, "tp"),
-            P(ed, "tp"),
-            P("tp", ed),
+            P(ed, tp),
+            P(ed, tp),
+            P(tp, ed),
         ),
-        out_specs=(P(ed, "tp"), P(ed, "tp")),
+        out_specs=(P(ed, tp), P(ed, tp)),
         check_vma=False,
     )

time: 254 us -> 258 us (1.016)
  starting transfers between devices: 70.6 us -> 89.5 us
  waiting for transfers between devices: 91.1 us -> 78 us
  blocking collectives: 8.69 us -> 0 us
  local copies, waits for them, and re-layouts: 37 us -> 43.7 us
    ppermute x0 -> x4, starting transfers between devices: none -> 19.9 us  [the longest x3 10.5 us: per_device(): from_shift.append(lax.ppermute(piece, 'ey', pairs))]
    reduce_scatter x1, waiting for transfers between devices: 45.4 us -> 27.1 us  [per_device(): summed = lax.psum_scatter(pair_sum, 'tx', scatter_dimension=2, tiled=True)]
    all_to_all x1 -> x0, blocking collectives: 8.69 us -> none  [per_device(): lax.all_to_all(rounded, 'ey', split_axis=0, concat_axis=0, tiled=True)]
    ppermute x0 -> x4, waiting for transfers between devices: none -> 3.68 us  [the longest x3 3.18 us: per_device(): from_shift.append(lax.ppermute(piece, 'ey', pairs))]
    gather x1 -> x6, local copies, waits for them, and re-layouts: 2.43 us -> 5.45 us  [the longest x2 2.44 us: per_device(): own = jnp.take(results, origin[base + core * per_out], axis=2)]
    ppermute x7, waiting for transfers between devices: 37.1 us -> 40 us  [per_device(): cw = lax.ppermute(cw, 'ez', forward)]
    unnamed x43 -> x42, local copies, waits for them, and re-layouts: 27.8 us -> 28.5 us
  transfers between devices with their start and end apart: 19 -> 23, of which waited for: 13 -> 11; matrix products, arithmetic and copies ran while one was open for 11% -> 12% of each run, Pallas kernels for 0% -> 0%
where the time goes in v5:
time: 258 us; the launch traced here: 255 us
  starting transfers between devices  89.5 us (35%)
  waiting for transfers between devices  78 us (30%)
  local copies, waits for them, and re-layouts  43.7 us (17%)
  matrix products  18.8 us (7%)
  between operations  14.7 us (6%)
  other arithmetic  10.8 us (4%)
    ppermute x7, waiting for transfers between devices, per_device(): cw = lax.ppermute(cw, 'ez', forward)  40 us
    ppermute x7, starting transfers between devices, per_device(): ccw = lax.ppermute(ccw, 'ez', backward)  37.8 us
    unnamed x42, local copies, waits for them, and re-layouts  28.5 us
    reduce_scatter x1, waiting for transfers between devices, per_device(): summed = lax.psum_scatter(pair_sum, 'tx', scatter_dimension=2, tiled=True)  27.1 us
    ppermute x7, starting transfers between devices, per_device(): cw = lax.ppermute(cw, 'ez', forward)  15.8 us
    ppermute x3, starting transfers between devices, per_device(): from_shift.append(lax.ppermute(piece, 'ey', pairs))  10.5 us
    ppermute x1, starting transfers between devices, per_device(): other = lax.ppermute(other, 'tc', [(0, 1), (1, 0)])  9.4 us
    ppermute x1, starting transfers between devices, per_device(): far_high = lax.ppermute(ccw[:, cut:], 'ez', backward)  5.5 us
  transfers between devices with their start and end apart: 23, of which 11 were waited for; matrix products, arithmetic and copies ran while one was open for 12% of the time, Pallas kernels for 0%

profile of v5, /device:TPU:1, one launch (start us, length us, event | category | flops | bytes accessed | tf_op | source)
XLA Modules:
  0.0 255.4 jit_solution(4928152548411759435)
XLA Ops:
  9.5 4.4 %collective-permute-start = (bf16[3,128,896]{2,1,0:T(8,128)(2,1)S(1)}, bf16[3,128,896]{2,1,0:T(8,128)(2,1)}, u32[]{:S(2)}, u32[]{:S(2)}) collective-permute-start(bf16[3,128,896]{2,1,0:T(8,128)(2,1)S(1)} %pad_maximum_fusion), channel_id=1, source_target_pairs={{0,8},{8,16},{16,24},{24,32},{32,40},{40,48},{48,56},{56,64},{64,7... | collective-permute-start | bytes 2064392 | tf_op jit(solution)/shard_map/ppermute | solution.py:60
  13.9 9.5 %collective-permute-start.8 = (bf16[3,128,896]{2,1,0:T(8,128)(2,1)S(1)}, bf16[3,128,896]{2,1,0:T(8,128)(2,1)S(1)}, u32[]{:S(2)}, u32[]{:S(2)}) collective-permute-start(bf16[3,128,896]{2,1,0:T(8,128)(2,1)S(1)} %pad_maximum_fusion), channel_id=1, source_target_pairs={{0,120},{8,0},{16,8},{24,16},{32,24},{40,32},{48,40},{56,48},{64,5... | collective-permute-start | bytes 2064392 | tf_op jit(solution)/shard_map/ppermute | solution.py:61
  26.3 10.4 %collective-permute-done = bf16[3,128,896]{2,1,0:T(8,128)(2,1)} collective-permute-done((bf16[3,128,896]{2,1,0:T(8,128)(2,1)S(1)}, bf16[3,128,896]{2,1,0:T(8,128)(2,1)}, u32[]{:S(2)}, u32[]{:S(2)}) %collective-permute-start) | collective-permute-done | bytes 688160 | tf_op jit(solution)/shard_map/ppermute | solution.py:60
  36.7 1.9 collective-permute-start.1
  38.6 4.6 %collective-permute-start.9 = (bf16[3,128,896]{2,1,0:T(8,128)(2,1)S(1)}, bf16[3,128,896]{2,1,0:T(8,128)(2,1)}, u32[]{:S(2)}, u32[]{:S(2)}) collective-permute-start(bf16[3,128,896]{2,1,0:T(8,128)(2,1)S(1)} %collective-permute-done.8), channel_id=1, source_target_pairs={{0,120},{8,0},{16,8},{24,16},{32,24},{40,32},{48,40},{56,48},{64,5... | collective-permute-start | bytes 2064392 | tf_op jit(solution)/shard_map/ppermute | solution.py:61
  46.4 4.3 %all-to-all-start.1 = ((bf16[4,80,2048]{2,1,0:T(8,128)(2,1)}), bf16[4,80,2048]{2,1,0:T(8,128)(2,1)S(1)}, u32[]{:S(2)}, u32[]{:S(2)}) async-start(bf16[4,80,2048]{2,1,0:T(8,128)(2,1)} %bitcast.54), calls=%async_computation.1 | async-start | bytes 2621440 | tf_op jit(solution)/shard_map/all_to_all | solution.py:73
  50.7 5.2 %collective-permute-done.1 = bf16[3,128,896]{2,1,0:T(8,128)(2,1)} collective-permute-done((bf16[3,128,896]{2,1,0:T(8,128)(2,1)}, bf16[3,128,896]{2,1,0:T(8,128)(2,1)}, u32[]{:S(2)}, u32[]{:S(2)}) %collective-permute-start.1) | collective-permute-done | bytes 688160 | tf_op jit(solution)/shard_map/ppermute | solution.py:60
  55.8 1.9 collective-permute-start.2
  57.8 4.6 %collective-permute-start.10 = (bf16[3,128,896]{2,1,0:T(8,128)(2,1)}, bf16[3,128,896]{2,1,0:T(8,128)(2,1)}, u32[]{:S(2)}, u32[]{:S(2)}) collective-permute-start(bf16[3,128,896]{2,1,0:T(8,128)(2,1)} %collective-permute-done.9), channel_id=1, source_target_pairs={{0,120},{8,0},{16,8},{24,16},{32,24},{40,32},{48,40},{56,48},{64,5... | collective-permute-start | bytes 2064392 | tf_op jit(solution)/shard_map/ppermute | solution.py:61
  63.3 10.9 %collective-permute-done.2 = bf16[3,128,896]{2,1,0:T(8,128)(2,1)} collective-permute-done((bf16[3,128,896]{2,1,0:T(8,128)(2,1)}, bf16[3,128,896]{2,1,0:T(8,128)(2,1)}, u32[]{:S(2)}, u32[]{:S(2)}) %collective-permute-start.2) | collective-permute-done | bytes 688160 | tf_op jit(solution)/shard_map/ppermute | solution.py:60
  74.1 1.9 collective-permute-start.3
  76.1 4.6 %collective-permute-start.11 = (bf16[3,128,896]{2,1,0:T(8,128)(2,1)}, bf16[3,128,896]{2,1,0:T(8,128)(2,1)}, u32[]{:S(2)}, u32[]{:S(2)}) collective-permute-start(bf16[3,128,896]{2,1,0:T(8,128)(2,1)} %collective-permute-done.10), channel_id=1, source_target_pairs={{0,120},{8,0},{16,8},{24,16},{32,24},{40,32},{48,40},{56,48},{64,5... | collective-permute-start | bytes 2064392 | tf_op jit(solution)/shard_map/ppermute | solution.py:61
  82.3 4.2 %all-to-all-start = ((bf16[4,80,2048]{2,1,0:T(8,128)(2,1)}), bf16[4,80,2048]{2,1,0:T(8,128)(2,1)S(1)}, u32[]{:S(2)}, u32[]{:S(2)}) async-start(bf16[4,80,2048]{2,1,0:T(8,128)(2,1)} %bitcast.3), calls=%async_computation | async-start | bytes 2621440 | tf_op jit(solution)/shard_map/all_to_all | solution.py:72
  86.5 5.1 %collective-permute-done.3 = bf16[3,128,896]{2,1,0:T(8,128)(2,1)} collective-permute-done((bf16[3,128,896]{2,1,0:T(8,128)(2,1)}, bf16[3,128,896]{2,1,0:T(8,128)(2,1)}, u32[]{:S(2)}, u32[]{:S(2)}) %collective-permute-start.3) | collective-permute-done | bytes 688160 | tf_op jit(solution)/shard_map/ppermute | solution.py:60
  91.6 1.9 collective-permute-start.4
  94.4 4.6 %collective-permute-start.12 = (bf16[3,128,896]{2,1,0:T(8,128)(2,1)}, bf16[3,128,896]{2,1,0:T(8,128)(2,1)}, u32[]{:S(2)}, u32[]{:S(2)}) collective-permute-start(bf16[3,128,896]{2,1,0:T(8,128)(2,1)} %collective-permute-done.11), channel_id=1, source_target_pairs={{0,120},{8,0},{16,8},{24,16},{32,24},{40,32},{48,40},{56,48},{64,5... | collective-permute-start | bytes 2064392 | tf_op jit(solution)/shard_map/ppermute | solution.py:61
  99.7 8.5 %collective-permute-done.4 = bf16[3,128,896]{2,1,0:T(8,128)(2,1)} collective-permute-done((bf16[3,128,896]{2,1,0:T(8,128)(2,1)}, bf16[3,128,896]{2,1,0:T(8,128)(2,1)}, u32[]{:S(2)}, u32[]{:S(2)}) %collective-permute-start.4) | collective-permute-done | bytes 688160 | tf_op jit(solution)/shard_map/ppermute | solution.py:60
  108.2 1.9 collective-permute-start.5
  110.1 2.0 fusion.61
  113.4 1.8 gather_fusion.4
  116.1 4.8 %collective-permute-start.13 = (bf16[3,128,896]{2,1,0:T(8,128)(2,1)}, bf16[3,128,896]{2,1,0:T(8,128)(2,1)S(1)}, u32[]{:S(2)}, u32[]{:S(2)}) collective-permute-start(bf16[3,128,896]{2,1,0:T(8,128)(2,1)} %collective-permute-done.12), channel_id=1, source_target_pairs={{0,120},{8,0},{16,8},{24,16},{32,24},{40,32},{48,40},{56,48},{64,5... | collective-permute-start | bytes 2064392 | tf_op jit(solution)/shard_map/ppermute | solution.py:61
  122.5 2.0 fusion.60
  124.6 1.9 collective-permute-start.6
  126.5 2.0 fusion.59
  128.5 2.6 %collective-permute-done.13 = bf16[3,128,896]{2,1,0:T(8,128)(2,1)S(1)} collective-permute-done((bf16[3,128,896]{2,1,0:T(8,128)(2,1)}, bf16[3,128,896]{2,1,0:T(8,128)(2,1)S(1)}, u32[]{:S(2)}, u32[]{:S(2)}) %collective-permute-start.13) | collective-permute-done | bytes 688160 | tf_op jit(solution)/shard_map/ppermute | solution.py:61
  131.1 5.2 %collective-permute-start.14 = (bf16[3,128,896]{2,1,0:T(8,128)(2,1)S(1)}, bf16[3,128,896]{2,1,0:T(8,128)(2,1)S(1)}, u32[]{:S(2)}, u32[]{:S(2)}) collective-permute-start(bf16[3,128,896]{2,1,0:T(8,128)(2,1)S(1)} %collective-permute-done.13), channel_id=1, source_target_pairs={{0,120},{8,0},{16,8},{24,16},{32,24},{40,32},{48,40},{56,48},{64,5... | collective-permute-start | bytes 2064392 | tf_op jit(solution)/shard_map/ppermute | solution.py:61
  136.3 2.0 fusion.58
  138.3 2.0 fusion.57
  140.3 1.9 collective-permute-start.7
  142.3 2.0 fusion.56
  145.3 5.5 %collective-permute-start.15 = (bf16[3,64,896]{2,1,0:T(8,128)(2,1)S(1)}, bf16[3,64,896]{2,1,0:T(8,128)(2,1)S(1)}, u32[]{:S(2)}, u32[]{:S(2)}) collective-permute-start(bf16[3,64,896]{2,1,0:T(8,128)(2,1)S(1)} %slice.227), channel_id=1, source_target_pairs={{0,120},{8,0},{16,8},{24,16},{32,24},{40,32},{48,40},{56,48},{64,5... | collective-permute-start | bytes 1032200 | tf_op jit(solution)/shard_map/ppermute | solution.py:66
  151.6 3.5 %collective-permute-done.15 = bf16[3,64,896]{2,1,0:T(8,128)(2,1)S(1)} collective-permute-done((bf16[3,64,896]{2,1,0:T(8,128)(2,1)S(1)}, bf16[3,64,896]{2,1,0:T(8,128)(2,1)S(1)}, u32[]{:S(2)}, u32[]{:S(2)}) %collective-permute-start.15) | collective-permute-done | bytes 344096 | tf_op jit(solution)/shard_map/ppermute | solution.py:66
  157.7 2.0 fusion.51
  159.7 2.0 fusion.50
  161.7 2.0 fusion.49
  163.7 2.0 fusion.48
  168.1 3.7 %fusion.7 = f32[320,896]{1,0:T(8,128)S(1)} fusion(bf16[2048,896]{1,0:T(8,128)(2,1)} %get-tuple-element.6, bf16[16,40,8,128]{3,2,1,0:T(8,128)(2,1)S(1)} %get-tuple-element.56), kind=kOutput, calls=%fused_computation.19 | convolution fusion | flops 1174405120 | bytes 6127616 | tf_op jit(solution)/shard_map/dot_general | solution.py:82
  173.3 3.6 %fusion.14 = f32[320,2048]{1,0:T(8,128)S(1)} fusion(bf16[2048,896]{1,0:T(8,128)(2,1)} %get-tuple-element.6, f32[320,896]{1,0:T(8,128)S(1)} %fusion.4, f32[320,896]{1,0:T(8,128)S(1)} %fusion.9), kind=kOutput, calls=%fused_computation.38 | convolution fusion | flops 1176125440 | bytes 8585216 | tf_op jit(solution)/shard_map/dot_general | solution.py:91
  181.6 1.8 gather_fusion.6
  183.4 2.6 %select_bitcast_fusion = bf16[320,2,8,128]{3,0,1,2:T(8,128)(2,1)} fusion(bf16[8,320,2,128]{3,1,2,0:T(8,128)(2,1)} %gather_fusion.6, pred[8]{0:T(512)(128)(4,1)S(1)} %compare_and_fusion), kind=kLoop, calls=%fused_computation.25 | loop fusion | flops 655360 | bytes 2621448 | tf_op jit(solution)/shard_map/jit(_take)/select_n | solution.py:106
  186.0 9.4 %collective-permute-start.16 = (bf16[320,2,8,128]{3,0,1,2:T(8,128)(2,1)}, bf16[320,2,8,128]{3,0,1,2:T(8,128)(2,1)}, u32[]{:S(2)}, u32[]{:S(2)}) collective-permute-start(bf16[320,2,8,128]{3,0,1,2:T(8,128)(2,1)} %select_bitcast_fusion), channel_id=1, source_target_pairs={{0,1},{1,0},{2,3},{3,2},{4,5},{5,4},{6,7},{7,6},{8,9},{9,8},{10,11... | collective-permute-start | bytes 3932168 | tf_op jit(solution)/shard_map/ppermute | solution.py:107
  196.1 1.8 gather_fusion.5
  198.3 2.2 add_convert_fusion
  203.9 27.1 %reduce-scatter.2.cloned.1.call-done = bf16[320,2,1,256]{3,0,1,2:T(8,128)(2,1)} async-done(((bf16[320,2,4,256]{3,0,1,2:T(8,128)(2,1)}), bf16[320,2,1,256]{3,0,1,2:T(8,128)(2,1)}) %reduce-scatter.2.cloned.1.call-update) | async-done | bytes 327696 | tf_op jit(solution)/shard_map/reduce_scatter | solution.py:110
  232.1 3.2 %collective-permute-start.17 = (bf16[80,2,256]{2,0,1:T(8,128)(2,1)S(1)}, bf16[80,2,256]{2,0,1:T(8,128)(2,1)S(1)}, u32[]{:S(2)}, u32[]{:S(2)}) collective-permute-start(bf16[80,2,256]{2,0,1:T(8,128)(2,1)S(1)} %get-tuple-element.52), channel_id=1, source_target_pairs={{0,128},{128,256},{256,384},{384,0},{1,129},{129,257},{257,385},{3... | collective-permute-start | bytes 245768 | tf_op jit(solution)/shard_map/ppermute | solution.py:119
  235.3 4.2 %collective-permute-start.18 = (bf16[80,2,256]{2,0,1:T(8,128)(2,1)S(1)}, bf16[80,2,256]{2,0,1:T(8,128)(2,1)S(1)}, u32[]{:S(2)}, u32[]{:S(2)}) collective-permute-start(bf16[80,2,256]{2,0,1:T(8,128)(2,1)S(1)} %get-tuple-element.51), channel_id=1, source_target_pairs={{0,256},{128,384},{256,0},{384,128},{1,257},{129,385},{257,1},{385... | collective-permute-start | bytes 245768 | tf_op jit(solution)/shard_map/ppermute | solution.py:119
  239.5 3.1 %collective-permute-start.19 = (bf16[80,2,256]{2,0,1:T(8,128)(2,1)S(1)}, bf16[80,2,256]{2,0,1:T(8,128)(2,1)S(1)}, u32[]{:S(2)}, u32[]{:S(2)}) collective-permute-start(bf16[80,2,256]{2,0,1:T(8,128)(2,1)S(1)} %get-tuple-element.50), channel_id=1, source_target_pairs={{0,384},{128,0},{256,128},{384,256},{1,385},{129,1},{257,129},{385... | collective-permute-start | bytes 245768 | tf_op jit(solution)/shard_map/ppermute | solution.py:119
  242.6 3.2 %collective-permute-done.19 = bf16[80,2,256]{2,0,1:T(8,128)(2,1)S(1)} collective-permute-done((bf16[80,2,256]{2,0,1:T(8,128)(2,1)S(1)}, bf16[80,2,256]{2,0,1:T(8,128)(2,1)S(1)}, u32[]{:S(2)}, u32[]{:S(2)}) %collective-permute-start.19) | collective-permute-done | bytes 81952 | tf_op jit(solution)/shard_map/ppermute | solution.py:119
  (113 shorter events, 37.2 us)
Async XLA Ops:
  7.2 37.6 %copy-start = (bf16[128,2048]{1,0:T(8,128)(2,1)S(1)}, bf16[128,2048]{1,0:T(8,128)(2,1)}, u32[]{:S(2)}) copy-start(bf16[128,2048]{1,0:T(8,128)(2,1)} %param.12) | copy-start | bytes 1572868
  7.2 73.5 %copy-start.6 = (bf16[128,2048]{1,0:T(8,128)(2,1)S(1)}, bf16[128,2048]{1,0:T(8,128)(2,1)}, u32[]{:S(2)}) copy-start(bf16[128,2048]{1,0:T(8,128)(2,1)} %param.11) | copy-start | bytes 1572868
  9.5 27.2 %collective-permute-start = (bf16[3,128,896]{2,1,0:T(8,128)(2,1)S(1)}, bf16[3,128,896]{2,1,0:T(8,128)(2,1)}, u32[]{:S(2)}, u32[]{:S(2)}) collective-permute-start(bf16[3,128,896]{2,1,0:T(8,128)(2,1)S(1)} %pad_maximum_fusion), channel_id=1, source_target_pairs={{0,8},{8,16},{16,24},{24,32},{32,40},{40,48},{48,56},{56,64},{64,7... | collective-permute-start | bytes 2064392 | tf_op jit(solution)/shard_map/ppermute | solution.py:60
  13.9 24.7 %collective-permute-start.8 = (bf16[3,128,896]{2,1,0:T(8,128)(2,1)S(1)}, bf16[3,128,896]{2,1,0:T(8,128)(2,1)S(1)}, u32[]{:S(2)}, u32[]{:S(2)}) collective-permute-start(bf16[3,128,896]{2,1,0:T(8,128)(2,1)S(1)} %pad_maximum_fusion), channel_id=1, source_target_pairs={{0,120},{8,0},{16,8},{24,16},{32,24},{40,32},{48,40},{56,48},{64,5... | collective-permute-start | bytes 2064392 | tf_op jit(solution)/shard_map/ppermute | solution.py:61
  36.7 19.2 %collective-permute-start.1 = (bf16[3,128,896]{2,1,0:T(8,128)(2,1)}, bf16[3,128,896]{2,1,0:T(8,128)(2,1)}, u32[]{:S(2)}, u32[]{:S(2)}) collective-permute-start(bf16[3,128,896]{2,1,0:T(8,128)(2,1)} %collective-permute-done), channel_id=1, source_target_pairs={{0,8},{8,16},{16,24},{24,32},{32,40},{40,48},{48,56},{56,64},{64,7... | collective-permute-start | bytes 2064392 | tf_op jit(solution)/shard_map/ppermute | solution.py:60
  38.6 43.7 %copy-start.4 = (bf16[3,128,896]{2,1,0:T(8,128)(2,1)}, bf16[3,128,896]{2,1,0:T(8,128)(2,1)S(1)}, u32[]{:S(2)}) copy-start(bf16[3,128,896]{2,1,0:T(8,128)(2,1)S(1)} %collective-permute-done.8) | copy-start | bytes 2064388
  38.6 19.2 %collective-permute-start.9 = (bf16[3,128,896]{2,1,0:T(8,128)(2,1)S(1)}, bf16[3,128,896]{2,1,0:T(8,128)(2,1)}, u32[]{:S(2)}, u32[]{:S(2)}) collective-permute-start(bf16[3,128,896]{2,1,0:T(8,128)(2,1)S(1)} %collective-permute-done.8), channel_id=1, source_target_pairs={{0,120},{8,0},{16,8},{24,16},{32,24},{40,32},{48,40},{56,48},{64,5... | collective-permute-start | bytes 2064392 | tf_op jit(solution)/shard_map/ppermute | solution.py:61
  46.4 47.2 %copy-start.2 = (bf16[128,896]{1,0:T(8,128)(2,1)S(1)}, bf16[128,896]{1,0:T(8,128)(2,1)}, u32[]{:S(2)}) copy-start(bf16[128,896]{1,0:T(8,128)(2,1)} %param.15) | copy-start | bytes 688132
  46.4 47.2 %copy-start.3 = (bf16[128,896]{1,0:T(8,128)(2,1)S(1)}, bf16[128,896]{1,0:T(8,128)(2,1)}, u32[]{:S(2)}) copy-start(bf16[128,896]{1,0:T(8,128)(2,1)} %param.16) | copy-start | bytes 688132
  46.4 35.9 %all-to-all-start.1 = ((bf16[4,80,2048]{2,1,0:T(8,128)(2,1)}), bf16[4,80,2048]{2,1,0:T(8,128)(2,1)S(1)}, u32[]{:S(2)}, u32[]{:S(2)}) async-start(bf16[4,80,2048]{2,1,0:T(8,128)(2,1)} %bitcast.54), calls=%async_computation.1 | async-start | bytes 2621440 | tf_op jit(solution)/shard_map/all_to_all | solution.py:73
  55.8 18.3 %collective-permute-start.2 = (bf16[3,128,896]{2,1,0:T(8,128)(2,1)}, bf16[3,128,896]{2,1,0:T(8,128)(2,1)}, u32[]{:S(2)}, u32[]{:S(2)}) collective-permute-start(bf16[3,128,896]{2,1,0:T(8,128)(2,1)} %collective-permute-done.1), channel_id=1, source_target_pairs={{0,8},{8,16},{16,24},{24,32},{32,40},{40,48},{48,56},{56,64},{64,7... | collective-permute-start | bytes 2064392 | tf_op jit(solution)/shard_map/ppermute | solution.py:60
  57.8 18.3 %collective-permute-start.10 = (bf16[3,128,896]{2,1,0:T(8,128)(2,1)}, bf16[3,128,896]{2,1,0:T(8,128)(2,1)}, u32[]{:S(2)}, u32[]{:S(2)}) collective-permute-start(bf16[3,128,896]{2,1,0:T(8,128)(2,1)} %collective-permute-done.9), channel_id=1, source_target_pairs={{0,120},{8,0},{16,8},{24,16},{32,24},{40,32},{48,40},{56,48},{64,5... | collective-permute-start | bytes 2064392 | tf_op jit(solution)/shard_map/ppermute | solution.py:61
  74.1 17.4 %collective-permute-start.3 = (bf16[3,128,896]{2,1,0:T(8,128)(2,1)}, bf16[3,128,896]{2,1,0:T(8,128)(2,1)}, u32[]{:S(2)}, u32[]{:S(2)}) collective-permute-start(bf16[3,128,896]{2,1,0:T(8,128)(2,1)} %collective-permute-done.2), channel_id=1, source_target_pairs={{0,8},{8,16},{16,24},{24,32},{32,40},{40,48},{48,56},{56,64},{64,7... | collective-permute-start | bytes 2064392 | tf_op jit(solution)/shard_map/ppermute | solution.py:60
  76.1 18.3 %collective-permute-start.11 = (bf16[3,128,896]{2,1,0:T(8,128)(2,1)}, bf16[3,128,896]{2,1,0:T(8,128)(2,1)}, u32[]{:S(2)}, u32[]{:S(2)}) collective-permute-start(bf16[3,128,896]{2,1,0:T(8,128)(2,1)} %collective-permute-done.10), channel_id=1, source_target_pairs={{0,120},{8,0},{16,8},{24,16},{32,24},{40,32},{48,40},{56,48},{64,5... | collective-permute-start | bytes 2064392 | tf_op jit(solution)/shard_map/ppermute | solution.py:61
  82.3 30.5 %all-to-all-start = ((bf16[4,80,2048]{2,1,0:T(8,128)(2,1)}), bf16[4,80,2048]{2,1,0:T(8,128)(2,1)S(1)}, u32[]{:S(2)}, u32[]{:S(2)}) async-start(bf16[4,80,2048]{2,1,0:T(8,128)(2,1)} %bitcast.3), calls=%async_computation | async-start | bytes 2621440 | tf_op jit(solution)/shard_map/all_to_all | solution.py:72
  86.5 144.6 %reduce-scatter.2.cloned.1.call-start = ((), (), s32[]{:S(2)}) async-start(), calls=%async_computation.3 | async-start | bytes 1638400 | tf_op jit(solution)/shard_map/reduce_scatter | solution.py:110
  91.6 16.6 %collective-permute-start.4 = (bf16[3,128,896]{2,1,0:T(8,128)(2,1)}, bf16[3,128,896]{2,1,0:T(8,128)(2,1)}, u32[]{:S(2)}, u32[]{:S(2)}) collective-permute-start(bf16[3,128,896]{2,1,0:T(8,128)(2,1)} %collective-permute-done.3), channel_id=1, source_target_pairs={{0,8},{8,16},{16,24},{24,32},{32,40},{40,48},{48,56},{56,64},{64,7... | collective-permute-start | bytes 2064392 | tf_op jit(solution)/shard_map/ppermute | solution.py:60
  94.4 21.7 %collective-permute-start.12 = (bf16[3,128,896]{2,1,0:T(8,128)(2,1)}, bf16[3,128,896]{2,1,0:T(8,128)(2,1)}, u32[]{:S(2)}, u32[]{:S(2)}) collective-permute-start(bf16[3,128,896]{2,1,0:T(8,128)(2,1)} %collective-permute-done.11), channel_id=1, source_target_pairs={{0,120},{8,0},{16,8},{24,16},{32,24},{40,32},{48,40},{56,48},{64,5... | collective-permute-start | bytes 2064392 | tf_op jit(solution)/shard_map/ppermute | solution.py:61
  108.2 16.4 %collective-permute-start.5 = (bf16[3,128,896]{2,1,0:T(8,128)(2,1)}, bf16[3,128,896]{2,1,0:T(8,128)(2,1)}, u32[]{:S(2)}, u32[]{:S(2)}) collective-permute-start(bf16[3,128,896]{2,1,0:T(8,128)(2,1)} %collective-permute-done.4), channel_id=1, source_target_pairs={{0,8},{8,16},{16,24},{24,32},{32,40},{40,48},{48,56},{56,64},{64,7... | collective-permute-start | bytes 2064392 | tf_op jit(solution)/shard_map/ppermute | solution.py:60
  116.1 6.5 %copy-start.7 = (bf16[2048,896]{1,0:T(8,128)(2,1)S(1)}, bf16[2048,896]{1,0:T(8,128)(2,1)}, u32[]{:S(2)}) copy-start(bf16[2048,896]{1,0:T(8,128)(2,1)} %get-tuple-element.46) | copy-start | bytes 11010052
  116.1 15.0 %collective-permute-start.13 = (bf16[3,128,896]{2,1,0:T(8,128)(2,1)}, bf16[3,128,896]{2,1,0:T(8,128)(2,1)S(1)}, u32[]{:S(2)}, u32[]{:S(2)}) collective-permute-start(bf16[3,128,896]{2,1,0:T(8,128)(2,1)} %collective-permute-done.12), channel_id=1, source_target_pairs={{0,120},{8,0},{16,8},{24,16},{32,24},{40,32},{48,40},{56,48},{64,5... | collective-permute-start | bytes 2064392 | tf_op jit(solution)/shard_map/ppermute | solution.py:61
  124.6 15.7 %collective-permute-start.6 = (bf16[3,128,896]{2,1,0:T(8,128)(2,1)}, bf16[3,128,896]{2,1,0:T(8,128)(2,1)S(1)}, u32[]{:S(2)}, u32[]{:S(2)}) collective-permute-start(bf16[3,128,896]{2,1,0:T(8,128)(2,1)} %collective-permute-done.5), channel_id=1, source_target_pairs={{0,8},{8,16},{16,24},{24,32},{32,40},{40,48},{48,56},{56,64},{64,7... | collective-permute-start | bytes 2064392 | tf_op jit(solution)/shard_map/ppermute | solution.py:60
  131.1 14.2 %collective-permute-start.14 = (bf16[3,128,896]{2,1,0:T(8,128)(2,1)S(1)}, bf16[3,128,896]{2,1,0:T(8,128)(2,1)S(1)}, u32[]{:S(2)}, u32[]{:S(2)}) collective-permute-start(bf16[3,128,896]{2,1,0:T(8,128)(2,1)S(1)} %collective-permute-done.13), channel_id=1, source_target_pairs={{0,120},{8,0},{16,8},{24,16},{32,24},{40,32},{48,40},{56,48},{64,5... | collective-permute-start | bytes 2064392 | tf_op jit(solution)/shard_map/ppermute | solution.py:61
  140.3 11.3 %collective-permute-start.7 = (bf16[3,64,896]{2,1,0:T(8,128)(2,1)S(1)}, bf16[3,64,896]{2,1,0:T(8,128)(2,1)S(1)}, u32[]{:S(2)}, u32[]{:S(2)}) collective-permute-start(bf16[3,64,896]{2,1,0:T(8,128)(2,1)S(1)} %slice.226), channel_id=1, source_target_pairs={{0,8},{8,16},{16,24},{24,32},{32,40},{40,48},{48,56},{56,64},{64,7... | collective-permute-start | bytes 1032200 | tf_op jit(solution)/shard_map/ppermute | solution.py:65
  145.3 9.9 %collective-permute-start.15 = (bf16[3,64,896]{2,1,0:T(8,128)(2,1)S(1)}, bf16[3,64,896]{2,1,0:T(8,128)(2,1)S(1)}, u32[]{:S(2)}, u32[]{:S(2)}) collective-permute-start(bf16[3,64,896]{2,1,0:T(8,128)(2,1)S(1)} %slice.227), channel_id=1, source_target_pairs={{0,120},{8,0},{16,8},{24,16},{32,24},{40,32},{48,40},{56,48},{64,5... | collective-permute-start | bytes 1032200 | tf_op jit(solution)/shard_map/ppermute | solution.py:66
  156.9 8.8 %copy-start.5 = (bf16[3,128,896]{2,1,0:T(8,128)(2,1)S(1)}, bf16[3,128,896]{2,1,0:T(8,128)(2,1)}, u32[]{:S(2)}) copy-start(bf16[3,128,896]{2,1,0:T(8,128)(2,1)} %copy-done.4) | copy-start | bytes 2064388
  168.1 3.7 %copy-start.8 = (bf16[2048,896]{1,0:T(8,128)(2,1)S(1)}, bf16[2048,896]{1,0:T(8,128)(2,1)}, u32[]{:S(2)}) copy-start(bf16[2048,896]{1,0:T(8,128)(2,1)} %get-tuple-element.5) | copy-start | bytes 11010052
  186.0 12.4 %collective-permute-start.16 = (bf16[320,2,8,128]{3,0,1,2:T(8,128)(2,1)}, bf16[320,2,8,128]{3,0,1,2:T(8,128)(2,1)}, u32[]{:S(2)}, u32[]{:S(2)}) collective-permute-start(bf16[320,2,8,128]{3,0,1,2:T(8,128)(2,1)} %select_bitcast_fusion), channel_id=1, source_target_pairs={{0,1},{1,0},{2,3},{3,2},{4,5},{5,4},{6,7},{7,6},{8,9},{9,8},{10,11... | collective-permute-start | bytes 3932168 | tf_op jit(solution)/shard_map/ppermute | solution.py:107
  201.4 47.1 %copy-start.1 = (bf16[128,2048]{1,0:T(8,128)(2,1)S(1)}, bf16[128,2048]{1,0:T(8,128)(2,1)}, u32[]{:S(2)}) copy-start(bf16[128,2048]{1,0:T(8,128)(2,1)} %param.12) | copy-start | bytes 1572868
  232.1 10.5 %collective-permute-start.17 = (bf16[80,2,256]{2,0,1:T(8,128)(2,1)S(1)}, bf16[80,2,256]{2,0,1:T(8,128)(2,1)S(1)}, u32[]{:S(2)}, u32[]{:S(2)}) collective-permute-start(bf16[80,2,256]{2,0,1:T(8,128)(2,1)S(1)} %get-tuple-element.52), channel_id=1, source_target_pairs={{0,128},{128,256},{256,384},{384,0},{1,129},{129,257},{257,385},{3... | collective-permute-start | bytes 245768 | tf_op jit(solution)/shard_map/ppermute | solution.py:119
  235.3 7.3 %collective-permute-start.18 = (bf16[80,2,256]{2,0,1:T(8,128)(2,1)S(1)}, bf16[80,2,256]{2,0,1:T(8,128)(2,1)S(1)}, u32[]{:S(2)}, u32[]{:S(2)}) collective-permute-start(bf16[80,2,256]{2,0,1:T(8,128)(2,1)S(1)} %get-tuple-element.51), channel_id=1, source_target_pairs={{0,256},{128,384},{256,0},{384,128},{1,257},{129,385},{257,1},{385... | collective-permute-start | bytes 245768 | tf_op jit(solution)/shard_map/ppermute | solution.py:119
  239.5 6.3 %collective-permute-start.19 = (bf16[80,2,256]{2,0,1:T(8,128)(2,1)S(1)}, bf16[80,2,256]{2,0,1:T(8,128)(2,1)S(1)}, u32[]{:S(2)}, u32[]{:S(2)}) collective-permute-start(bf16[80,2,256]{2,0,1:T(8,128)(2,1)S(1)} %get-tuple-element.50), channel_id=1, source_target_pairs={{0,384},{128,0},{256,128},{384,256},{1,385},{129,1},{257,129},{385... | collective-permute-start | bytes 245768 | tf_op jit(solution)/shard_map/ppermute | solution.py:119
Sparse Core Ops, SparseCore 0:
  203.8 27.2 reduce-scatter.1

commit v6 on v3

--- a/solution.py
+++ b/solution.py
@@ -48,7 +48,8 @@
     member_count = lax.axis_size("ez")
     place = lax.axis_index("ez")
     block_width = w_gate.shape[0]
-    stacked = jnp.stack([w_gate, w_up, w_down.T], axis=0)
+    down_pieces = lax.all_gather(w_down, "ez", axis=0, tiled=False)
+    stacked = jnp.stack([w_gate, w_up], axis=0)
     forward = [(i, (i + 1) % member_count) for i in range(member_count)]
     backward = [(i, (i - 1) % member_count) for i in range(member_count)]
     half_steps = member_count // 2
@@ -68,22 +69,21 @@
     origin = (place - jnp.arange(member_count, dtype=jnp.int32)) % member_count
     gate_full = jnp.concatenate([chunk[0] for chunk in by_distance], axis=0)
     up_full = jnp.concatenate([chunk[1] for chunk in by_distance], axis=0)
-    down_full = jnp.concatenate([chunk[2] for chunk in by_distance], axis=0)
     member_tokens = lax.all_to_all(sent_tokens, "ey", split_axis=0, concat_axis=0, tiled=True)
     member_cot = lax.all_to_all(sent_cot, "ey", split_axis=0, concat_axis=0, tiled=True)
     row_total = plane_count * CAP
     member_tokens = jnp.take(
         member_tokens.reshape(row_total, member_count, block_width), origin, axis=1
     ).reshape(row_total, model_width)
-    member_cot = jnp.take(
-        member_cot.reshape(row_total, member_count, block_width), origin, axis=1
-    ).reshape(row_total, model_width)
+    member_cot = member_cot.reshape(row_total, member_count, block_width)
     gate_pre = jnp.dot(member_tokens, gate_full, preferred_element_type=jnp.float32)
     up_pre = jnp.dot(member_tokens, up_full, preferred_element_type=jnp.float32)
-    hidden_grad = jnp.dot(member_cot, down_full, preferred_element_type=jnp.float32)
+    hidden_grad = lax.dot_general(
+        member_cot, down_pieces, (((1, 2), (0, 2)), ((), ())), preferred_element_type=jnp.float32
+    )
     hidden, gate_grad, up_grad = activate(gate_pre, up_pre, hidden_grad)
     out_part = lax.dot_general(
-        hidden, down_full, (((1,), (1,)), ((), ())), preferred_element_type=jnp.float32
+        hidden, down_pieces, (((1,), (1,)), ((), ())), preferred_element_type=jnp.float32
     )
     in_part = lax.dot_general(
         gate_grad, gate_full, (((1,), (1,)), ((), ())), preferred_element_type=jnp.float32
@@ -91,10 +91,9 @@
     in_part = in_part + lax.dot_general(
         up_grad, up_full, (((1,), (1,)), ((), ())), preferred_element_type=jnp.float32
     )
+    in_part = jnp.take(in_part.reshape(row_total, member_count, block_width), origin, axis=1)
     results = jnp.stack([out_part, in_part], axis=1).astype(jnp.bfloat16)
-    results = jnp.take(
-        results.reshape(row_total, 2, member_count, block_width), origin, axis=2
-    ).reshape(row_total, 2, model_width)
+    results = results.reshape(row_total, 2, model_width)
     summed = lax.psum_scatter(results, "tp", scatter_dimension=2, tiled=True)
     rounded = summed.reshape(plane_count, CAP, 2, -1)
     returned = lax.all_to_all(rounded, "ey", split_axis=0, concat_axis=0, tiled=True)

time: 254 us -> 262 us (1.031)
  matrix products: 17.6 us -> 22.7 us
  waiting for transfers between devices: 91.1 us -> 95 us
  other arithmetic: 9.77 us -> 6.27 us
    reduce_scatter x1, waiting for transfers between devices: 45.4 us -> 53.4 us  [per_device(): summed = lax.psum_scatter(results, 'tp', scatter_dimension=2, tiled=True)]
    ppermute x7, waiting for transfers between devices: 37.1 us -> 31.7 us  [per_device(): cw = lax.ppermute(cw, 'ez', forward)]
    dot_general x2, matrix products: 3.08 us -> 8.07 us  [the longest x1 4.14 us: per_device(): lax.dot_general(member_cot, down_pieces, (((1, 2), (0, 2)), ((), ())), pr...]
    ppermute x7, starting transfers between devices: 15.8 us -> 19.8 us  [per_device(): cw = lax.ppermute(cw, 'ez', forward)]
    select_n x3 -> x1, other arithmetic: 3.82 us -> 0.02 us  [per_device(): jnp.take(member_tokens.reshape(row_total, member_count, block_width), ori...]
    gather x2 -> x3, local copies, waits for them, and re-layouts: 4.22 us -> 7.39 us  [per_device(): jnp.take(in_part.reshape(row_total, member_count, block_width), origin, a...]
    ppermute x1, waiting for transfers between devices: 0.01 us -> 2.92 us  [per_device(): far_low = lax.ppermute(cw[:, :cut], 'ez', forward)]
  transfers between devices with their start and end apart: 19 -> 20, of which waited for: 13 -> 11; matrix products, arithmetic and copies ran while one was open for 11% -> 15% of each run, Pallas kernels for 0% -> 0%
where the time goes in v6:
time: 262 us; the launch traced here: 258 us
  waiting for transfers between devices  95 us (36%)
  starting transfers between devices  72 us (27%)
  local copies, waits for them, and re-layouts  39.1 us (15%)
  matrix products  22.7 us (9%)
  between operations  14.5 us (6%)
  blocking collectives  8.74 us (3%)
  other arithmetic  6.27 us (2%)
    reduce_scatter x1, waiting for transfers between devices, per_device(): summed = lax.psum_scatter(results, 'tp', scatter_dimension=2, tiled=True)  53.4 us
    ppermute x7, starting transfers between devices, per_device(): ccw = lax.ppermute(ccw, 'ez', backward)  37.3 us
    ppermute x7, waiting for transfers between devices, per_device(): cw = lax.ppermute(cw, 'ez', forward)  31.7 us
    unnamed x43, local copies, waits for them, and re-layouts  26.1 us
    ppermute x7, starting transfers between devices, per_device(): cw = lax.ppermute(cw, 'ez', forward)  19.8 us
    all_to_all x1, blocking collectives, per_device(): lax.all_to_all(rounded, 'ey', split_axis=0, concat_axis=0, tiled=True)  8.74 us
    gather x3, local copies, waits for them, and re-layouts, per_device(): jnp.take(in_part.reshape(row_total, member_count, block_width), origin, a...  7.39 us
    ppermute x7, waiting for transfers between devices, per_device(): ccw = lax.ppermute(ccw, 'ez', backward)  5.44 us
  transfers between devices with their start and end apart: 20, of which 11 were waited for; matrix products, arithmetic and copies ran while one was open for 15% of the time, Pallas kernels for 0%

profile of v6, /device:TPU:1, one launch (start us, length us, event | category | flops | bytes accessed | tf_op | source)
XLA Modules:
  0.0 258.3 jit_solution(7158914976403734654)
XLA Ops:
  7.2 2.0 pad_maximum_fusion.1
  9.2 4.4 %collective-permute-start = (bf16[2,128,896]{2,1,0:T(8,128)(2,1)}, bf16[2,128,896]{2,1,0:T(8,128)(2,1)}, u32[]{:S(2)}, u32[]{:S(2)}) collective-permute-start(bf16[2,128,896]{2,1,0:T(8,128)(2,1)} %pad_maximum_fusion.1), channel_id=1, source_target_pairs={{0,8},{8,16},{16,24},{24,32},{32,40},{40,48},{48,56},{56,64},{64,7... | collective-permute-start | bytes 1376264 | tf_op jit(solution)/shard_map/ppermute | solution.py:61
  13.6 9.5 %collective-permute-start.8 = (bf16[2,128,896]{2,1,0:T(8,128)(2,1)}, bf16[2,128,896]{2,1,0:T(8,128)(2,1)S(1)}, u32[]{:S(2)}, u32[]{:S(2)}) collective-permute-start(bf16[2,128,896]{2,1,0:T(8,128)(2,1)} %pad_maximum_fusion.1), channel_id=1, source_target_pairs={{0,120},{8,0},{16,8},{24,16},{32,24},{40,32},{48,40},{56,48},{64,5... | collective-permute-start | bytes 1376264 | tf_op jit(solution)/shard_map/ppermute | solution.py:62
  28.3 4.3 %all-to-all-start = ((bf16[4,80,2048]{2,1,0:T(8,128)(2,1)}), bf16[4,80,2048]{2,1,0:T(8,128)(2,1)S(1)}, u32[]{:S(2)}, u32[]{:S(2)}) async-start(bf16[4,80,2048]{2,1,0:T(8,128)(2,1)} %bitcast.3), calls=%async_computation | async-start | bytes 2621440 | tf_op jit(solution)/shard_map/all_to_all | solution.py:72
  32.7 1.9 collective-permute-start.1
  34.6 4.6 %collective-permute-start.9 = (bf16[2,128,896]{2,1,0:T(8,128)(2,1)S(1)}, bf16[2,128,896]{2,1,0:T(8,128)(2,1)}, u32[]{:S(2)}, u32[]{:S(2)}) collective-permute-start(bf16[2,128,896]{2,1,0:T(8,128)(2,1)S(1)} %collective-permute-done.8), channel_id=1, source_target_pairs={{0,120},{8,0},{16,8},{24,16},{32,24},{40,32},{48,40},{56,48},{64,5... | collective-permute-start | bytes 1376264 | tf_op jit(solution)/shard_map/ppermute | solution.py:62
  39.3 11.6 %collective-permute-done.1 = bf16[2,128,896]{2,1,0:T(8,128)(2,1)} collective-permute-done((bf16[2,128,896]{2,1,0:T(8,128)(2,1)}, bf16[2,128,896]{2,1,0:T(8,128)(2,1)}, u32[]{:S(2)}, u32[]{:S(2)}) %collective-permute-start.1) | collective-permute-done | bytes 458784 | tf_op jit(solution)/shard_map/ppermute | solution.py:61
  51.0 1.9 collective-permute-start.2
  52.9 2.5 collective-permute-done.9
  55.4 4.5 %collective-permute-start.10 = (bf16[2,128,896]{2,1,0:T(8,128)(2,1)}, bf16[2,128,896]{2,1,0:T(8,128)(2,1)}, u32[]{:S(2)}, u32[]{:S(2)}) collective-permute-start(bf16[2,128,896]{2,1,0:T(8,128)(2,1)} %collective-permute-done.9), channel_id=1, source_target_pairs={{0,120},{8,0},{16,8},{24,16},{32,24},{40,32},{48,40},{56,48},{64,5... | collective-permute-start | bytes 1376264 | tf_op jit(solution)/shard_map/ppermute | solution.py:62
  61.5 3.5 %all-to-all-start.1 = ((bf16[4,80,2048]{2,1,0:T(8,128)(2,1)}), bf16[4,80,2048]{2,1,0:T(8,128)(2,1)S(1)}, u32[]{:S(2)}, u32[]{:S(2)}) async-start(bf16[4,80,2048]{2,1,0:T(8,128)(2,1)} %bitcast.40), calls=%async_computation.1 | async-start | bytes 2621440 | tf_op jit(solution)/shard_map/all_to_all | solution.py:73
  65.1 6.9 %collective-permute-done.2 = bf16[2,128,896]{2,1,0:T(8,128)(2,1)} collective-permute-done((bf16[2,128,896]{2,1,0:T(8,128)(2,1)}, bf16[2,128,896]{2,1,0:T(8,128)(2,1)}, u32[]{:S(2)}, u32[]{:S(2)}) %collective-permute-start.2) | collective-permute-done | bytes 458784 | tf_op jit(solution)/shard_map/ppermute | solution.py:61
  72.1 3.4 %collective-permute-start.3 = (bf16[2,128,896]{2,1,0:T(8,128)(2,1)}, bf16[2,128,896]{2,1,0:T(8,128)(2,1)}, u32[]{:S(2)}, u32[]{:S(2)}) collective-permute-start(bf16[2,128,896]{2,1,0:T(8,128)(2,1)} %collective-permute-done.2), channel_id=1, source_target_pairs={{0,8},{8,16},{16,24},{24,32},{32,40},{40,48},{48,56},{56,64},{64,7... | collective-permute-start | bytes 1376264 | tf_op jit(solution)/shard_map/ppermute | solution.py:61
  75.4 1.7 collective-permute-done.10
  77.2 5.3 %collective-permute-start.11 = (bf16[2,128,896]{2,1,0:T(8,128)(2,1)}, bf16[2,128,896]{2,1,0:T(8,128)(2,1)}, u32[]{:S(2)}, u32[]{:S(2)}) collective-permute-start(bf16[2,128,896]{2,1,0:T(8,128)(2,1)} %collective-permute-done.10), channel_id=1, source_target_pairs={{0,120},{8,0},{16,8},{24,16},{32,24},{40,32},{48,40},{56,48},{64,5... | collective-permute-start | bytes 1376264 | tf_op jit(solution)/shard_map/ppermute | solution.py:62
  82.5 1.8 constant_dynamic-update-slice_fusion.2
  84.4 9.4 %collective-permute-done.3 = bf16[2,128,896]{2,1,0:T(8,128)(2,1)} collective-permute-done((bf16[2,128,896]{2,1,0:T(8,128)(2,1)}, bf16[2,128,896]{2,1,0:T(8,128)(2,1)}, u32[]{:S(2)}, u32[]{:S(2)}) %collective-permute-start.3) | collective-permute-done | bytes 458784 | tf_op jit(solution)/shard_map/ppermute | solution.py:61
  93.7 3.4 %collective-permute-start.4 = (bf16[2,128,896]{2,1,0:T(8,128)(2,1)}, bf16[2,128,896]{2,1,0:T(8,128)(2,1)}, u32[]{:S(2)}, u32[]{:S(2)}) collective-permute-start(bf16[2,128,896]{2,1,0:T(8,128)(2,1)} %collective-permute-done.3), channel_id=1, source_target_pairs={{0,8},{8,16},{16,24},{24,32},{32,40},{40,48},{48,56},{56,64},{64,7... | collective-permute-start | bytes 1376264 | tf_op jit(solution)/shard_map/ppermute | solution.py:61
  98.3 5.3 %collective-permute-start.12 = (bf16[2,128,896]{2,1,0:T(8,128)(2,1)}, bf16[2,128,896]{2,1,0:T(8,128)(2,1)}, u32[]{:S(2)}, u32[]{:S(2)}) collective-permute-start(bf16[2,128,896]{2,1,0:T(8,128)(2,1)} %collective-permute-done.11), channel_id=1, source_target_pairs={{0,120},{8,0},{16,8},{24,16},{32,24},{40,32},{48,40},{56,48},{64,5... | collective-permute-start | bytes 1376264 | tf_op jit(solution)/shard_map/ppermute | solution.py:62
  103.6 1.9 fusion.42
  105.5 1.8 fusion.41
  110.2 2.9 %collective-permute-start.5 = (bf16[2,128,896]{2,1,0:T(8,128)(2,1)}, bf16[2,128,896]{2,1,0:T(8,128)(2,1)S(1)}, u32[]{:S(2)}, u32[]{:S(2)}) collective-permute-start(bf16[2,128,896]{2,1,0:T(8,128)(2,1)} %collective-permute-done.4), channel_id=1, source_target_pairs={{0,8},{8,16},{16,24},{24,32},{32,40},{40,48},{48,56},{56,64},{64,7... | collective-permute-start | bytes 1376264 | tf_op jit(solution)/shard_map/ppermute | solution.py:61
  113.2 3.6 %collective-permute-start.13 = (bf16[2,128,896]{2,1,0:T(8,128)(2,1)}, bf16[2,128,896]{2,1,0:T(8,128)(2,1)S(1)}, u32[]{:S(2)}, u32[]{:S(2)}) collective-permute-start(bf16[2,128,896]{2,1,0:T(8,128)(2,1)} %collective-permute-done.12), channel_id=1, source_target_pairs={{0,120},{8,0},{16,8},{24,16},{32,24},{40,32},{48,40},{56,48},{64,5... | collective-permute-start | bytes 1376264 | tf_op jit(solution)/shard_map/ppermute | solution.py:62
  116.7 1.9 fusion.40
  118.6 1.9 fusion.39
  120.9 1.9 collective-permute-start.6
  122.8 4.6 %collective-permute-start.14 = (bf16[2,128,896]{2,1,0:T(8,128)(2,1)S(1)}, bf16[2,128,896]{2,1,0:T(8,128)(2,1)S(1)}, u32[]{:S(2)}, u32[]{:S(2)}) collective-permute-start(bf16[2,128,896]{2,1,0:T(8,128)(2,1)S(1)} %collective-permute-done.13), channel_id=1, source_target_pairs={{0,120},{8,0},{16,8},{24,16},{32,24},{40,32},{48,40},{56,48},{64,5... | collective-permute-start | bytes 1376264 | tf_op jit(solution)/shard_map/ppermute | solution.py:62
  127.4 2.0 fusion.38
  130.1 3.4 %collective-permute-done.6 = bf16[2,128,896]{2,1,0:T(8,128)(2,1)S(1)} collective-permute-done((bf16[2,128,896]{2,1,0:T(8,128)(2,1)S(1)}, bf16[2,128,896]{2,1,0:T(8,128)(2,1)S(1)}, u32[]{:S(2)}, u32[]{:S(2)}) %collective-permute-start.6) | collective-permute-done | bytes 458784 | tf_op jit(solution)/shard_map/ppermute | solution.py:61
  133.6 1.9 collective-permute-start.7
  135.5 5.0 %collective-permute-start.15 = (bf16[2,64,896]{2,1,0:T(8,128)(2,1)S(1)}, bf16[2,64,896]{2,1,0:T(8,128)(2,1)S(1)}, u32[]{:S(2)}, u32[]{:S(2)}) collective-permute-start(bf16[2,64,896]{2,1,0:T(8,128)(2,1)S(1)} %slice.157), channel_id=1, source_target_pairs={{0,120},{8,0},{16,8},{24,16},{32,24},{40,32},{48,40},{56,48},{64,5... | collective-permute-start | bytes 688136 | tf_op jit(solution)/shard_map/ppermute | solution.py:67
  141.4 2.9 %collective-permute-done.7 = bf16[2,64,896]{2,1,0:T(8,128)(2,1)S(1)} collective-permute-done((bf16[2,64,896]{2,1,0:T(8,128)(2,1)S(1)}, bf16[2,64,896]{2,1,0:T(8,128)(2,1)S(1)}, u32[]{:S(2)}, u32[]{:S(2)}) %collective-permute-start.7) | collective-permute-done | bytes 229408 | tf_op jit(solution)/shard_map/ppermute | solution.py:66
  148.3 1.9 fusion.32
  150.1 1.9 fusion.31
  152.0 1.9 fusion.30
  153.9 1.9 fusion.29
  156.6 3.7 %fusion.4 = f32[320,896]{1,0:T(8,128)S(1)} fusion(bf16[2048,896]{1,0:T(8,128)(2,1)} %get-tuple-element.3, pred[2048]{0:T(1024)(128)(4,1)S(1)} %broadcast_bitcast_fusion, bf16[16,320,128]{2,1,0:T(8,128)(2,1)S(1)} %gather_fusion), kind=kOutput, calls=%fused_computation.21 | convolution fusion | flops 1175060480 | bytes 6129664 | tf_op jit(solution)/shard_map/dot_general | solution.py:80
  160.3 2.6 fusion.5
  162.9 3.9 %convolution_convert_fusion.1 = bf16[320,16,128]{2,0,1:T(8,128)(2,1)S(1)} fusion(bf16[16,896,128]{2,1,0:T(8,128)(2,1)} %bitcast.208, f32[320,896]{1,0:T(8,128)S(1)} %fusion.4, f32[320,896]{1,0:T(8,128)} %fusion.5), kind=kOutput, calls=%fused_computation.10 | convolution fusion | flops 1176780800 | bytes 7274496 | tf_op jit(solution)/shard_map/dot_general | solution.py:85
  168.3 4.1 %convolution_bitcast_fusion = f32[320,896]{1,0:T(8,128)S(1)} fusion(bf16[16,896,128]{2,1,0:T(8,128)(2,1)} %bitcast.209, bf16[320,16,128]{2,1,0:T(8,128)(2,1)} %bitcast.201), kind=kOutput, calls=%fused_computation.11 | convolution fusion | flops 1174405120 | bytes 6127616 | tf_op jit(solution)/shard_map/dot_general | solution.py:81
  172.5 1.6 fusion.10
  174.8 1.7 fusion.1
  176.9 1.8 gather_fusion.1
  178.7 3.2 %copy.90 = bf16[320,16,128]{2,1,0:T(8,128)(2,1)} copy(bf16[320,16,128]{2,0,1:T(8,128)(2,1)} %bitcast.199) | data formatting | bytes 2621440 | tf_op jit(solution)/shard_map/jit(_take)/gather | solution.py:94
  181.9 2.4 gather.15
  184.6 1.7 pad_maximum_fusion
  186.3 53.4 %reduce-scatter.2.cloned.1.call-done = bf16[320,2,256]{2,0,1:T(8,128)(2,1)} async-done(((bf16[320,2,2048]{2,0,1:T(8,128)(2,1)}), bf16[320,2,256]{2,0,1:T(8,128)(2,1)}) %reduce-scatter.2.cloned.1.call-update) | async-done | bytes 327696 | tf_op jit(solution)/shard_map/reduce_scatter | solution.py:97
  240.8 8.7 %all_to_all.15 = bf16[4,80,2,256]{3,1,2,0:T(8,128)(2,1)S(1)} all-to-all(bf16[4,80,2,256]{3,1,2,0:T(8,128)(2,1)S(1)} %copy.91), channel_id=1, replica_groups=mesh['ey'=4,'ez'=16,'tp'=8] {'ey'}, dimensions={0} | all-to-all | bytes 655360 | tf_op jit(solution)/shard_map/all_to_all | solution.py:99
  (85 shorter events, 23.9 us)
Async XLA Ops:
  7.2 19.6 %copy-start = (bf16[128,2048]{1,0:T(8,128)(2,1)S(1)}, bf16[128,2048]{1,0:T(8,128)(2,1)}, u32[]{:S(2)}) copy-start(bf16[128,2048]{1,0:T(8,128)(2,1)} %param.7) | copy-start | bytes 1572868
  7.2 32.0 %copy-start.8 = (f32[128,2]{0,1:T(2,128)S(1)}, f32[128,2]{0,1:T(2,128)}, u32[]{:S(2)}) copy-start(f32[128,2]{0,1:T(2,128)} %param.10) | copy-start | bytes 3076
  7.2 52.7 %copy-start.2 = (bf16[128,2048]{1,0:T(8,128)(2,1)S(1)}, bf16[128,2048]{1,0:T(8,128)(2,1)}, u32[]{:S(2)}) copy-start(bf16[128,2048]{1,0:T(8,128)(2,1)} %param.8) | copy-start | bytes 1572868
  7.2 155.7 %all-gather.3.cloned.1.call-start = ((), (), s32[]{:S(2)}) async-start(), calls=%async_computation.5 | async-start | bytes 3899392 | tf_op jit(solution)/shard_map/all_gather | solution.py:51
  9.2 23.5 %collective-permute-start = (bf16[2,128,896]{2,1,0:T(8,128)(2,1)}, bf16[2,128,896]{2,1,0:T(8,128)(2,1)}, u32[]{:S(2)}, u32[]{:S(2)}) collective-permute-start(bf16[2,128,896]{2,1,0:T(8,128)(2,1)} %pad_maximum_fusion.1), channel_id=1, source_target_pairs={{0,8},{8,16},{16,24},{24,32},{32,40},{40,48},{48,56},{56,64},{64,7... | collective-permute-start | bytes 1376264 | tf_op jit(solution)/shard_map/ppermute | solution.py:61
  13.6 21.0 %collective-permute-start.8 = (bf16[2,128,896]{2,1,0:T(8,128)(2,1)}, bf16[2,128,896]{2,1,0:T(8,128)(2,1)S(1)}, u32[]{:S(2)}, u32[]{:S(2)}) collective-permute-start(bf16[2,128,896]{2,1,0:T(8,128)(2,1)} %pad_maximum_fusion.1), channel_id=1, source_target_pairs={{0,120},{8,0},{16,8},{24,16},{32,24},{40,32},{48,40},{56,48},{64,5... | collective-permute-start | bytes 1376264 | tf_op jit(solution)/shard_map/ppermute | solution.py:62
  28.3 54.2 %copy-start.1 = (bf16[128,896]{1,0:T(8,128)(2,1)S(1)}, bf16[128,896]{1,0:T(8,128)(2,1)}, u32[]{:S(2)}) copy-start(bf16[128,896]{1,0:T(8,128)(2,1)} %param.11) | copy-start | bytes 688132
  28.3 33.2 %all-to-all-start = ((bf16[4,80,2048]{2,1,0:T(8,128)(2,1)}), bf16[4,80,2048]{2,1,0:T(8,128)(2,1)S(1)}, u32[]{:S(2)}, u32[]{:S(2)}) async-start(bf16[4,80,2048]{2,1,0:T(8,128)(2,1)} %bitcast.3), calls=%async_computation | async-start | bytes 2621440 | tf_op jit(solution)/shard_map/all_to_all | solution.py:72
  32.7 18.3 %collective-permute-start.1 = (bf16[2,128,896]{2,1,0:T(8,128)(2,1)}, bf16[2,128,896]{2,1,0:T(8,128)(2,1)}, u32[]{:S(2)}, u32[]{:S(2)}) collective-permute-start(bf16[2,128,896]{2,1,0:T(8,128)(2,1)} %collective-permute-done), channel_id=1, source_target_pairs={{0,8},{8,16},{16,24},{24,32},{32,40},{40,48},{48,56},{56,64},{64,7... | collective-permute-start | bytes 1376264 | tf_op jit(solution)/shard_map/ppermute | solution.py:61
  34.6 26.9 %copy-start.3 = (bf16[2,128,896]{2,1,0:T(8,128)(2,1)}, bf16[2,128,896]{2,1,0:T(8,128)(2,1)S(1)}, u32[]{:S(2)}) copy-start(bf16[2,128,896]{2,1,0:T(8,128)(2,1)S(1)} %collective-permute-done.8) | copy-start | bytes 1376260
  34.6 20.8 %collective-permute-start.9 = (bf16[2,128,896]{2,1,0:T(8,128)(2,1)S(1)}, bf16[2,128,896]{2,1,0:T(8,128)(2,1)}, u32[]{:S(2)}, u32[]{:S(2)}) collective-permute-start(bf16[2,128,896]{2,1,0:T(8,128)(2,1)S(1)} %collective-permute-done.8), channel_id=1, source_target_pairs={{0,120},{8,0},{16,8},{24,16},{32,24},{40,32},{48,40},{56,48},{64,5... | collective-permute-start | bytes 1376264 | tf_op jit(solution)/shard_map/ppermute | solution.py:62
  51.0 21.1 %collective-permute-start.2 = (bf16[2,128,896]{2,1,0:T(8,128)(2,1)}, bf16[2,128,896]{2,1,0:T(8,128)(2,1)}, u32[]{:S(2)}, u32[]{:S(2)}) collective-permute-start(bf16[2,128,896]{2,1,0:T(8,128)(2,1)} %collective-permute-done.1), channel_id=1, source_target_pairs={{0,8},{8,16},{16,24},{24,32},{32,40},{40,48},{48,56},{56,64},{64,7... | collective-permute-start | bytes 1376264 | tf_op jit(solution)/shard_map/ppermute | solution.py:61
  55.4 21.8 %collective-permute-start.10 = (bf16[2,128,896]{2,1,0:T(8,128)(2,1)}, bf16[2,128,896]{2,1,0:T(8,128)(2,1)}, u32[]{:S(2)}, u32[]{:S(2)}) collective-permute-start(bf16[2,128,896]{2,1,0:T(8,128)(2,1)} %collective-permute-done.9), channel_id=1, source_target_pairs={{0,120},{8,0},{16,8},{24,16},{32,24},{40,32},{48,40},{56,48},{64,5... | collective-permute-start | bytes 1376264 | tf_op jit(solution)/shard_map/ppermute | solution.py:62
  61.5 46.5 %all-to-all-start.1 = ((bf16[4,80,2048]{2,1,0:T(8,128)(2,1)}), bf16[4,80,2048]{2,1,0:T(8,128)(2,1)S(1)}, u32[]{:S(2)}, u32[]{:S(2)}) async-start(bf16[4,80,2048]{2,1,0:T(8,128)(2,1)} %bitcast.40), calls=%async_computation.1 | async-start | bytes 2621440 | tf_op jit(solution)/shard_map/all_to_all | solution.py:73
  65.1 174.7 %reduce-scatter.2.cloned.1.call-start = ((), (), s32[]{:S(2)}) async-start(), calls=%async_computation.4 | async-start | bytes 2949120 | tf_op jit(solution)/shard_map/reduce_scatter | solution.py:97
  72.1 21.6 %collective-permute-start.3 = (bf16[2,128,896]{2,1,0:T(8,128)(2,1)}, bf16[2,128,896]{2,1,0:T(8,128)(2,1)}, u32[]{:S(2)}, u32[]{:S(2)}) collective-permute-start(bf16[2,128,896]{2,1,0:T(8,128)(2,1)} %collective-permute-done.2), channel_id=1, source_target_pairs={{0,8},{8,16},{16,24},{24,32},{32,40},{40,48},{48,56},{56,64},{64,7... | collective-permute-start | bytes 1376264 | tf_op jit(solution)/shard_map/ppermute | solution.py:61
  77.2 21.1 %collective-permute-start.11 = (bf16[2,128,896]{2,1,0:T(8,128)(2,1)}, bf16[2,128,896]{2,1,0:T(8,128)(2,1)}, u32[]{:S(2)}, u32[]{:S(2)}) collective-permute-start(bf16[2,128,896]{2,1,0:T(8,128)(2,1)} %collective-permute-done.10), channel_id=1, source_target_pairs={{0,120},{8,0},{16,8},{24,16},{32,24},{40,32},{48,40},{56,48},{64,5... | collective-permute-start | bytes 1376264 | tf_op jit(solution)/shard_map/ppermute | solution.py:62
  93.7 16.5 %collective-permute-start.4 = (bf16[2,128,896]{2,1,0:T(8,128)(2,1)}, bf16[2,128,896]{2,1,0:T(8,128)(2,1)}, u32[]{:S(2)}, u32[]{:S(2)}) collective-permute-start(bf16[2,128,896]{2,1,0:T(8,128)(2,1)} %collective-permute-done.3), channel_id=1, source_target_pairs={{0,8},{8,16},{16,24},{24,32},{32,40},{40,48},{48,56},{56,64},{64,7... | collective-permute-start | bytes 1376264 | tf_op jit(solution)/shard_map/ppermute | solution.py:61
  98.3 14.9 %collective-permute-start.12 = (bf16[2,128,896]{2,1,0:T(8,128)(2,1)}, bf16[2,128,896]{2,1,0:T(8,128)(2,1)}, u32[]{:S(2)}, u32[]{:S(2)}) collective-permute-start(bf16[2,128,896]{2,1,0:T(8,128)(2,1)} %collective-permute-done.11), channel_id=1, source_target_pairs={{0,120},{8,0},{16,8},{24,16},{32,24},{40,32},{48,40},{56,48},{64,5... | collective-permute-start | bytes 1376264 | tf_op jit(solution)/shard_map/ppermute | solution.py:62
  110.2 10.6 %collective-permute-start.5 = (bf16[2,128,896]{2,1,0:T(8,128)(2,1)}, bf16[2,128,896]{2,1,0:T(8,128)(2,1)S(1)}, u32[]{:S(2)}, u32[]{:S(2)}) collective-permute-start(bf16[2,128,896]{2,1,0:T(8,128)(2,1)} %collective-permute-done.4), channel_id=1, source_target_pairs={{0,8},{8,16},{16,24},{24,32},{32,40},{40,48},{48,56},{56,64},{64,7... | collective-permute-start | bytes 1376264 | tf_op jit(solution)/shard_map/ppermute | solution.py:61
  113.2 9.6 %collective-permute-start.13 = (bf16[2,128,896]{2,1,0:T(8,128)(2,1)}, bf16[2,128,896]{2,1,0:T(8,128)(2,1)S(1)}, u32[]{:S(2)}, u32[]{:S(2)}) collective-permute-start(bf16[2,128,896]{2,1,0:T(8,128)(2,1)} %collective-permute-done.12), channel_id=1, source_target_pairs={{0,120},{8,0},{16,8},{24,16},{32,24},{40,32},{48,40},{56,48},{64,5... | collective-permute-start | bytes 1376264 | tf_op jit(solution)/shard_map/ppermute | solution.py:62
  120.9 12.7 %collective-permute-start.6 = (bf16[2,128,896]{2,1,0:T(8,128)(2,1)S(1)}, bf16[2,128,896]{2,1,0:T(8,128)(2,1)S(1)}, u32[]{:S(2)}, u32[]{:S(2)}) collective-permute-start(bf16[2,128,896]{2,1,0:T(8,128)(2,1)S(1)} %collective-permute-done.5), channel_id=1, source_target_pairs={{0,8},{8,16},{16,24},{24,32},{32,40},{40,48},{48,56},{56,64},{64,7... | collective-permute-start | bytes 1376264 | tf_op jit(solution)/shard_map/ppermute | solution.py:61
  122.8 12.7 %collective-permute-start.14 = (bf16[2,128,896]{2,1,0:T(8,128)(2,1)S(1)}, bf16[2,128,896]{2,1,0:T(8,128)(2,1)S(1)}, u32[]{:S(2)}, u32[]{:S(2)}) collective-permute-start(bf16[2,128,896]{2,1,0:T(8,128)(2,1)S(1)} %collective-permute-done.13), channel_id=1, source_target_pairs={{0,120},{8,0},{16,8},{24,16},{32,24},{40,32},{48,40},{56,48},{64,5... | collective-permute-start | bytes 1376264 | tf_op jit(solution)/shard_map/ppermute | solution.py:62
  133.6 10.7 %collective-permute-start.7 = (bf16[2,64,896]{2,1,0:T(8,128)(2,1)S(1)}, bf16[2,64,896]{2,1,0:T(8,128)(2,1)S(1)}, u32[]{:S(2)}, u32[]{:S(2)}) collective-permute-start(bf16[2,64,896]{2,1,0:T(8,128)(2,1)S(1)} %slice.156), channel_id=1, source_target_pairs={{0,8},{8,16},{16,24},{24,32},{32,40},{40,48},{48,56},{56,64},{64,7... | collective-permute-start | bytes 688136 | tf_op jit(solution)/shard_map/ppermute | solution.py:66
  135.5 10.2 %collective-permute-start.15 = (bf16[2,64,896]{2,1,0:T(8,128)(2,1)S(1)}, bf16[2,64,896]{2,1,0:T(8,128)(2,1)S(1)}, u32[]{:S(2)}, u32[]{:S(2)}) collective-permute-start(bf16[2,64,896]{2,1,0:T(8,128)(2,1)S(1)} %slice.157), channel_id=1, source_target_pairs={{0,120},{8,0},{16,8},{24,16},{32,24},{40,32},{48,40},{56,48},{64,5... | collective-permute-start | bytes 688136 | tf_op jit(solution)/shard_map/ppermute | solution.py:67
  141.4 14.4 %copy-start.4 = (bf16[2,128,896]{2,1,0:T(8,128)(2,1)S(1)}, bf16[2,128,896]{2,1,0:T(8,128)(2,1)}, u32[]{:S(2)}) copy-start(bf16[2,128,896]{2,1,0:T(8,128)(2,1)} %copy-done.3) | copy-start | bytes 1376260
  156.6 3.7 %copy-start.5 = (bf16[2048,896]{1,0:T(8,128)(2,1)S(1)}, bf16[2048,896]{1,0:T(8,128)(2,1)}, u32[]{:S(2)}) copy-start(bf16[2048,896]{1,0:T(8,128)(2,1)} %get-tuple-element.2) | copy-start | bytes 11010052
  160.3 2.6 copy-start.9
  168.3 4.2 %copy-start.7 = (bf16[2048,896]{1,0:T(8,128)(2,1)S(1)}, bf16[2048,896]{1,0:T(8,128)(2,1)}, u32[]{:S(2)}) copy-start(bf16[2048,896]{1,0:T(8,128)(2,1)} %get-tuple-element.3) | copy-start | bytes 11010052
  168.3 4.2 %copy-start.11 = (f32[320,896]{1,0:T(8,128)S(1)}, f32[320,896]{1,0:T(8,128)}, u32[]{:S(2)}) copy-start(f32[320,896]{1,0:T(8,128)} %fusion.5) | copy-start | bytes 3440644
  172.5 2.0 copy-start.6
  172.5 2.4 copy-start.10
Sparse Core Ops, SparseCore 0:
  23.2 83.2 all-gather.2
  186.5 53.2 reduce-scatter.1

commit v7 on v3

--- a/solution.py
+++ b/solution.py
@@ -49,22 +49,33 @@
     place = lax.axis_index("ez")
     block_width = w_gate.shape[0]
     stacked = jnp.stack([w_gate, w_up, w_down.T], axis=0)
-    forward = [(i, (i + 1) % member_count) for i in range(member_count)]
-    backward = [(i, (i - 1) % member_count) for i in range(member_count)]
-    half_steps = member_count // 2
-    cw = stacked
-    ccw = stacked
+    far = 4
+    group = member_count // far
+
+    def shifted(value, distance):
+        pairs = [(i, (i + distance) % member_count) for i in range(member_count)]
+        return lax.ppermute(value, "ez", pairs)
+
+    cut = block_width // 2
     by_distance = [None] * member_count
-    by_distance[0] = stacked
-    for step in range(1, half_steps):
-        cw = lax.ppermute(cw, "ez", forward)
-        ccw = lax.ppermute(ccw, "ez", backward)
-        by_distance[step] = cw
-        by_distance[member_count - step] = ccw
-    cut = block_width // 2
-    far_low = lax.ppermute(cw[:, :cut], "ez", forward)
-    far_high = lax.ppermute(ccw[:, cut:], "ez", backward)
-    by_distance[half_steps] = jnp.concatenate([far_low, far_high], axis=1)
+    long_cw = shifted(stacked, far)
+    long_ccw = shifted(stacked, -far)
+    long_low = shifted(long_cw[:, :cut], far)
+    long_high = shifted(long_ccw[:, cut:], -far)
+    long_block = [stacked, long_cw, jnp.concatenate([long_low, long_high], axis=1), long_ccw]
+    for m in range(group):
+        by_distance[far * m] = long_block[m]
+    long_block = jnp.stack(long_block, axis=0)
+    near_cw = shifted(long_block, 1)
+    near_ccw = shifted(long_block, -1)
+    near_low = shifted(near_cw[:, :, :cut], 1)
+    near_high = shifted(near_ccw[:, :, cut:], -1)
+    for m in range(group):
+        by_distance[1 + far * m] = near_cw[m]
+        by_distance[(far * m - 1) % member_count] = near_ccw[m]
+        by_distance[2 + far * m] = jnp.concatenate(
+            [near_low[m], near_high[(m + 1) % group]], axis=1
+        )
     origin = (place - jnp.arange(member_count, dtype=jnp.int32)) % member_count
     gate_full = jnp.concatenate([chunk[0] for chunk in by_distance], axis=0)
     up_full = jnp.concatenate([chunk[1] for chunk in by_distance], axis=0)

time: 254 us -> 323 us (1.27)
  waiting for transfers between devices: 91.1 us -> 133 us
  starting transfers between devices: 70.6 us -> 87.9 us
  local copies, waits for them, and re-layouts: 37 us -> 45.3 us
  other arithmetic: 9.77 us -> 13.9 us
    ppermute x16 -> x8, waiting for transfers between devices: 45.4 us -> 82.4 us  [shifted(): return lax.ppermute(value, 'ez', pairs)]
    ppermute x16 -> x8, starting transfers between devices: 62.6 us -> 79.3 us  [shifted(): return lax.ppermute(value, 'ez', pairs)]
    all_to_all x1, waiting for transfers between devices: 0.39 us -> 14.3 us  [per_device(): lax.all_to_all(sent_cot, 'ey', split_axis=0, concat_axis=0, tiled=True)]
    reduce_scatter x1, waiting for transfers between devices: 45.4 us -> 36.4 us  [per_device(): summed = lax.psum_scatter(results, 'tp', scatter_dimension=2, tiled=True)]
    unnamed x43 -> x49, local copies, waits for them, and re-layouts: 27.8 us -> 20.7 us
    slice x4 -> x6, local copies, waits for them, and re-layouts: 0.23 us -> 4.01 us  [the longest x1 2.56 us: per_device(): near_low = shifted(near_cw[:, :, :cut], 1)]
    unnamed x2 -> x6, other arithmetic: 1.69 us -> 5.26 us
  transfers between devices with their start and end apart: 19 -> 11, of which waited for: 13 -> 8; matrix products, arithmetic and copies ran while one was open for 11% -> 11% of each run, Pallas kernels for 0% -> 0%
where the time goes in v7:
time: 323 us; the launch traced here: 319 us
  waiting for transfers between devices  133 us (41%)
  starting transfers between devices  87.9 us (27%)
  local copies, waits for them, and re-layouts  45.3 us (14%)
  matrix products  15.6 us (5%)
  between operations  14.5 us (4%)
  other arithmetic  13.9 us (4%)
  blocking collectives  8.72 us (3%)
    ppermute x8, waiting for transfers between devices, shifted(): return lax.ppermute(value, 'ez', pairs)  82.4 us
    ppermute x8, starting transfers between devices, shifted(): return lax.ppermute(value, 'ez', pairs)  79.3 us
    reduce_scatter x1, waiting for transfers between devices, per_device(): summed = lax.psum_scatter(results, 'tp', scatter_dimension=2, tiled=True)  36.4 us
    unnamed x49, local copies, waits for them, and re-layouts  20.7 us
    all_to_all x1, waiting for transfers between devices, per_device(): lax.all_to_all(sent_cot, 'ey', split_axis=0, concat_axis=0, tiled=True)  14.3 us
    all_to_all x1, blocking collectives, per_device(): lax.all_to_all(rounded, 'ey', split_axis=0, concat_axis=0, tiled=True)  8.72 us
  transfers between devices with their start and end apart: 11, of which 8 were waited for; matrix products, arithmetic and copies ran while one was open for 11% of the time, Pallas kernels for 0%

profile of v7, /device:TPU:1, one launch (start us, length us, event | category | flops | bytes accessed | tf_op | source)
XLA Modules:
  0.0 319.0 jit_solution(704012893565422223)
XLA Ops:
  7.2 1.1 copy.89
  8.3 1.2 fusion.97
  9.5 9.6 %collective-permute-start = (bf16[3,128,896]{2,1,0:T(8,128)(2,1)S(1)}, bf16[3,128,896]{2,1,0:T(8,128)(2,1)S(1)}, u32[]{:S(2)}, u32[]{:S(2)}) collective-permute-start(bf16[3,128,896]{2,1,0:T(8,128)(2,1)S(1)} %get-tuple-element.57), channel_id=1, source_target_pairs={{0,32},{8,40},{16,48},{24,56},{32,64},{40,72},{48,80},{56,88},{64,... | collective-permute-start | bytes 2064392 | tf_op jit(solution)/shard_map/ppermute | solution.py:57
  19.1 5.6 %collective-permute-start.2 = (bf16[3,128,896]{2,1,0:T(8,128)(2,1)S(1)}, bf16[3,128,896]{2,1,0:T(8,128)(2,1)S(1)}, u32[]{:S(2)}, u32[]{:S(2)}) collective-permute-start(bf16[3,128,896]{2,1,0:T(8,128)(2,1)S(1)} %get-tuple-element.57), channel_id=1, source_target_pairs={{0,96},{8,104},{16,112},{24,120},{32,0},{40,8},{48,16},{56,24},{64... | collective-permute-start | bytes 2064392 | tf_op jit(solution)/shard_map/ppermute | solution.py:57
  24.7 21.9 %collective-permute-done = bf16[3,128,896]{2,1,0:T(8,128)(2,1)S(1)} collective-permute-done((bf16[3,128,896]{2,1,0:T(8,128)(2,1)S(1)}, bf16[3,128,896]{2,1,0:T(8,128)(2,1)S(1)}, u32[]{:S(2)}, u32[]{:S(2)}) %collective-permute-start) | collective-permute-done | bytes 688160 | tf_op jit(solution)/shard_map/ppermute | solution.py:57
  46.6 40.3 %collective-permute-start.1 = (bf16[3,64,896]{2,1,0:T(8,128)(2,1)S(1)}, bf16[3,64,896]{2,1,0:T(8,128)(2,1)S(1)}, u32[]{:S(2)}, u32[]{:S(2)}) collective-permute-start(bf16[3,64,896]{2,1,0:T(8,128)(2,1)S(1)} %slice.307), channel_id=1, source_target_pairs={{0,32},{8,40},{16,48},{24,56},{32,64},{40,72},{48,80},{56,88},{64,... | collective-permute-start | bytes 1032200 | tf_op jit(solution)/shard_map/ppermute | solution.py:57
  87.8 4.2 %collective-permute-start.3 = (bf16[3,64,896]{2,1,0:T(8,128)(2,1)S(1)}, bf16[3,64,896]{2,1,0:T(8,128)(2,1)S(1)}, u32[]{:S(2)}, u32[]{:S(2)}) collective-permute-start(bf16[3,64,896]{2,1,0:T(8,128)(2,1)S(1)} %slice.308), channel_id=1, source_target_pairs={{0,96},{8,104},{16,112},{24,120},{32,0},{40,8},{48,16},{56,24},{64... | collective-permute-start | bytes 1032200 | tf_op jit(solution)/shard_map/ppermute | solution.py:57
  92.0 24.5 %collective-permute-done.1 = bf16[3,64,896]{2,1,0:T(8,128)(2,1)S(1)} collective-permute-done((bf16[3,64,896]{2,1,0:T(8,128)(2,1)S(1)}, bf16[3,64,896]{2,1,0:T(8,128)(2,1)S(1)}, u32[]{:S(2)}, u32[]{:S(2)}) %collective-permute-start.1) | collective-permute-done | bytes 344096 | tf_op jit(solution)/shard_map/ppermute | solution.py:57
  116.5 1.8 pad_maximum_fusion
  118.4 10.4 %collective-permute-start.6 = (bf16[4,3,128,896]{3,2,1,0:T(8,128)(2,1)}, bf16[4,3,128,896]{3,2,1,0:T(8,128)(2,1)S(1)}, u32[]{:S(2)}, u32[]{:S(2)}) collective-permute-start(bf16[4,3,128,896]{3,2,1,0:T(8,128)(2,1)} %pad_maximum_fusion), channel_id=1, source_target_pairs={{0,120},{8,0},{16,8},{24,16},{32,24},{40,32},{48,40},{56,48},{64,5... | collective-permute-start | bytes 8257544 | tf_op jit(solution)/shard_map/ppermute | solution.py:57
  128.7 1.9 collective-permute-start.4
  133.4 1.2 reduce-window.6
  136.9 1.6 fusion.1
  138.5 4.3 %all-to-all-start.1 = ((bf16[4,80,2048]{2,1,0:T(8,128)(2,1)}), bf16[4,80,2048]{2,1,0:T(8,128)(2,1)}, u32[]{:S(2)}, u32[]{:S(2)}) async-start(bf16[4,80,2048]{2,1,0:T(8,128)(2,1)} %bitcast.288), calls=%async_computation.1 | async-start | bytes 2621440 | tf_op jit(solution)/shard_map/all_to_all | solution.py:84
  142.9 2.7 convolution_convert_fusion
  145.5 14.3 %all-to-all-done.1 = bf16[4,80,2048]{2,1,0:T(8,128)(2,1)} async-done(((bf16[4,80,2048]{2,1,0:T(8,128)(2,1)}), bf16[4,80,2048]{2,1,0:T(8,128)(2,1)}, u32[]{:S(2)}, u32[]{:S(2)}) %all-to-all-start.1) | async-done | bytes 1310752 | tf_op jit(solution)/shard_map/all_to_all | solution.py:84
  159.9 4.3 %all-to-all-start = ((bf16[4,80,2048]{2,1,0:T(8,128)(2,1)}), bf16[4,80,2048]{2,1,0:T(8,128)(2,1)}, u32[]{:S(2)}, u32[]{:S(2)}) async-start(bf16[4,80,2048]{2,1,0:T(8,128)(2,1)} %bitcast.287), calls=%async_computation | async-start | bytes 2621440 | tf_op jit(solution)/shard_map/all_to_all | solution.py:83
  164.2 23.3 %collective-permute-done.6 = bf16[4,3,128,896]{3,2,1,0:T(8,128)(2,1)S(1)} collective-permute-done((bf16[4,3,128,896]{3,2,1,0:T(8,128)(2,1)}, bf16[4,3,128,896]{3,2,1,0:T(8,128)(2,1)S(1)}, u32[]{:S(2)}, u32[]{:S(2)}) %collective-permute-start.6) | collective-permute-done | bytes 2752544 | tf_op jit(solution)/shard_map/ppermute | solution.py:57
  187.5 1.2 slice.312
  188.7 5.2 %collective-permute-start.7 = (bf16[4,3,64,896]{3,2,1,0:T(8,128)(2,1)}, bf16[4,3,64,896]{3,2,1,0:T(8,128)(2,1)}, u32[]{:S(2)}, u32[]{:S(2)}) collective-permute-start(bf16[4,3,64,896]{3,2,1,0:T(8,128)(2,1)} %slice.312), channel_id=1, source_target_pairs={{0,120},{8,0},{16,8},{24,16},{32,24},{40,32},{48,40},{56,48},{64,5... | collective-permute-start | bytes 4128776 | tf_op jit(solution)/shard_map/ppermute | solution.py:57
  194.8 2.6 slice.310
  197.3 2.1 collective-permute-start.5
  200.2 1.6 copy.103
  201.8 1.4 copy.90
  203.3 1.6 copy.101
  204.9 1.4 copy.87
  206.3 3.1 gather_fusion.2
  209.4 3.1 gather_fusion.1
  212.5 2.2 select_bitcast_fusion.1
  215.3 2.0 fusion.81
  217.4 5.0 %collective-permute-done.7 = bf16[4,3,64,896]{3,2,1,0:T(8,128)(2,1)} collective-permute-done((bf16[4,3,64,896]{3,2,1,0:T(8,128)(2,1)}, bf16[4,3,64,896]{3,2,1,0:T(8,128)(2,1)}, u32[]{:S(2)}, u32[]{:S(2)}) %collective-permute-start.7) | collective-permute-done | bytes 1376288 | tf_op jit(solution)/shard_map/ppermute | solution.py:57
  222.4 1.4 slice_bitcast_fusion
  223.8 7.0 %collective-permute-done.5 = bf16[4,3,64,896]{3,2,1,0:T(8,128)(2,1)} collective-permute-done((bf16[4,3,64,896]{3,2,1,0:T(8,128)(2,1)}, bf16[4,3,64,896]{3,2,1,0:T(8,128)(2,1)}, u32[]{:S(2)}, u32[]{:S(2)}) %collective-permute-start.5) | collective-permute-done | bytes 1376288 | tf_op jit(solution)/shard_map/ppermute | solution.py:57
  230.8 1.4 slice_bitcast_fusion.1
  234.5 1.9 fusion.78
  238.7 1.9 fusion.75
  242.9 1.9 fusion.72
  246.2 1.5 fusion.7
  247.8 1.5 fusion.9
  249.8 1.6 fusion.3
  252.0 1.5 fusion.4
  253.5 1.6 fusion.14
  255.1 1.7 fusion.2
  257.7 2.4 gather_fusion
  260.1 3.9 %bitcast_select_fusion = bf16[320,2,2048]{2,0,1:T(8,128)(2,1)} fusion(pred[2048]{0:T(1024)(128)(4,1)S(1)} %broadcast_bitcast_fusion, bf16[16,320,2,128]{3,1,2,0:T(8,128)(2,1)} %gather_fusion), kind=kLoop, calls=%fused_computation.10 | loop fusion | flops 1310720 | bytes 5244928 | tf_op jit(solution)/shard_map/jit(_take)/select_n | solution.py:106
  264.0 36.4 %reduce-scatter.2.cloned.1.call-done = bf16[320,2,256]{2,0,1:T(8,128)(2,1)} async-done(((bf16[320,2,2048]{2,0,1:T(8,128)(2,1)}), bf16[320,2,256]{2,0,1:T(8,128)(2,1)}) %reduce-scatter.2.cloned.1.call-update) | async-done | bytes 327696 | tf_op jit(solution)/shard_map/reduce_scatter | solution.py:109
  301.4 8.7 %all_to_all.15 = bf16[4,80,2,256]{3,1,2,0:T(8,128)(2,1)S(1)} all-to-all(bf16[4,80,2,256]{3,1,2,0:T(8,128)(2,1)S(1)} %copy.95), channel_id=1, replica_groups=mesh['ey'=4,'ez'=16,'tp'=8] {'ey'}, dimensions={0} | all-to-all | bytes 655360 | tf_op jit(solution)/shard_map/all_to_all | solution.py:111
  311.1 1.1 convolution_convert_fusion.3
  (82 shorter events, 20.5 us)
Async XLA Ops:
  7.2 129.8 %copy-start = (bf16[128,2048]{1,0:T(8,128)(2,1)S(1)}, bf16[128,2048]{1,0:T(8,128)(2,1)}, u32[]{:S(2)}) copy-start(bf16[128,2048]{1,0:T(8,128)(2,1)} %param.10) | copy-start | bytes 1572868
  9.5 37.1 %collective-permute-start = (bf16[3,128,896]{2,1,0:T(8,128)(2,1)S(1)}, bf16[3,128,896]{2,1,0:T(8,128)(2,1)S(1)}, u32[]{:S(2)}, u32[]{:S(2)}) collective-permute-start(bf16[3,128,896]{2,1,0:T(8,128)(2,1)S(1)} %get-tuple-element.57), channel_id=1, source_target_pairs={{0,32},{8,40},{16,48},{24,56},{32,64},{40,72},{48,80},{56,88},{64,... | collective-permute-start | bytes 2064392 | tf_op jit(solution)/shard_map/ppermute | solution.py:57
  19.1 68.6 %collective-permute-start.2 = (bf16[3,128,896]{2,1,0:T(8,128)(2,1)S(1)}, bf16[3,128,896]{2,1,0:T(8,128)(2,1)S(1)}, u32[]{:S(2)}, u32[]{:S(2)}) collective-permute-start(bf16[3,128,896]{2,1,0:T(8,128)(2,1)S(1)} %get-tuple-element.57), channel_id=1, source_target_pairs={{0,96},{8,104},{16,112},{24,120},{32,0},{40,8},{48,16},{56,24},{64... | collective-permute-start | bytes 2064392 | tf_op jit(solution)/shard_map/ppermute | solution.py:57
  46.6 71.8 %copy-start.4 = (bf16[3,128,896]{2,1,0:T(8,128)(2,1)}, bf16[3,128,896]{2,1,0:T(8,128)(2,1)S(1)}, u32[]{:S(2)}) copy-start(bf16[3,128,896]{2,1,0:T(8,128)(2,1)S(1)} %collective-permute-done) | copy-start | bytes 2064388
  46.6 84.1 %copy-start.13 = (s32[128,2]{0,1:T(2,128)S(1)}, s32[128,2]{0,1:T(2,128)}, u32[]{:S(2)}) copy-start(s32[128,2]{0,1:T(2,128)} %param.11) | copy-start | bytes 3076
  46.6 69.8 %collective-permute-start.1 = (bf16[3,64,896]{2,1,0:T(8,128)(2,1)S(1)}, bf16[3,64,896]{2,1,0:T(8,128)(2,1)S(1)}, u32[]{:S(2)}, u32[]{:S(2)}) collective-permute-start(bf16[3,64,896]{2,1,0:T(8,128)(2,1)S(1)} %slice.307), channel_id=1, source_target_pairs={{0,32},{8,40},{16,48},{24,56},{32,64},{40,72},{48,80},{56,88},{64,... | collective-permute-start | bytes 1032200 | tf_op jit(solution)/shard_map/ppermute | solution.py:57
  87.7 30.6 %copy-start.2 = (bf16[3,128,896]{2,1,0:T(8,128)(2,1)}, bf16[3,128,896]{2,1,0:T(8,128)(2,1)S(1)}, u32[]{:S(2)}) copy-start(bf16[3,128,896]{2,1,0:T(8,128)(2,1)S(1)} %collective-permute-done.2) | copy-start | bytes 2064388
  87.8 49.0 %copy-start.14 = (f32[128,2]{0,1:T(2,128)S(1)}, f32[128,2]{0,1:T(2,128)}, u32[]{:S(2)}) copy-start(f32[128,2]{0,1:T(2,128)} %param.12) | copy-start | bytes 3076
  87.8 28.7 %collective-permute-start.3 = (bf16[3,64,896]{2,1,0:T(8,128)(2,1)S(1)}, bf16[3,64,896]{2,1,0:T(8,128)(2,1)S(1)}, u32[]{:S(2)}, u32[]{:S(2)}) collective-permute-start(bf16[3,64,896]{2,1,0:T(8,128)(2,1)S(1)} %slice.308), channel_id=1, source_target_pairs={{0,96},{8,104},{16,112},{24,120},{32,0},{40,8},{48,16},{56,24},{64... | collective-permute-start | bytes 1032200 | tf_op jit(solution)/shard_map/ppermute | solution.py:57
  116.5 12.2 %copy-start.6 = (bf16[3,128,896]{2,1,0:T(8,128)(2,1)}, bf16[3,128,896]{2,1,0:T(8,128)(2,1)S(1)}, u32[]{:S(2)}) copy-start(bf16[3,128,896]{2,1,0:T(8,128)(2,1)S(1)} %constant_dynamic-update-slice_fusion) | copy-start | bytes 2064388
  118.4 69.1 %collective-permute-start.6 = (bf16[4,3,128,896]{3,2,1,0:T(8,128)(2,1)}, bf16[4,3,128,896]{3,2,1,0:T(8,128)(2,1)S(1)}, u32[]{:S(2)}, u32[]{:S(2)}) collective-permute-start(bf16[4,3,128,896]{3,2,1,0:T(8,128)(2,1)} %pad_maximum_fusion), channel_id=1, source_target_pairs={{0,120},{8,0},{16,8},{24,16},{32,24},{40,32},{48,40},{56,48},{64,5... | collective-permute-start | bytes 8257544 | tf_op jit(solution)/shard_map/ppermute | solution.py:57
  128.7 66.0 %collective-permute-start.4 = (bf16[4,3,128,896]{3,2,1,0:T(8,128)(2,1)}, bf16[4,3,128,896]{3,2,1,0:T(8,128)(2,1)}, u32[]{:S(2)}, u32[]{:S(2)}) collective-permute-start(bf16[4,3,128,896]{3,2,1,0:T(8,128)(2,1)} %pad_maximum_fusion), channel_id=1, source_target_pairs={{0,8},{8,16},{16,24},{24,32},{32,40},{40,48},{48,56},{56,64},{64,7... | collective-permute-start | bytes 8257544 | tf_op jit(solution)/shard_map/ppermute | solution.py:57
  138.5 21.4 %all-to-all-start.1 = ((bf16[4,80,2048]{2,1,0:T(8,128)(2,1)}), bf16[4,80,2048]{2,1,0:T(8,128)(2,1)}, u32[]{:S(2)}, u32[]{:S(2)}) async-start(bf16[4,80,2048]{2,1,0:T(8,128)(2,1)} %bitcast.288), calls=%async_computation.1 | async-start | bytes 2621440 | tf_op jit(solution)/shard_map/all_to_all | solution.py:84
  142.8 51.1 %copy-start.8 = (bf16[128,896]{1,0:T(8,128)(2,1)S(1)}, bf16[128,896]{1,0:T(8,128)(2,1)}, u32[]{:S(2)}) copy-start(bf16[128,896]{1,0:T(8,128)(2,1)} %param.13) | copy-start | bytes 688132
  142.8 51.1 %copy-start.9 = (bf16[128,896]{1,0:T(8,128)(2,1)S(1)}, bf16[128,896]{1,0:T(8,128)(2,1)}, u32[]{:S(2)}) copy-start(bf16[128,896]{1,0:T(8,128)(2,1)} %param.14) | copy-start | bytes 688132
  159.9 43.4 %all-to-all-start = ((bf16[4,80,2048]{2,1,0:T(8,128)(2,1)}), bf16[4,80,2048]{2,1,0:T(8,128)(2,1)}, u32[]{:S(2)}, u32[]{:S(2)}) async-start(bf16[4,80,2048]{2,1,0:T(8,128)(2,1)} %bitcast.287), calls=%async_computation | async-start | bytes 2621440 | tf_op jit(solution)/shard_map/all_to_all | solution.py:83
  164.2 136.3 %reduce-scatter.2.cloned.1.call-start = ((), (), s32[]{:S(2)}) async-start(), calls=%async_computation.4 | async-start | bytes 2949120 | tf_op jit(solution)/shard_map/reduce_scatter | solution.py:109
  188.7 33.6 %collective-permute-start.7 = (bf16[4,3,64,896]{3,2,1,0:T(8,128)(2,1)}, bf16[4,3,64,896]{3,2,1,0:T(8,128)(2,1)}, u32[]{:S(2)}, u32[]{:S(2)}) collective-permute-start(bf16[4,3,64,896]{3,2,1,0:T(8,128)(2,1)} %slice.312), channel_id=1, source_target_pairs={{0,120},{8,0},{16,8},{24,16},{32,24},{40,32},{48,40},{56,48},{64,5... | collective-permute-start | bytes 4128776 | tf_op jit(solution)/shard_map/ppermute | solution.py:57
  197.3 33.5 %collective-permute-start.5 = (bf16[4,3,64,896]{3,2,1,0:T(8,128)(2,1)}, bf16[4,3,64,896]{3,2,1,0:T(8,128)(2,1)}, u32[]{:S(2)}, u32[]{:S(2)}) collective-permute-start(bf16[4,3,64,896]{3,2,1,0:T(8,128)(2,1)} %slice.310), channel_id=1, source_target_pairs={{0,8},{8,16},{16,24},{24,32},{32,40},{40,48},{48,56},{56,64},{64,7... | collective-permute-start | bytes 4128776 | tf_op jit(solution)/shard_map/ppermute | solution.py:57
  212.5 2.8 copy-start.10
  217.4 14.9 %copy-start.11 = (bf16[2048,896]{1,0:T(8,128)(2,1)S(1)}, bf16[2048,896]{1,0:T(8,128)(2,1)}, u32[]{:S(2)}) copy-start(bf16[2048,896]{1,0:T(8,128)(2,1)} %get-tuple-element.26) | copy-start | bytes 11010052
  217.4 16.4 %copy-start.5 = (bf16[3,128,896]{2,1,0:T(8,128)(2,1)S(1)}, bf16[3,128,896]{2,1,0:T(8,128)(2,1)}, u32[]{:S(2)}) copy-start(bf16[3,128,896]{2,1,0:T(8,128)(2,1)} %copy-done.4) | copy-start | bytes 2064388
  233.0 4.9 %copy-start.7 = (bf16[3,128,896]{2,1,0:T(8,128)(2,1)S(1)}, bf16[3,128,896]{2,1,0:T(8,128)(2,1)}, u32[]{:S(2)}) copy-start(bf16[3,128,896]{2,1,0:T(8,128)(2,1)} %copy-done.6) | copy-start | bytes 2064388
  237.2 4.9 %copy-start.3 = (bf16[3,128,896]{2,1,0:T(8,128)(2,1)S(1)}, bf16[3,128,896]{2,1,0:T(8,128)(2,1)}, u32[]{:S(2)}) copy-start(bf16[3,128,896]{2,1,0:T(8,128)(2,1)} %copy-done.2) | copy-start | bytes 2064388
  247.8 2.0 copy-start.12
  260.1 52.0 %copy-start.1 = (bf16[128,2048]{1,0:T(8,128)(2,1)S(1)}, bf16[128,2048]{1,0:T(8,128)(2,1)}, u32[]{:S(2)}) copy-start(bf16[128,2048]{1,0:T(8,128)(2,1)} %param.10) | copy-start | bytes 1572868
Sparse Core Ops, SparseCore 0:
  264.1 36.2 reduce-scatter.1

commit v8 on v3

--- a/solution.py
+++ b/solution.py
@@ -82,22 +82,38 @@
     up_pre = jnp.dot(member_tokens, up_full, preferred_element_type=jnp.float32)
     hidden_grad = jnp.dot(member_cot, down_full, preferred_element_type=jnp.float32)
     hidden, gate_grad, up_grad = activate(gate_pre, up_pre, hidden_grad)
-    out_part = lax.dot_general(
-        hidden, down_full, (((1,), (1,)), ((), ())), preferred_element_type=jnp.float32
-    )
-    in_part = lax.dot_general(
-        gate_grad, gate_full, (((1,), (1,)), ((), ())), preferred_element_type=jnp.float32
-    )
-    in_part = in_part + lax.dot_general(
-        up_grad, up_full, (((1,), (1,)), ((), ())), preferred_element_type=jnp.float32
-    )
-    results = jnp.stack([out_part, in_part], axis=1).astype(jnp.bfloat16)
-    results = jnp.take(
-        results.reshape(row_total, 2, member_count, block_width), origin, axis=2
-    ).reshape(row_total, 2, model_width)
-    summed = lax.psum_scatter(results, "tp", scatter_dimension=2, tiled=True)
-    rounded = summed.reshape(plane_count, CAP, 2, -1)
-    returned = lax.all_to_all(rounded, "ey", split_axis=0, concat_axis=0, tiled=True)
+    halves = 2
+    part_slots = CAP // halves
+
+    def slot_half(value, half):
+        value = value.reshape(plane_count, CAP, -1)[:, half * part_slots : (half + 1) * part_slots]
+        return value.reshape(plane_count * part_slots, -1)
+
+    returned_parts = []
+    for half in range(halves):
+        hidden_h = slot_half(hidden, half)
+        gate_grad_h = slot_half(gate_grad, half)
+        up_grad_h = slot_half(up_grad, half)
+        out_part = lax.dot_general(
+            hidden_h, down_full, (((1,), (1,)), ((), ())), preferred_element_type=jnp.float32
+        )
+        in_part = lax.dot_general(
+            gate_grad_h, gate_full, (((1,), (1,)), ((), ())), preferred_element_type=jnp.float32
+        )
+        in_part = in_part + lax.dot_general(
+            up_grad_h, up_full, (((1,), (1,)), ((), ())), preferred_element_type=jnp.float32
+        )
+        part_rows = plane_count * part_slots
+        results = jnp.stack([out_part, in_part], axis=1).astype(jnp.bfloat16)
+        results = jnp.take(
+            results.reshape(part_rows, 2, member_count, block_width), origin, axis=2
+        ).reshape(part_rows, 2, model_width)
+        summed = lax.psum_scatter(results, "tp", scatter_dimension=2, tiled=True)
+        rounded = summed.reshape(plane_count, part_slots, 2, -1)
+        returned_parts.append(
+            lax.all_to_all(rounded, "ey", split_axis=0, concat_axis=0, tiled=True)
+        )
+    returned = jnp.concatenate(returned_parts, axis=1)
     returned = returned.reshape(slot_count, 2, -1).astype(jnp.float32)
     picker_full = picker.astype(jnp.float32)
     weighted = picker_full * slot_weight[:, None]

time: 254 us -> 312 us (1.23)
  waiting for transfers between devices: 91.1 us -> 126 us
  matrix products: 17.6 us -> 36.5 us
  local copies, waits for them, and re-layouts: 37 us -> 41.5 us
    reduce_scatter x1 -> x2, waiting for transfers between devices: 45.4 us -> 78.7 us  [per_device(): summed = lax.psum_scatter(results, 'tp', scatter_dimension=2, tiled=True)]
    dot_general x3 -> x6, matrix products: 4.81 us -> 20.4 us  [the longest x2 6.81 us: per_device(): lax.dot_general(up_grad_h, up_full, (((1,), (1,)), ((), ())), preferred_e...]
    reshape x1 -> x4, local copies, waits for them, and re-layouts: 0.99 us -> 5.4 us  [the longest x2 2.9 us: per_device(): results = jnp.take(results.reshape(part_rows, 2, member_count, block_widt...]
    select_n x3 -> x1, other arithmetic: 3.82 us -> 0.02 us  [per_device(): jnp.take(results.reshape(part_rows, 2, member_count, block_width), origin...]
    all_to_all x0 -> x1, starting transfers between devices: none -> 3.34 us  [per_device(): lax.all_to_all(rounded, 'ey', split_axis=0, concat_axis=0, tiled=True)]
  transfers between devices with their start and end apart: 19 -> 21, of which waited for: 13 -> 12; matrix products, arithmetic and copies ran while one was open for 11% -> 10% of each run, Pallas kernels for 0% -> 0%
where the time goes in v8:
time: 312 us; the launch traced here: 307 us
  waiting for transfers between devices  126 us (40%)
  starting transfers between devices  73.7 us (24%)
  local copies, waits for them, and re-layouts  41.5 us (13%)
  matrix products  36.5 us (12%)
  between operations  14.6 us (5%)
  blocking collectives  7.81 us (3%)
  other arithmetic  7.6 us (2%)
    reduce_scatter x2, waiting for transfers between devices, per_device(): summed = lax.psum_scatter(results, 'tp', scatter_dimension=2, tiled=True)  78.7 us
    ppermute x7, starting transfers between devices, per_device(): ccw = lax.ppermute(ccw, 'ez', backward)  39.2 us
    ppermute x7, waiting for transfers between devices, per_device(): cw = lax.ppermute(cw, 'ez', forward)  38.1 us
    unnamed x43, local copies, waits for them, and re-layouts  27.3 us
    ppermute x7, starting transfers between devices, per_device(): cw = lax.ppermute(cw, 'ez', forward)  15.8 us
    all_to_all x1, blocking collectives, per_device(): lax.all_to_all(rounded, 'ey', split_axis=0, concat_axis=0, tiled=True)  7.81 us
    dot_general x2, matrix products, per_device(): lax.dot_general(up_grad_h, up_full, (((1,), (1,)), ((), ())), preferred_e...  6.81 us
    dot_general x2, matrix products, per_device(): lax.dot_general(hidden_h, down_full, (((1,), (1,)), ((), ())), preferred_...  6.79 us
  transfers between devices with their start and end apart: 21, of which 12 were waited for; matrix products, arithmetic and copies ran while one was open for 10% of the time, Pallas kernels for 0%

profile of v8, /device:TPU:1, one launch (start us, length us, event | category | flops | bytes accessed | tf_op | source)
XLA Modules:
  0.0 307.2 jit_solution(5086956648806574496)
XLA Ops:
  9.5 4.4 %collective-permute-start = (bf16[3,128,896]{2,1,0:T(8,128)(2,1)S(1)}, bf16[3,128,896]{2,1,0:T(8,128)(2,1)}, u32[]{:S(2)}, u32[]{:S(2)}) collective-permute-start(bf16[3,128,896]{2,1,0:T(8,128)(2,1)S(1)} %pad_maximum_fusion.2), channel_id=1, source_target_pairs={{0,8},{8,16},{16,24},{24,32},{32,40},{40,48},{48,56},{56,64},{64,7... | collective-permute-start | bytes 2064392 | tf_op jit(solution)/shard_map/ppermute | solution.py:60
  13.9 9.5 %collective-permute-start.8 = (bf16[3,128,896]{2,1,0:T(8,128)(2,1)S(1)}, bf16[3,128,896]{2,1,0:T(8,128)(2,1)S(1)}, u32[]{:S(2)}, u32[]{:S(2)}) collective-permute-start(bf16[3,128,896]{2,1,0:T(8,128)(2,1)S(1)} %pad_maximum_fusion.2), channel_id=1, source_target_pairs={{0,120},{8,0},{16,8},{24,16},{32,24},{40,32},{48,40},{56,48},{64,5... | collective-permute-start | bytes 2064392 | tf_op jit(solution)/shard_map/ppermute | solution.py:61
  24.3 12.4 %collective-permute-done = bf16[3,128,896]{2,1,0:T(8,128)(2,1)} collective-permute-done((bf16[3,128,896]{2,1,0:T(8,128)(2,1)S(1)}, bf16[3,128,896]{2,1,0:T(8,128)(2,1)}, u32[]{:S(2)}, u32[]{:S(2)}) %collective-permute-start) | collective-permute-done | bytes 688160 | tf_op jit(solution)/shard_map/ppermute | solution.py:60
  36.7 1.9 collective-permute-start.1
  40.3 4.6 %collective-permute-start.9 = (bf16[3,128,896]{2,1,0:T(8,128)(2,1)S(1)}, bf16[3,128,896]{2,1,0:T(8,128)(2,1)S(1)}, u32[]{:S(2)}, u32[]{:S(2)}) collective-permute-start(bf16[3,128,896]{2,1,0:T(8,128)(2,1)S(1)} %collective-permute-done.8), channel_id=1, source_target_pairs={{0,120},{8,0},{16,8},{24,16},{32,24},{40,32},{48,40},{56,48},{64,5... | collective-permute-start | bytes 2064392 | tf_op jit(solution)/shard_map/ppermute | solution.py:61
  46.7 9.1 %collective-permute-done.1 = bf16[3,128,896]{2,1,0:T(8,128)(2,1)} collective-permute-done((bf16[3,128,896]{2,1,0:T(8,128)(2,1)}, bf16[3,128,896]{2,1,0:T(8,128)(2,1)}, u32[]{:S(2)}, u32[]{:S(2)}) %collective-permute-start.1) | collective-permute-done | bytes 688160 | tf_op jit(solution)/shard_map/ppermute | solution.py:60
  55.8 1.9 collective-permute-start.2
  58.1 5.3 %collective-permute-start.10 = (bf16[3,128,896]{2,1,0:T(8,128)(2,1)S(1)}, bf16[3,128,896]{2,1,0:T(8,128)(2,1)}, u32[]{:S(2)}, u32[]{:S(2)}) collective-permute-start(bf16[3,128,896]{2,1,0:T(8,128)(2,1)S(1)} %collective-permute-done.9), channel_id=1, source_target_pairs={{0,120},{8,0},{16,8},{24,16},{32,24},{40,32},{48,40},{56,48},{64,5... | collective-permute-start | bytes 2064392 | tf_op jit(solution)/shard_map/ppermute | solution.py:61
  65.0 4.3 %all-to-all-start.1 = ((bf16[4,80,2048]{2,1,0:T(8,128)(2,1)}), bf16[4,80,2048]{2,1,0:T(8,128)(2,1)S(1)}, u32[]{:S(2)}, u32[]{:S(2)}) async-start(bf16[4,80,2048]{2,1,0:T(8,128)(2,1)} %bitcast.58), calls=%async_computation.1 | async-start | bytes 2621440 | tf_op jit(solution)/shard_map/all_to_all | solution.py:73
  69.4 4.8 %collective-permute-done.2 = bf16[3,128,896]{2,1,0:T(8,128)(2,1)} collective-permute-done((bf16[3,128,896]{2,1,0:T(8,128)(2,1)}, bf16[3,128,896]{2,1,0:T(8,128)(2,1)}, u32[]{:S(2)}, u32[]{:S(2)}) %collective-permute-start.2) | collective-permute-done | bytes 688160 | tf_op jit(solution)/shard_map/ppermute | solution.py:60
  74.1 1.9 collective-permute-start.3
  76.1 5.2 %collective-permute-start.11 = (bf16[3,128,896]{2,1,0:T(8,128)(2,1)}, bf16[3,128,896]{2,1,0:T(8,128)(2,1)}, u32[]{:S(2)}, u32[]{:S(2)}) collective-permute-start(bf16[3,128,896]{2,1,0:T(8,128)(2,1)} %collective-permute-done.10), channel_id=1, source_target_pairs={{0,120},{8,0},{16,8},{24,16},{32,24},{40,32},{48,40},{56,48},{64,5... | collective-permute-start | bytes 2064392 | tf_op jit(solution)/shard_map/ppermute | solution.py:61
  84.4 3.5 %all-to-all-start = ((bf16[4,80,2048]{2,1,0:T(8,128)(2,1)}), bf16[4,80,2048]{2,1,0:T(8,128)(2,1)S(1)}, u32[]{:S(2)}, u32[]{:S(2)}) async-start(bf16[4,80,2048]{2,1,0:T(8,128)(2,1)} %bitcast.2), calls=%async_computation | async-start | bytes 2621440 | tf_op jit(solution)/shard_map/all_to_all | solution.py:72
  88.0 3.6 %collective-permute-done.3 = bf16[3,128,896]{2,1,0:T(8,128)(2,1)} collective-permute-done((bf16[3,128,896]{2,1,0:T(8,128)(2,1)}, bf16[3,128,896]{2,1,0:T(8,128)(2,1)}, u32[]{:S(2)}, u32[]{:S(2)}) %collective-permute-start.3) | collective-permute-done | bytes 688160 | tf_op jit(solution)/shard_map/ppermute | solution.py:60
  91.6 1.9 collective-permute-start.4
  93.5 4.9 %collective-permute-start.12 = (bf16[3,128,896]{2,1,0:T(8,128)(2,1)}, bf16[3,128,896]{2,1,0:T(8,128)(2,1)}, u32[]{:S(2)}, u32[]{:S(2)}) collective-permute-start(bf16[3,128,896]{2,1,0:T(8,128)(2,1)} %collective-permute-done.11), channel_id=1, source_target_pairs={{0,120},{8,0},{16,8},{24,16},{32,24},{40,32},{48,40},{56,48},{64,5... | collective-permute-start | bytes 2064392 | tf_op jit(solution)/shard_map/ppermute | solution.py:61
  100.0 8.2 %collective-permute-done.4 = bf16[3,128,896]{2,1,0:T(8,128)(2,1)} collective-permute-done((bf16[3,128,896]{2,1,0:T(8,128)(2,1)}, bf16[3,128,896]{2,1,0:T(8,128)(2,1)}, u32[]{:S(2)}, u32[]{:S(2)}) %collective-permute-start.4) | collective-permute-done | bytes 688160 | tf_op jit(solution)/shard_map/ppermute | solution.py:60
  108.2 1.9 collective-permute-start.5
  110.1 2.0 fusion.47
  113.4 1.8 gather_fusion.1
  116.1 4.6 %collective-permute-start.13 = (bf16[3,128,896]{2,1,0:T(8,128)(2,1)}, bf16[3,128,896]{2,1,0:T(8,128)(2,1)S(1)}, u32[]{:S(2)}, u32[]{:S(2)}) collective-permute-start(bf16[3,128,896]{2,1,0:T(8,128)(2,1)} %collective-permute-done.12), channel_id=1, source_target_pairs={{0,120},{8,0},{16,8},{24,16},{32,24},{40,32},{48,40},{56,48},{64,5... | collective-permute-start | bytes 2064392 | tf_op jit(solution)/shard_map/ppermute | solution.py:61
  122.3 2.1 fusion.46
  124.3 1.9 collective-permute-start.6
  126.3 2.1 fusion.45
  128.3 2.4 collective-permute-done.13
  130.8 5.2 %collective-permute-start.14 = (bf16[3,128,896]{2,1,0:T(8,128)(2,1)S(1)}, bf16[3,128,896]{2,1,0:T(8,128)(2,1)S(1)}, u32[]{:S(2)}, u32[]{:S(2)}) collective-permute-start(bf16[3,128,896]{2,1,0:T(8,128)(2,1)S(1)} %collective-permute-done.13), channel_id=1, source_target_pairs={{0,120},{8,0},{16,8},{24,16},{32,24},{40,32},{48,40},{56,48},{64,5... | collective-permute-start | bytes 2064392 | tf_op jit(solution)/shard_map/ppermute | solution.py:61
  136.0 2.1 fusion.44
  138.0 2.1 fusion.43
  140.1 1.9 collective-permute-start.7
  142.1 2.1 fusion.42
  145.0 5.5 %collective-permute-start.15 = (bf16[3,64,896]{2,1,0:T(8,128)(2,1)S(1)}, bf16[3,64,896]{2,1,0:T(8,128)(2,1)S(1)}, u32[]{:S(2)}, u32[]{:S(2)}) collective-permute-start(bf16[3,64,896]{2,1,0:T(8,128)(2,1)S(1)} %slice.245), channel_id=1, source_target_pairs={{0,120},{8,0},{16,8},{24,16},{32,24},{40,32},{48,40},{56,48},{64,5... | collective-permute-start | bytes 1032200 | tf_op jit(solution)/shard_map/ppermute | solution.py:66
  151.4 3.5 %collective-permute-done.15 = bf16[3,64,896]{2,1,0:T(8,128)(2,1)S(1)} collective-permute-done((bf16[3,64,896]{2,1,0:T(8,128)(2,1)S(1)}, bf16[3,64,896]{2,1,0:T(8,128)(2,1)S(1)}, u32[]{:S(2)}, u32[]{:S(2)}) %collective-permute-start.15) | collective-permute-done | bytes 344096 | tf_op jit(solution)/shard_map/ppermute | solution.py:66
  157.6 2.1 fusion.37
  159.6 2.0 fusion.36
  161.7 2.1 fusion.35
  165.5 3.6 %fusion.3 = f32[320,896]{1,0:T(8,128)S(1)} fusion(bf16[2048,896]{1,0:T(8,128)(2,1)} %get-tuple-element.8, bf16[16,40,8,128]{3,2,1,0:T(8,128)(2,1)S(1)} %get-tuple-element.61), kind=kOutput, calls=%fused_computation.15 | convolution fusion | flops 1174405120 | bytes 6127616 | tf_op jit(solution)/shard_map/dot_general | solution.py:83
  169.0 3.6 %fusion.8 = f32[320,896]{1,0:T(8,128)S(1)} fusion(bf16[2048,896]{1,0:T(8,128)(2,1)} %get-tuple-element.9, bf16[16,40,8,128]{3,2,1,0:T(8,128)(2,1)S(1)} %get-tuple-element.60), kind=kOutput, calls=%fused_computation.20 | convolution fusion | flops 1174405120 | bytes 6127616 | tf_op jit(solution)/shard_map/dot_general | solution.py:81
  172.6 3.9 %multiply_convert_fusion.2 = (bf16[320,896]{1,0:T(8,128)(2,1)S(1)}, bf16[320,896]{1,0:T(8,128)(2,1)S(1)}, bf16[320,896]{1,0:T(8,128)(2,1)S(1)}) fusion(f32[320,896]{1,0:T(8,128)S(1)} %fusion.8, f32[320,896]{1,0:T(8,128)S(1)} %fusion.3, bf16[2048,896]{1,0:T(8,128)(2,1)} %get-tuple-element.7, bf16[16,40,8,128]{3,2,1,0:T(8,128)(2,1)S(1)} %get-tuple-element.60), kind=kOutput, calls=%fused_computation.36 | convolution fusion | flops 1178705920 | bytes 8994816 | tf_op jit(solution)/shard_map/dot_general | solution.py:82
  176.6 3.4 %fusion.75 = f32[160,2048]{1,0:T(8,128)S(1)} fusion(bf16[160,896]{1,0:T(8,128)(2,1)S(1)} %bitcast.312, bf16[2048,896]{1,0:T(8,128)(2,1)} %get-tuple-element.7), kind=kOutput, calls=%fused_computation.166 | convolution fusion | flops 587202560 | bytes 5267456 | tf_op jit(solution)/shard_map/dot_general | solution.py:103
  180.8 3.4 %fusion.10 = bf16[20,8,16,128]{3,1,2,0:T(8,128)(2,1)S(1)} fusion(f32[160,2048]{1,0:T(8,128)S(1)} %fusion.75, bf16[160,896]{1,0:T(8,128)(2,1)S(1)} %bitcast.311, bf16[2048,896]{1,0:T(8,128)(2,1)} %get-tuple-element.9), kind=kOutput, calls=%fused_computation.28 | convolution fusion | flops 587857920 | bytes 5922816 | tf_op jit(solution)/shard_map/dot_general | solution.py:100
  184.5 3.4 %fusion.13 = bf16[160,1,16,128]{3,0,2,1:T(8,128)(2,1)S(1)} fusion(bf16[160,896,1]{1,0,2:T(8,128)(2,1)S(1)} %bitcast.310, bf16[16,128,896]{2,1,0:T(8,128)(2,1)} %bitcast.56), kind=kOutput, calls=%fused_computation.31 | convolution fusion | flops 587530240 | bytes 4612096 | tf_op jit(solution)/shard_map/dot_general | solution.py:97
  188.9 3.4 %fusion.12 = bf16[160,1,16,128]{3,0,2,1:T(8,128)(2,1)S(1)} fusion(bf16[160,896,1]{1,0,2:T(8,128)(2,1)S(1)} %bitcast.307, bf16[16,128,896]{2,1,0:T(8,128)(2,1)} %bitcast.56), kind=kOutput, calls=%fused_computation.30 | convolution fusion | flops 587530240 | bytes 4612096 | tf_op jit(solution)/shard_map/dot_general | solution.py:97
  192.2 3.4 %fusion.74 = f32[160,2048]{1,0:T(8,128)S(1)} fusion(bf16[160,896]{1,0:T(8,128)(2,1)S(1)} %bitcast.308, bf16[2048,896]{1,0:T(8,128)(2,1)} %get-tuple-element.7), kind=kOutput, calls=%fused_computation.165 | convolution fusion | flops 587202560 | bytes 5267456 | tf_op jit(solution)/shard_map/dot_general | solution.py:103
  195.7 3.4 %fusion.11 = bf16[20,8,16,128]{3,1,2,0:T(8,128)(2,1)S(1)} fusion(f32[160,2048]{1,0:T(8,128)S(1)} %fusion.74, bf16[160,896]{1,0:T(8,128)(2,1)S(1)} %bitcast.309, bf16[2048,896]{1,0:T(8,128)(2,1)} %get-tuple-element.9), kind=kOutput, calls=%fused_computation.29 | convolution fusion | flops 587857920 | bytes 5922816 | tf_op jit(solution)/shard_map/dot_general | solution.py:100
  205.9 41.6 %reduce-scatter.3.cloned.1.call-done = bf16[160,2,256]{2,0,1:T(8,128)(2,1)} async-done(((bf16[160,2,2048]{2,0,1:T(8,128)(2,1)}), bf16[160,2,256]{2,0,1:T(8,128)(2,1)}) %reduce-scatter.3.cloned.1.call-update) | async-done | bytes 163856 | tf_op jit(solution)/shard_map/reduce_scatter | solution.py:111
  249.2 3.3 %all-to-all-start.2 = ((bf16[4,40,2,256]{3,1,2,0:T(8,128)(2,1)}), bf16[4,40,2,256]{3,1,2,0:T(8,128)(2,1)S(1)}, u32[]{:S(2)}, u32[]{:S(2)}) async-start(bf16[4,40,2,256]{3,1,2,0:T(8,128)(2,1)} %copy.104), calls=%async_computation.3 | async-start | bytes 327680 | tf_op jit(solution)/shard_map/all_to_all | solution.py:114
  252.5 37.1 %reduce-scatter.5.cloned.1.call-done = bf16[160,2,256]{2,0,1:T(8,128)(2,1)} async-done(((bf16[160,2,2048]{2,0,1:T(8,128)(2,1)}), bf16[160,2,256]{2,0,1:T(8,128)(2,1)}) %reduce-scatter.5.cloned.1.call-update) | async-done | bytes 163856 | tf_op jit(solution)/shard_map/reduce_scatter | solution.py:111
  290.6 7.8 %all_to_all.20 = bf16[4,40,2,256]{3,1,2,0:T(8,128)(2,1)S(1)} all-to-all(bf16[4,40,2,256]{3,1,2,0:T(8,128)(2,1)S(1)} %copy.107), channel_id=1, replica_groups=mesh['ey'=4,'ez'=16,'tp'=8] {'ey'}, dimensions={0} | all-to-all | bytes 327680 | tf_op jit(solution)/shard_map/all_to_all | solution.py:114
  (98 shorter events, 36.8 us)
Async XLA Ops:
  7.2 56.3 %copy-start = (bf16[128,2048]{1,0:T(8,128)(2,1)S(1)}, bf16[128,2048]{1,0:T(8,128)(2,1)}, u32[]{:S(2)}) copy-start(bf16[128,2048]{1,0:T(8,128)(2,1)} %param.12) | copy-start | bytes 1572868
  7.2 74.1 %copy-start.9 = (bf16[128,2048]{1,0:T(8,128)(2,1)S(1)}, bf16[128,2048]{1,0:T(8,128)(2,1)}, u32[]{:S(2)}) copy-start(bf16[128,2048]{1,0:T(8,128)(2,1)} %param.11) | copy-start | bytes 1572868
  9.5 27.2 %collective-permute-start = (bf16[3,128,896]{2,1,0:T(8,128)(2,1)S(1)}, bf16[3,128,896]{2,1,0:T(8,128)(2,1)}, u32[]{:S(2)}, u32[]{:S(2)}) collective-permute-start(bf16[3,128,896]{2,1,0:T(8,128)(2,1)S(1)} %pad_maximum_fusion.2), channel_id=1, source_target_pairs={{0,8},{8,16},{16,24},{24,32},{32,40},{40,48},{48,56},{56,64},{64,7... | collective-permute-start | bytes 2064392 | tf_op jit(solution)/shard_map/ppermute | solution.py:60
  13.9 26.4 %collective-permute-start.8 = (bf16[3,128,896]{2,1,0:T(8,128)(2,1)S(1)}, bf16[3,128,896]{2,1,0:T(8,128)(2,1)S(1)}, u32[]{:S(2)}, u32[]{:S(2)}) collective-permute-start(bf16[3,128,896]{2,1,0:T(8,128)(2,1)S(1)} %pad_maximum_fusion.2), channel_id=1, source_target_pairs={{0,120},{8,0},{16,8},{24,16},{32,24},{40,32},{48,40},{56,48},{64,5... | collective-permute-start | bytes 2064392 | tf_op jit(solution)/shard_map/ppermute | solution.py:61
  36.7 19.2 %collective-permute-start.1 = (bf16[3,128,896]{2,1,0:T(8,128)(2,1)}, bf16[3,128,896]{2,1,0:T(8,128)(2,1)}, u32[]{:S(2)}, u32[]{:S(2)}) collective-permute-start(bf16[3,128,896]{2,1,0:T(8,128)(2,1)} %collective-permute-done), channel_id=1, source_target_pairs={{0,8},{8,16},{16,24},{24,32},{32,40},{40,48},{48,56},{56,64},{64,7... | collective-permute-start | bytes 2064392 | tf_op jit(solution)/shard_map/ppermute | solution.py:60
  40.3 24.7 %copy-start.5 = (bf16[3,128,896]{2,1,0:T(8,128)(2,1)}, bf16[3,128,896]{2,1,0:T(8,128)(2,1)S(1)}, u32[]{:S(2)}) copy-start(bf16[3,128,896]{2,1,0:T(8,128)(2,1)S(1)} %collective-permute-done.8) | copy-start | bytes 2064388
  40.3 17.8 %collective-permute-start.9 = (bf16[3,128,896]{2,1,0:T(8,128)(2,1)S(1)}, bf16[3,128,896]{2,1,0:T(8,128)(2,1)S(1)}, u32[]{:S(2)}, u32[]{:S(2)}) collective-permute-start(bf16[3,128,896]{2,1,0:T(8,128)(2,1)S(1)} %collective-permute-done.8), channel_id=1, source_target_pairs={{0,120},{8,0},{16,8},{24,16},{32,24},{40,32},{48,40},{56,48},{64,5... | collective-permute-start | bytes 2064392 | tf_op jit(solution)/shard_map/ppermute | solution.py:61
  55.8 18.3 %collective-permute-start.2 = (bf16[3,128,896]{2,1,0:T(8,128)(2,1)}, bf16[3,128,896]{2,1,0:T(8,128)(2,1)}, u32[]{:S(2)}, u32[]{:S(2)}) collective-permute-start(bf16[3,128,896]{2,1,0:T(8,128)(2,1)} %collective-permute-done.1), channel_id=1, source_target_pairs={{0,8},{8,16},{16,24},{24,32},{32,40},{40,48},{48,56},{56,64},{64,7... | collective-permute-start | bytes 2064392 | tf_op jit(solution)/shard_map/ppermute | solution.py:60
  58.1 26.3 %copy-start.7 = (bf16[3,128,896]{2,1,0:T(8,128)(2,1)}, bf16[3,128,896]{2,1,0:T(8,128)(2,1)S(1)}, u32[]{:S(2)}) copy-start(bf16[3,128,896]{2,1,0:T(8,128)(2,1)S(1)} %collective-permute-done.9) | copy-start | bytes 2064388
  58.1 17.9 %collective-permute-start.10 = (bf16[3,128,896]{2,1,0:T(8,128)(2,1)S(1)}, bf16[3,128,896]{2,1,0:T(8,128)(2,1)}, u32[]{:S(2)}, u32[]{:S(2)}) collective-permute-start(bf16[3,128,896]{2,1,0:T(8,128)(2,1)S(1)} %collective-permute-done.9), channel_id=1, source_target_pairs={{0,120},{8,0},{16,8},{24,16},{32,24},{40,32},{48,40},{56,48},{64,5... | collective-permute-start | bytes 2064392 | tf_op jit(solution)/shard_map/ppermute | solution.py:61
  65.0 33.4 %copy-start.3 = (bf16[128,896]{1,0:T(8,128)(2,1)S(1)}, bf16[128,896]{1,0:T(8,128)(2,1)}, u32[]{:S(2)}) copy-start(bf16[128,896]{1,0:T(8,128)(2,1)} %param.15) | copy-start | bytes 688132
  65.0 33.4 %copy-start.4 = (bf16[128,896]{1,0:T(8,128)(2,1)S(1)}, bf16[128,896]{1,0:T(8,128)(2,1)}, u32[]{:S(2)}) copy-start(bf16[128,896]{1,0:T(8,128)(2,1)} %param.16) | copy-start | bytes 688132
  65.0 19.4 %all-to-all-start.1 = ((bf16[4,80,2048]{2,1,0:T(8,128)(2,1)}), bf16[4,80,2048]{2,1,0:T(8,128)(2,1)S(1)}, u32[]{:S(2)}, u32[]{:S(2)}) async-start(bf16[4,80,2048]{2,1,0:T(8,128)(2,1)} %bitcast.58), calls=%async_computation.1 | async-start | bytes 2621440 | tf_op jit(solution)/shard_map/all_to_all | solution.py:73
  74.1 17.4 %collective-permute-start.3 = (bf16[3,128,896]{2,1,0:T(8,128)(2,1)}, bf16[3,128,896]{2,1,0:T(8,128)(2,1)}, u32[]{:S(2)}, u32[]{:S(2)}) collective-permute-start(bf16[3,128,896]{2,1,0:T(8,128)(2,1)} %collective-permute-done.2), channel_id=1, source_target_pairs={{0,8},{8,16},{16,24},{24,32},{32,40},{40,48},{48,56},{56,64},{64,7... | collective-permute-start | bytes 2064392 | tf_op jit(solution)/shard_map/ppermute | solution.py:60
  76.1 17.5 %collective-permute-start.11 = (bf16[3,128,896]{2,1,0:T(8,128)(2,1)}, bf16[3,128,896]{2,1,0:T(8,128)(2,1)}, u32[]{:S(2)}, u32[]{:S(2)}) collective-permute-start(bf16[3,128,896]{2,1,0:T(8,128)(2,1)} %collective-permute-done.10), channel_id=1, source_target_pairs={{0,120},{8,0},{16,8},{24,16},{32,24},{40,32},{48,40},{56,48},{64,5... | collective-permute-start | bytes 2064392 | tf_op jit(solution)/shard_map/ppermute | solution.py:61
  84.4 28.4 %all-to-all-start = ((bf16[4,80,2048]{2,1,0:T(8,128)(2,1)}), bf16[4,80,2048]{2,1,0:T(8,128)(2,1)S(1)}, u32[]{:S(2)}, u32[]{:S(2)}) async-start(bf16[4,80,2048]{2,1,0:T(8,128)(2,1)} %bitcast.2), calls=%async_computation | async-start | bytes 2621440 | tf_op jit(solution)/shard_map/all_to_all | solution.py:72
  88.0 159.6 %reduce-scatter.3.cloned.1.call-start = ((), (), s32[]{:S(2)}) async-start(), calls=%async_computation.6 | async-start | bytes 1474560 | tf_op jit(solution)/shard_map/reduce_scatter | solution.py:111
  91.6 16.6 %collective-permute-start.4 = (bf16[3,128,896]{2,1,0:T(8,128)(2,1)}, bf16[3,128,896]{2,1,0:T(8,128)(2,1)}, u32[]{:S(2)}, u32[]{:S(2)}) collective-permute-start(bf16[3,128,896]{2,1,0:T(8,128)(2,1)} %collective-permute-done.3), channel_id=1, source_target_pairs={{0,8},{8,16},{16,24},{24,32},{32,40},{40,48},{48,56},{56,64},{64,7... | collective-permute-start | bytes 2064392 | tf_op jit(solution)/shard_map/ppermute | solution.py:60
  93.5 22.5 %collective-permute-start.12 = (bf16[3,128,896]{2,1,0:T(8,128)(2,1)}, bf16[3,128,896]{2,1,0:T(8,128)(2,1)}, u32[]{:S(2)}, u32[]{:S(2)}) collective-permute-start(bf16[3,128,896]{2,1,0:T(8,128)(2,1)} %collective-permute-done.11), channel_id=1, source_target_pairs={{0,120},{8,0},{16,8},{24,16},{32,24},{40,32},{48,40},{56,48},{64,5... | collective-permute-start | bytes 2064392 | tf_op jit(solution)/shard_map/ppermute | solution.py:61
  108.2 16.2 %collective-permute-start.5 = (bf16[3,128,896]{2,1,0:T(8,128)(2,1)}, bf16[3,128,896]{2,1,0:T(8,128)(2,1)}, u32[]{:S(2)}, u32[]{:S(2)}) collective-permute-start(bf16[3,128,896]{2,1,0:T(8,128)(2,1)} %collective-permute-done.4), channel_id=1, source_target_pairs={{0,8},{8,16},{16,24},{24,32},{32,40},{40,48},{48,56},{56,64},{64,7... | collective-permute-start | bytes 2064392 | tf_op jit(solution)/shard_map/ppermute | solution.py:60
  116.1 14.7 %collective-permute-start.13 = (bf16[3,128,896]{2,1,0:T(8,128)(2,1)}, bf16[3,128,896]{2,1,0:T(8,128)(2,1)S(1)}, u32[]{:S(2)}, u32[]{:S(2)}) collective-permute-start(bf16[3,128,896]{2,1,0:T(8,128)(2,1)} %collective-permute-done.12), channel_id=1, source_target_pairs={{0,120},{8,0},{16,8},{24,16},{32,24},{40,32},{48,40},{56,48},{64,5... | collective-permute-start | bytes 2064392 | tf_op jit(solution)/shard_map/ppermute | solution.py:61
  124.3 15.8 %collective-permute-start.6 = (bf16[3,128,896]{2,1,0:T(8,128)(2,1)}, bf16[3,128,896]{2,1,0:T(8,128)(2,1)S(1)}, u32[]{:S(2)}, u32[]{:S(2)}) collective-permute-start(bf16[3,128,896]{2,1,0:T(8,128)(2,1)} %collective-permute-done.5), channel_id=1, source_target_pairs={{0,8},{8,16},{16,24},{24,32},{32,40},{40,48},{48,56},{56,64},{64,7... | collective-permute-start | bytes 2064392 | tf_op jit(solution)/shard_map/ppermute | solution.py:60
  130.8 14.2 %collective-permute-start.14 = (bf16[3,128,896]{2,1,0:T(8,128)(2,1)S(1)}, bf16[3,128,896]{2,1,0:T(8,128)(2,1)S(1)}, u32[]{:S(2)}, u32[]{:S(2)}) collective-permute-start(bf16[3,128,896]{2,1,0:T(8,128)(2,1)S(1)} %collective-permute-done.13), channel_id=1, source_target_pairs={{0,120},{8,0},{16,8},{24,16},{32,24},{40,32},{48,40},{56,48},{64,5... | collective-permute-start | bytes 2064392 | tf_op jit(solution)/shard_map/ppermute | solution.py:61
  140.1 11.2 %collective-permute-start.7 = (bf16[3,64,896]{2,1,0:T(8,128)(2,1)S(1)}, bf16[3,64,896]{2,1,0:T(8,128)(2,1)S(1)}, u32[]{:S(2)}, u32[]{:S(2)}) collective-permute-start(bf16[3,64,896]{2,1,0:T(8,128)(2,1)S(1)} %slice.244), channel_id=1, source_target_pairs={{0,8},{8,16},{16,24},{24,32},{32,40},{40,48},{48,56},{56,64},{64,7... | collective-permute-start | bytes 1032200 | tf_op jit(solution)/shard_map/ppermute | solution.py:65
  145.0 9.9 %collective-permute-start.15 = (bf16[3,64,896]{2,1,0:T(8,128)(2,1)S(1)}, bf16[3,64,896]{2,1,0:T(8,128)(2,1)S(1)}, u32[]{:S(2)}, u32[]{:S(2)}) collective-permute-start(bf16[3,64,896]{2,1,0:T(8,128)(2,1)S(1)} %slice.245), channel_id=1, source_target_pairs={{0,120},{8,0},{16,8},{24,16},{32,24},{40,32},{48,40},{56,48},{64,5... | collective-permute-start | bytes 1032200 | tf_op jit(solution)/shard_map/ppermute | solution.py:66
  155.8 7.9 %copy-start.8 = (bf16[3,128,896]{2,1,0:T(8,128)(2,1)S(1)}, bf16[3,128,896]{2,1,0:T(8,128)(2,1)}, u32[]{:S(2)}) copy-start(bf16[3,128,896]{2,1,0:T(8,128)(2,1)} %copy-done.7) | copy-start | bytes 2064388
  156.7 7.9 %copy-start.6 = (bf16[3,128,896]{2,1,0:T(8,128)(2,1)S(1)}, bf16[3,128,896]{2,1,0:T(8,128)(2,1)}, u32[]{:S(2)}) copy-start(bf16[3,128,896]{2,1,0:T(8,128)(2,1)} %copy-done.5) | copy-start | bytes 2064388
  192.2 3.4 %copy-start.2 = (bf16[4,40,896]{2,1,0:T(8,128)(2,1)S(1)}, bf16[4,40,896]{2,1,0:T(8,128)(2,1)}, u32[]{:S(2)}) copy-start(bf16[4,40,896]{2,1,0:T(8,128)(2,1)} %get-tuple-element.54) | copy-start | bytes 860164
  204.4 96.0 %copy-start.1 = (bf16[128,2048]{1,0:T(8,128)(2,1)S(1)}, bf16[128,2048]{1,0:T(8,128)(2,1)}, u32[]{:S(2)}) copy-start(bf16[128,2048]{1,0:T(8,128)(2,1)} %param.12) | copy-start | bytes 1572868
  204.4 85.2 %reduce-scatter.5.cloned.1.call-start = ((), (), s32[]{:S(2)}) async-start(), calls=%async_computation.7 | async-start | bytes 1474560 | tf_op jit(solution)/shard_map/reduce_scatter | solution.py:111
  249.2 41.4 %all-to-all-start.2 = ((bf16[4,40,2,256]{3,1,2,0:T(8,128)(2,1)}), bf16[4,40,2,256]{3,1,2,0:T(8,128)(2,1)S(1)}, u32[]{:S(2)}, u32[]{:S(2)}) async-start(bf16[4,40,2,256]{3,1,2,0:T(8,128)(2,1)} %copy.104), calls=%async_computation.3 | async-start | bytes 327680 | tf_op jit(solution)/shard_map/all_to_all | solution.py:114
Sparse Core Ops, SparseCore 0:
  204.5 43.0 reduce-scatter.2
  250.4 39.1 reduce-scatter.4

commit v9 on v3

--- a/solution.py
+++ b/solution.py
@@ -95,7 +95,10 @@
     results = jnp.take(
         results.reshape(row_total, 2, member_count, block_width), origin, axis=2
     ).reshape(row_total, 2, model_width)
-    summed = lax.psum_scatter(results, "tp", scatter_dimension=2, tiled=True)
+    tp_count = lax.axis_size("tp")
+    pieces = results.reshape(row_total, 2, tp_count, model_width // tp_count)
+    pieces = lax.all_to_all(pieces, "tp", split_axis=2, concat_axis=2, tiled=True)
+    summed = jnp.sum(pieces.astype(jnp.float32), axis=2).astype(jnp.bfloat16)
     rounded = summed.reshape(plane_count, CAP, 2, -1)
     returned = lax.all_to_all(rounded, "ey", split_axis=0, concat_axis=0, tiled=True)
     returned = returned.reshape(slot_count, 2, -1).astype(jnp.float32)

time: 254 us -> 248 us (0.976); the launches traced: 249 us -> 246 us
  blocking collectives: 8.69 us -> 53.4 us
  waiting for transfers between devices: 91.1 us -> 47.3 us
  between operations: 14.5 us -> 1.14 us
  local copies, waits for them, and re-layouts: 37 us -> 46.3 us
    reduce_scatter x1 -> x0, waiting for transfers between devices: 45.4 us -> none  [per_device(): summed = lax.psum_scatter(results, 'tp', scatter_dimension=2, tiled=True)]
    all_to_all x0 -> x1, blocking collectives: none -> 43.5 us  [per_device(): lax.all_to_all(pieces, 'tp', split_axis=2, concat_axis=2, tiled=True)]
    gather x1 -> x3, local copies, waits for them, and re-layouts: 2.43 us -> 11 us  [per_device(): jnp.take(results.reshape(row_total, 2, member_count, block_width), origin...]
    select_n x3 -> x2, other arithmetic: 3.82 us -> 0.27 us  [per_device(): jnp.take(results.reshape(row_total, 2, member_count, block_width), origin...]
    reduce_sum x0 -> x1, other arithmetic: none -> 3.05 us  [per_device(): summed = jnp.sum(pieces.astype(jnp.float32), axis=2).astype(jnp.bfloat16)]
    unnamed x43 -> x45, local copies, waits for them, and re-layouts: 27.8 us -> 27.5 us
  transfers between devices with their start and end apart: 19 -> 18, of which waited for: 13 -> 10; matrix products, arithmetic and copies ran while one was open for 11% -> 11% of each run, Pallas kernels for 0% -> 0%
where the time goes in v9:
time: 248 us; the launch traced here: 246 us
  starting transfers between devices  70.2 us (28%)
  blocking collectives  53.4 us (22%)
  waiting for transfers between devices  47.3 us (19%)
  local copies, waits for them, and re-layouts  46.3 us (19%)
  matrix products  18.6 us (8%)
  other arithmetic  9.3 us (4%)
    all_to_all x1, blocking collectives, per_device(): lax.all_to_all(pieces, 'tp', split_axis=2, concat_axis=2, tiled=True)  43.5 us
    ppermute x7, starting transfers between devices, per_device(): ccw = lax.ppermute(ccw, 'ez', backward)  39.1 us
    ppermute x7, waiting for transfers between devices, per_device(): cw = lax.ppermute(cw, 'ez', forward)  38.3 us
    unnamed x45, local copies, waits for them, and re-layouts  27.5 us
    ppermute x7, starting transfers between devices, per_device(): cw = lax.ppermute(cw, 'ez', forward)  15.8 us
    gather x3, local copies, waits for them, and re-layouts, per_device(): jnp.take(results.reshape(row_total, 2, member_count, block_width), origin...  11 us
    all_to_all x1, blocking collectives, per_device(): lax.all_to_all(rounded, 'ey', split_axis=0, concat_axis=0, tiled=True)  9.86 us
    ppermute x1, starting transfers between devices, per_device(): far_high = lax.ppermute(ccw[:, cut:], 'ez', backward)  5.5 us
  transfers between devices with their start and end apart: 18, of which 10 were waited for; matrix products, arithmetic and copies ran while one was open for 11% of the time, Pallas kernels for 0%

profile of v9, /device:TPU:1, one launch (start us, length us, event | category | flops | bytes accessed | tf_op | source)
XLA Modules:
  0.0 246.3 jit_solution(3155774404797784052)
XLA Ops:
  3.0 4.4 %collective-permute-start = (bf16[3,128,896]{2,1,0:T(8,128)(2,1)S(1)}, bf16[3,128,896]{2,1,0:T(8,128)(2,1)}, u32[]{:S(2)}, u32[]{:S(2)}) collective-permute-start(bf16[3,128,896]{2,1,0:T(8,128)(2,1)S(1)} %pad_maximum_fusion.1), channel_id=1, source_target_pairs={{0,8},{8,16},{16,24},{24,32},{32,40},{40,48},{48,56},{56,64},{64,7... | collective-permute-start | bytes 2064392 | tf_op jit(solution)/shard_map/ppermute | solution.py:60
  7.4 9.5 %collective-permute-start.8 = (bf16[3,128,896]{2,1,0:T(8,128)(2,1)S(1)}, bf16[3,128,896]{2,1,0:T(8,128)(2,1)S(1)}, u32[]{:S(2)}, u32[]{:S(2)}) collective-permute-start(bf16[3,128,896]{2,1,0:T(8,128)(2,1)S(1)} %pad_maximum_fusion.1), channel_id=1, source_target_pairs={{0,120},{8,0},{16,8},{24,16},{32,24},{40,32},{48,40},{56,48},{64,5... | collective-permute-start | bytes 2064392 | tf_op jit(solution)/shard_map/ppermute | solution.py:61
  17.8 12.4 %collective-permute-done = bf16[3,128,896]{2,1,0:T(8,128)(2,1)} collective-permute-done((bf16[3,128,896]{2,1,0:T(8,128)(2,1)S(1)}, bf16[3,128,896]{2,1,0:T(8,128)(2,1)}, u32[]{:S(2)}, u32[]{:S(2)}) %collective-permute-start) | collective-permute-done | bytes 688160 | tf_op jit(solution)/shard_map/ppermute | solution.py:60
  30.2 1.9 collective-permute-start.1
  33.8 4.6 %collective-permute-start.9 = (bf16[3,128,896]{2,1,0:T(8,128)(2,1)S(1)}, bf16[3,128,896]{2,1,0:T(8,128)(2,1)S(1)}, u32[]{:S(2)}, u32[]{:S(2)}) collective-permute-start(bf16[3,128,896]{2,1,0:T(8,128)(2,1)S(1)} %collective-permute-done.8), channel_id=1, source_target_pairs={{0,120},{8,0},{16,8},{24,16},{32,24},{40,32},{48,40},{56,48},{64,5... | collective-permute-start | bytes 2064392 | tf_op jit(solution)/shard_map/ppermute | solution.py:61
  40.2 9.1 %collective-permute-done.1 = bf16[3,128,896]{2,1,0:T(8,128)(2,1)} collective-permute-done((bf16[3,128,896]{2,1,0:T(8,128)(2,1)}, bf16[3,128,896]{2,1,0:T(8,128)(2,1)}, u32[]{:S(2)}, u32[]{:S(2)}) %collective-permute-start.1) | collective-permute-done | bytes 688160 | tf_op jit(solution)/shard_map/ppermute | solution.py:60
  49.3 1.9 collective-permute-start.2
  51.6 5.3 %collective-permute-start.10 = (bf16[3,128,896]{2,1,0:T(8,128)(2,1)S(1)}, bf16[3,128,896]{2,1,0:T(8,128)(2,1)}, u32[]{:S(2)}, u32[]{:S(2)}) collective-permute-start(bf16[3,128,896]{2,1,0:T(8,128)(2,1)S(1)} %collective-permute-done.9), channel_id=1, source_target_pairs={{0,120},{8,0},{16,8},{24,16},{32,24},{40,32},{48,40},{56,48},{64,5... | collective-permute-start | bytes 2064392 | tf_op jit(solution)/shard_map/ppermute | solution.py:61
  56.9 1.6 fusion.1
  58.5 4.3 %all-to-all-start.1 = ((bf16[4,80,2048]{2,1,0:T(8,128)(2,1)}), bf16[4,80,2048]{2,1,0:T(8,128)(2,1)S(1)}, u32[]{:S(2)}, u32[]{:S(2)}) async-start(bf16[4,80,2048]{2,1,0:T(8,128)(2,1)} %bitcast.54), calls=%async_computation.1 | async-start | bytes 2621440 | tf_op jit(solution)/shard_map/all_to_all | solution.py:73
  62.8 4.8 %collective-permute-done.2 = bf16[3,128,896]{2,1,0:T(8,128)(2,1)} collective-permute-done((bf16[3,128,896]{2,1,0:T(8,128)(2,1)}, bf16[3,128,896]{2,1,0:T(8,128)(2,1)}, u32[]{:S(2)}, u32[]{:S(2)}) %collective-permute-start.2) | collective-permute-done | bytes 688160 | tf_op jit(solution)/shard_map/ppermute | solution.py:60
  67.6 1.9 collective-permute-start.3
  69.6 5.1 %collective-permute-start.11 = (bf16[3,128,896]{2,1,0:T(8,128)(2,1)}, bf16[3,128,896]{2,1,0:T(8,128)(2,1)}, u32[]{:S(2)}, u32[]{:S(2)}) collective-permute-start(bf16[3,128,896]{2,1,0:T(8,128)(2,1)} %collective-permute-done.10), channel_id=1, source_target_pairs={{0,120},{8,0},{16,8},{24,16},{32,24},{40,32},{48,40},{56,48},{64,5... | collective-permute-start | bytes 2064392 | tf_op jit(solution)/shard_map/ppermute | solution.py:61
  76.3 1.6 all-to-all-done.1
  77.9 3.5 %all-to-all-start = ((bf16[4,80,2048]{2,1,0:T(8,128)(2,1)}), bf16[4,80,2048]{2,1,0:T(8,128)(2,1)S(1)}, u32[]{:S(2)}, u32[]{:S(2)}) async-start(bf16[4,80,2048]{2,1,0:T(8,128)(2,1)} %bitcast.3), calls=%async_computation | async-start | bytes 2621440 | tf_op jit(solution)/shard_map/all_to_all | solution.py:72
  81.5 3.6 %collective-permute-done.3 = bf16[3,128,896]{2,1,0:T(8,128)(2,1)} collective-permute-done((bf16[3,128,896]{2,1,0:T(8,128)(2,1)}, bf16[3,128,896]{2,1,0:T(8,128)(2,1)}, u32[]{:S(2)}, u32[]{:S(2)}) %collective-permute-start.3) | collective-permute-done | bytes 688160 | tf_op jit(solution)/shard_map/ppermute | solution.py:60
  85.1 1.9 collective-permute-start.4
  87.8 4.6 %collective-permute-start.12 = (bf16[3,128,896]{2,1,0:T(8,128)(2,1)}, bf16[3,128,896]{2,1,0:T(8,128)(2,1)}, u32[]{:S(2)}, u32[]{:S(2)}) collective-permute-start(bf16[3,128,896]{2,1,0:T(8,128)(2,1)} %collective-permute-done.11), channel_id=1, source_target_pairs={{0,120},{8,0},{16,8},{24,16},{32,24},{40,32},{48,40},{56,48},{64,5... | collective-permute-start | bytes 2064392 | tf_op jit(solution)/shard_map/ppermute | solution.py:61
  93.2 8.5 %collective-permute-done.4 = bf16[3,128,896]{2,1,0:T(8,128)(2,1)} collective-permute-done((bf16[3,128,896]{2,1,0:T(8,128)(2,1)}, bf16[3,128,896]{2,1,0:T(8,128)(2,1)}, u32[]{:S(2)}, u32[]{:S(2)}) %collective-permute-start.4) | collective-permute-done | bytes 688160 | tf_op jit(solution)/shard_map/ppermute | solution.py:60
  101.6 1.9 collective-permute-start.5
  103.6 2.0 fusion.61
  106.9 1.8 gather_fusion.2
  109.5 4.8 %collective-permute-start.13 = (bf16[3,128,896]{2,1,0:T(8,128)(2,1)}, bf16[3,128,896]{2,1,0:T(8,128)(2,1)S(1)}, u32[]{:S(2)}, u32[]{:S(2)}) collective-permute-start(bf16[3,128,896]{2,1,0:T(8,128)(2,1)} %collective-permute-done.12), channel_id=1, source_target_pairs={{0,120},{8,0},{16,8},{24,16},{32,24},{40,32},{48,40},{56,48},{64,5... | collective-permute-start | bytes 2064392 | tf_op jit(solution)/shard_map/ppermute | solution.py:61
  114.4 1.6 select_bitcast_fusion.1
  116.0 2.0 fusion.60
  118.0 1.9 collective-permute-start.6
  119.9 2.0 fusion.59
  122.0 2.5 %collective-permute-done.13 = bf16[3,128,896]{2,1,0:T(8,128)(2,1)S(1)} collective-permute-done((bf16[3,128,896]{2,1,0:T(8,128)(2,1)}, bf16[3,128,896]{2,1,0:T(8,128)(2,1)S(1)}, u32[]{:S(2)}, u32[]{:S(2)}) %collective-permute-start.13) | collective-permute-done | bytes 688160 | tf_op jit(solution)/shard_map/ppermute | solution.py:61
  124.5 5.2 %collective-permute-start.14 = (bf16[3,128,896]{2,1,0:T(8,128)(2,1)S(1)}, bf16[3,128,896]{2,1,0:T(8,128)(2,1)S(1)}, u32[]{:S(2)}, u32[]{:S(2)}) collective-permute-start(bf16[3,128,896]{2,1,0:T(8,128)(2,1)S(1)} %collective-permute-done.13), channel_id=1, source_target_pairs={{0,120},{8,0},{16,8},{24,16},{32,24},{40,32},{48,40},{56,48},{64,5... | collective-permute-start | bytes 2064392 | tf_op jit(solution)/shard_map/ppermute | solution.py:61
  129.7 2.0 fusion.58
  131.7 2.0 fusion.57
  133.7 1.9 collective-permute-start.7
  135.7 2.0 fusion.56
  138.7 5.5 %collective-permute-start.15 = (bf16[3,64,896]{2,1,0:T(8,128)(2,1)S(1)}, bf16[3,64,896]{2,1,0:T(8,128)(2,1)S(1)}, u32[]{:S(2)}, u32[]{:S(2)}) collective-permute-start(bf16[3,64,896]{2,1,0:T(8,128)(2,1)S(1)} %slice.219), channel_id=1, source_target_pairs={{0,120},{8,0},{16,8},{24,16},{32,24},{40,32},{48,40},{56,48},{64,5... | collective-permute-start | bytes 1032200 | tf_op jit(solution)/shard_map/ppermute | solution.py:66
  145.1 3.5 %collective-permute-done.15 = bf16[3,64,896]{2,1,0:T(8,128)(2,1)S(1)} collective-permute-done((bf16[3,64,896]{2,1,0:T(8,128)(2,1)S(1)}, bf16[3,64,896]{2,1,0:T(8,128)(2,1)S(1)}, u32[]{:S(2)}, u32[]{:S(2)}) %collective-permute-start.15) | collective-permute-done | bytes 344096 | tf_op jit(solution)/shard_map/ppermute | solution.py:66
  151.2 2.0 fusion.51
  153.2 2.0 fusion.50
  155.2 2.0 fusion.49
  158.9 3.6 %fusion.7 = f32[320,896]{1,0:T(8,128)S(1)} fusion(bf16[2048,896]{1,0:T(8,128)(2,1)} %get-tuple-element.5, bf16[16,40,8,128]{3,2,1,0:T(8,128)(2,1)S(1)} %get-tuple-element.48), kind=kOutput, calls=%fused_computation.16 | convolution fusion | flops 1174405120 | bytes 6127616 | tf_op jit(solution)/shard_map/dot_general | solution.py:82
  168.2 3.6 %fusion.14 = f32[320,2048]{1,0:T(8,128)S(1)} fusion(bf16[2048,896]{1,0:T(8,128)(2,1)} %get-tuple-element.5, f32[320,896]{1,0:T(8,128)S(1)} %fusion.4, f32[320,896]{1,0:T(8,128)S(1)} %fusion.9), kind=kOutput, calls=%fused_computation.32 | convolution fusion | flops 1176125440 | bytes 8585216 | tf_op jit(solution)/shard_map/dot_general | solution.py:91
  171.9 1.7 fusion.2
  174.5 2.4 gather_fusion
  176.9 5.0 %copy.98 = bf16[320,2,16,128]{3,2,1,0:T(8,128)(2,1)} copy(bf16[320,2,16,128]{3,0,1,2:T(8,128)(2,1)} %bitcast.263) | data formatting | bytes 5242880 | tf_op jit(solution)/shard_map/jit(_take)/gather | solution.py:95
  181.8 3.7 %gather.10 = bf16[320,2,8,256]{3,2,1,0:T(8,128)(2,1)S(1)} reshape(bf16[320,2,16,128]{3,2,1,0:T(8,128)(2,1)} %copy.98) | data formatting | bytes 5242880 | tf_op jit(solution)/shard_map/jit(_take)/gather | solution.py:95
  185.8 2.0 copy.99
  187.8 43.5 %all_to_all.20 = bf16[320,2,8,256]{3,1,0,2:T(2,128)(2,1)S(1)} all-to-all(bf16[320,2,8,256]{3,1,0,2:T(2,128)(2,1)S(1)} %copy.99), channel_id=1, replica_groups=mesh['ey'=4,'ez'=16,'tp'=8] {'tp'}, dimensions={2} | all-to-all | bytes 5242880 | tf_op jit(solution)/shard_map/all_to_all | solution.py:100
  231.3 3.0 %reduce_sum.35 = bf16[320,2,256]{2,1,0:T(2,128)(2,1)S(1)} reduce(bf16[320,2,8,256]{3,1,0,2:T(2,128)(2,1)S(1)} %all_to_all.20, bf16[]{:T(256)} %constant.63.clone.1), dimensions={2}, to_apply=%region_5.7 | reduce | flops 1146880 | bytes 2949122 | tf_op jit(solution)/shard_map/reduce_sum | solution.py:101
  234.4 9.9 %all_to_all.21 = bf16[4,80,2,256]{3,1,2,0:T(8,128)(2,1)S(1)} all-to-all(bf16[4,80,2,256]{3,1,2,0:T(8,128)(2,1)S(1)} %copy.101), channel_id=1, replica_groups=mesh['ey'=4,'ez'=16,'tp'=8] {'ey'}, dimensions={0} | all-to-all | bytes 655360 | tf_op jit(solution)/shard_map/all_to_all | solution.py:103
  (88 shorter events, 27.5 us)
Async XLA Ops:
  0.6 56.3 %copy-start = (bf16[128,2048]{1,0:T(8,128)(2,1)S(1)}, bf16[128,2048]{1,0:T(8,128)(2,1)}, u32[]{:S(2)}) copy-start(bf16[128,2048]{1,0:T(8,128)(2,1)} %param.10) | copy-start | bytes 1572868
  0.6 74.1 %copy-start.8 = (bf16[128,2048]{1,0:T(8,128)(2,1)S(1)}, bf16[128,2048]{1,0:T(8,128)(2,1)}, u32[]{:S(2)}) copy-start(bf16[128,2048]{1,0:T(8,128)(2,1)} %param.9) | copy-start | bytes 1572868
  3.0 27.2 %collective-permute-start = (bf16[3,128,896]{2,1,0:T(8,128)(2,1)S(1)}, bf16[3,128,896]{2,1,0:T(8,128)(2,1)}, u32[]{:S(2)}, u32[]{:S(2)}) collective-permute-start(bf16[3,128,896]{2,1,0:T(8,128)(2,1)S(1)} %pad_maximum_fusion.1), channel_id=1, source_target_pairs={{0,8},{8,16},{16,24},{24,32},{32,40},{40,48},{48,56},{56,64},{64,7... | collective-permute-start | bytes 2064392 | tf_op jit(solution)/shard_map/ppermute | solution.py:60
  7.4 26.4 %collective-permute-start.8 = (bf16[3,128,896]{2,1,0:T(8,128)(2,1)S(1)}, bf16[3,128,896]{2,1,0:T(8,128)(2,1)S(1)}, u32[]{:S(2)}, u32[]{:S(2)}) collective-permute-start(bf16[3,128,896]{2,1,0:T(8,128)(2,1)S(1)} %pad_maximum_fusion.1), channel_id=1, source_target_pairs={{0,120},{8,0},{16,8},{24,16},{32,24},{40,32},{48,40},{56,48},{64,5... | collective-permute-start | bytes 2064392 | tf_op jit(solution)/shard_map/ppermute | solution.py:61
  30.2 19.2 %collective-permute-start.1 = (bf16[3,128,896]{2,1,0:T(8,128)(2,1)}, bf16[3,128,896]{2,1,0:T(8,128)(2,1)}, u32[]{:S(2)}, u32[]{:S(2)}) collective-permute-start(bf16[3,128,896]{2,1,0:T(8,128)(2,1)} %collective-permute-done), channel_id=1, source_target_pairs={{0,8},{8,16},{16,24},{24,32},{32,40},{40,48},{48,56},{56,64},{64,7... | collective-permute-start | bytes 2064392 | tf_op jit(solution)/shard_map/ppermute | solution.py:60
  33.8 24.7 %copy-start.4 = (bf16[3,128,896]{2,1,0:T(8,128)(2,1)}, bf16[3,128,896]{2,1,0:T(8,128)(2,1)S(1)}, u32[]{:S(2)}) copy-start(bf16[3,128,896]{2,1,0:T(8,128)(2,1)S(1)} %collective-permute-done.8) | copy-start | bytes 2064388
  33.8 17.8 %collective-permute-start.9 = (bf16[3,128,896]{2,1,0:T(8,128)(2,1)S(1)}, bf16[3,128,896]{2,1,0:T(8,128)(2,1)S(1)}, u32[]{:S(2)}, u32[]{:S(2)}) collective-permute-start(bf16[3,128,896]{2,1,0:T(8,128)(2,1)S(1)} %collective-permute-done.8), channel_id=1, source_target_pairs={{0,120},{8,0},{16,8},{24,16},{32,24},{40,32},{48,40},{56,48},{64,5... | collective-permute-start | bytes 2064392 | tf_op jit(solution)/shard_map/ppermute | solution.py:61
  49.3 18.3 %collective-permute-start.2 = (bf16[3,128,896]{2,1,0:T(8,128)(2,1)}, bf16[3,128,896]{2,1,0:T(8,128)(2,1)}, u32[]{:S(2)}, u32[]{:S(2)}) collective-permute-start(bf16[3,128,896]{2,1,0:T(8,128)(2,1)} %collective-permute-done.1), channel_id=1, source_target_pairs={{0,8},{8,16},{16,24},{24,32},{32,40},{40,48},{48,56},{56,64},{64,7... | collective-permute-start | bytes 2064392 | tf_op jit(solution)/shard_map/ppermute | solution.py:60
  51.6 26.3 %copy-start.6 = (bf16[3,128,896]{2,1,0:T(8,128)(2,1)}, bf16[3,128,896]{2,1,0:T(8,128)(2,1)S(1)}, u32[]{:S(2)}) copy-start(bf16[3,128,896]{2,1,0:T(8,128)(2,1)S(1)} %collective-permute-done.9) | copy-start | bytes 2064388
  51.6 18.0 %collective-permute-start.10 = (bf16[3,128,896]{2,1,0:T(8,128)(2,1)S(1)}, bf16[3,128,896]{2,1,0:T(8,128)(2,1)}, u32[]{:S(2)}, u32[]{:S(2)}) collective-permute-start(bf16[3,128,896]{2,1,0:T(8,128)(2,1)S(1)} %collective-permute-done.9), channel_id=1, source_target_pairs={{0,120},{8,0},{16,8},{24,16},{32,24},{40,32},{48,40},{56,48},{64,5... | collective-permute-start | bytes 2064392 | tf_op jit(solution)/shard_map/ppermute | solution.py:61
  58.5 28.5 %copy-start.2 = (bf16[128,896]{1,0:T(8,128)(2,1)S(1)}, bf16[128,896]{1,0:T(8,128)(2,1)}, u32[]{:S(2)}) copy-start(bf16[128,896]{1,0:T(8,128)(2,1)} %param.13) | copy-start | bytes 688132
  58.5 28.5 %copy-start.3 = (bf16[128,896]{1,0:T(8,128)(2,1)S(1)}, bf16[128,896]{1,0:T(8,128)(2,1)}, u32[]{:S(2)}) copy-start(bf16[128,896]{1,0:T(8,128)(2,1)} %param.14) | copy-start | bytes 688132
  58.5 19.4 %all-to-all-start.1 = ((bf16[4,80,2048]{2,1,0:T(8,128)(2,1)}), bf16[4,80,2048]{2,1,0:T(8,128)(2,1)S(1)}, u32[]{:S(2)}, u32[]{:S(2)}) async-start(bf16[4,80,2048]{2,1,0:T(8,128)(2,1)} %bitcast.54), calls=%async_computation.1 | async-start | bytes 2621440 | tf_op jit(solution)/shard_map/all_to_all | solution.py:73
  67.6 17.4 %collective-permute-start.3 = (bf16[3,128,896]{2,1,0:T(8,128)(2,1)}, bf16[3,128,896]{2,1,0:T(8,128)(2,1)}, u32[]{:S(2)}, u32[]{:S(2)}) collective-permute-start(bf16[3,128,896]{2,1,0:T(8,128)(2,1)} %collective-permute-done.2), channel_id=1, source_target_pairs={{0,8},{8,16},{16,24},{24,32},{32,40},{40,48},{48,56},{56,64},{64,7... | collective-permute-start | bytes 2064392 | tf_op jit(solution)/shard_map/ppermute | solution.py:60
  69.6 18.3 %collective-permute-start.11 = (bf16[3,128,896]{2,1,0:T(8,128)(2,1)}, bf16[3,128,896]{2,1,0:T(8,128)(2,1)}, u32[]{:S(2)}, u32[]{:S(2)}) collective-permute-start(bf16[3,128,896]{2,1,0:T(8,128)(2,1)} %collective-permute-done.10), channel_id=1, source_target_pairs={{0,120},{8,0},{16,8},{24,16},{32,24},{40,32},{48,40},{56,48},{64,5... | collective-permute-start | bytes 2064392 | tf_op jit(solution)/shard_map/ppermute | solution.py:61
  77.9 28.4 %all-to-all-start = ((bf16[4,80,2048]{2,1,0:T(8,128)(2,1)}), bf16[4,80,2048]{2,1,0:T(8,128)(2,1)S(1)}, u32[]{:S(2)}, u32[]{:S(2)}) async-start(bf16[4,80,2048]{2,1,0:T(8,128)(2,1)} %bitcast.3), calls=%async_computation | async-start | bytes 2621440 | tf_op jit(solution)/shard_map/all_to_all | solution.py:72
  85.1 16.6 %collective-permute-start.4 = (bf16[3,128,896]{2,1,0:T(8,128)(2,1)}, bf16[3,128,896]{2,1,0:T(8,128)(2,1)}, u32[]{:S(2)}, u32[]{:S(2)}) collective-permute-start(bf16[3,128,896]{2,1,0:T(8,128)(2,1)} %collective-permute-done.3), channel_id=1, source_target_pairs={{0,8},{8,16},{16,24},{24,32},{32,40},{40,48},{48,56},{56,64},{64,7... | collective-permute-start | bytes 2064392 | tf_op jit(solution)/shard_map/ppermute | solution.py:60
  87.8 21.7 %collective-permute-start.12 = (bf16[3,128,896]{2,1,0:T(8,128)(2,1)}, bf16[3,128,896]{2,1,0:T(8,128)(2,1)}, u32[]{:S(2)}, u32[]{:S(2)}) collective-permute-start(bf16[3,128,896]{2,1,0:T(8,128)(2,1)} %collective-permute-done.11), channel_id=1, source_target_pairs={{0,120},{8,0},{16,8},{24,16},{32,24},{40,32},{48,40},{56,48},{64,5... | collective-permute-start | bytes 2064392 | tf_op jit(solution)/shard_map/ppermute | solution.py:61
  101.6 16.4 %collective-permute-start.5 = (bf16[3,128,896]{2,1,0:T(8,128)(2,1)}, bf16[3,128,896]{2,1,0:T(8,128)(2,1)}, u32[]{:S(2)}, u32[]{:S(2)}) collective-permute-start(bf16[3,128,896]{2,1,0:T(8,128)(2,1)} %collective-permute-done.4), channel_id=1, source_target_pairs={{0,8},{8,16},{16,24},{24,32},{32,40},{40,48},{48,56},{56,64},{64,7... | collective-permute-start | bytes 2064392 | tf_op jit(solution)/shard_map/ppermute | solution.py:60
  109.5 6.5 %copy-start.9 = (bf16[2048,896]{1,0:T(8,128)(2,1)S(1)}, bf16[2048,896]{1,0:T(8,128)(2,1)}, u32[]{:S(2)}) copy-start(bf16[2048,896]{1,0:T(8,128)(2,1)} %get-tuple-element.45) | copy-start | bytes 11010052
  109.5 15.0 %collective-permute-start.13 = (bf16[3,128,896]{2,1,0:T(8,128)(2,1)}, bf16[3,128,896]{2,1,0:T(8,128)(2,1)S(1)}, u32[]{:S(2)}, u32[]{:S(2)}) collective-permute-start(bf16[3,128,896]{2,1,0:T(8,128)(2,1)} %collective-permute-done.12), channel_id=1, source_target_pairs={{0,120},{8,0},{16,8},{24,16},{32,24},{40,32},{48,40},{56,48},{64,5... | collective-permute-start | bytes 2064392 | tf_op jit(solution)/shard_map/ppermute | solution.py:61
  118.0 15.7 %collective-permute-start.6 = (bf16[3,128,896]{2,1,0:T(8,128)(2,1)}, bf16[3,128,896]{2,1,0:T(8,128)(2,1)S(1)}, u32[]{:S(2)}, u32[]{:S(2)}) collective-permute-start(bf16[3,128,896]{2,1,0:T(8,128)(2,1)} %collective-permute-done.5), channel_id=1, source_target_pairs={{0,8},{8,16},{16,24},{24,32},{32,40},{40,48},{48,56},{56,64},{64,7... | collective-permute-start | bytes 2064392 | tf_op jit(solution)/shard_map/ppermute | solution.py:60
  124.5 14.2 %collective-permute-start.14 = (bf16[3,128,896]{2,1,0:T(8,128)(2,1)S(1)}, bf16[3,128,896]{2,1,0:T(8,128)(2,1)S(1)}, u32[]{:S(2)}, u32[]{:S(2)}) collective-permute-start(bf16[3,128,896]{2,1,0:T(8,128)(2,1)S(1)} %collective-permute-done.13), channel_id=1, source_target_pairs={{0,120},{8,0},{16,8},{24,16},{32,24},{40,32},{48,40},{56,48},{64,5... | collective-permute-start | bytes 2064392 | tf_op jit(solution)/shard_map/ppermute | solution.py:61
  133.7 11.3 %collective-permute-start.7 = (bf16[3,64,896]{2,1,0:T(8,128)(2,1)S(1)}, bf16[3,64,896]{2,1,0:T(8,128)(2,1)S(1)}, u32[]{:S(2)}, u32[]{:S(2)}) collective-permute-start(bf16[3,64,896]{2,1,0:T(8,128)(2,1)S(1)} %slice.218), channel_id=1, source_target_pairs={{0,8},{8,16},{16,24},{24,32},{32,40},{40,48},{48,56},{56,64},{64,7... | collective-permute-start | bytes 1032200 | tf_op jit(solution)/shard_map/ppermute | solution.py:65
  138.7 9.9 %collective-permute-start.15 = (bf16[3,64,896]{2,1,0:T(8,128)(2,1)S(1)}, bf16[3,64,896]{2,1,0:T(8,128)(2,1)S(1)}, u32[]{:S(2)}, u32[]{:S(2)}) collective-permute-start(bf16[3,64,896]{2,1,0:T(8,128)(2,1)S(1)} %slice.219), channel_id=1, source_target_pairs={{0,120},{8,0},{16,8},{24,16},{32,24},{40,32},{48,40},{56,48},{64,5... | collective-permute-start | bytes 1032200 | tf_op jit(solution)/shard_map/ppermute | solution.py:66
  149.5 7.7 %copy-start.7 = (bf16[3,128,896]{2,1,0:T(8,128)(2,1)S(1)}, bf16[3,128,896]{2,1,0:T(8,128)(2,1)}, u32[]{:S(2)}) copy-start(bf16[3,128,896]{2,1,0:T(8,128)(2,1)} %copy-done.6) | copy-start | bytes 2064388
  150.3 7.7 %copy-start.5 = (bf16[3,128,896]{2,1,0:T(8,128)(2,1)S(1)}, bf16[3,128,896]{2,1,0:T(8,128)(2,1)}, u32[]{:S(2)}) copy-start(bf16[3,128,896]{2,1,0:T(8,128)(2,1)} %copy-done.4) | copy-start | bytes 2064388
  162.4 2.0 copy-start.10
  187.8 58.5 %copy-start.1 = (bf16[128,2048]{1,0:T(8,128)(2,1)S(1)}, bf16[128,2048]{1,0:T(8,128)(2,1)}, u32[]{:S(2)}) copy-start(bf16[128,2048]{1,0:T(8,128)(2,1)} %param.10) | copy-start | bytes 1572868

commit v10 on v9

--- a/solution.py
+++ b/solution.py
@@ -97,8 +97,9 @@
     ).reshape(row_total, 2, model_width)
     tp_count = lax.axis_size("tp")
     pieces = results.reshape(row_total, 2, tp_count, model_width // tp_count)
-    pieces = lax.all_to_all(pieces, "tp", split_axis=2, concat_axis=2, tiled=True)
-    summed = jnp.sum(pieces.astype(jnp.float32), axis=2).astype(jnp.bfloat16)
+    pieces = jnp.transpose(pieces, (2, 0, 1, 3))
+    pieces = lax.all_to_all(pieces, "tp", split_axis=0, concat_axis=0, tiled=True)
+    summed = jnp.sum(pieces.astype(jnp.float32), axis=0).astype(jnp.bfloat16)
     rounded = summed.reshape(plane_count, CAP, 2, -1)
     returned = lax.all_to_all(rounded, "ey", split_axis=0, concat_axis=0, tiled=True)
     returned = returned.reshape(slot_count, 2, -1).astype(jnp.float32)

time: 248 us -> 248 us (level)
  no operation moved by 1% of the time
where the time goes in v10:
time: 248 us; the launch traced here: 246 us
  starting transfers between devices  70.2 us (28%)
  blocking collectives  53.4 us (22%)
  waiting for transfers between devices  47.3 us (19%)
  local copies, waits for them, and re-layouts  46.3 us (19%)
  matrix products  18.6 us (8%)
  other arithmetic  9.3 us (4%)
    all_to_all x1, blocking collectives, per_device(): lax.all_to_all(pieces, 'tp', split_axis=0, concat_axis=0, tiled=True)  43.5 us
    ppermute x7, starting transfers between devices, per_device(): ccw = lax.ppermute(ccw, 'ez', backward)  39.1 us
    ppermute x7, waiting for transfers between devices, per_device(): cw = lax.ppermute(cw, 'ez', forward)  38.3 us
    unnamed x45, local copies, waits for them, and re-layouts  27.5 us
    ppermute x7, starting transfers between devices, per_device(): cw = lax.ppermute(cw, 'ez', forward)  15.8 us
    gather x3, local copies, waits for them, and re-layouts, per_device(): jnp.take(results.reshape(row_total, 2, member_count, block_width), origin...  11 us
    all_to_all x1, blocking collectives, per_device(): lax.all_to_all(rounded, 'ey', split_axis=0, concat_axis=0, tiled=True)  9.86 us
    ppermute x1, starting transfers between devices, per_device(): far_high = lax.ppermute(ccw[:, cut:], 'ez', backward)  5.5 us
  transfers between devices with their start and end apart: 18, of which 10 were waited for; matrix products, arithmetic and copies ran while one was open for 11% of the time, Pallas kernels for 0%

profile of v10, /device:TPU:1, one launch (start us, length us, event | category | flops | bytes accessed | tf_op | source)
XLA Modules:
  0.0 246.3 jit_solution(3155774404797784052)
XLA Ops:
  3.0 4.4 %collective-permute-start = (bf16[3,128,896]{2,1,0:T(8,128)(2,1)S(1)}, bf16[3,128,896]{2,1,0:T(8,128)(2,1)}, u32[]{:S(2)}, u32[]{:S(2)}) collective-permute-start(bf16[3,128,896]{2,1,0:T(8,128)(2,1)S(1)} %pad_maximum_fusion.1), channel_id=1, source_target_pairs={{0,8},{8,16},{16,24},{24,32},{32,40},{40,48},{48,56},{56,64},{64,7... | collective-permute-start | bytes 2064392 | tf_op jit(solution)/shard_map/ppermute | solution.py:60
  7.4 9.5 %collective-permute-start.8 = (bf16[3,128,896]{2,1,0:T(8,128)(2,1)S(1)}, bf16[3,128,896]{2,1,0:T(8,128)(2,1)S(1)}, u32[]{:S(2)}, u32[]{:S(2)}) collective-permute-start(bf16[3,128,896]{2,1,0:T(8,128)(2,1)S(1)} %pad_maximum_fusion.1), channel_id=1, source_target_pairs={{0,120},{8,0},{16,8},{24,16},{32,24},{40,32},{48,40},{56,48},{64,5... | collective-permute-start | bytes 2064392 | tf_op jit(solution)/shard_map/ppermute | solution.py:61
  17.8 12.4 %collective-permute-done = bf16[3,128,896]{2,1,0:T(8,128)(2,1)} collective-permute-done((bf16[3,128,896]{2,1,0:T(8,128)(2,1)S(1)}, bf16[3,128,896]{2,1,0:T(8,128)(2,1)}, u32[]{:S(2)}, u32[]{:S(2)}) %collective-permute-start) | collective-permute-done | bytes 688160 | tf_op jit(solution)/shard_map/ppermute | solution.py:60
  30.2 1.9 collective-permute-start.1
  33.8 4.6 %collective-permute-start.9 = (bf16[3,128,896]{2,1,0:T(8,128)(2,1)S(1)}, bf16[3,128,896]{2,1,0:T(8,128)(2,1)S(1)}, u32[]{:S(2)}, u32[]{:S(2)}) collective-permute-start(bf16[3,128,896]{2,1,0:T(8,128)(2,1)S(1)} %collective-permute-done.8), channel_id=1, source_target_pairs={{0,120},{8,0},{16,8},{24,16},{32,24},{40,32},{48,40},{56,48},{64,5... | collective-permute-start | bytes 2064392 | tf_op jit(solution)/shard_map/ppermute | solution.py:61
  40.2 9.1 %collective-permute-done.1 = bf16[3,128,896]{2,1,0:T(8,128)(2,1)} collective-permute-done((bf16[3,128,896]{2,1,0:T(8,128)(2,1)}, bf16[3,128,896]{2,1,0:T(8,128)(2,1)}, u32[]{:S(2)}, u32[]{:S(2)}) %collective-permute-start.1) | collective-permute-done | bytes 688160 | tf_op jit(solution)/shard_map/ppermute | solution.py:60
  49.3 1.9 collective-permute-start.2
  51.6 5.3 %collective-permute-start.10 = (bf16[3,128,896]{2,1,0:T(8,128)(2,1)S(1)}, bf16[3,128,896]{2,1,0:T(8,128)(2,1)}, u32[]{:S(2)}, u32[]{:S(2)}) collective-permute-start(bf16[3,128,896]{2,1,0:T(8,128)(2,1)S(1)} %collective-permute-done.9), channel_id=1, source_target_pairs={{0,120},{8,0},{16,8},{24,16},{32,24},{40,32},{48,40},{56,48},{64,5... | collective-permute-start | bytes 2064392 | tf_op jit(solution)/shard_map/ppermute | solution.py:61
  56.9 1.6 fusion.1
  58.5 4.3 %all-to-all-start.1 = ((bf16[4,80,2048]{2,1,0:T(8,128)(2,1)}), bf16[4,80,2048]{2,1,0:T(8,128)(2,1)S(1)}, u32[]{:S(2)}, u32[]{:S(2)}) async-start(bf16[4,80,2048]{2,1,0:T(8,128)(2,1)} %bitcast.54), calls=%async_computation.1 | async-start | bytes 2621440 | tf_op jit(solution)/shard_map/all_to_all | solution.py:73
  62.8 4.8 %collective-permute-done.2 = bf16[3,128,896]{2,1,0:T(8,128)(2,1)} collective-permute-done((bf16[3,128,896]{2,1,0:T(8,128)(2,1)}, bf16[3,128,896]{2,1,0:T(8,128)(2,1)}, u32[]{:S(2)}, u32[]{:S(2)}) %collective-permute-start.2) | collective-permute-done | bytes 688160 | tf_op jit(solution)/shard_map/ppermute | solution.py:60
  67.6 1.9 collective-permute-start.3
  69.6 5.1 %collective-permute-start.11 = (bf16[3,128,896]{2,1,0:T(8,128)(2,1)}, bf16[3,128,896]{2,1,0:T(8,128)(2,1)}, u32[]{:S(2)}, u32[]{:S(2)}) collective-permute-start(bf16[3,128,896]{2,1,0:T(8,128)(2,1)} %collective-permute-done.10), channel_id=1, source_target_pairs={{0,120},{8,0},{16,8},{24,16},{32,24},{40,32},{48,40},{56,48},{64,5... | collective-permute-start | bytes 2064392 | tf_op jit(solution)/shard_map/ppermute | solution.py:61
  76.3 1.6 all-to-all-done.1
  77.9 3.5 %all-to-all-start = ((bf16[4,80,2048]{2,1,0:T(8,128)(2,1)}), bf16[4,80,2048]{2,1,0:T(8,128)(2,1)S(1)}, u32[]{:S(2)}, u32[]{:S(2)}) async-start(bf16[4,80,2048]{2,1,0:T(8,128)(2,1)} %bitcast.3), calls=%async_computation | async-start | bytes 2621440 | tf_op jit(solution)/shard_map/all_to_all | solution.py:72
  81.5 3.6 %collective-permute-done.3 = bf16[3,128,896]{2,1,0:T(8,128)(2,1)} collective-permute-done((bf16[3,128,896]{2,1,0:T(8,128)(2,1)}, bf16[3,128,896]{2,1,0:T(8,128)(2,1)}, u32[]{:S(2)}, u32[]{:S(2)}) %collective-permute-start.3) | collective-permute-done | bytes 688160 | tf_op jit(solution)/shard_map/ppermute | solution.py:60
  85.1 1.9 collective-permute-start.4
  87.8 4.6 %collective-permute-start.12 = (bf16[3,128,896]{2,1,0:T(8,128)(2,1)}, bf16[3,128,896]{2,1,0:T(8,128)(2,1)}, u32[]{:S(2)}, u32[]{:S(2)}) collective-permute-start(bf16[3,128,896]{2,1,0:T(8,128)(2,1)} %collective-permute-done.11), channel_id=1, source_target_pairs={{0,120},{8,0},{16,8},{24,16},{32,24},{40,32},{48,40},{56,48},{64,5... | collective-permute-start | bytes 2064392 | tf_op jit(solution)/shard_map/ppermute | solution.py:61
  93.2 8.5 %collective-permute-done.4 = bf16[3,128,896]{2,1,0:T(8,128)(2,1)} collective-permute-done((bf16[3,128,896]{2,1,0:T(8,128)(2,1)}, bf16[3,128,896]{2,1,0:T(8,128)(2,1)}, u32[]{:S(2)}, u32[]{:S(2)}) %collective-permute-start.4) | collective-permute-done | bytes 688160 | tf_op jit(solution)/shard_map/ppermute | solution.py:60
  101.6 1.9 collective-permute-start.5
  103.6 2.0 fusion.61
  106.9 1.8 gather_fusion.2
  109.5 4.8 %collective-permute-start.13 = (bf16[3,128,896]{2,1,0:T(8,128)(2,1)}, bf16[3,128,896]{2,1,0:T(8,128)(2,1)S(1)}, u32[]{:S(2)}, u32[]{:S(2)}) collective-permute-start(bf16[3,128,896]{2,1,0:T(8,128)(2,1)} %collective-permute-done.12), channel_id=1, source_target_pairs={{0,120},{8,0},{16,8},{24,16},{32,24},{40,32},{48,40},{56,48},{64,5... | collective-permute-start | bytes 2064392 | tf_op jit(solution)/shard_map/ppermute | solution.py:61
  114.4 1.6 select_bitcast_fusion.2
  116.0 2.0 fusion.60
  118.0 1.9 collective-permute-start.6
  119.9 2.0 fusion.59
  122.0 2.5 %collective-permute-done.13 = bf16[3,128,896]{2,1,0:T(8,128)(2,1)S(1)} collective-permute-done((bf16[3,128,896]{2,1,0:T(8,128)(2,1)}, bf16[3,128,896]{2,1,0:T(8,128)(2,1)S(1)}, u32[]{:S(2)}, u32[]{:S(2)}) %collective-permute-start.13) | collective-permute-done | bytes 688160 | tf_op jit(solution)/shard_map/ppermute | solution.py:61
  124.5 5.2 %collective-permute-start.14 = (bf16[3,128,896]{2,1,0:T(8,128)(2,1)S(1)}, bf16[3,128,896]{2,1,0:T(8,128)(2,1)S(1)}, u32[]{:S(2)}, u32[]{:S(2)}) collective-permute-start(bf16[3,128,896]{2,1,0:T(8,128)(2,1)S(1)} %collective-permute-done.13), channel_id=1, source_target_pairs={{0,120},{8,0},{16,8},{24,16},{32,24},{40,32},{48,40},{56,48},{64,5... | collective-permute-start | bytes 2064392 | tf_op jit(solution)/shard_map/ppermute | solution.py:61
  129.7 2.0 fusion.58
  131.7 2.0 fusion.57
  133.7 1.9 collective-permute-start.7
  135.7 2.0 fusion.56
  138.7 5.5 %collective-permute-start.15 = (bf16[3,64,896]{2,1,0:T(8,128)(2,1)S(1)}, bf16[3,64,896]{2,1,0:T(8,128)(2,1)S(1)}, u32[]{:S(2)}, u32[]{:S(2)}) collective-permute-start(bf16[3,64,896]{2,1,0:T(8,128)(2,1)S(1)} %slice.219), channel_id=1, source_target_pairs={{0,120},{8,0},{16,8},{24,16},{32,24},{40,32},{48,40},{56,48},{64,5... | collective-permute-start | bytes 1032200 | tf_op jit(solution)/shard_map/ppermute | solution.py:66
  145.1 3.5 %collective-permute-done.15 = bf16[3,64,896]{2,1,0:T(8,128)(2,1)S(1)} collective-permute-done((bf16[3,64,896]{2,1,0:T(8,128)(2,1)S(1)}, bf16[3,64,896]{2,1,0:T(8,128)(2,1)S(1)}, u32[]{:S(2)}, u32[]{:S(2)}) %collective-permute-start.15) | collective-permute-done | bytes 344096 | tf_op jit(solution)/shard_map/ppermute | solution.py:66
  151.2 2.0 fusion.51
  153.2 2.0 fusion.50
  155.2 2.0 fusion.49
  158.9 3.6 %fusion.7 = f32[320,896]{1,0:T(8,128)S(1)} fusion(bf16[2048,896]{1,0:T(8,128)(2,1)} %get-tuple-element.5, bf16[16,40,8,128]{3,2,1,0:T(8,128)(2,1)S(1)} %get-tuple-element.48), kind=kOutput, calls=%fused_computation.16 | convolution fusion | flops 1174405120 | bytes 6127616 | tf_op jit(solution)/shard_map/dot_general | solution.py:82
  168.2 3.6 %fusion.14 = f32[320,2048]{1,0:T(8,128)S(1)} fusion(bf16[2048,896]{1,0:T(8,128)(2,1)} %get-tuple-element.5, f32[320,896]{1,0:T(8,128)S(1)} %fusion.4, f32[320,896]{1,0:T(8,128)S(1)} %fusion.9), kind=kOutput, calls=%fused_computation.32 | convolution fusion | flops 1176125440 | bytes 8585216 | tf_op jit(solution)/shard_map/dot_general | solution.py:91
  171.9 1.7 fusion.2
  174.5 2.4 gather_fusion
  176.9 5.0 %copy.98 = bf16[320,2,16,128]{3,2,1,0:T(8,128)(2,1)} copy(bf16[320,2,16,128]{3,0,1,2:T(8,128)(2,1)} %bitcast.265) | data formatting | bytes 5242880 | tf_op jit(solution)/shard_map/jit(_take)/gather | solution.py:95
  181.8 3.7 %gather.10 = bf16[320,2,8,256]{3,2,1,0:T(8,128)(2,1)S(1)} reshape(bf16[320,2,16,128]{3,2,1,0:T(8,128)(2,1)} %copy.98) | data formatting | bytes 5242880 | tf_op jit(solution)/shard_map/jit(_take)/gather | solution.py:95
  185.8 2.0 copy.99
  187.8 43.5 %all_to_all.20 = bf16[8,320,2,256]{3,2,1,0:T(2,128)(2,1)S(1)} all-to-all(bf16[8,320,2,256]{3,2,1,0:T(2,128)(2,1)S(1)} %copy.99), channel_id=1, replica_groups=mesh['ey'=4,'ez'=16,'tp'=8] {'tp'}, dimensions={0} | all-to-all | bytes 5242880 | tf_op jit(solution)/shard_map/all_to_all | solution.py:101
  231.3 3.0 %reduce_sum.35 = bf16[320,2,256]{2,1,0:T(2,128)(2,1)S(1)} reduce(bf16[8,320,2,256]{3,2,1,0:T(2,128)(2,1)S(1)} %all_to_all.20, bf16[]{:T(256)} %constant.63.clone.1), dimensions={0}, to_apply=%region_5.7 | reduce | flops 1146880 | bytes 2949122 | tf_op jit(solution)/shard_map/reduce_sum | solution.py:102
  234.4 9.9 %all_to_all.21 = bf16[4,80,2,256]{3,1,2,0:T(8,128)(2,1)S(1)} all-to-all(bf16[4,80,2,256]{3,1,2,0:T(8,128)(2,1)S(1)} %copy.101), channel_id=1, replica_groups=mesh['ey'=4,'ez'=16,'tp'=8] {'ey'}, dimensions={0} | all-to-all | bytes 655360 | tf_op jit(solution)/shard_map/all_to_all | solution.py:104
  (88 shorter events, 27.5 us)
Async XLA Ops:
  0.6 56.3 %copy-start = (bf16[128,2048]{1,0:T(8,128)(2,1)S(1)}, bf16[128,2048]{1,0:T(8,128)(2,1)}, u32[]{:S(2)}) copy-start(bf16[128,2048]{1,0:T(8,128)(2,1)} %param.10) | copy-start | bytes 1572868
  0.6 74.1 %copy-start.8 = (bf16[128,2048]{1,0:T(8,128)(2,1)S(1)}, bf16[128,2048]{1,0:T(8,128)(2,1)}, u32[]{:S(2)}) copy-start(bf16[128,2048]{1,0:T(8,128)(2,1)} %param.9) | copy-start | bytes 1572868
  3.0 27.2 %collective-permute-start = (bf16[3,128,896]{2,1,0:T(8,128)(2,1)S(1)}, bf16[3,128,896]{2,1,0:T(8,128)(2,1)}, u32[]{:S(2)}, u32[]{:S(2)}) collective-permute-start(bf16[3,128,896]{2,1,0:T(8,128)(2,1)S(1)} %pad_maximum_fusion.1), channel_id=1, source_target_pairs={{0,8},{8,16},{16,24},{24,32},{32,40},{40,48},{48,56},{56,64},{64,7... | collective-permute-start | bytes 2064392 | tf_op jit(solution)/shard_map/ppermute | solution.py:60
  7.4 26.4 %collective-permute-start.8 = (bf16[3,128,896]{2,1,0:T(8,128)(2,1)S(1)}, bf16[3,128,896]{2,1,0:T(8,128)(2,1)S(1)}, u32[]{:S(2)}, u32[]{:S(2)}) collective-permute-start(bf16[3,128,896]{2,1,0:T(8,128)(2,1)S(1)} %pad_maximum_fusion.1), channel_id=1, source_target_pairs={{0,120},{8,0},{16,8},{24,16},{32,24},{40,32},{48,40},{56,48},{64,5... | collective-permute-start | bytes 2064392 | tf_op jit(solution)/shard_map/ppermute | solution.py:61
  30.2 19.2 %collective-permute-start.1 = (bf16[3,128,896]{2,1,0:T(8,128)(2,1)}, bf16[3,128,896]{2,1,0:T(8,128)(2,1)}, u32[]{:S(2)}, u32[]{:S(2)}) collective-permute-start(bf16[3,128,896]{2,1,0:T(8,128)(2,1)} %collective-permute-done), channel_id=1, source_target_pairs={{0,8},{8,16},{16,24},{24,32},{32,40},{40,48},{48,56},{56,64},{64,7... | collective-permute-start | bytes 2064392 | tf_op jit(solution)/shard_map/ppermute | solution.py:60
  33.8 24.7 %copy-start.4 = (bf16[3,128,896]{2,1,0:T(8,128)(2,1)}, bf16[3,128,896]{2,1,0:T(8,128)(2,1)S(1)}, u32[]{:S(2)}) copy-start(bf16[3,128,896]{2,1,0:T(8,128)(2,1)S(1)} %collective-permute-done.8) | copy-start | bytes 2064388
  33.8 17.8 %collective-permute-start.9 = (bf16[3,128,896]{2,1,0:T(8,128)(2,1)S(1)}, bf16[3,128,896]{2,1,0:T(8,128)(2,1)S(1)}, u32[]{:S(2)}, u32[]{:S(2)}) collective-permute-start(bf16[3,128,896]{2,1,0:T(8,128)(2,1)S(1)} %collective-permute-done.8), channel_id=1, source_target_pairs={{0,120},{8,0},{16,8},{24,16},{32,24},{40,32},{48,40},{56,48},{64,5... | collective-permute-start | bytes 2064392 | tf_op jit(solution)/shard_map/ppermute | solution.py:61
  49.3 18.3 %collective-permute-start.2 = (bf16[3,128,896]{2,1,0:T(8,128)(2,1)}, bf16[3,128,896]{2,1,0:T(8,128)(2,1)}, u32[]{:S(2)}, u32[]{:S(2)}) collective-permute-start(bf16[3,128,896]{2,1,0:T(8,128)(2,1)} %collective-permute-done.1), channel_id=1, source_target_pairs={{0,8},{8,16},{16,24},{24,32},{32,40},{40,48},{48,56},{56,64},{64,7... | collective-permute-start | bytes 2064392 | tf_op jit(solution)/shard_map/ppermute | solution.py:60
  51.6 26.3 %copy-start.6 = (bf16[3,128,896]{2,1,0:T(8,128)(2,1)}, bf16[3,128,896]{2,1,0:T(8,128)(2,1)S(1)}, u32[]{:S(2)}) copy-start(bf16[3,128,896]{2,1,0:T(8,128)(2,1)S(1)} %collective-permute-done.9) | copy-start | bytes 2064388
  51.6 18.0 %collective-permute-start.10 = (bf16[3,128,896]{2,1,0:T(8,128)(2,1)S(1)}, bf16[3,128,896]{2,1,0:T(8,128)(2,1)}, u32[]{:S(2)}, u32[]{:S(2)}) collective-permute-start(bf16[3,128,896]{2,1,0:T(8,128)(2,1)S(1)} %collective-permute-done.9), channel_id=1, source_target_pairs={{0,120},{8,0},{16,8},{24,16},{32,24},{40,32},{48,40},{56,48},{64,5... | collective-permute-start | bytes 2064392 | tf_op jit(solution)/shard_map/ppermute | solution.py:61
  58.5 28.5 %copy-start.2 = (bf16[128,896]{1,0:T(8,128)(2,1)S(1)}, bf16[128,896]{1,0:T(8,128)(2,1)}, u32[]{:S(2)}) copy-start(bf16[128,896]{1,0:T(8,128)(2,1)} %param.13) | copy-start | bytes 688132
  58.5 28.5 %copy-start.3 = (bf16[128,896]{1,0:T(8,128)(2,1)S(1)}, bf16[128,896]{1,0:T(8,128)(2,1)}, u32[]{:S(2)}) copy-start(bf16[128,896]{1,0:T(8,128)(2,1)} %param.14) | copy-start | bytes 688132
  58.5 19.4 %all-to-all-start.1 = ((bf16[4,80,2048]{2,1,0:T(8,128)(2,1)}), bf16[4,80,2048]{2,1,0:T(8,128)(2,1)S(1)}, u32[]{:S(2)}, u32[]{:S(2)}) async-start(bf16[4,80,2048]{2,1,0:T(8,128)(2,1)} %bitcast.54), calls=%async_computation.1 | async-start | bytes 2621440 | tf_op jit(solution)/shard_map/all_to_all | solution.py:73
  67.6 17.4 %collective-permute-start.3 = (bf16[3,128,896]{2,1,0:T(8,128)(2,1)}, bf16[3,128,896]{2,1,0:T(8,128)(2,1)}, u32[]{:S(2)}, u32[]{:S(2)}) collective-permute-start(bf16[3,128,896]{2,1,0:T(8,128)(2,1)} %collective-permute-done.2), channel_id=1, source_target_pairs={{0,8},{8,16},{16,24},{24,32},{32,40},{40,48},{48,56},{56,64},{64,7... | collective-permute-start | bytes 2064392 | tf_op jit(solution)/shard_map/ppermute | solution.py:60
  69.6 18.3 %collective-permute-start.11 = (bf16[3,128,896]{2,1,0:T(8,128)(2,1)}, bf16[3,128,896]{2,1,0:T(8,128)(2,1)}, u32[]{:S(2)}, u32[]{:S(2)}) collective-permute-start(bf16[3,128,896]{2,1,0:T(8,128)(2,1)} %collective-permute-done.10), channel_id=1, source_target_pairs={{0,120},{8,0},{16,8},{24,16},{32,24},{40,32},{48,40},{56,48},{64,5... | collective-permute-start | bytes 2064392 | tf_op jit(solution)/shard_map/ppermute | solution.py:61
  77.9 28.4 %all-to-all-start = ((bf16[4,80,2048]{2,1,0:T(8,128)(2,1)}), bf16[4,80,2048]{2,1,0:T(8,128)(2,1)S(1)}, u32[]{:S(2)}, u32[]{:S(2)}) async-start(bf16[4,80,2048]{2,1,0:T(8,128)(2,1)} %bitcast.3), calls=%async_computation | async-start | bytes 2621440 | tf_op jit(solution)/shard_map/all_to_all | solution.py:72
  85.1 16.6 %collective-permute-start.4 = (bf16[3,128,896]{2,1,0:T(8,128)(2,1)}, bf16[3,128,896]{2,1,0:T(8,128)(2,1)}, u32[]{:S(2)}, u32[]{:S(2)}) collective-permute-start(bf16[3,128,896]{2,1,0:T(8,128)(2,1)} %collective-permute-done.3), channel_id=1, source_target_pairs={{0,8},{8,16},{16,24},{24,32},{32,40},{40,48},{48,56},{56,64},{64,7... | collective-permute-start | bytes 2064392 | tf_op jit(solution)/shard_map/ppermute | solution.py:60
  87.8 21.7 %collective-permute-start.12 = (bf16[3,128,896]{2,1,0:T(8,128)(2,1)}, bf16[3,128,896]{2,1,0:T(8,128)(2,1)}, u32[]{:S(2)}, u32[]{:S(2)}) collective-permute-start(bf16[3,128,896]{2,1,0:T(8,128)(2,1)} %collective-permute-done.11), channel_id=1, source_target_pairs={{0,120},{8,0},{16,8},{24,16},{32,24},{40,32},{48,40},{56,48},{64,5... | collective-permute-start | bytes 2064392 | tf_op jit(solution)/shard_map/ppermute | solution.py:61
  101.6 16.4 %collective-permute-start.5 = (bf16[3,128,896]{2,1,0:T(8,128)(2,1)}, bf16[3,128,896]{2,1,0:T(8,128)(2,1)}, u32[]{:S(2)}, u32[]{:S(2)}) collective-permute-start(bf16[3,128,896]{2,1,0:T(8,128)(2,1)} %collective-permute-done.4), channel_id=1, source_target_pairs={{0,8},{8,16},{16,24},{24,32},{32,40},{40,48},{48,56},{56,64},{64,7... | collective-permute-start | bytes 2064392 | tf_op jit(solution)/shard_map/ppermute | solution.py:60
  109.5 6.5 %copy-start.9 = (bf16[2048,896]{1,0:T(8,128)(2,1)S(1)}, bf16[2048,896]{1,0:T(8,128)(2,1)}, u32[]{:S(2)}) copy-start(bf16[2048,896]{1,0:T(8,128)(2,1)} %get-tuple-element.45) | copy-start | bytes 11010052
  109.5 15.0 %collective-permute-start.13 = (bf16[3,128,896]{2,1,0:T(8,128)(2,1)}, bf16[3,128,896]{2,1,0:T(8,128)(2,1)S(1)}, u32[]{:S(2)}, u32[]{:S(2)}) collective-permute-start(bf16[3,128,896]{2,1,0:T(8,128)(2,1)} %collective-permute-done.12), channel_id=1, source_target_pairs={{0,120},{8,0},{16,8},{24,16},{32,24},{40,32},{48,40},{56,48},{64,5... | collective-permute-start | bytes 2064392 | tf_op jit(solution)/shard_map/ppermute | solution.py:61
  118.0 15.7 %collective-permute-start.6 = (bf16[3,128,896]{2,1,0:T(8,128)(2,1)}, bf16[3,128,896]{2,1,0:T(8,128)(2,1)S(1)}, u32[]{:S(2)}, u32[]{:S(2)}) collective-permute-start(bf16[3,128,896]{2,1,0:T(8,128)(2,1)} %collective-permute-done.5), channel_id=1, source_target_pairs={{0,8},{8,16},{16,24},{24,32},{32,40},{40,48},{48,56},{56,64},{64,7... | collective-permute-start | bytes 2064392 | tf_op jit(solution)/shard_map/ppermute | solution.py:60
  124.5 14.2 %collective-permute-start.14 = (bf16[3,128,896]{2,1,0:T(8,128)(2,1)S(1)}, bf16[3,128,896]{2,1,0:T(8,128)(2,1)S(1)}, u32[]{:S(2)}, u32[]{:S(2)}) collective-permute-start(bf16[3,128,896]{2,1,0:T(8,128)(2,1)S(1)} %collective-permute-done.13), channel_id=1, source_target_pairs={{0,120},{8,0},{16,8},{24,16},{32,24},{40,32},{48,40},{56,48},{64,5... | collective-permute-start | bytes 2064392 | tf_op jit(solution)/shard_map/ppermute | solution.py:61
  133.7 11.3 %collective-permute-start.7 = (bf16[3,64,896]{2,1,0:T(8,128)(2,1)S(1)}, bf16[3,64,896]{2,1,0:T(8,128)(2,1)S(1)}, u32[]{:S(2)}, u32[]{:S(2)}) collective-permute-start(bf16[3,64,896]{2,1,0:T(8,128)(2,1)S(1)} %slice.218), channel_id=1, source_target_pairs={{0,8},{8,16},{16,24},{24,32},{32,40},{40,48},{48,56},{56,64},{64,7... | collective-permute-start | bytes 1032200 | tf_op jit(solution)/shard_map/ppermute | solution.py:65
  138.7 9.9 %collective-permute-start.15 = (bf16[3,64,896]{2,1,0:T(8,128)(2,1)S(1)}, bf16[3,64,896]{2,1,0:T(8,128)(2,1)S(1)}, u32[]{:S(2)}, u32[]{:S(2)}) collective-permute-start(bf16[3,64,896]{2,1,0:T(8,128)(2,1)S(1)} %slice.219), channel_id=1, source_target_pairs={{0,120},{8,0},{16,8},{24,16},{32,24},{40,32},{48,40},{56,48},{64,5... | collective-permute-start | bytes 1032200 | tf_op jit(solution)/shard_map/ppermute | solution.py:66
  149.5 7.7 %copy-start.7 = (bf16[3,128,896]{2,1,0:T(8,128)(2,1)S(1)}, bf16[3,128,896]{2,1,0:T(8,128)(2,1)}, u32[]{:S(2)}) copy-start(bf16[3,128,896]{2,1,0:T(8,128)(2,1)} %copy-done.6) | copy-start | bytes 2064388
  150.3 7.7 %copy-start.5 = (bf16[3,128,896]{2,1,0:T(8,128)(2,1)S(1)}, bf16[3,128,896]{2,1,0:T(8,128)(2,1)}, u32[]{:S(2)}) copy-start(bf16[3,128,896]{2,1,0:T(8,128)(2,1)} %copy-done.4) | copy-start | bytes 2064388
  162.4 2.0 copy-start.10
  187.8 58.5 %copy-start.1 = (bf16[128,2048]{1,0:T(8,128)(2,1)S(1)}, bf16[128,2048]{1,0:T(8,128)(2,1)}, u32[]{:S(2)}) copy-start(bf16[128,2048]{1,0:T(8,128)(2,1)} %param.10) | copy-start | bytes 1572868

commit v11 on v3

--- a/solution.py
+++ b/solution.py
@@ -95,9 +95,12 @@
     results = jnp.take(
         results.reshape(row_total, 2, member_count, block_width), origin, axis=2
     ).reshape(row_total, 2, model_width)
-    summed = lax.psum_scatter(results, "tp", scatter_dimension=2, tiled=True)
-    rounded = summed.reshape(plane_count, CAP, 2, -1)
-    returned = lax.all_to_all(rounded, "ey", split_axis=0, concat_axis=0, tiled=True)
+    tp_count = lax.axis_size("tp")
+    pieces = results.reshape(plane_count, CAP, 2, tp_count, model_width // tp_count)
+    pieces = jnp.transpose(pieces, (0, 3, 1, 2, 4)).reshape(plane_count * tp_count, CAP, 2, -1)
+    pieces = lax.all_to_all(pieces, ("ey", "tp"), split_axis=0, concat_axis=0, tiled=True)
+    pieces = pieces.reshape(plane_count, tp_count, CAP, 2, -1).astype(jnp.float32)
+    returned = jnp.sum(pieces, axis=1).astype(jnp.bfloat16)
     returned = returned.reshape(slot_count, 2, -1).astype(jnp.float32)
     picker_full = picker.astype(jnp.float32)
     weighted = picker_full * slot_weight[:, None]

time: 254 us -> 239 us (0.941); the launches traced: 249 us -> 238 us
  waiting for transfers between devices: 91.1 us -> 47.3 us
  blocking collectives: 8.69 us -> 48.4 us
  between operations: 14.5 us -> 1.13 us
  local copies, waits for them, and re-layouts: 37 us -> 45.3 us
  other arithmetic: 9.77 us -> 6.61 us
    reduce_scatter x1 -> x0, waiting for transfers between devices: 45.4 us -> none  [per_device(): summed = lax.psum_scatter(results, 'tp', scatter_dimension=2, tiled=True)]
    all_to_all x1, blocking collectives: 8.69 us -> 48.4 us  [per_device(): lax.all_to_all(pieces, ('ey', 'tp'), split_axis=0, concat_axis=0, tiled=T...]
    gather x1 -> x3, local copies, waits for them, and re-layouts: 2.43 us -> 11 us  [per_device(): jnp.take(results.reshape(row_total, 2, member_count, block_width), origin...]
    select_n x3 -> x1, other arithmetic: 3.82 us -> 0.01 us  [per_device(): jnp.take(results.reshape(row_total, 2, member_count, block_width), origin...]
    unnamed x43 -> x45, local copies, waits for them, and re-layouts: 27.8 us -> 27.5 us
  transfers between devices with their start and end apart: 19 -> 18, of which waited for: 13 -> 10; matrix products, arithmetic and copies ran while one was open for 11% -> 12% of each run, Pallas kernels for 0% -> 0%
where the time goes in v11:
time: 239 us; the launch traced here: 238 us
  starting transfers between devices  70.2 us (29%)
  blocking collectives  48.4 us (20%)
  waiting for transfers between devices  47.3 us (20%)
  local copies, waits for them, and re-layouts  45.3 us (19%)
  matrix products  18.6 us (8%)
  other arithmetic  6.61 us (3%)
    all_to_all x1, blocking collectives, per_device(): lax.all_to_all(pieces, ('ey', 'tp'), split_axis=0, concat_axis=0, tiled=T...  48.4 us
    ppermute x7, starting transfers between devices, per_device(): ccw = lax.ppermute(ccw, 'ez', backward)  39.1 us
    ppermute x7, waiting for transfers between devices, per_device(): cw = lax.ppermute(cw, 'ez', forward)  38.3 us
    unnamed x45, local copies, waits for them, and re-layouts  27.5 us
    ppermute x7, starting transfers between devices, per_device(): cw = lax.ppermute(cw, 'ez', forward)  15.8 us
    gather x3, local copies, waits for them, and re-layouts, per_device(): jnp.take(results.reshape(row_total, 2, member_count, block_width), origin...  11 us
    ppermute x1, starting transfers between devices, per_device(): far_high = lax.ppermute(ccw[:, cut:], 'ez', backward)  5.5 us
  transfers between devices with their start and end apart: 18, of which 10 were waited for; matrix products, arithmetic and copies ran while one was open for 12% of the time, Pallas kernels for 0%

profile of v11, /device:TPU:1, one launch (start us, length us, event | category | flops | bytes accessed | tf_op | source)
XLA Modules:
  0.0 237.6 jit_solution(15508846312009713325)
XLA Ops:
  3.0 4.4 %collective-permute-start = (bf16[3,128,896]{2,1,0:T(8,128)(2,1)S(1)}, bf16[3,128,896]{2,1,0:T(8,128)(2,1)}, u32[]{:S(2)}, u32[]{:S(2)}) collective-permute-start(bf16[3,128,896]{2,1,0:T(8,128)(2,1)S(1)} %pad_maximum_fusion.1), channel_id=1, source_target_pairs={{0,8},{8,16},{16,24},{24,32},{32,40},{40,48},{48,56},{56,64},{64,7... | collective-permute-start | bytes 2064392 | tf_op jit(solution)/shard_map/ppermute | solution.py:60
  7.4 9.5 %collective-permute-start.8 = (bf16[3,128,896]{2,1,0:T(8,128)(2,1)S(1)}, bf16[3,128,896]{2,1,0:T(8,128)(2,1)S(1)}, u32[]{:S(2)}, u32[]{:S(2)}) collective-permute-start(bf16[3,128,896]{2,1,0:T(8,128)(2,1)S(1)} %pad_maximum_fusion.1), channel_id=1, source_target_pairs={{0,120},{8,0},{16,8},{24,16},{32,24},{40,32},{48,40},{56,48},{64,5... | collective-permute-start | bytes 2064392 | tf_op jit(solution)/shard_map/ppermute | solution.py:61
  17.8 12.4 %collective-permute-done = bf16[3,128,896]{2,1,0:T(8,128)(2,1)} collective-permute-done((bf16[3,128,896]{2,1,0:T(8,128)(2,1)S(1)}, bf16[3,128,896]{2,1,0:T(8,128)(2,1)}, u32[]{:S(2)}, u32[]{:S(2)}) %collective-permute-start) | collective-permute-done | bytes 688160 | tf_op jit(solution)/shard_map/ppermute | solution.py:60
  30.2 1.9 collective-permute-start.1
  33.8 4.6 %collective-permute-start.9 = (bf16[3,128,896]{2,1,0:T(8,128)(2,1)S(1)}, bf16[3,128,896]{2,1,0:T(8,128)(2,1)S(1)}, u32[]{:S(2)}, u32[]{:S(2)}) collective-permute-start(bf16[3,128,896]{2,1,0:T(8,128)(2,1)S(1)} %collective-permute-done.8), channel_id=1, source_target_pairs={{0,120},{8,0},{16,8},{24,16},{32,24},{40,32},{48,40},{56,48},{64,5... | collective-permute-start | bytes 2064392 | tf_op jit(solution)/shard_map/ppermute | solution.py:61
  40.2 9.1 %collective-permute-done.1 = bf16[3,128,896]{2,1,0:T(8,128)(2,1)} collective-permute-done((bf16[3,128,896]{2,1,0:T(8,128)(2,1)}, bf16[3,128,896]{2,1,0:T(8,128)(2,1)}, u32[]{:S(2)}, u32[]{:S(2)}) %collective-permute-start.1) | collective-permute-done | bytes 688160 | tf_op jit(solution)/shard_map/ppermute | solution.py:60
  49.3 1.9 collective-permute-start.2
  51.6 5.3 %collective-permute-start.10 = (bf16[3,128,896]{2,1,0:T(8,128)(2,1)S(1)}, bf16[3,128,896]{2,1,0:T(8,128)(2,1)}, u32[]{:S(2)}, u32[]{:S(2)}) collective-permute-start(bf16[3,128,896]{2,1,0:T(8,128)(2,1)S(1)} %collective-permute-done.9), channel_id=1, source_target_pairs={{0,120},{8,0},{16,8},{24,16},{32,24},{40,32},{48,40},{56,48},{64,5... | collective-permute-start | bytes 2064392 | tf_op jit(solution)/shard_map/ppermute | solution.py:61
  56.9 1.6 fusion.1
  58.5 4.3 %all-to-all-start.1 = ((bf16[4,80,2048]{2,1,0:T(8,128)(2,1)}), bf16[4,80,2048]{2,1,0:T(8,128)(2,1)S(1)}, u32[]{:S(2)}, u32[]{:S(2)}) async-start(bf16[4,80,2048]{2,1,0:T(8,128)(2,1)} %bitcast.54), calls=%async_computation.1 | async-start | bytes 2621440 | tf_op jit(solution)/shard_map/all_to_all | solution.py:73
  62.8 4.8 %collective-permute-done.2 = bf16[3,128,896]{2,1,0:T(8,128)(2,1)} collective-permute-done((bf16[3,128,896]{2,1,0:T(8,128)(2,1)}, bf16[3,128,896]{2,1,0:T(8,128)(2,1)}, u32[]{:S(2)}, u32[]{:S(2)}) %collective-permute-start.2) | collective-permute-done | bytes 688160 | tf_op jit(solution)/shard_map/ppermute | solution.py:60
  67.6 1.9 collective-permute-start.3
  69.6 5.1 %collective-permute-start.11 = (bf16[3,128,896]{2,1,0:T(8,128)(2,1)}, bf16[3,128,896]{2,1,0:T(8,128)(2,1)}, u32[]{:S(2)}, u32[]{:S(2)}) collective-permute-start(bf16[3,128,896]{2,1,0:T(8,128)(2,1)} %collective-permute-done.10), channel_id=1, source_target_pairs={{0,120},{8,0},{16,8},{24,16},{32,24},{40,32},{48,40},{56,48},{64,5... | collective-permute-start | bytes 2064392 | tf_op jit(solution)/shard_map/ppermute | solution.py:61
  74.7 1.6 convolution_convert_fusion
  76.3 1.6 all-to-all-done.1
  77.9 3.5 %all-to-all-start = ((bf16[4,80,2048]{2,1,0:T(8,128)(2,1)}), bf16[4,80,2048]{2,1,0:T(8,128)(2,1)S(1)}, u32[]{:S(2)}, u32[]{:S(2)}) async-start(bf16[4,80,2048]{2,1,0:T(8,128)(2,1)} %bitcast.3), calls=%async_computation | async-start | bytes 2621440 | tf_op jit(solution)/shard_map/all_to_all | solution.py:72
  81.5 3.6 %collective-permute-done.3 = bf16[3,128,896]{2,1,0:T(8,128)(2,1)} collective-permute-done((bf16[3,128,896]{2,1,0:T(8,128)(2,1)}, bf16[3,128,896]{2,1,0:T(8,128)(2,1)}, u32[]{:S(2)}, u32[]{:S(2)}) %collective-permute-start.3) | collective-permute-done | bytes 688160 | tf_op jit(solution)/shard_map/ppermute | solution.py:60
  85.1 1.9 collective-permute-start.4
  87.8 4.6 %collective-permute-start.12 = (bf16[3,128,896]{2,1,0:T(8,128)(2,1)}, bf16[3,128,896]{2,1,0:T(8,128)(2,1)}, u32[]{:S(2)}, u32[]{:S(2)}) collective-permute-start(bf16[3,128,896]{2,1,0:T(8,128)(2,1)} %collective-permute-done.11), channel_id=1, source_target_pairs={{0,120},{8,0},{16,8},{24,16},{32,24},{40,32},{48,40},{56,48},{64,5... | collective-permute-start | bytes 2064392 | tf_op jit(solution)/shard_map/ppermute | solution.py:61
  93.2 8.5 %collective-permute-done.4 = bf16[3,128,896]{2,1,0:T(8,128)(2,1)} collective-permute-done((bf16[3,128,896]{2,1,0:T(8,128)(2,1)}, bf16[3,128,896]{2,1,0:T(8,128)(2,1)}, u32[]{:S(2)}, u32[]{:S(2)}) %collective-permute-start.4) | collective-permute-done | bytes 688160 | tf_op jit(solution)/shard_map/ppermute | solution.py:60
  101.6 1.9 collective-permute-start.5
  103.6 2.0 fusion.61
  106.9 1.8 gather_fusion.2
  109.5 4.8 %collective-permute-start.13 = (bf16[3,128,896]{2,1,0:T(8,128)(2,1)}, bf16[3,128,896]{2,1,0:T(8,128)(2,1)S(1)}, u32[]{:S(2)}, u32[]{:S(2)}) collective-permute-start(bf16[3,128,896]{2,1,0:T(8,128)(2,1)} %collective-permute-done.12), channel_id=1, source_target_pairs={{0,120},{8,0},{16,8},{24,16},{32,24},{40,32},{48,40},{56,48},{64,5... | collective-permute-start | bytes 2064392 | tf_op jit(solution)/shard_map/ppermute | solution.py:61
  114.4 1.6 select_bitcast_fusion.2
  116.0 2.0 fusion.60
  118.0 1.9 collective-permute-start.6
  119.9 2.0 fusion.59
  122.0 2.5 %collective-permute-done.13 = bf16[3,128,896]{2,1,0:T(8,128)(2,1)S(1)} collective-permute-done((bf16[3,128,896]{2,1,0:T(8,128)(2,1)}, bf16[3,128,896]{2,1,0:T(8,128)(2,1)S(1)}, u32[]{:S(2)}, u32[]{:S(2)}) %collective-permute-start.13) | collective-permute-done | bytes 688160 | tf_op jit(solution)/shard_map/ppermute | solution.py:61
  124.5 5.2 %collective-permute-start.14 = (bf16[3,128,896]{2,1,0:T(8,128)(2,1)S(1)}, bf16[3,128,896]{2,1,0:T(8,128)(2,1)S(1)}, u32[]{:S(2)}, u32[]{:S(2)}) collective-permute-start(bf16[3,128,896]{2,1,0:T(8,128)(2,1)S(1)} %collective-permute-done.13), channel_id=1, source_target_pairs={{0,120},{8,0},{16,8},{24,16},{32,24},{40,32},{48,40},{56,48},{64,5... | collective-permute-start | bytes 2064392 | tf_op jit(solution)/shard_map/ppermute | solution.py:61
  129.7 2.0 fusion.58
  131.7 2.0 fusion.57
  133.7 1.9 collective-permute-start.7
  135.7 2.0 fusion.56
  138.7 5.5 %collective-permute-start.15 = (bf16[3,64,896]{2,1,0:T(8,128)(2,1)S(1)}, bf16[3,64,896]{2,1,0:T(8,128)(2,1)S(1)}, u32[]{:S(2)}, u32[]{:S(2)}) collective-permute-start(bf16[3,64,896]{2,1,0:T(8,128)(2,1)S(1)} %slice.219), channel_id=1, source_target_pairs={{0,120},{8,0},{16,8},{24,16},{32,24},{40,32},{48,40},{56,48},{64,5... | collective-permute-start | bytes 1032200 | tf_op jit(solution)/shard_map/ppermute | solution.py:66
  145.1 3.5 %collective-permute-done.15 = bf16[3,64,896]{2,1,0:T(8,128)(2,1)S(1)} collective-permute-done((bf16[3,64,896]{2,1,0:T(8,128)(2,1)S(1)}, bf16[3,64,896]{2,1,0:T(8,128)(2,1)S(1)}, u32[]{:S(2)}, u32[]{:S(2)}) %collective-permute-start.15) | collective-permute-done | bytes 344096 | tf_op jit(solution)/shard_map/ppermute | solution.py:66
  151.2 2.0 fusion.51
  153.2 2.0 fusion.50
  155.2 2.0 fusion.49
  158.9 3.6 %fusion.7 = f32[320,896]{1,0:T(8,128)S(1)} fusion(bf16[2048,896]{1,0:T(8,128)(2,1)} %get-tuple-element.5, bf16[16,40,8,128]{3,2,1,0:T(8,128)(2,1)S(1)} %get-tuple-element.48), kind=kOutput, calls=%fused_computation.17 | convolution fusion | flops 1174405120 | bytes 6127616 | tf_op jit(solution)/shard_map/dot_general | solution.py:82
  162.4 1.5 fusion.9
  164.5 1.6 fusion.3
  168.2 3.6 %fusion.14 = f32[320,2048]{1,0:T(8,128)S(1)} fusion(bf16[2048,896]{1,0:T(8,128)(2,1)} %get-tuple-element.5, f32[320,896]{1,0:T(8,128)S(1)} %fusion.4, f32[320,896]{1,0:T(8,128)S(1)} %fusion.9), kind=kOutput, calls=%fused_computation.33 | convolution fusion | flops 1176125440 | bytes 8585216 | tf_op jit(solution)/shard_map/dot_general | solution.py:91
  171.9 1.7 fusion.2
  174.5 2.4 %gather_fusion = bf16[16,320,2,128]{3,1,2,0:T(8,128)(2,1)} fusion(bf16[320,2,16,128]{3,0,2,1:T(8,128)(2,1)S(1)} %pad_maximum_fusion, s32[1024]{0:T(1024)S(1)} %get-tuple-element.52), kind=kCustom, calls=%fused_computation.2 | custom fusion | bytes 5242944 | tf_op jit(solution)/shard_map/jit(_take)/gather | solution.py:95
  176.9 5.0 %copy.111 = bf16[320,2,16,128]{3,2,1,0:T(8,128)(2,1)} copy(bf16[320,2,16,128]{3,0,1,2:T(8,128)(2,1)} %bitcast.267) | data formatting | bytes 5242880 | tf_op jit(solution)/shard_map/jit(_take)/gather | solution.py:95
  181.8 3.7 %gather.10 = bf16[4,80,2,8,256]{4,3,2,1,0:T(8,128)(2,1)S(1)} reshape(bf16[320,2,16,128]{3,2,1,0:T(8,128)(2,1)} %copy.111) | data formatting | bytes 5242880 | tf_op jit(solution)/shard_map/jit(_take)/gather | solution.py:95
  186.8 48.4 %all_to_all.15 = bf16[32,80,2,256]{3,1,2,0:T(8,128)(2,1)S(1)} all-to-all(bf16[32,80,2,256]{3,1,2,0:T(8,128)(2,1)S(1)} %bitcast.268), channel_id=1, replica_groups=mesh['ey'=4,'ez'=16,'tp'=8] {'ey','tp'}, dimensions={0} | all-to-all | bytes 5242880 | tf_op jit(solution)/shard_map/all_to_all | solution.py:101
  (86 shorter events, 24.2 us)
Async XLA Ops:
  0.6 56.3 %copy-start = (bf16[128,2048]{1,0:T(8,128)(2,1)S(1)}, bf16[128,2048]{1,0:T(8,128)(2,1)}, u32[]{:S(2)}) copy-start(bf16[128,2048]{1,0:T(8,128)(2,1)} %param.10) | copy-start | bytes 1572868
  0.6 74.1 %copy-start.8 = (bf16[128,2048]{1,0:T(8,128)(2,1)S(1)}, bf16[128,2048]{1,0:T(8,128)(2,1)}, u32[]{:S(2)}) copy-start(bf16[128,2048]{1,0:T(8,128)(2,1)} %param.9) | copy-start | bytes 1572868
  3.0 27.2 %collective-permute-start = (bf16[3,128,896]{2,1,0:T(8,128)(2,1)S(1)}, bf16[3,128,896]{2,1,0:T(8,128)(2,1)}, u32[]{:S(2)}, u32[]{:S(2)}) collective-permute-start(bf16[3,128,896]{2,1,0:T(8,128)(2,1)S(1)} %pad_maximum_fusion.1), channel_id=1, source_target_pairs={{0,8},{8,16},{16,24},{24,32},{32,40},{40,48},{48,56},{56,64},{64,7... | collective-permute-start | bytes 2064392 | tf_op jit(solution)/shard_map/ppermute | solution.py:60
  7.4 26.4 %collective-permute-start.8 = (bf16[3,128,896]{2,1,0:T(8,128)(2,1)S(1)}, bf16[3,128,896]{2,1,0:T(8,128)(2,1)S(1)}, u32[]{:S(2)}, u32[]{:S(2)}) collective-permute-start(bf16[3,128,896]{2,1,0:T(8,128)(2,1)S(1)} %pad_maximum_fusion.1), channel_id=1, source_target_pairs={{0,120},{8,0},{16,8},{24,16},{32,24},{40,32},{48,40},{56,48},{64,5... | collective-permute-start | bytes 2064392 | tf_op jit(solution)/shard_map/ppermute | solution.py:61
  30.2 19.2 %collective-permute-start.1 = (bf16[3,128,896]{2,1,0:T(8,128)(2,1)}, bf16[3,128,896]{2,1,0:T(8,128)(2,1)}, u32[]{:S(2)}, u32[]{:S(2)}) collective-permute-start(bf16[3,128,896]{2,1,0:T(8,128)(2,1)} %collective-permute-done), channel_id=1, source_target_pairs={{0,8},{8,16},{16,24},{24,32},{32,40},{40,48},{48,56},{56,64},{64,7... | collective-permute-start | bytes 2064392 | tf_op jit(solution)/shard_map/ppermute | solution.py:60
  33.8 24.7 %copy-start.4 = (bf16[3,128,896]{2,1,0:T(8,128)(2,1)}, bf16[3,128,896]{2,1,0:T(8,128)(2,1)S(1)}, u32[]{:S(2)}) copy-start(bf16[3,128,896]{2,1,0:T(8,128)(2,1)S(1)} %collective-permute-done.8) | copy-start | bytes 2064388
  33.8 17.8 %collective-permute-start.9 = (bf16[3,128,896]{2,1,0:T(8,128)(2,1)S(1)}, bf16[3,128,896]{2,1,0:T(8,128)(2,1)S(1)}, u32[]{:S(2)}, u32[]{:S(2)}) collective-permute-start(bf16[3,128,896]{2,1,0:T(8,128)(2,1)S(1)} %collective-permute-done.8), channel_id=1, source_target_pairs={{0,120},{8,0},{16,8},{24,16},{32,24},{40,32},{48,40},{56,48},{64,5... | collective-permute-start | bytes 2064392 | tf_op jit(solution)/shard_map/ppermute | solution.py:61
  49.3 18.3 %collective-permute-start.2 = (bf16[3,128,896]{2,1,0:T(8,128)(2,1)}, bf16[3,128,896]{2,1,0:T(8,128)(2,1)}, u32[]{:S(2)}, u32[]{:S(2)}) collective-permute-start(bf16[3,128,896]{2,1,0:T(8,128)(2,1)} %collective-permute-done.1), channel_id=1, source_target_pairs={{0,8},{8,16},{16,24},{24,32},{32,40},{40,48},{48,56},{56,64},{64,7... | collective-permute-start | bytes 2064392 | tf_op jit(solution)/shard_map/ppermute | solution.py:60
  51.6 26.3 %copy-start.6 = (bf16[3,128,896]{2,1,0:T(8,128)(2,1)}, bf16[3,128,896]{2,1,0:T(8,128)(2,1)S(1)}, u32[]{:S(2)}) copy-start(bf16[3,128,896]{2,1,0:T(8,128)(2,1)S(1)} %collective-permute-done.9) | copy-start | bytes 2064388
  51.6 18.0 %collective-permute-start.10 = (bf16[3,128,896]{2,1,0:T(8,128)(2,1)S(1)}, bf16[3,128,896]{2,1,0:T(8,128)(2,1)}, u32[]{:S(2)}, u32[]{:S(2)}) collective-permute-start(bf16[3,128,896]{2,1,0:T(8,128)(2,1)S(1)} %collective-permute-done.9), channel_id=1, source_target_pairs={{0,120},{8,0},{16,8},{24,16},{32,24},{40,32},{48,40},{56,48},{64,5... | collective-permute-start | bytes 2064392 | tf_op jit(solution)/shard_map/ppermute | solution.py:61
  58.5 28.5 %copy-start.2 = (bf16[128,896]{1,0:T(8,128)(2,1)S(1)}, bf16[128,896]{1,0:T(8,128)(2,1)}, u32[]{:S(2)}) copy-start(bf16[128,896]{1,0:T(8,128)(2,1)} %param.13) | copy-start | bytes 688132
  58.5 28.5 %copy-start.3 = (bf16[128,896]{1,0:T(8,128)(2,1)S(1)}, bf16[128,896]{1,0:T(8,128)(2,1)}, u32[]{:S(2)}) copy-start(bf16[128,896]{1,0:T(8,128)(2,1)} %param.14) | copy-start | bytes 688132
  58.5 19.4 %all-to-all-start.1 = ((bf16[4,80,2048]{2,1,0:T(8,128)(2,1)}), bf16[4,80,2048]{2,1,0:T(8,128)(2,1)S(1)}, u32[]{:S(2)}, u32[]{:S(2)}) async-start(bf16[4,80,2048]{2,1,0:T(8,128)(2,1)} %bitcast.54), calls=%async_computation.1 | async-start | bytes 2621440 | tf_op jit(solution)/shard_map/all_to_all | solution.py:73
  67.6 17.4 %collective-permute-start.3 = (bf16[3,128,896]{2,1,0:T(8,128)(2,1)}, bf16[3,128,896]{2,1,0:T(8,128)(2,1)}, u32[]{:S(2)}, u32[]{:S(2)}) collective-permute-start(bf16[3,128,896]{2,1,0:T(8,128)(2,1)} %collective-permute-done.2), channel_id=1, source_target_pairs={{0,8},{8,16},{16,24},{24,32},{32,40},{40,48},{48,56},{56,64},{64,7... | collective-permute-start | bytes 2064392 | tf_op jit(solution)/shard_map/ppermute | solution.py:60
  69.6 18.3 %collective-permute-start.11 = (bf16[3,128,896]{2,1,0:T(8,128)(2,1)}, bf16[3,128,896]{2,1,0:T(8,128)(2,1)}, u32[]{:S(2)}, u32[]{:S(2)}) collective-permute-start(bf16[3,128,896]{2,1,0:T(8,128)(2,1)} %collective-permute-done.10), channel_id=1, source_target_pairs={{0,120},{8,0},{16,8},{24,16},{32,24},{40,32},{48,40},{56,48},{64,5... | collective-permute-start | bytes 2064392 | tf_op jit(solution)/shard_map/ppermute | solution.py:61
  77.9 28.4 %all-to-all-start = ((bf16[4,80,2048]{2,1,0:T(8,128)(2,1)}), bf16[4,80,2048]{2,1,0:T(8,128)(2,1)S(1)}, u32[]{:S(2)}, u32[]{:S(2)}) async-start(bf16[4,80,2048]{2,1,0:T(8,128)(2,1)} %bitcast.3), calls=%async_computation | async-start | bytes 2621440 | tf_op jit(solution)/shard_map/all_to_all | solution.py:72
  85.1 16.6 %collective-permute-start.4 = (bf16[3,128,896]{2,1,0:T(8,128)(2,1)}, bf16[3,128,896]{2,1,0:T(8,128)(2,1)}, u32[]{:S(2)}, u32[]{:S(2)}) collective-permute-start(bf16[3,128,896]{2,1,0:T(8,128)(2,1)} %collective-permute-done.3), channel_id=1, source_target_pairs={{0,8},{8,16},{16,24},{24,32},{32,40},{40,48},{48,56},{56,64},{64,7... | collective-permute-start | bytes 2064392 | tf_op jit(solution)/shard_map/ppermute | solution.py:60
  87.8 21.7 %collective-permute-start.12 = (bf16[3,128,896]{2,1,0:T(8,128)(2,1)}, bf16[3,128,896]{2,1,0:T(8,128)(2,1)}, u32[]{:S(2)}, u32[]{:S(2)}) collective-permute-start(bf16[3,128,896]{2,1,0:T(8,128)(2,1)} %collective-permute-done.11), channel_id=1, source_target_pairs={{0,120},{8,0},{16,8},{24,16},{32,24},{40,32},{48,40},{56,48},{64,5... | collective-permute-start | bytes 2064392 | tf_op jit(solution)/shard_map/ppermute | solution.py:61
  101.6 16.4 %collective-permute-start.5 = (bf16[3,128,896]{2,1,0:T(8,128)(2,1)}, bf16[3,128,896]{2,1,0:T(8,128)(2,1)}, u32[]{:S(2)}, u32[]{:S(2)}) collective-permute-start(bf16[3,128,896]{2,1,0:T(8,128)(2,1)} %collective-permute-done.4), channel_id=1, source_target_pairs={{0,8},{8,16},{16,24},{24,32},{32,40},{40,48},{48,56},{56,64},{64,7... | collective-permute-start | bytes 2064392 | tf_op jit(solution)/shard_map/ppermute | solution.py:60
  109.5 6.5 %copy-start.9 = (bf16[2048,896]{1,0:T(8,128)(2,1)S(1)}, bf16[2048,896]{1,0:T(8,128)(2,1)}, u32[]{:S(2)}) copy-start(bf16[2048,896]{1,0:T(8,128)(2,1)} %get-tuple-element.45) | copy-start | bytes 11010052
  109.5 15.0 %collective-permute-start.13 = (bf16[3,128,896]{2,1,0:T(8,128)(2,1)}, bf16[3,128,896]{2,1,0:T(8,128)(2,1)S(1)}, u32[]{:S(2)}, u32[]{:S(2)}) collective-permute-start(bf16[3,128,896]{2,1,0:T(8,128)(2,1)} %collective-permute-done.12), channel_id=1, source_target_pairs={{0,120},{8,0},{16,8},{24,16},{32,24},{40,32},{48,40},{56,48},{64,5... | collective-permute-start | bytes 2064392 | tf_op jit(solution)/shard_map/ppermute | solution.py:61
  118.0 15.7 %collective-permute-start.6 = (bf16[3,128,896]{2,1,0:T(8,128)(2,1)}, bf16[3,128,896]{2,1,0:T(8,128)(2,1)S(1)}, u32[]{:S(2)}, u32[]{:S(2)}) collective-permute-start(bf16[3,128,896]{2,1,0:T(8,128)(2,1)} %collective-permute-done.5), channel_id=1, source_target_pairs={{0,8},{8,16},{16,24},{24,32},{32,40},{40,48},{48,56},{56,64},{64,7... | collective-permute-start | bytes 2064392 | tf_op jit(solution)/shard_map/ppermute | solution.py:60
  124.5 14.2 %collective-permute-start.14 = (bf16[3,128,896]{2,1,0:T(8,128)(2,1)S(1)}, bf16[3,128,896]{2,1,0:T(8,128)(2,1)S(1)}, u32[]{:S(2)}, u32[]{:S(2)}) collective-permute-start(bf16[3,128,896]{2,1,0:T(8,128)(2,1)S(1)} %collective-permute-done.13), channel_id=1, source_target_pairs={{0,120},{8,0},{16,8},{24,16},{32,24},{40,32},{48,40},{56,48},{64,5... | collective-permute-start | bytes 2064392 | tf_op jit(solution)/shard_map/ppermute | solution.py:61
  133.7 11.3 %collective-permute-start.7 = (bf16[3,64,896]{2,1,0:T(8,128)(2,1)S(1)}, bf16[3,64,896]{2,1,0:T(8,128)(2,1)S(1)}, u32[]{:S(2)}, u32[]{:S(2)}) collective-permute-start(bf16[3,64,896]{2,1,0:T(8,128)(2,1)S(1)} %slice.218), channel_id=1, source_target_pairs={{0,8},{8,16},{16,24},{24,32},{32,40},{40,48},{48,56},{56,64},{64,7... | collective-permute-start | bytes 1032200 | tf_op jit(solution)/shard_map/ppermute | solution.py:65
  138.7 9.9 %collective-permute-start.15 = (bf16[3,64,896]{2,1,0:T(8,128)(2,1)S(1)}, bf16[3,64,896]{2,1,0:T(8,128)(2,1)S(1)}, u32[]{:S(2)}, u32[]{:S(2)}) collective-permute-start(bf16[3,64,896]{2,1,0:T(8,128)(2,1)S(1)} %slice.219), channel_id=1, source_target_pairs={{0,120},{8,0},{16,8},{24,16},{32,24},{40,32},{48,40},{56,48},{64,5... | collective-permute-start | bytes 1032200 | tf_op jit(solution)/shard_map/ppermute | solution.py:66
  149.5 7.7 %copy-start.7 = (bf16[3,128,896]{2,1,0:T(8,128)(2,1)S(1)}, bf16[3,128,896]{2,1,0:T(8,128)(2,1)}, u32[]{:S(2)}) copy-start(bf16[3,128,896]{2,1,0:T(8,128)(2,1)} %copy-done.6) | copy-start | bytes 2064388
  150.3 7.7 %copy-start.5 = (bf16[3,128,896]{2,1,0:T(8,128)(2,1)S(1)}, bf16[3,128,896]{2,1,0:T(8,128)(2,1)}, u32[]{:S(2)}) copy-start(bf16[3,128,896]{2,1,0:T(8,128)(2,1)} %copy-done.4) | copy-start | bytes 2064388
  162.4 2.0 copy-start.10
  186.8 50.8 %copy-start.1 = (bf16[128,2048]{1,0:T(8,128)(2,1)S(1)}, bf16[128,2048]{1,0:T(8,128)(2,1)}, u32[]{:S(2)}) copy-start(bf16[128,2048]{1,0:T(8,128)(2,1)} %param.10) | copy-start | bytes 1572868

commit v12 on v11

--- a/solution.py
+++ b/solution.py
@@ -69,8 +69,10 @@
     gate_full = jnp.concatenate([chunk[0] for chunk in by_distance], axis=0)
     up_full = jnp.concatenate([chunk[1] for chunk in by_distance], axis=0)
     down_full = jnp.concatenate([chunk[2] for chunk in by_distance], axis=0)
-    member_tokens = lax.all_to_all(sent_tokens, "ey", split_axis=0, concat_axis=0, tiled=True)
-    member_cot = lax.all_to_all(sent_cot, "ey", split_axis=0, concat_axis=0, tiled=True)
+    member_both = lax.all_to_all(
+        jnp.stack([sent_tokens, sent_cot], axis=1), "ey", split_axis=0, concat_axis=0, tiled=True
+    )
+    member_tokens, member_cot = member_both[:, 0], member_both[:, 1]
     row_total = plane_count * CAP
     member_tokens = jnp.take(
         member_tokens.reshape(row_total, member_count, block_width), origin, axis=1

time: 239 us -> 234 us (0.979)
  starting transfers between devices: 70.2 us -> 63.7 us
  matrix products: 18.6 us -> 15.4 us
    ppermute x7, waiting for transfers between devices: 38.3 us -> 46.2 us  [per_device(): cw = lax.ppermute(cw, 'ez', forward)]
    ppermute x7, waiting for transfers between devices: 3.85 us -> 0.02 us  [per_device(): ccw = lax.ppermute(ccw, 'ez', backward)]
    all_to_all x2 -> x1, starting transfers between devices: 7.86 us -> 4.33 us  [per_device(): lax.all_to_all(jnp.stack([sent_tokens, sent_cot], axis=1), 'ey', split_ax...]
    unnamed x45 -> x51, local copies, waits for them, and re-layouts: 27.5 us -> 28 us
  transfers between devices with their start and end apart: 18 -> 17, of which waited for: 10 -> 8; matrix products, arithmetic and copies ran while one was open for 12% -> 12% of each run, Pallas kernels for 0% -> 0%
where the time goes in v12:
time: 234 us; the launch traced here: 233 us
  starting transfers between devices  63.7 us (27%)
  waiting for transfers between devices  49.4 us (21%)
  blocking collectives  48.5 us (21%)
  local copies, waits for them, and re-layouts  46.1 us (20%)
  matrix products  15.4 us (7%)
  other arithmetic  8.59 us (4%)
    all_to_all x1, blocking collectives, per_device(): lax.all_to_all(pieces, ('ey', 'tp'), split_axis=0, concat_axis=0, tiled=T...  48.5 us
    ppermute x7, waiting for transfers between devices, per_device(): cw = lax.ppermute(cw, 'ez', forward)  46.2 us
    ppermute x7, starting transfers between devices, per_device(): ccw = lax.ppermute(ccw, 'ez', backward)  36.9 us
    unnamed x51, local copies, waits for them, and re-layouts  28 us
    ppermute x7, starting transfers between devices, per_device(): cw = lax.ppermute(cw, 'ez', forward)  15.8 us
    gather x3, local copies, waits for them, and re-layouts, per_device(): jnp.take(results.reshape(row_total, 2, member_count, block_width), origin...  11 us
    ppermute x1, starting transfers between devices, per_device(): far_high = lax.ppermute(ccw[:, cut:], 'ez', backward)  4.75 us
  transfers between devices with their start and end apart: 17, of which 8 were waited for; matrix products, arithmetic and copies ran while one was open for 12% of the time, Pallas kernels for 0%

profile of v12, /device:TPU:1, one launch (start us, length us, event | category | flops | bytes accessed | tf_op | source)
XLA Modules:
  0.0 233.0 jit_solution(13058575962744715761)
XLA Ops:
  2.9 4.4 %collective-permute-start = (bf16[3,128,896]{2,1,0:T(8,128)(2,1)S(1)}, bf16[3,128,896]{2,1,0:T(8,128)(2,1)S(1)}, u32[]{:S(2)}, u32[]{:S(2)}) collective-permute-start(bf16[3,128,896]{2,1,0:T(8,128)(2,1)S(1)} %pad_maximum_fusion.2), channel_id=1, source_target_pairs={{0,8},{8,16},{16,24},{24,32},{32,40},{40,48},{48,56},{56,64},{64,7... | collective-permute-start | bytes 2064392 | tf_op jit(solution)/shard_map/ppermute | solution.py:60
  7.3 9.5 %collective-permute-start.8 = (bf16[3,128,896]{2,1,0:T(8,128)(2,1)S(1)}, bf16[3,128,896]{2,1,0:T(8,128)(2,1)S(1)}, u32[]{:S(2)}, u32[]{:S(2)}) collective-permute-start(bf16[3,128,896]{2,1,0:T(8,128)(2,1)S(1)} %pad_maximum_fusion.2), channel_id=1, source_target_pairs={{0,120},{8,0},{16,8},{24,16},{32,24},{40,32},{48,40},{56,48},{64,5... | collective-permute-start | bytes 2064392 | tf_op jit(solution)/shard_map/ppermute | solution.py:61
  20.5 9.6 %collective-permute-done = bf16[3,128,896]{2,1,0:T(8,128)(2,1)S(1)} collective-permute-done((bf16[3,128,896]{2,1,0:T(8,128)(2,1)S(1)}, bf16[3,128,896]{2,1,0:T(8,128)(2,1)S(1)}, u32[]{:S(2)}, u32[]{:S(2)}) %collective-permute-start) | collective-permute-done | bytes 688160 | tf_op jit(solution)/shard_map/ppermute | solution.py:60
  30.0 1.9 collective-permute-start.1
  32.0 4.6 %collective-permute-start.9 = (bf16[3,128,896]{2,1,0:T(8,128)(2,1)S(1)}, bf16[3,128,896]{2,1,0:T(8,128)(2,1)}, u32[]{:S(2)}, u32[]{:S(2)}) collective-permute-start(bf16[3,128,896]{2,1,0:T(8,128)(2,1)S(1)} %collective-permute-done.8), channel_id=1, source_target_pairs={{0,120},{8,0},{16,8},{24,16},{32,24},{40,32},{48,40},{56,48},{64,5... | collective-permute-start | bytes 2064392 | tf_op jit(solution)/shard_map/ppermute | solution.py:61
  37.9 1.5 fusion.1
  39.5 9.5 %collective-permute-done.1 = bf16[3,128,896]{2,1,0:T(8,128)(2,1)} collective-permute-done((bf16[3,128,896]{2,1,0:T(8,128)(2,1)S(1)}, bf16[3,128,896]{2,1,0:T(8,128)(2,1)}, u32[]{:S(2)}, u32[]{:S(2)}) %collective-permute-start.1) | collective-permute-done | bytes 688160 | tf_op jit(solution)/shard_map/ppermute | solution.py:60
  49.0 1.9 collective-permute-start.2
  50.9 4.6 %collective-permute-start.10 = (bf16[3,128,896]{2,1,0:T(8,128)(2,1)}, bf16[3,128,896]{2,1,0:T(8,128)(2,1)}, u32[]{:S(2)}, u32[]{:S(2)}) collective-permute-start(bf16[3,128,896]{2,1,0:T(8,128)(2,1)} %collective-permute-done.9), channel_id=1, source_target_pairs={{0,120},{8,0},{16,8},{24,16},{32,24},{40,32},{48,40},{56,48},{64,5... | collective-permute-start | bytes 2064392 | tf_op jit(solution)/shard_map/ppermute | solution.py:61
  55.5 1.8 pad_maximum_fusion
  57.3 4.3 %all-to-all-start = ((bf16[4,2,80,2048]{3,2,1,0:T(8,128)(2,1)}), bf16[4,2,80,2048]{3,2,1,0:T(8,128)(2,1)S(1)}, u32[]{:S(2)}, u32[]{:S(2)}) async-start(bf16[4,2,80,2048]{3,2,1,0:T(8,128)(2,1)} %pad_maximum_fusion), calls=%async_computation | async-start | bytes 5242880 | tf_op jit(solution)/shard_map/all_to_all | solution.py:72
  61.7 5.6 %collective-permute-done.2 = bf16[3,128,896]{2,1,0:T(8,128)(2,1)} collective-permute-done((bf16[3,128,896]{2,1,0:T(8,128)(2,1)}, bf16[3,128,896]{2,1,0:T(8,128)(2,1)}, u32[]{:S(2)}, u32[]{:S(2)}) %collective-permute-start.2) | collective-permute-done | bytes 688160 | tf_op jit(solution)/shard_map/ppermute | solution.py:60
  67.3 1.9 collective-permute-start.3
  69.2 4.6 %collective-permute-start.11 = (bf16[3,128,896]{2,1,0:T(8,128)(2,1)}, bf16[3,128,896]{2,1,0:T(8,128)(2,1)S(1)}, u32[]{:S(2)}, u32[]{:S(2)}) collective-permute-start(bf16[3,128,896]{2,1,0:T(8,128)(2,1)} %collective-permute-done.10), channel_id=1, source_target_pairs={{0,120},{8,0},{16,8},{24,16},{32,24},{40,32},{48,40},{56,48},{64,5... | collective-permute-start | bytes 2064392 | tf_op jit(solution)/shard_map/ppermute | solution.py:61
  75.3 9.3 %collective-permute-done.3 = bf16[3,128,896]{2,1,0:T(8,128)(2,1)S(1)} collective-permute-done((bf16[3,128,896]{2,1,0:T(8,128)(2,1)}, bf16[3,128,896]{2,1,0:T(8,128)(2,1)S(1)}, u32[]{:S(2)}, u32[]{:S(2)}) %collective-permute-start.3) | collective-permute-done | bytes 688160 | tf_op jit(solution)/shard_map/ppermute | solution.py:60
  84.6 1.9 collective-permute-start.4
  86.5 4.6 %collective-permute-start.12 = (bf16[3,128,896]{2,1,0:T(8,128)(2,1)S(1)}, bf16[3,128,896]{2,1,0:T(8,128)(2,1)}, u32[]{:S(2)}, u32[]{:S(2)}) collective-permute-start(bf16[3,128,896]{2,1,0:T(8,128)(2,1)S(1)} %collective-permute-done.11), channel_id=1, source_target_pairs={{0,120},{8,0},{16,8},{24,16},{32,24},{40,32},{48,40},{56,48},{64,5... | collective-permute-start | bytes 2064392 | tf_op jit(solution)/shard_map/ppermute | solution.py:61
  91.2 2.0 fusion.61
  93.2 2.0 fusion.60
  95.3 5.7 %collective-permute-done.4 = bf16[3,128,896]{2,1,0:T(8,128)(2,1)} collective-permute-done((bf16[3,128,896]{2,1,0:T(8,128)(2,1)S(1)}, bf16[3,128,896]{2,1,0:T(8,128)(2,1)}, u32[]{:S(2)}, u32[]{:S(2)}) %collective-permute-start.4) | collective-permute-done | bytes 688160 | tf_op jit(solution)/shard_map/ppermute | solution.py:60
  101.0 1.9 collective-permute-start.5
  102.9 4.6 %collective-permute-start.13 = (bf16[3,128,896]{2,1,0:T(8,128)(2,1)}, bf16[3,128,896]{2,1,0:T(8,128)(2,1)}, u32[]{:S(2)}, u32[]{:S(2)}) collective-permute-start(bf16[3,128,896]{2,1,0:T(8,128)(2,1)} %collective-permute-done.12), channel_id=1, source_target_pairs={{0,120},{8,0},{16,8},{24,16},{32,24},{40,32},{48,40},{56,48},{64,5... | collective-permute-start | bytes 2064392 | tf_op jit(solution)/shard_map/ppermute | solution.py:61
  109.1 1.8 gather_fusion.1
  111.7 1.8 select_bitcast_fusion.2
  113.5 3.2 %collective-permute-done.5 = bf16[3,128,896]{2,1,0:T(8,128)(2,1)} collective-permute-done((bf16[3,128,896]{2,1,0:T(8,128)(2,1)}, bf16[3,128,896]{2,1,0:T(8,128)(2,1)}, u32[]{:S(2)}, u32[]{:S(2)}) %collective-permute-start.5) | collective-permute-done | bytes 688160 | tf_op jit(solution)/shard_map/ppermute | solution.py:60
  116.7 1.9 collective-permute-start.6
  118.6 2.0 fusion.59
  120.6 4.6 %collective-permute-start.14 = (bf16[3,128,896]{2,1,0:T(8,128)(2,1)}, bf16[3,128,896]{2,1,0:T(8,128)(2,1)S(1)}, u32[]{:S(2)}, u32[]{:S(2)}) collective-permute-start(bf16[3,128,896]{2,1,0:T(8,128)(2,1)} %collective-permute-done.13), channel_id=1, source_target_pairs={{0,120},{8,0},{16,8},{24,16},{32,24},{40,32},{48,40},{56,48},{64,5... | collective-permute-start | bytes 2064392 | tf_op jit(solution)/shard_map/ppermute | solution.py:61
  126.0 2.0 fusion.57
  128.0 3.4 %collective-permute-done.6 = bf16[3,128,896]{2,1,0:T(8,128)(2,1)S(1)} collective-permute-done((bf16[3,128,896]{2,1,0:T(8,128)(2,1)}, bf16[3,128,896]{2,1,0:T(8,128)(2,1)S(1)}, u32[]{:S(2)}, u32[]{:S(2)}) %collective-permute-start.6) | collective-permute-done | bytes 688160 | tf_op jit(solution)/shard_map/ppermute | solution.py:60
  131.5 1.9 collective-permute-start.7
  133.4 2.0 fusion.56
  135.5 4.8 %collective-permute-start.15 = (bf16[3,64,896]{2,1,0:T(8,128)(2,1)S(1)}, bf16[3,64,896]{2,1,0:T(8,128)(2,1)S(1)}, u32[]{:S(2)}, u32[]{:S(2)}) collective-permute-start(bf16[3,64,896]{2,1,0:T(8,128)(2,1)S(1)} %slice.228), channel_id=1, source_target_pairs={{0,120},{8,0},{16,8},{24,16},{32,24},{40,32},{48,40},{56,48},{64,5... | collective-permute-start | bytes 1032200 | tf_op jit(solution)/shard_map/ppermute | solution.py:66
  141.1 3.2 %collective-permute-done.15 = bf16[3,64,896]{2,1,0:T(8,128)(2,1)S(1)} collective-permute-done((bf16[3,64,896]{2,1,0:T(8,128)(2,1)S(1)}, bf16[3,64,896]{2,1,0:T(8,128)(2,1)S(1)}, u32[]{:S(2)}, u32[]{:S(2)}) %collective-permute-start.15) | collective-permute-done | bytes 344096 | tf_op jit(solution)/shard_map/ppermute | solution.py:66
  146.1 2.1 fusion.52
  148.1 2.0 fusion.51
  150.9 2.0 fusion.49
  152.9 2.0 fusion.48
  155.8 3.6 %fusion.7 = f32[320,896]{1,0:T(8,128)S(1)} fusion(bf16[2048,896]{1,0:T(8,128)(2,1)} %get-tuple-element.7, bf16[16,40,8,128]{3,2,1,0:T(8,128)(2,1)S(1)} %get-tuple-element.50), kind=kOutput, calls=%fused_computation.18 | convolution fusion | flops 1174405120 | bytes 6127616 | tf_op jit(solution)/shard_map/dot_general | solution.py:84
  159.3 1.5 fusion.9
  161.4 1.6 fusion.3
  163.6 1.5 fusion.4
  165.6 1.6 fusion.14
  167.2 1.7 fusion.2
  169.8 2.4 %gather_fusion = bf16[16,320,2,128]{3,1,2,0:T(8,128)(2,1)} fusion(bf16[320,2,16,128]{3,0,2,1:T(8,128)(2,1)S(1)} %pad_maximum_fusion.1, s32[1024]{0:T(1024)S(1)} %get-tuple-element.54), kind=kCustom, calls=%fused_computation.2 | custom fusion | bytes 5242944 | tf_op jit(solution)/shard_map/jit(_take)/gather | solution.py:97
  172.2 5.0 %copy.119 = bf16[320,2,16,128]{3,2,1,0:T(8,128)(2,1)} copy(bf16[320,2,16,128]{3,0,1,2:T(8,128)(2,1)} %bitcast.273) | data formatting | bytes 5242880 | tf_op jit(solution)/shard_map/jit(_take)/gather | solution.py:97
  177.1 3.7 %gather.10 = bf16[4,80,2,8,256]{4,3,2,1,0:T(8,128)(2,1)S(1)} reshape(bf16[320,2,16,128]{3,2,1,0:T(8,128)(2,1)} %copy.119) | data formatting | bytes 5242880 | tf_op jit(solution)/shard_map/jit(_take)/gather | solution.py:97
  182.1 48.5 %all_to_all.10 = bf16[32,80,2,256]{3,1,2,0:T(8,128)(2,1)S(1)} all-to-all(bf16[32,80,2,256]{3,1,2,0:T(8,128)(2,1)S(1)} %bitcast.274), channel_id=1, replica_groups=mesh['ey'=4,'ez'=16,'tp'=8] {'ey','tp'}, dimensions={0} | all-to-all | bytes 5242880 | tf_op jit(solution)/shard_map/all_to_all | solution.py:103
  (92 shorter events, 22.7 us)
Async XLA Ops:
  0.6 36.8 %copy-start = (bf16[128,2048]{1,0:T(8,128)(2,1)S(1)}, bf16[128,2048]{1,0:T(8,128)(2,1)}, u32[]{:S(2)}) copy-start(bf16[128,2048]{1,0:T(8,128)(2,1)} %param.9) | copy-start | bytes 1572868
  2.9 27.1 %collective-permute-start = (bf16[3,128,896]{2,1,0:T(8,128)(2,1)S(1)}, bf16[3,128,896]{2,1,0:T(8,128)(2,1)S(1)}, u32[]{:S(2)}, u32[]{:S(2)}) collective-permute-start(bf16[3,128,896]{2,1,0:T(8,128)(2,1)S(1)} %pad_maximum_fusion.2), channel_id=1, source_target_pairs={{0,8},{8,16},{16,24},{24,32},{32,40},{40,48},{48,56},{56,64},{64,7... | collective-permute-start | bytes 2064392 | tf_op jit(solution)/shard_map/ppermute | solution.py:60
  7.3 24.6 %collective-permute-start.8 = (bf16[3,128,896]{2,1,0:T(8,128)(2,1)S(1)}, bf16[3,128,896]{2,1,0:T(8,128)(2,1)S(1)}, u32[]{:S(2)}, u32[]{:S(2)}) collective-permute-start(bf16[3,128,896]{2,1,0:T(8,128)(2,1)S(1)} %pad_maximum_fusion.2), channel_id=1, source_target_pairs={{0,120},{8,0},{16,8},{24,16},{32,24},{40,32},{48,40},{56,48},{64,5... | collective-permute-start | bytes 2064392 | tf_op jit(solution)/shard_map/ppermute | solution.py:61
  30.0 27.3 %copy-start.8 = (bf16[3,128,896]{2,1,0:T(8,128)(2,1)}, bf16[3,128,896]{2,1,0:T(8,128)(2,1)S(1)}, u32[]{:S(2)}) copy-start(bf16[3,128,896]{2,1,0:T(8,128)(2,1)S(1)} %collective-permute-done) | copy-start | bytes 2064388
  30.0 18.9 %collective-permute-start.1 = (bf16[3,128,896]{2,1,0:T(8,128)(2,1)S(1)}, bf16[3,128,896]{2,1,0:T(8,128)(2,1)}, u32[]{:S(2)}, u32[]{:S(2)}) collective-permute-start(bf16[3,128,896]{2,1,0:T(8,128)(2,1)S(1)} %collective-permute-done), channel_id=1, source_target_pairs={{0,8},{8,16},{16,24},{24,32},{32,40},{40,48},{48,56},{56,64},{64,7... | collective-permute-start | bytes 2064392 | tf_op jit(solution)/shard_map/ppermute | solution.py:60
  31.9 25.4 %copy-start.4 = (bf16[3,128,896]{2,1,0:T(8,128)(2,1)}, bf16[3,128,896]{2,1,0:T(8,128)(2,1)S(1)}, u32[]{:S(2)}) copy-start(bf16[3,128,896]{2,1,0:T(8,128)(2,1)S(1)} %collective-permute-done.8) | copy-start | bytes 2064388
  32.0 18.9 %collective-permute-start.9 = (bf16[3,128,896]{2,1,0:T(8,128)(2,1)S(1)}, bf16[3,128,896]{2,1,0:T(8,128)(2,1)}, u32[]{:S(2)}, u32[]{:S(2)}) collective-permute-start(bf16[3,128,896]{2,1,0:T(8,128)(2,1)S(1)} %collective-permute-done.8), channel_id=1, source_target_pairs={{0,120},{8,0},{16,8},{24,16},{32,24},{40,32},{48,40},{56,48},{64,5... | collective-permute-start | bytes 2064392 | tf_op jit(solution)/shard_map/ppermute | solution.py:61
  49.0 18.3 %collective-permute-start.2 = (bf16[3,128,896]{2,1,0:T(8,128)(2,1)}, bf16[3,128,896]{2,1,0:T(8,128)(2,1)}, u32[]{:S(2)}, u32[]{:S(2)}) collective-permute-start(bf16[3,128,896]{2,1,0:T(8,128)(2,1)} %collective-permute-done.1), channel_id=1, source_target_pairs={{0,8},{8,16},{16,24},{24,32},{32,40},{40,48},{48,56},{56,64},{64,7... | collective-permute-start | bytes 2064392 | tf_op jit(solution)/shard_map/ppermute | solution.py:60
  50.9 18.3 %collective-permute-start.10 = (bf16[3,128,896]{2,1,0:T(8,128)(2,1)}, bf16[3,128,896]{2,1,0:T(8,128)(2,1)}, u32[]{:S(2)}, u32[]{:S(2)}) collective-permute-start(bf16[3,128,896]{2,1,0:T(8,128)(2,1)} %collective-permute-done.9), channel_id=1, source_target_pairs={{0,120},{8,0},{16,8},{24,16},{32,24},{40,32},{48,40},{56,48},{64,5... | collective-permute-start | bytes 2064392 | tf_op jit(solution)/shard_map/ppermute | solution.py:61
  57.3 16.5 %copy-start.2 = (bf16[128,896]{1,0:T(8,128)(2,1)S(1)}, bf16[128,896]{1,0:T(8,128)(2,1)}, u32[]{:S(2)}) copy-start(bf16[128,896]{1,0:T(8,128)(2,1)} %param.13) | copy-start | bytes 688132
  57.3 16.5 %copy-start.3 = (bf16[128,896]{1,0:T(8,128)(2,1)S(1)}, bf16[128,896]{1,0:T(8,128)(2,1)}, u32[]{:S(2)}) copy-start(bf16[128,896]{1,0:T(8,128)(2,1)} %param.14) | copy-start | bytes 688132
  57.3 50.2 %all-to-all-start = ((bf16[4,2,80,2048]{3,2,1,0:T(8,128)(2,1)}), bf16[4,2,80,2048]{3,2,1,0:T(8,128)(2,1)S(1)}, u32[]{:S(2)}, u32[]{:S(2)}) async-start(bf16[4,2,80,2048]{3,2,1,0:T(8,128)(2,1)} %pad_maximum_fusion), calls=%async_computation | async-start | bytes 5242880 | tf_op jit(solution)/shard_map/all_to_all | solution.py:72
  67.3 17.3 %collective-permute-start.3 = (bf16[3,128,896]{2,1,0:T(8,128)(2,1)}, bf16[3,128,896]{2,1,0:T(8,128)(2,1)S(1)}, u32[]{:S(2)}, u32[]{:S(2)}) collective-permute-start(bf16[3,128,896]{2,1,0:T(8,128)(2,1)} %collective-permute-done.2), channel_id=1, source_target_pairs={{0,8},{8,16},{16,24},{24,32},{32,40},{40,48},{48,56},{56,64},{64,7... | collective-permute-start | bytes 2064392 | tf_op jit(solution)/shard_map/ppermute | solution.py:60
  69.2 17.3 %collective-permute-start.11 = (bf16[3,128,896]{2,1,0:T(8,128)(2,1)}, bf16[3,128,896]{2,1,0:T(8,128)(2,1)S(1)}, u32[]{:S(2)}, u32[]{:S(2)}) collective-permute-start(bf16[3,128,896]{2,1,0:T(8,128)(2,1)} %collective-permute-done.10), channel_id=1, source_target_pairs={{0,120},{8,0},{16,8},{24,16},{32,24},{40,32},{48,40},{56,48},{64,5... | collective-permute-start | bytes 2064392 | tf_op jit(solution)/shard_map/ppermute | solution.py:61
  84.6 18.3 %copy-start.9 = (bf16[3,128,896]{2,1,0:T(8,128)(2,1)}, bf16[3,128,896]{2,1,0:T(8,128)(2,1)S(1)}, u32[]{:S(2)}) copy-start(bf16[3,128,896]{2,1,0:T(8,128)(2,1)S(1)} %collective-permute-done.3) | copy-start | bytes 2064388
  84.6 16.4 %collective-permute-start.4 = (bf16[3,128,896]{2,1,0:T(8,128)(2,1)S(1)}, bf16[3,128,896]{2,1,0:T(8,128)(2,1)}, u32[]{:S(2)}, u32[]{:S(2)}) collective-permute-start(bf16[3,128,896]{2,1,0:T(8,128)(2,1)S(1)} %collective-permute-done.3), channel_id=1, source_target_pairs={{0,8},{8,16},{16,24},{24,32},{32,40},{40,48},{48,56},{56,64},{64,7... | collective-permute-start | bytes 2064392 | tf_op jit(solution)/shard_map/ppermute | solution.py:60
  86.5 16.4 %copy-start.6 = (bf16[3,128,896]{2,1,0:T(8,128)(2,1)}, bf16[3,128,896]{2,1,0:T(8,128)(2,1)S(1)}, u32[]{:S(2)}) copy-start(bf16[3,128,896]{2,1,0:T(8,128)(2,1)S(1)} %collective-permute-done.11) | copy-start | bytes 2064388
  86.5 16.4 %collective-permute-start.12 = (bf16[3,128,896]{2,1,0:T(8,128)(2,1)S(1)}, bf16[3,128,896]{2,1,0:T(8,128)(2,1)}, u32[]{:S(2)}, u32[]{:S(2)}) collective-permute-start(bf16[3,128,896]{2,1,0:T(8,128)(2,1)S(1)} %collective-permute-done.11), channel_id=1, source_target_pairs={{0,120},{8,0},{16,8},{24,16},{32,24},{40,32},{48,40},{56,48},{64,5... | collective-permute-start | bytes 2064392 | tf_op jit(solution)/shard_map/ppermute | solution.py:61
  101.0 15.7 %collective-permute-start.5 = (bf16[3,128,896]{2,1,0:T(8,128)(2,1)}, bf16[3,128,896]{2,1,0:T(8,128)(2,1)}, u32[]{:S(2)}, u32[]{:S(2)}) collective-permute-start(bf16[3,128,896]{2,1,0:T(8,128)(2,1)} %collective-permute-done.4), channel_id=1, source_target_pairs={{0,8},{8,16},{16,24},{24,32},{32,40},{40,48},{48,56},{56,64},{64,7... | collective-permute-start | bytes 2064392 | tf_op jit(solution)/shard_map/ppermute | solution.py:60
  102.9 17.7 %collective-permute-start.13 = (bf16[3,128,896]{2,1,0:T(8,128)(2,1)}, bf16[3,128,896]{2,1,0:T(8,128)(2,1)}, u32[]{:S(2)}, u32[]{:S(2)}) collective-permute-start(bf16[3,128,896]{2,1,0:T(8,128)(2,1)} %collective-permute-done.12), channel_id=1, source_target_pairs={{0,120},{8,0},{16,8},{24,16},{32,24},{40,32},{48,40},{56,48},{64,5... | collective-permute-start | bytes 2064392 | tf_op jit(solution)/shard_map/ppermute | solution.py:61
  111.7 6.9 %copy-start.11 = (bf16[2048,896]{1,0:T(8,128)(2,1)S(1)}, bf16[2048,896]{1,0:T(8,128)(2,1)}, u32[]{:S(2)}) copy-start(bf16[2048,896]{1,0:T(8,128)(2,1)} %get-tuple-element.44) | copy-start | bytes 11010052
  111.7 13.5 %copy-start.10 = (bf16[3,128,896]{2,1,0:T(8,128)(2,1)S(1)}, bf16[3,128,896]{2,1,0:T(8,128)(2,1)}, u32[]{:S(2)}) copy-start(bf16[3,128,896]{2,1,0:T(8,128)(2,1)} %copy-done.9) | copy-start | bytes 2064388
  116.7 14.8 %collective-permute-start.6 = (bf16[3,128,896]{2,1,0:T(8,128)(2,1)}, bf16[3,128,896]{2,1,0:T(8,128)(2,1)S(1)}, u32[]{:S(2)}, u32[]{:S(2)}) collective-permute-start(bf16[3,128,896]{2,1,0:T(8,128)(2,1)} %collective-permute-done.5), channel_id=1, source_target_pairs={{0,8},{8,16},{16,24},{24,32},{32,40},{40,48},{48,56},{56,64},{64,7... | collective-permute-start | bytes 2064392 | tf_op jit(solution)/shard_map/ppermute | solution.py:60
  120.6 14.8 %collective-permute-start.14 = (bf16[3,128,896]{2,1,0:T(8,128)(2,1)}, bf16[3,128,896]{2,1,0:T(8,128)(2,1)S(1)}, u32[]{:S(2)}, u32[]{:S(2)}) collective-permute-start(bf16[3,128,896]{2,1,0:T(8,128)(2,1)} %collective-permute-done.13), channel_id=1, source_target_pairs={{0,120},{8,0},{16,8},{24,16},{32,24},{40,32},{48,40},{56,48},{64,5... | collective-permute-start | bytes 2064392 | tf_op jit(solution)/shard_map/ppermute | solution.py:61
  131.5 9.6 %collective-permute-start.7 = (bf16[3,64,896]{2,1,0:T(8,128)(2,1)S(1)}, bf16[3,64,896]{2,1,0:T(8,128)(2,1)S(1)}, u32[]{:S(2)}, u32[]{:S(2)}) collective-permute-start(bf16[3,64,896]{2,1,0:T(8,128)(2,1)S(1)} %slice.227), channel_id=1, source_target_pairs={{0,8},{8,16},{16,24},{24,32},{32,40},{40,48},{48,56},{56,64},{64,7... | collective-permute-start | bytes 1032200 | tf_op jit(solution)/shard_map/ppermute | solution.py:65
  135.5 8.8 %collective-permute-start.15 = (bf16[3,64,896]{2,1,0:T(8,128)(2,1)S(1)}, bf16[3,64,896]{2,1,0:T(8,128)(2,1)S(1)}, u32[]{:S(2)}, u32[]{:S(2)}) collective-permute-start(bf16[3,64,896]{2,1,0:T(8,128)(2,1)S(1)} %slice.228), channel_id=1, source_target_pairs={{0,120},{8,0},{16,8},{24,16},{32,24},{40,32},{48,40},{56,48},{64,5... | collective-permute-start | bytes 1032200 | tf_op jit(solution)/shard_map/ppermute | solution.py:66
  141.1 9.0 %copy-start.7 = (bf16[3,128,896]{2,1,0:T(8,128)(2,1)S(1)}, bf16[3,128,896]{2,1,0:T(8,128)(2,1)}, u32[]{:S(2)}) copy-start(bf16[3,128,896]{2,1,0:T(8,128)(2,1)} %copy-done.6) | copy-start | bytes 2064388
  146.1 8.9 %copy-start.5 = (bf16[3,128,896]{2,1,0:T(8,128)(2,1)S(1)}, bf16[3,128,896]{2,1,0:T(8,128)(2,1)}, u32[]{:S(2)}) copy-start(bf16[3,128,896]{2,1,0:T(8,128)(2,1)} %copy-done.4) | copy-start | bytes 2064388
  159.3 2.0 copy-start.13
  163.6 2.0 copy-start.12
  182.1 50.9 %copy-start.1 = (bf16[128,2048]{1,0:T(8,128)(2,1)S(1)}, bf16[128,2048]{1,0:T(8,128)(2,1)}, u32[]{:S(2)}) copy-start(bf16[128,2048]{1,0:T(8,128)(2,1)} %param.9) | copy-start | bytes 1572868
